TPU v7x, 32 devices: a whole 2x2x4 slice. The times are simulated.
32 devices in a mesh: dp: 16 (over z, x, core), tensor: 2 (over y).
Axes of the slice: x: 2, y: 2, z: 4, core: 2. Of those that a mesh axis runs over, the one named last changes fastest.
Arguments:
- pixels: bfloat16 [8192, 3328], P('dp', 'tensor'), may hold values from -6 to 6
- item_kinds: int32 [32], P('dp'), may hold values from 0 to 1
- gsd_codes: int32 [32], P('dp'), may hold values from 0 to 7
- w_spectral: bfloat16 [3328, 1024], P('tensor'), may hold values from -0.109375 to 0.109375
- w_rgb: bfloat16 [768, 1024], P('tensor'), may hold values from -0.21875 to 0.21875
- ln1_gain: float32 [1024], replicated, may hold values from 0.5 to 1.5
- ln1_bias: float32 [1024], replicated, may hold values from -1.5 to 1.5
- w_qkv: bfloat16 [1024, 3, 1024], P(None, None, 'tensor'), may hold values from -0.1875 to 0.1875
- q_bias: float32 [1024], P('tensor'), may hold values from -1.5 to 1.5
- v_bias: float32 [1024], P('tensor'), may hold values from -1.5 to 1.5
- w_out: bfloat16 [1024, 1024], P('tensor'), may hold values from -0.5 to 0.5
- out_bias: float32 [1024], replicated, may hold values from -1.5 to 1.5
- ln2_gain: float32 [1024], replicated, may hold values from 0.5 to 1.5
- ln2_bias: float32 [1024], replicated, may hold values from -1.5 to 1.5
- w_fc1: bfloat16 [1024, 4096], P(None, 'tensor'), may hold values from -0.1875 to 0.1875
- fc1_bias: float32 [4096], P('tensor'), may hold values from -1.5 to 1.5
- w_fc2: bfloat16 [4096, 1024], P('tensor'), may hold values from -0.09375 to 0.09375
- fc2_bias: float32 [1024], replicated, may hold values from -1.5 to 1.5
- cotangent: bfloat16 [8192, 1024], P('dp'), may hold values from -6 to 6
Outputs:
- block_out: bfloat16 [8192, 1024], P('dp')
- pixels_grad: bfloat16 [8192, 3328], P('dp', 'tensor')
- spectral_grad: float32 [3328, 1024], P('tensor', 'dp')
- rgb_grad: float32 [768, 1024], P('tensor', 'dp')
- ln1_gain_grad: float32 [1024], P('dp')
- ln1_bias_grad: float32 [1024], P('dp')
- qkv_grad: float32 [1024, 3, 1024], P('dp', None, 'tensor')
- q_bias_grad: float32 [1024], P(('tensor', 'dp'))
- v_bias_grad: float32 [1024], P(('tensor', 'dp'))
- out_grad: float32 [1024, 1024], P('tensor', 'dp')
- out_bias_grad: float32 [1024], P('dp')
- ln2_gain_grad: float32 [1024], P('dp')
- ln2_bias_grad: float32 [1024], P('dp')
- fc1_grad: float32 [1024, 4096], P('dp', 'tensor')
- fc1_bias_grad: float32 [4096], P(('tensor', 'dp'))
- fc2_grad: float32 [4096, 1024], P('tensor', 'dp')
- fc2_bias_grad: float32 [1024], P('dp')
Inputs may be any that keep to these rules, and one draw needn't show every extreme that they name: `item_kinds`: 1 marks an item with all 13 bands, 0 an RGB item whose bands 3 and above are unused. `gsd_codes`: code c stands for a ground sample distance (c + 1) / 4 times the reference one.
All inputs are finite; a program needn't handle non-finite values.
Results may differ from a plain program's by a relative error of at most 0.015.
Values sent between devices are 32-bit elements; how exact they have to be, the bound alone decides.
No kernel may reach another device: no remote copies, remote signals or barrier semaphores. Data moves between devices by JAX's collectives and lax.ppermute only.
A program may use at most 192 MiB of HBM per device.

v0:
```python
import jax
import jax.numpy as jnp
from jax import lax
from jax.sharding import PartitionSpec as P

HEAD_DIM = 64
GRID = 16


EPS = 1e-06
F32 = jnp.float32
BF16 = jnp.bfloat16


def layer_norm(values, gain_vec, shift_vec):
    center = values - jnp.mean(values, -1, keepdims=True)
    spread = jnp.mean(center * center, -1, keepdims=True)
    return center * lax.rsqrt(spread + EPS) * gain_vec + shift_vec


def gsd_positions(codes, grid_side, width):
    gsd_ratio = (codes.astype(jnp.float32) + 1.0) / 4.0
    grid_cells = jnp.arange(grid_side * grid_side)
    row_place = (grid_cells // grid_side).astype(jnp.float32)
    col_place = (grid_cells % grid_side).astype(jnp.float32)
    quarter = width // 4
    frequency = 1.0 / 10000.0 ** (jnp.arange(quarter).astype(jnp.float32) / quarter)
    row_angle = gsd_ratio[:, None, None] * row_place[None, :, None] * frequency[None, None, :]
    col_angle = gsd_ratio[:, None, None] * col_place[None, :, None] * frequency[None, None, :]
    return jnp.concatenate(
        [jnp.sin(row_angle), jnp.cos(row_angle), jnp.sin(col_angle), jnp.cos(col_angle)], -1
    )


def matmul(left, right):
    return jnp.dot(left, right, preferred_element_type=F32)


def matmul_tn(left, right):
    return lax.dot_general(left, right, (((0,), (0,)), ((), ())), preferred_element_type=F32)


def matmul_nt(left, right):
    return lax.dot_general(left, right, (((1,), (1,)), ((), ())), preferred_element_type=F32)


def exact_gelu(values):
    return jax.nn.gelu(values, approximate=False)


def local(
    pixels,
    item_kinds,
    gsd_codes,
    w_spectral,
    w_rgb,
    ln1_gain,
    ln1_bias,
    w_qkv,
    q_bias,
    v_bias,
    w_out,
    out_bias,
    ln2_gain,
    ln2_bias,
    w_fc1,
    fc1_bias,
    w_fc2,
    fc2_bias,
    cotangent,
):
    item_count = item_kinds.shape[0]
    row_count = pixels.shape[0]
    per_item = row_count // item_count
    width = w_out.shape[1]
    half_pix = w_rgb.shape[0] // 3
    band_count = pixels.shape[1] // half_pix
    head_size = HEAD_DIM
    local_heads = w_out.shape[0] // head_size
    score_scale = head_size ** (-0.5)
    pix_items = pixels.reshape(item_count, per_item, pixels.shape[1])

    def narrow_rgb(block):
        return block.reshape(per_item, half_pix, band_count)[:, :, :3].reshape(
            per_item, half_pix * 3
        )

    def embed_item(pair):
        block, kind_val = pair

        def spectral_embed(block_in):
            return matmul(block_in, w_spectral)

        def rgb_embed(block_in):
            return matmul(narrow_rgb(block_in), w_rgb)

        return lax.cond(kind_val == 1, spectral_embed, rgb_embed, block)

    embed_part = lax.map(embed_item, (pix_items, item_kinds)).reshape(row_count, width)
    embed_full = lax.psum(embed_part, "tensor")
    resid0 = embed_full + gsd_positions(gsd_codes, GRID, width).reshape(row_count, width)
    norm1_val, norm1_pull = jax.vjp(layer_norm, resid0, ln1_gain, ln1_bias)
    attn_in = norm1_val.astype(BF16)
    qkv_bias = jnp.stack([q_bias, jnp.zeros_like(q_bias), v_bias])
    qkv_val = (
        jnp.einsum("td,dch->tch", attn_in, w_qkv, preferred_element_type=F32) + qkv_bias
    ).astype(BF16)
    shaped = qkv_val.reshape(item_count, per_item, 3, local_heads, head_size)
    query_rows = shaped[:, :, 0]
    key_rows = shaped[:, :, 1]
    value_rows = shaped[:, :, 2]
    scores = (
        jnp.einsum("iqhe,ikhe->ihqk", query_rows, key_rows, preferred_element_type=F32)
        * score_scale
    )
    top_score = jnp.max(scores, -1, keepdims=True)
    expo = jnp.exp(scores - top_score)
    total = jnp.sum(expo, -1, keepdims=True)
    probs = expo / total
    probs_low = probs.astype(BF16)
    log_total = top_score + jnp.log(total)
    mixed = jnp.einsum("ihqk,ikhe->iqhe", probs_low, value_rows, preferred_element_type=F32)
    attn_val = mixed.reshape(row_count, local_heads * head_size).astype(BF16)
    resid1 = resid0 + (lax.psum(matmul(attn_val, w_out), "tensor") + out_bias)
    norm2_val, norm2_pull = jax.vjp(layer_norm, resid1, ln2_gain, ln2_bias)
    norm2_low = norm2_val.astype(BF16)
    hidden_pre = matmul(norm2_low, w_fc1) + fc1_bias
    hidden_val, gelu_pull = jax.vjp(exact_gelu, hidden_pre)
    hidden_act = hidden_val.astype(BF16)
    resid2 = resid1 + (lax.psum(matmul(hidden_act, w_fc2), "tensor") + fc2_bias)
    block_out = resid2.astype(BF16)
    grad_out = cotangent.astype(F32)
    fc2_bias_grad = jnp.sum(grad_out, 0)
    fc2_grad = matmul_tn(hidden_act, cotangent)
    grad_act = matmul_nt(cotangent, w_fc2)
    grad_pre = gelu_pull(grad_act)[0].astype(BF16)
    fc1_grad = matmul_tn(norm2_low, grad_pre)
    fc1_bias_grad = jnp.sum(grad_pre.astype(F32), 0)
    grad_norm2 = lax.psum(matmul_nt(grad_pre, w_fc1), "tensor")
    grad_resid1_norm, ln2_gain_grad, ln2_bias_grad = norm2_pull(grad_norm2)
    grad_resid1 = grad_out + grad_resid1_norm
    mlp_summed = (
        lax.psum_scatter(ln2_gain_grad, "dp", scatter_dimension=0, tiled=True),
        lax.psum_scatter(ln2_bias_grad, "dp", scatter_dimension=0, tiled=True),
        lax.psum_scatter(fc1_grad, "dp", scatter_dimension=0, tiled=True),
        lax.psum_scatter(fc1_bias_grad, "dp", scatter_dimension=0, tiled=True),
        lax.psum_scatter(fc2_grad, "dp", scatter_dimension=1, tiled=True),
        lax.psum_scatter(fc2_bias_grad, "dp", scatter_dimension=0, tiled=True),
    )
    grad_attn = grad_resid1.astype(BF16)
    out_bias_grad = jnp.sum(grad_attn.astype(F32), 0)
    out_grad = matmul_tn(attn_val, grad_attn)
    grad_mixed = (
        matmul_nt(grad_attn, w_out)
        .astype(BF16)
        .reshape(item_count, per_item, local_heads, head_size)
    )
    again = (
        jnp.einsum("iqhe,ikhe->ihqk", query_rows, key_rows, preferred_element_type=F32)
        * score_scale
    )
    probs_used = jnp.exp(again - log_total)
    probs_used_low = probs_used.astype(BF16)
    grad_probs = jnp.einsum("iqhe,ikhe->ihqk", grad_mixed, value_rows, preferred_element_type=F32)
    grad_value = jnp.einsum(
        "ihqk,iqhe->ikhe", probs_used_low, grad_mixed, preferred_element_type=F32
    )
    row_dot = jnp.sum(probs_used * grad_probs, -1, keepdims=True)
    grad_scores = (probs_used * (grad_probs - row_dot)).astype(BF16)
    grad_query = (
        jnp.einsum("ihqk,ikhe->iqhe", grad_scores, key_rows, preferred_element_type=F32)
        * score_scale
    )
    grad_key = (
        jnp.einsum("ihqk,iqhe->ikhe", grad_scores, query_rows, preferred_element_type=F32)
        * score_scale
    )
    grad_qkv = jnp.stack([grad_query, grad_key, grad_value], 2).reshape(
        row_count, 3, local_heads * head_size
    )
    grad_qkv = grad_qkv.astype(BF16)
    qkv_grad = jnp.einsum("td,tch->dch", attn_in, grad_qkv, preferred_element_type=F32)
    bias_sums = jnp.sum(grad_qkv.astype(F32), 0)
    q_bias_grad = bias_sums[0]
    v_bias_grad = bias_sums[2]
    grad_norm1_part = jnp.einsum("tch,dch->td", grad_qkv, w_qkv, preferred_element_type=F32)
    grad_norm1 = lax.psum(grad_norm1_part, "tensor")
    grad_resid0_norm, ln1_gain_grad, ln1_bias_grad = norm1_pull(grad_norm1)
    grad_resid0 = (grad_resid1 + grad_resid0_norm).astype(BF16)
    grad_items = grad_resid0.reshape(item_count, per_item, width)

    def embed_back(carry, triple):
        block, grad_block, kind_val = triple

        def spectral_back(sums_in):
            spec_sum, rgb_sum = sums_in
            pix_grad = matmul_nt(grad_block, w_spectral)
            return (spec_sum + matmul_tn(block, grad_block), rgb_sum, pix_grad)

        def rgb_back(sums_in):
            spec_sum, rgb_sum = sums_in
            narrow_grad = matmul_nt(grad_block, w_rgb).reshape(per_item, half_pix, 3)
            padded = jnp.pad(narrow_grad, ((0, 0), (0, 0), (0, band_count - 3))).reshape(
                per_item, half_pix * band_count
            )
            return (spec_sum, rgb_sum + matmul_tn(narrow_rgb(block), grad_block), padded)

        spec_sum, rgb_sum, pix_grad = lax.cond(kind_val == 1, spectral_back, rgb_back, carry)
        return ((spec_sum, rgb_sum), pix_grad.astype(BF16))

    zero_sums = (jnp.zeros(w_spectral.shape, F32), jnp.zeros(w_rgb.shape, F32))
    (spectral_grad, rgb_grad), pix_grads = lax.scan(
        embed_back, zero_sums, (pix_items, grad_items, item_kinds)
    )
    pixels_grad = pix_grads.reshape(row_count, pixels.shape[1])
    rest_summed = (
        lax.psum_scatter(spectral_grad, "dp", scatter_dimension=1, tiled=True),
        lax.psum_scatter(rgb_grad, "dp", scatter_dimension=1, tiled=True),
        lax.psum_scatter(ln1_gain_grad, "dp", scatter_dimension=0, tiled=True),
        lax.psum_scatter(ln1_bias_grad, "dp", scatter_dimension=0, tiled=True),
        lax.psum_scatter(qkv_grad, "dp", scatter_dimension=0, tiled=True),
        lax.psum_scatter(q_bias_grad, "dp", scatter_dimension=0, tiled=True),
        lax.psum_scatter(v_bias_grad, "dp", scatter_dimension=0, tiled=True),
        lax.psum_scatter(out_grad, "dp", scatter_dimension=1, tiled=True),
        lax.psum_scatter(out_bias_grad, "dp", scatter_dimension=0, tiled=True),
    )
    summed = tuple(rest_summed) + tuple(mlp_summed)
    return (
        block_out,
        pixels_grad,
        summed[0],
        summed[1],
        summed[2],
        summed[3],
        summed[4],
        summed[5],
        summed[6],
        summed[7],
        summed[8],
        summed[9],
        summed[10],
        summed[11],
        summed[12],
        summed[13],
        summed[14],
    )


def solution(mesh):
    in_specs = (
        P("dp", "tensor"),
        P("dp"),
        P("dp"),
        P("tensor", None),
        P("tensor", None),
        P(),
        P(),
        P(None, None, "tensor"),
        P("tensor"),
        P("tensor"),
        P("tensor", None),
        P(),
        P(),
        P(),
        P(None, "tensor"),
        P("tensor"),
        P("tensor", None),
        P(),
        P("dp", None),
    )
    out_specs = (
        P("dp", None),
        P("dp", "tensor"),
        P("tensor", "dp"),
        P("tensor", "dp"),
        P("dp"),
        P("dp"),
        P("dp", None, "tensor"),
        P(("tensor", "dp")),
        P(("tensor", "dp")),
        P("tensor", "dp"),
        P("dp"),
        P("dp"),
        P("dp"),
        P("dp", "tensor"),
        P(("tensor", "dp")),
        P("tensor", "dp"),
        P("dp"),
    )
    return jax.shard_map(local, mesh=mesh, in_specs=in_specs, out_specs=out_specs, check_vma=False)
```

profile of v0, /device:TPU:0, one launch (start us, length us, event | category | flops | bytes accessed | tf_op | source)
XLA Modules:
  0.0 976.0 jit_solution(6887879415420435455)
XLA Ops:
  7.3 30.9 %while.24 = (s32[]{:T(128)}, f32[2,256,1024]{2,1,0:T(8,128)}, s32[2]{0:T(128)}, bf16[2,256,1664]{2,1,0:T(8,128)(2,1)}, bf16[384,1024]{1,0:T(8,128)(2,1)}, /*inde...) while((s32[]{:T(128)}, f32[2,256,1024]{2,1,0:T(8,128)}, s32[2]{0:T(128)}, bf16[2,256,1664]{2,1,0:T(8,128)(2,1)}, ...), condition=%wide.region_3.4_spmd, body=%wide.region_0.3_spmd.sunk | while | flops 872415232 | bytes 10027175 | solution.py:99
  9.3 2.1 dynamic-slice_bitcast_fusion.6
  11.4 9.0 conditional.4
  11.4 2.2 copy.104
  13.7 2.2 reshape.263
  17.8 2.7 convolution_bitcast_fusion
  20.5 2.3 constant_dynamic-update-slice_fusion.7
  24.6 2.1 dynamic-slice_bitcast_fusion.6
  26.8 9.0 conditional.4
  26.8 2.2 copy.104
  29.0 2.2 reshape.263
  33.1 2.7 convolution_bitcast_fusion
  35.8 2.3 constant_dynamic-update-slice_fusion.7
  39.0 5.4 multiply_sine_fusion.1
  44.4 59.5 %all-reduce.17.cloned.1.call-done = f32[512,1024]{1,0:T(8,128)} async-done(((f32[512,1024]{1,0:T(8,128)}), f32[512,1024]{1,0:T(8,128)}) %all-reduce.17.cloned.1.call-update) | async-done | bytes 2097168 | tf_op jit(solution)/shard_map/psum | solution.py:100
  103.9 2.4 fusion.54
  107.7 3.1 add_convert_fusion.1
  110.8 5.1 reshape.297
  115.9 3.6 fusion.55
  119.5 2.5 copy.151
  122.0 2.5 copy.152
  124.5 2.5 copy.153
  127.0 2.0 multiply_reduce_fusion.1
  133.4 2.1 fusion.58
  136.0 62.6 %all-reduce.19.cloned.1.call-done = f32[512,1024]{1,0:T(8,128)} async-done(((f32[512,1024]{1,0:T(8,128)}), f32[512,1024]{1,0:T(8,128)}) %all-reduce.19.cloned.1.call-update) | async-done | bytes 2097168 | tf_op jit(solution)/shard_map/psum | solution.py:124
  198.6 2.7 fusion.53
  202.7 2.5 fusion.48
  205.2 13.4 %convert_reduce_fusion = (f32[2048]{0:T(1024)S(1)}, bf16[512,2048]{1,0:T(8,128)(2,1)S(1)}, f32[512,2048]{1,0:T(8,128)}) fusion(f32[512,2048]{1,0:T(8,128)S(1)} %fusion.48, f32[2048]{0:T(1024)S(1)} %copy-done.38, bf16[512,1024]{1,0:T(8,128)(2,1)S(1)} %copy-done.23, bf16[2048,1024]{1,0:T(8,128)(2,1)S(1)} %copy-done.44), kind=kOutput, calls=%fused_computation.14 | convolution fusion | flops 2226124800 | bytes 15745024 | tf_op jit(solution)/shard_map/dot_general | solution.py:44
  220.0 3.7 fusion.60
  223.8 4.6 multiply_convert_fusion.1
  229.8 3.7 fusion.59
  233.5 53.3 %all-reduce.21.cloned.1.call-done = f32[512,1024]{1,0:T(8,128)} async-done(((f32[512,1024]{1,0:T(8,128)}), f32[512,1024]{1,0:T(8,128)}) %all-reduce.21.cloned.1.call-update) | async-done | bytes 2097168 | tf_op jit(solution)/shard_map/psum | solution.py:139
  286.8 3.1 multiply_reduce_fusion.2
  294.9 2.5 reshape.298
  297.4 2.5 copy.116
  299.9 4.1 fusion.24
  309.2 2.5 copy.139
  311.7 2.5 reshape.287
  314.2 2.5 copy.137
  316.7 2.6 reshape.285
  319.3 2.5 copy.138
  321.8 2.6 reshape.286
  327.8 3.2 convolution_bitcast_fusion.2
  332.0 3.3 fusion.61
  335.6 103.7 %all-reduce.23.cloned.1.call-done = (f32[512,1024]{1,0:T(8,128)}, f32[512,1024]{1,0:T(8,128)}) async-done(((f32[512,1024]{1,0:T(8,128)}, f32[512,1024]{1,0:T(8,128)}), (f32[512,1024]{1,0:T(8,128)}, f32[512,1024]{1,0:T(8,128)})) %all-reduce.23.cloned.1.call-update) | async-done | bytes 4194320 | tf_op jit(solution)/shard_map/psum | solution.py:130
  439.4 2.5 multiply_reduce_fusion.3
  446.6 3.7 broadcast_in_dim.30
  450.4 28.6 %while.25 = (s32[]{:T(128)}, f32[1664,1024]{1,0:T(8,128)}, f32[384,1024]{1,0:T(8,128)}, bf16[2,256,1664]{2,1,0:T(8,128)(2,1)}, s32[2]{0:T(128)S(1)}, /*index=5*/...) while((s32[]{:T(128)}, f32[1664,1024]{1,0:T(8,128)}, ...), condition=%wide.region_23.24_spmd, body=%wide.region_20.23_spmd.sunk | while | flops 1746960384 | bytes 30802216 | solution.py:212
  454.0 8.2 conditional.5
  459.2 3.0 convolution_add_fusion
  462.1 1.6 copy.157
  468.3 8.1 conditional.5
  473.5 2.9 convolution_add_fusion
  479.0 3.2 copy.130
  482.2 6.0 fusion.44
  489.8 7.4 fusion.47
  499.1 5.6 fusion.62
  504.8 7.7 copy.129
  516.0 68.1 %all-reduce.10 = (f32[1024]{0:T(1024)S(1)}, f32[1024]{0:T(1024)S(1)}, f32[512]{0:T(512)S(1)}, f32[512]{0:T(512)S(1)}, f32[1024]{0:T(1024)S(1)}, /*index=5*/f32[1...) all-reduce(f32[1024]{0:T(1024)S(1)} %get-tuple-element.208, ...), channel_id=4, replica_groups=mesh['dp'=16,'tensor'=2] {'dp'}, use_global_device_ids=true, to_apply=%region_27.28.clone | all-reduce | flops 9216 | bytes 73728
  589.3 4.2 add_convert_fusion.3
  593.5 63.6 %reduce-scatter.11.cloned.1.call-done = f32[64,3,512]{2,0,1:T(8,128)} async-done(((f32[1024,3,512]{2,0,1:T(8,128)}), f32[64,3,512]{2,0,1:T(8,128)}) %reduce-scatter.11.cloned.1.call-update) | async-done | bytes 393232 | tf_op jit(solution)/shard_map/reduce_scatter | solution.py:221
  657.1 109.1 %reduce-scatter.15.cloned.1.call-done = f32[64,2048]{1,0:T(8,128)} async-done(((f32[1024,2048]{1,0:T(8,128)}), f32[64,2048]{1,0:T(8,128)}) %reduce-scatter.15.cloned.1.call-update) | async-done | bytes 524304 | tf_op jit(solution)/shard_map/reduce_scatter | solution.py:145
  766.2 109.6 %reduce-scatter.17.cloned.1.call-done = f32[2048,64]{0,1:T(8,128)} async-done(((f32[2048,1024]{0,1:T(8,128)}), f32[2048,64]{0,1:T(8,128)}) %reduce-scatter.17.cloned.1.call-update) | async-done | bytes 524304 | tf_op jit(solution)/shard_map/reduce_scatter | solution.py:147
  875.7 93.0 %reduce-scatter.7.cloned.1.call-done = f32[1664,64]{0,1:T(8,128)} async-done(((f32[1664,1024]{0,1:T(8,128)}), f32[1664,64]{0,1:T(8,128)}) %reduce-scatter.7.cloned.1.call-update) | async-done | bytes 426000 | tf_op jit(solution)/shard_map/reduce_scatter | solution.py:217
  (216 shorter events, 67.2 us)
Async XLA Ops:
  7.2 100.5 %copy-start = (bf16[1024,3,512]{2,0,1:T(8,128)(2,1)S(1)}, bf16[1024,3,512]{2,0,1:T(8,128)(2,1)}, u32[]{:S(2)}) copy-start(bf16[1024,3,512]{2,0,1:T(8,128)(2,1)} %param.34) | copy-start | bytes 9437188
  7.2 96.7 %all-reduce.17.cloned.1.call-start = ((), (), s32[]{:S(2)}) async-start(), calls=%async_computation.6 | async-start | bytes 4194304 | tf_op jit(solution)/shard_map/psum | solution.py:100
  38.1 0.7 copy-start.49
  38.1 0.8 copy-start.41
  38.1 0.8 copy-start.42
  38.1 160.5 %all-reduce.19.cloned.1.call-start = ((), (), s32[]{:S(2)}) async-start(), calls=%async_computation.7 | async-start | bytes 4194304 | tf_op jit(solution)/shard_map/psum | solution.py:124
  106.3 1.4 copy-start.9
  106.4 1.4 copy-start.36
  106.4 1.3 copy-start.46
  129.0 2.0 copy-start.2
  129.0 1.9 copy-start.29
  132.0 1.5 copy-start.34
  132.6 0.8 copy-start.17
  133.4 65.2 %copy-start.39 = (f32[1024]{0:T(1024)S(1)}, f32[1024]{0:T(1024)}, u32[]{:S(2)}) copy-start(f32[1024]{0:T(1024)} %param.38) | copy-start | bytes 12292
  135.5 151.2 %all-reduce.21.cloned.1.call-start = ((), (), s32[]{:S(2)}) async-start(), calls=%async_computation.8 | async-start | bytes 4194304 | tf_op jit(solution)/shard_map/psum | solution.py:139
  198.6 4.0 copy-start.43
  201.3 1.3 copy-start.6
  201.3 1.3 copy-start.37
  201.3 1.3 copy-start.48
  202.7 2.5 copy-start.23
  202.7 2.5 copy-start.38
  202.7 2.5 copy-start.44
  205.2 13.5 %copy-start.22 = (f32[512,2048]{1,0:T(8,128)}, f32[512,2048]{1,0:T(8,128)S(1)}, u32[]{:S(2)}) copy-start(f32[512,2048]{1,0:T(8,128)S(1)} %fusion.48) | copy-start | bytes 12582916
  218.7 1.3 copy-start.52
  223.7 215.6 %all-reduce.23.cloned.1.call-start = ((), (), s32[]{:S(2)}) async-start(), calls=%async_computation.15 | async-start | bytes 8388608 | tf_op jit(solution)/shard_map/psum | solution.py:130
  223.8 6.0 copy-start.45
  228.4 1.4 copy-start.32
  286.8 3.2 copy-start.7
  286.8 3.5 copy-start.15
  290.2 1.2 copy-start.24
  291.0 1.4 copy-start.12
  291.5 1.8 copy-start.35
  292.3 1.0 copy-start.21
  299.9 4.1 copy-start.3
  299.9 4.1 copy-start.16
  299.9 4.1 copy-start.30
  305.2 1.1 copy-start.19
  306.3 1.6 copy-start.20
  324.3 2.2 copy-start.31
  326.6 1.2 copy-start.27
  330.9 1.0 copy-start.18
  331.0 108.4 %copy-start.10 = (f32[512,1024]{1,0:T(8,128)S(1)}, f32[512,1024]{1,0:T(8,128)}, u32[]{:S(2)}) copy-start(f32[512,1024]{1,0:T(8,128)} %copy-done.9) | copy-start | bytes 6291460
  331.0 262.5 %reduce-scatter.13.cloned.1.call-start = ((), (), s32[]{:S(2)}) async-start(), calls=%async_computation.12 | async-start | bytes 2228224 | tf_op jit(solution)/shard_map/reduce_scatter | solution.py:224
  335.3 258.1 %reduce-scatter.9.cloned.1.call-start = ((), (), s32[]{:S(2)}) async-start(), calls=%async_computation.10 | async-start | bytes 1671168 | tf_op jit(solution)/shard_map/reduce_scatter | solution.py:218
  439.4 2.5 copy-start.14
  441.9 1.6 copy-start.13
  441.9 1.8 copy-start.25
  446.6 3.8 copy-start.4
  446.6 3.8 copy-start.50
  462.1 2.6 copy-start.5
  476.4 2.6 copy-start.5
  479.0 3.3 copy-start.11
  479.0 3.3 copy-start.47
  482.2 174.9 %reduce-scatter.11.cloned.1.call-start = ((), (), s32[]{:S(2)}) async-start(), calls=%async_computation.11 | async-start | bytes 6684672 | tf_op jit(solution)/shard_map/reduce_scatter | solution.py:221
  488.3 1.6 copy-start.8
  488.3 277.9 %reduce-scatter.15.cloned.1.call-start = ((), (), s32[]{:S(2)}) async-start(), calls=%async_computation.13 | async-start | bytes 8912896 | tf_op jit(solution)/shard_map/reduce_scatter | solution.py:145
  497.2 1.2 copy-start.26
  497.2 1.9 copy-start.33
  497.2 378.5 %reduce-scatter.17.cloned.1.call-start = ((), (), s32[]{:S(2)}) async-start(), calls=%async_computation.14 | async-start | bytes 8912896 | tf_op jit(solution)/shard_map/reduce_scatter | solution.py:147
  504.8 464.0 %reduce-scatter.7.cloned.1.call-start = ((), (), s32[]{:S(2)}) async-start(), calls=%async_computation.9 | async-start | bytes 7241728 | tf_op jit(solution)/shard_map/reduce_scatter | solution.py:217
  512.5 0.7 copy-start.51
  512.5 3.2 copy-start.28
  512.5 76.7 %copy-start.40 = (f32[1024]{0:T(1024)S(1)}, f32[1024]{0:T(1024)}, u32[]{:S(2)}) copy-start(f32[1024]{0:T(1024)} %param.44) | copy-start | bytes 12292
  589.3 379.5 %copy-start.1 = (bf16[1024,3,512]{2,0,1:T(8,128)(2,1)S(1)}, bf16[1024,3,512]{2,0,1:T(8,128)(2,1)}, u32[]{:S(2)}) copy-start(bf16[1024,3,512]{2,0,1:T(8,128)(2,1)} %param.34) | copy-start | bytes 9437188
Sparse Core Ops, SparseCore 0:
  38.3 65.5 all-reduce.16
  135.7 62.9 all-reduce.18
  223.8 62.8 all-reduce.20
  331.1 108.2 all-reduce.22
  443.5 61.5 reduce-scatter.12
  509.7 58.6 reduce-scatter.8
  572.9 84.1 reduce-scatter.10
  662.3 103.8 reduce-scatter.14
  771.4 104.3 reduce-scatter.16
  880.6 88.0 reduce-scatter.6
where the time goes:
time: 985 us; the launch traced here: 976 us
  waiting for transfers between devices  655 us (66%)
  local copies, waits for them, and re-layouts  122 us (12%)
  matrix products  78.8 us (8%)
  blocking collectives  68.1 us (7%)
  other arithmetic  31.2 us (3%)
  between operations  17.1 us (2%)
    reduce_scatter x1, waiting for transfers between devices, local(): lax.psum_scatter(fc2_grad, 'dp', scatter_dimension=1, tiled=True)  110 us
    reduce_scatter x1, waiting for transfers between devices, local(): lax.psum_scatter(fc1_grad, 'dp', scatter_dimension=0, tiled=True)  109 us
    psum x1, waiting for transfers between devices, local(): resid2 = resid1 + (lax.psum(matmul(hidden_act, w_fc2), 'tensor') + fc2_bias)  104 us
    reduce_scatter x1, waiting for transfers between devices, local(): lax.psum_scatter(spectral_grad, 'dp', scatter_dimension=1, tiled=True)  93 us
    unnamed x1, blocking collectives  68.1 us
    reduce_scatter x1, waiting for transfers between devices, local(): lax.psum_scatter(qkv_grad, 'dp', scatter_dimension=0, tiled=True)  63.6 us
    psum x1, waiting for transfers between devices, local(): resid1 = resid0 + (lax.psum(matmul(attn_val, w_out), 'tensor') + out_bias)  62.6 us
    psum x1, waiting for transfers between devices, local(): embed_full = lax.psum(embed_part, 'tensor')  59.5 us
  transfers between devices with their start and end apart: 10, of which 8 were waited for; matrix products, arithmetic and copies ran while one was open for 10% of the time, Pallas kernels for 0%

commit v1 on v0

v1 whole, which is shorter than its diff:
```python
import functools

import jax
import jax.numpy as jnp
from jax import lax
from jax.experimental import pallas as pl
from jax.experimental.pallas import tpu as pltpu
from jax.sharding import PartitionSpec as P

HEAD_DIM = 64
GRID = 16
EPS = 1e-06
F32 = jnp.float32
BF16 = jnp.bfloat16
LANES = 128
VMEM_LIMIT = 56 * 1024 * 1024
QUAD = 256


def nn(left, right):
    return lax.dot_general(left, right, (((1,), (0,)), ((), ())), preferred_element_type=F32)


def nt(left, right):
    return lax.dot_general(left, right, (((1,), (1,)), ((), ())), preferred_element_type=F32)


def tn(left, right):
    return lax.dot_general(left, right, (((0,), (0,)), ((), ())), preferred_element_type=F32)


def params(**extra):
    return pltpu.CompilerParams(vmem_limit_bytes=VMEM_LIMIT, **extra)


def cost(flops, nbytes, trans=0):
    return pl.CostEstimate(flops=int(flops), bytes_accessed=int(nbytes), transcendentals=int(trans))


def whole(shape):
    return pl.BlockSpec(shape, lambda *_: (0,) * len(shape))


def norm_parts(values):
    center = values - jnp.mean(values, -1, keepdims=True)
    spread = jnp.mean(center * center, -1, keepdims=True)
    inverse = lax.rsqrt(spread + EPS)
    return center * inverse, inverse


def norm_back(normed, inverse, grad, gain):
    scaled = grad * gain
    mean_scaled = jnp.mean(scaled, -1, keepdims=True)
    mean_cross = jnp.mean(scaled * normed, -1, keepdims=True)
    return inverse * (scaled - mean_scaled - normed * mean_cross)


def column_sum(values):
    return jnp.sum(values, 0, keepdims=True)


def embed_kernel(kinds, pix_ref, wspec_ref, wrgb_ref, pick_ref, part_ref, mixed_ref, *, item):
    step = pl.program_id(0)
    wide = pix_ref.shape[1]
    spectral = kinds[item] == 1

    @pl.when(spectral)
    def _():
        @pl.when(step == 0)
        def _():
            mixed_ref[:, :wide] = pix_ref[...]
            mixed_ref[:, wide:] = jnp.zeros((pix_ref.shape[0], wrgb_ref.shape[0]), BF16)

        part_ref[...] = nn(pix_ref[...], wspec_ref[...])

    @pl.when(jnp.logical_not(spectral))
    def _():
        @pl.when(step == 0)
        def _():
            mixed_ref[:, :wide] = jnp.zeros(pix_ref.shape, BF16)
            mixed_ref[:, wide:] = nn(pix_ref[...], pick_ref[...]).astype(BF16)

        part_ref[...] = nn(mixed_ref[:, wide:], wrgb_ref[...])


def embed(kinds, pixels, w_spectral, w_rgb, pick, item, rows):
    wide, width = w_spectral.shape
    narrow = w_rgb.shape[0]
    tile = 256
    return pl.pallas_call(
        functools.partial(embed_kernel, item=item),
        grid_spec=pltpu.PrefetchScalarGridSpec(
            num_scalar_prefetch=1,
            grid=(width // tile,),
            in_specs=[
                pl.BlockSpec((rows, wide), lambda n, *_: (item, 0)),
                pl.BlockSpec((wide, tile), lambda n, *_: (0, n)),
                pl.BlockSpec((narrow, tile), lambda n, *_: (0, n)),
                whole((wide, narrow)),
            ],
            out_specs=[
                pl.BlockSpec((rows, tile), lambda n, *_: (0, n)),
                whole((rows, wide + narrow)),
            ],
        ),
        out_shape=[
            jax.ShapeDtypeStruct((rows, width), F32),
            jax.ShapeDtypeStruct((rows, wide + narrow), BF16),
        ],
        compiler_params=params(),
        cost_estimate=cost(2 * rows * wide * width, 2 * wide * width + 4 * rows * width),
        name="embed",
    )(kinds, pixels, w_spectral, w_rgb, pick)


def pair_masks(rows):
    lane = lax.broadcasted_iota(jnp.int32, (rows, LANES), 1)
    return lane < HEAD_DIM, lane >= HEAD_DIM


def only(mask, values):
    return jnp.where(mask, values, jnp.zeros_like(values))


def softmax_rows(query, key):
    scores = nt(query, key) * (HEAD_DIM**-0.5)
    expo = jnp.exp(scores - jnp.max(scores, -1, keepdims=True))
    return expo / jnp.sum(expo, -1, keepdims=True)


def attn_forward_kernel(
    part_ref, recv_ref, table_ref, gain_ref, bias_ref, wqkv_ref, qb_ref, vb_ref, wout_ref,
    x0_ref, a1_ref, qkv_ref, o_ref, opart_ref,
):
    quad = pl.program_id(0)
    rows, width = part_ref.shape

    @pl.when(quad == 0)
    def _():
        side = table_ref.shape[0]
        half = table_ref.shape[1]
        table = table_ref[...]
        by_row = jnp.broadcast_to(table[:, None, :], (side, side, half)).reshape(rows, half)
        by_col = jnp.broadcast_to(table[None, :, :], (side, side, half)).reshape(rows, half)
        left = part_ref[:, :half] + recv_ref[:, :half] + by_row
        right = part_ref[:, half:] + recv_ref[:, half:] + by_col
        x0_ref[:, :half] = left
        x0_ref[:, half:] = right
        normed, _inv = norm_parts(x0_ref[...])
        a1_ref[...] = (normed * gain_ref[...] + bias_ref[...]).astype(BF16)
        opart_ref[...] = jnp.zeros_like(opart_ref)

    a1 = a1_ref[...]
    query = (nn(a1, wqkv_ref[0]) + qb_ref[...]).astype(BF16)
    key = nn(a1, wqkv_ref[1]).astype(BF16)
    value = (nn(a1, wqkv_ref[2]) + vb_ref[...]).astype(BF16)
    qkv_ref[0] = query
    qkv_ref[1] = key
    qkv_ref[2] = value
    masks = pair_masks(rows)
    for pair in range(query.shape[1] // LANES):
        span = slice(pair * LANES, (pair + 1) * LANES)
        q2, k2, v2 = query[:, span], key[:, span], value[:, span]
        mixed = None
        for mask in masks:
            probs = softmax_rows(only(mask, q2), k2).astype(BF16)
            term = nn(probs, only(mask, v2))
            mixed = term if mixed is None else mixed + term
        o_ref[:, span] = mixed.astype(BF16)
    opart_ref[...] += nn(o_ref[...], wout_ref[...])


def attn_forward(part, recv, table, gain, bias, w_qkv, q_bias, v_bias, w_out):
    rows, width = part.shape
    heads_wide = w_out.shape[0]
    steps = heads_wide // QUAD
    return pl.pallas_call(
        attn_forward_kernel,
        grid=(steps,),
        in_specs=[
            whole(part.shape),
            whole(recv.shape),
            whole(table.shape),
            whole(gain.shape),
            whole(bias.shape),
            pl.BlockSpec((3, width, QUAD), lambda n: (0, 0, n)),
            pl.BlockSpec((1, QUAD), lambda n: (0, n)),
            pl.BlockSpec((1, QUAD), lambda n: (0, n)),
            pl.BlockSpec((QUAD, width), lambda n: (n, 0)),
        ],
        out_specs=[
            whole((rows, width)),
            whole((rows, width)),
            pl.BlockSpec((3, rows, QUAD), lambda n: (0, 0, n)),
            pl.BlockSpec((rows, QUAD), lambda n: (0, n)),
            whole((rows, width)),
        ],
        out_shape=[
            jax.ShapeDtypeStruct((rows, width), F32),
            jax.ShapeDtypeStruct((rows, width), BF16),
            jax.ShapeDtypeStruct((3, rows, heads_wide), BF16),
            jax.ShapeDtypeStruct((rows, heads_wide), BF16),
            jax.ShapeDtypeStruct((rows, width), F32),
        ],
        compiler_params=params(),
        cost_estimate=cost(8 * rows * width * heads_wide * 2, 12 * rows * width * 2, rows * rows * 8),
        name="attn_forward",
    )(part, recv, table, gain, bias, w_qkv, q_bias, v_bias, w_out)


def attn_backward_kernel(
    gpart_ref, grecv_ref, x1_ref, cot_ref, gain_ref, wout_ref, qkv_ref, wqkv_ref,
    dx1_ref, dya_ref, dqkv_ref, da1_ref, sums_ref, qvsum_ref,
):
    quad = pl.program_id(0)
    rows = x1_ref.shape[0]

    @pl.when(quad == 0)
    def _():
        normed, inverse = norm_parts(x1_ref[...])
        grad = gpart_ref[...] + grecv_ref[...]
        cot = cot_ref[...].astype(F32)
        dx1 = cot + norm_back(normed, inverse, grad, gain_ref[...])
        dx1_ref[...] = dx1
        dya = dx1.astype(BF16)
        dya_ref[...] = dya
        da1_ref[...] = jnp.zeros_like(da1_ref)
        sums_ref[0:1, :] = column_sum(grad * normed)
        sums_ref[1:2, :] = column_sum(grad)
        sums_ref[2:3, :] = column_sum(dya.astype(F32))
        sums_ref[3:4, :] = column_sum(cot)
        sums_ref[4:8, :] = jnp.zeros((4, sums_ref.shape[1]), F32)

    dmix = nt(dya_ref[...], wout_ref[...]).astype(BF16)
    scale = HEAD_DIM**-0.5
    masks = pair_masks(rows)
    for pair in range(dmix.shape[1] // LANES):
        span = slice(pair * LANES, (pair + 1) * LANES)
        q2, k2, v2, d2 = qkv_ref[0, :, span], qkv_ref[1, :, span], qkv_ref[2, :, span], dmix[:, span]
        totals = [None, None, None]
        for mask in masks:
            qm, km, dm = only(mask, q2), only(mask, k2), only(mask, d2)
            probs = softmax_rows(qm, k2)
            dprobs = nt(dm, v2)
            dot_row = jnp.sum(probs * dprobs, -1, keepdims=True)
            dscores = (probs * (dprobs - dot_row)).astype(BF16)
            terms = [nn(dscores, km), tn(dscores, qm), tn(probs.astype(BF16), dm)]
            totals = [t if o is None else o + t for o, t in zip(totals, terms)]
        dqkv_ref[0, :, span] = (totals[0] * scale).astype(BF16)
        dqkv_ref[1, :, span] = (totals[1] * scale).astype(BF16)
        dqkv_ref[2, :, span] = totals[2].astype(BF16)
    da1_ref[...] += (
        nt(dqkv_ref[0], wqkv_ref[0]) + nt(dqkv_ref[1], wqkv_ref[1]) + nt(dqkv_ref[2], wqkv_ref[2])
    )
    qvsum_ref[0:1, :] = column_sum(dqkv_ref[0].astype(F32))
    qvsum_ref[1:2, :] = column_sum(dqkv_ref[2].astype(F32))
    qvsum_ref[2:8, :] = jnp.zeros((6, qvsum_ref.shape[1]), F32)


def attn_backward(gpart, grecv, x1, cotangent, gain, w_out, qkv, w_qkv, item):
    rows, width = x1.shape
    heads_wide = w_out.shape[0]
    steps = heads_wide // QUAD
    return pl.pallas_call(
        attn_backward_kernel,
        grid=(steps,),
        in_specs=[
            whole(gpart.shape),
            whole(grecv.shape),
            whole(x1.shape),
            pl.BlockSpec((rows, width), lambda n: (item, 0)),
            whole(gain.shape),
            pl.BlockSpec((QUAD, width), lambda n: (n, 0)),
            pl.BlockSpec((3, rows, QUAD), lambda n: (0, 0, n)),
            pl.BlockSpec((3, width, QUAD), lambda n: (0, 0, n)),
        ],
        out_specs=[
            whole((rows, width)),
            whole((rows, width)),
            pl.BlockSpec((3, rows, QUAD), lambda n: (0, 0, n)),
            whole((rows, width)),
            whole((8, width)),
            pl.BlockSpec((8, QUAD), lambda n: (0, n)),
        ],
        out_shape=[
            jax.ShapeDtypeStruct((rows, width), F32),
            jax.ShapeDtypeStruct((rows, width), BF16),
            jax.ShapeDtypeStruct((3, rows, heads_wide), BF16),
            jax.ShapeDtypeStruct((rows, width), F32),
            jax.ShapeDtypeStruct((8, width), F32),
            jax.ShapeDtypeStruct((8, heads_wide), F32),
        ],
        compiler_params=params(),
        cost_estimate=cost(8 * rows * width * heads_wide * 3, 20 * rows * width * 2, rows * rows * 8),
        name="attn_backward",
    )(gpart, grecv, x1, cotangent, gain, w_out, qkv, w_qkv)


def mlp_kernel(
    x0_ref, opart_ref, orecv_ref, obias_ref, gain_ref, bias_ref, wfc1_ref, b1_ref, wfc2_ref, cot_ref,
    x1_ref, a2_ref, act_ref, dpre_ref, da2_ref, b1sum_ref,
):
    step = pl.program_id(0)

    @pl.when(step == 0)
    def _():
        x1_ref[...] = x0_ref[...] + (opart_ref[...] + orecv_ref[...] + obias_ref[...])
        normed, _inv = norm_parts(x1_ref[...])
        a2_ref[...] = (normed * gain_ref[...] + bias_ref[...]).astype(BF16)
        da2_ref[...] = jnp.zeros_like(da2_ref)

    pre = nn(a2_ref[...], wfc1_ref[...]) + b1_ref[...]
    dact = nt(cot_ref[...], wfc2_ref[...])
    cdf = 0.5 * (1.0 + lax.erf(pre * (2.0**-0.5)))
    act_ref[...] = (pre * cdf).astype(BF16)
    density = jnp.exp(-0.5 * pre * pre) * 0.3989422804014327
    dpre = (dact * (cdf + pre * density)).astype(BF16)
    dpre_ref[...] = dpre
    b1sum_ref[...] = column_sum(dpre.astype(F32))
    da2_ref[...] += nt(dpre, wfc1_ref[...])


def mlp(x0, opart, orecv, out_bias, gain, bias, w_fc1, fc1_bias, w_fc2, cotangent, item):
    rows, width = x0.shape
    hidden = w_fc1.shape[1]
    tile = 512
    return pl.pallas_call(
        mlp_kernel,
        grid=(hidden // tile,),
        in_specs=[
            whole(x0.shape),
            whole(opart.shape),
            whole(orecv.shape),
            whole(out_bias.shape),
            whole(gain.shape),
            whole(bias.shape),
            pl.BlockSpec((width, tile), lambda n: (0, n)),
            pl.BlockSpec((1, tile), lambda n: (0, n)),
            pl.BlockSpec((tile, width), lambda n: (n, 0)),
            pl.BlockSpec((rows, width), lambda n: (item, 0)),
        ],
        out_specs=[
            whole((rows, width)),
            whole((rows, width)),
            pl.BlockSpec((rows, tile), lambda n: (0, n)),
            pl.BlockSpec((rows, tile), lambda n: (0, n)),
            whole((rows, width)),
            pl.BlockSpec((1, tile), lambda n: (0, n)),
        ],
        out_shape=[
            jax.ShapeDtypeStruct((rows, width), F32),
            jax.ShapeDtypeStruct((rows, width), BF16),
            jax.ShapeDtypeStruct((rows, hidden), BF16),
            jax.ShapeDtypeStruct((rows, hidden), BF16),
            jax.ShapeDtypeStruct((rows, width), F32),
            jax.ShapeDtypeStruct((1, hidden), F32),
        ],
        compiler_params=params(),
        cost_estimate=cost(6 * rows * width * hidden, 8 * width * hidden, 2 * rows * hidden),
        name="mlp",
    )(x0, opart, orecv, out_bias, gain, bias, w_fc1, fc1_bias, w_fc2, cotangent)


def first_norm_back_kernel(gpart_ref, grecv_ref, x0_ref, dx1_ref, gain_ref, dx0_ref, sums_ref):
    @pl.when(pl.program_id(0) == 0)
    def _():
        sums_ref[...] = jnp.zeros_like(sums_ref)

    normed, inverse = norm_parts(x0_ref[...])
    grad = gpart_ref[...] + grecv_ref[...]
    dx0_ref[...] = (dx1_ref[...] + norm_back(normed, inverse, grad, gain_ref[...])).astype(BF16)
    sums_ref[0:1, :] += column_sum(grad * normed)
    sums_ref[1:2, :] += column_sum(grad)


def first_norm_back(gpart, grecv, x0, dx1, gain):
    rows, width = x0.shape
    tile = 64
    block = pl.BlockSpec((tile, width), lambda n: (n, 0))
    return pl.pallas_call(
        first_norm_back_kernel,
        grid=(rows // tile,),
        in_specs=[block, block, block, block, whole(gain.shape)],
        out_specs=[block, whole((8, width))],
        out_shape=[
            jax.ShapeDtypeStruct((rows, width), BF16),
            jax.ShapeDtypeStruct((8, width), F32),
        ],
        compiler_params=params(),
        cost_estimate=cost(20 * rows * width, 18 * rows * width),
        name="first_norm_back",
    )(gpart, grecv, x0, dx1, gain)


def pixel_grad_kernel(kinds, da_ref, db_ref, wspec_ref, wrgb_ref, pick_ref, out_ref):
    item = pl.program_id(0)
    spectral = kinds[item] == 1
    grad = jnp.where(item == 0, da_ref[...], db_ref[...])
    wide = wspec_ref.shape[0]
    cut = (wide // 2 + LANES - 1) // LANES * LANES

    @pl.when(spectral)
    def _():
        out_ref[:, :cut] = nt(grad, wspec_ref[:cut, :]).astype(BF16)
        out_ref[:, cut:] = nt(grad, wspec_ref[cut:, :]).astype(BF16)

    @pl.when(jnp.logical_not(spectral))
    def _():
        small = nt(grad, wrgb_ref[...]).astype(BF16)
        out_ref[...] = nt(small, pick_ref[...]).astype(BF16)


def pixel_grad(kinds, grad_a, grad_b, w_spectral, w_rgb, pick):
    rows = grad_a.shape[0]
    wide, width = w_spectral.shape
    return pl.pallas_call(
        pixel_grad_kernel,
        grid_spec=pltpu.PrefetchScalarGridSpec(
            num_scalar_prefetch=1,
            grid=(2,),
            in_specs=[
                whole(grad_a.shape),
                whole(grad_b.shape),
                whole(w_spectral.shape),
                whole(w_rgb.shape),
                whole(pick.shape),
            ],
            out_specs=pl.BlockSpec((rows, wide), lambda i, *_: (i, 0)),
        ),
        out_shape=jax.ShapeDtypeStruct((2 * rows, wide), BF16),
        compiler_params=params(),
        cost_estimate=cost(4 * rows * wide * width, 4 * wide * width + 4 * rows * wide),
        name="pixel_grad",
    )(kinds, grad_a, grad_b, w_spectral, w_rgb, pick)


def weight_grad_kernel(place, *refs, groups):
    count = sum(2 + 2 * g for g in groups)
    send_ref, keep_ref = refs[count:]
    half = send_ref.shape[1] // sum(groups)
    core = place[8]
    base = 0
    cursor = 0
    for planes in groups:
        left_a, left_b = refs[cursor], refs[cursor + 1]
        for plane in range(planes):
            right_a = refs[cursor + 2 + 2 * plane]
            right_b = refs[cursor + 3 + 2 * plane]
            total = tn(left_a[...], right_a[...]) + tn(left_b[...], right_b[...])
            low, high = total[:half], total[half:]
            spot = slice(base, base + half)

            @pl.when(core == 0)
            def _(low=low, high=high, spot=spot):
                keep_ref[0, spot, :] = low
                send_ref[0, spot, :] = high

            @pl.when(core != 0)
            def _(low=low, high=high, spot=spot):
                send_ref[0, spot, :] = low
                keep_ref[0, spot, :] = high

            base += half
        cursor += 2 + 2 * planes


def weight_grad(place, sides, name):
    operands, specs, groups = [], [], []
    flops = 0
    for left_a, left_b, rights in sides:
        rows, width = left_a.shape
        groups.append(len(rights))
        for left in (left_a, left_b):
            operands.append(left)
            specs.append(pl.BlockSpec((rows, LANES), lambda n, pr: (0, pr[n])))
        for right_a, right_b, plane in rights:
            for right in (right_a, right_b):
                operands.append(right)
                if plane is None:
                    specs.append(pl.BlockSpec(right.shape, lambda n, pr: (0, 0)))
                else:
                    specs.append(
                        pl.BlockSpec((None,) + right.shape[1:], lambda n, pr, q=plane: (q, 0, 0))
                    )
            columns = right_a.shape[-1]
            flops += 4 * rows * width * columns
    chips = width // LANES
    half = LANES // 2
    block = (1, half * sum(groups), columns)
    shape = jax.ShapeDtypeStruct((chips,) + block[1:], F32)
    return pl.pallas_call(
        functools.partial(weight_grad_kernel, groups=tuple(groups)),
        grid_spec=pltpu.PrefetchScalarGridSpec(
            num_scalar_prefetch=1,
            grid=(chips,),
            in_specs=specs,
            out_specs=[pl.BlockSpec(block, lambda n, pr: (n, 0, 0))] * 2,
        ),
        out_shape=[shape, shape],
        compiler_params=params(),
        cost_estimate=cost(flops, 8 * chips * block[1] * columns),
        name=name,
    )(place, *operands)


def exchange(values, axis, bit, size):
    return lax.ppermute(values, axis, [(i, i ^ bit) for i in range(size)])


def swap(values):
    return exchange(values, "tensor", 1, 2)


def after(first, values):
    return lax.optimization_barrier((first, values))[1]


def halve(send, keep, size):
    recv = exchange(send, "dp", 1, size)
    block = keep.shape[0]
    bit = 2
    while block > 1:
        block //= 2
        out = keep[:block] + recv[:block]
        kept = keep[block:] + recv[block:]
        recv = exchange(out, "dp", bit, size)
        keep = kept
        bit *= 2
    return (keep + recv)[0]


def places(size):
    me = lax.axis_index("dp")
    chip = me // 2
    core = me % 2
    order = []
    for p in range(8):
        b2, b1, b0 = (p >> 2) & 1, (p >> 1) & 1, p & 1
        order.append((1 - b2) + 2 * (1 - b1) + 4 * (1 - b0))
    flips = jnp.array(order, jnp.int32)
    return jnp.concatenate([chip ^ flips, core[None]]).astype(jnp.int32)


def local(
    pixels, item_kinds, gsd_codes, w_spectral, w_rgb, ln1_gain, ln1_bias, w_qkv, q_bias, v_bias,
    w_out, out_bias, ln2_gain, ln2_bias, w_fc1, fc1_bias, w_fc2, fc2_bias, cotangent, *, size,
):
    items = item_kinds.shape[0]
    rows = pixels.shape[0] // items
    width = w_out.shape[1]
    wide = pixels.shape[1]
    narrow = w_rgb.shape[0]
    bands = wide // (narrow // 3)
    custom = size == 16

    def row(vector):
        return vector.reshape(1, -1)

    g1, c1, g2, c2 = row(ln1_gain), row(ln1_bias), row(ln2_gain), row(ln2_bias)
    qb, vb, ob, b1 = row(q_bias), row(v_bias), row(out_bias), row(fc1_bias)
    wqkv = jnp.transpose(w_qkv, (1, 0, 2))

    source = lax.broadcasted_iota(jnp.int32, (wide, narrow), 0)
    target = lax.broadcasted_iota(jnp.int32, (wide, narrow), 1)
    pick = (source == (target // 3) * bands + target % 3).astype(BF16)

    ratio = (gsd_codes.astype(F32) + 1.0) / 4.0
    quarter = width // 4
    frequency = 1.0 / 10000.0 ** (jnp.arange(quarter).astype(F32) / quarter)
    spot = jnp.arange(GRID).astype(F32)
    angle = ratio[:, None, None] * spot[None, :, None] * frequency[None, None, :]
    tables = jnp.concatenate([jnp.sin(angle), jnp.cos(angle)], -1)

    part, mixed = [None] * items, [None] * items
    for i in range(items):
        part[i], mixed[i] = embed(item_kinds, pixels, w_spectral, w_rgb, pick, i, rows)

    gate = None

    def send(values):
        nonlocal gate
        if gate is not None:
            values = after(gate, values)
        gate = swap(values)
        return gate

    erecv = [send(part[i]) for i in range(items)]
    fwd = []
    orecv = []
    for i in range(items):
        fwd.append(attn_forward(part[i], erecv[i], tables[i], g1, c1, wqkv, qb, vb, w_out))
        orecv.append(send(fwd[i][4]))
    ffn = []
    grecv = []
    for i in range(items):
        ffn.append(
            mlp(fwd[i][0], fwd[i][4], orecv[i], ob, g2, c2, w_fc1, b1, w_fc2, cotangent, i)
        )
        grecv.append(send(ffn[i][4]))
    bwd = []
    arecv = []
    for i in range(items):
        bwd.append(
            attn_backward(ffn[i][4], grecv[i], ffn[i][0], cotangent, g2, w_out, fwd[i][2], wqkv, i)
        )
        arecv.append(send(bwd[i][3]))
    last = []
    for i in range(items):
        last.append(first_norm_back(bwd[i][3], arecv[i], fwd[i][0], bwd[i][0], g1))

    x0, a1, qkv, mix, _ = zip(*fwd)
    x1, a2, act, dpre, _, b1sum = zip(*ffn)
    dx1, dya, dqkv, _, sums2, qvsum = zip(*bwd)
    dx0, sums1 = zip(*last)

    cot = [cotangent[i * rows : (i + 1) * rows] for i in range(items)]
    out_terms = [nn(act[i], w_fc2) for i in range(items)]
    block_rows = []
    for i in range(items):
        got = send(out_terms[i])
        block_rows.append((x1[i] + (out_terms[i] + got + fc2_bias)).astype(BF16))
    block_out = jnp.concatenate(block_rows, 0)

    pixels_grad = pixel_grad(item_kinds, dx0[0], dx0[1], w_spectral, w_rgb, pick)

    vec2 = sums2[0] + sums2[1]
    vec1 = sums1[0] + sums1[1]
    qv = qvsum[0] + qvsum[1]
    b1s = b1sum[0] + b1sum[1]

    if custom:
        place = places(size)
        fc2_s = weight_grad(place, [(cot[0], cot[1], [(act[0], act[1], None)])], "fc2_grad")
        fc1_s = weight_grad(place, [(a2[0], a2[1], [(dpre[0], dpre[1], None)])], "fc1_grad")
        att_s = weight_grad(
            place,
            [
                (a1[0], a1[1], [(dqkv[0], dqkv[1], p) for p in range(3)]),
                (dya[0], dya[1], [(mix[0], mix[1], None)]),
            ],
            "attn_grad",
        )
        emb_s = weight_grad(place, [(dx0[0], dx0[1], [(mixed[0], mixed[1], None)])], "embed_grad")
        fc2_g = halve(*fc2_s, size)
        fc1_g = halve(*fc1_s, size)
        att_g = halve(*att_s, size)
        emb_g = halve(*emb_s, size)
        shard = width // size
        att_g = att_g.reshape(4, shard, -1)
        qkv_grad = jnp.transpose(att_g[:3], (1, 0, 2))
        out_grad = att_g[3].T
    else:

        def scatter(values):
            return lax.psum_scatter(values, "dp", scatter_dimension=0, tiled=True)

        def both(left, right):
            return sum(tn(left[i], right[i]) for i in range(items))

        fc2_g = scatter(both(cot, act))
        fc1_g = scatter(both(a2, dpre))
        emb_g = scatter(both(dx0, mixed))
        qkv_grad = scatter(
            sum(
                lax.dot_general(
                    a1[i], dqkv[i], (((0,), (1,)), ((), ())), preferred_element_type=F32
                )
                for i in range(items)
            )
        )
        out_grad = scatter(both(dya, mix)).T

    pieces = [vec2[0], vec2[1], vec2[2], vec2[3], vec1[0], vec1[1], qv[0], qv[1], b1s[0]]
    small = jnp.concatenate([v.reshape(size, -1) for v in pieces], 1)
    if custom:
        cube = small.reshape(2, 2, 2, 2, -1)
        chip, core = lax.axis_index("dp") // 2, place[8]
        for axis, bit in ((0, 4), (1, 2), (2, 1)):
            cube = jnp.where((chip & bit) == 0, jnp.flip(cube, axis), cube)
        cube = jnp.transpose(cube, (2, 1, 0, 3, 4)).reshape(8, 2, 1, -1)
        kept = jnp.where(core == 0, cube[:, 0], cube[:, 1])
        gone = jnp.where(core == 0, cube[:, 1], cube[:, 0])
        small = halve(gone, kept, size)[0]
    else:
        small = lax.psum_scatter(small, "dp", scatter_dimension=0, tiled=True)[0]
    outs = []
    start = 0
    for v in pieces:
        length = v.shape[0] // size
        outs.append(small[start : start + length])
        start += length
    ln2_g, ln2_b, ob_g, b2_g, ln1_g, ln1_b, q_g, v_g, b1_g = outs
    spectral_grad = emb_g[:, :wide].T
    rgb_grad = emb_g[:, wide:].T
    return (
        block_out, pixels_grad, spectral_grad, rgb_grad, ln1_g, ln1_b, qkv_grad, q_g, v_g, out_grad,
        ob_g, ln2_g, ln2_b, fc1_g, b1_g, fc2_g.T, b2_g,
    )


def solution(mesh):
    in_specs = (
        P("dp", "tensor"),
        P("dp"),
        P("dp"),
        P("tensor", None),
        P("tensor", None),
        P(),
        P(),
        P(None, None, "tensor"),
        P("tensor"),
        P("tensor"),
        P("tensor", None),
        P(),
        P(),
        P(),
        P(None, "tensor"),
        P("tensor"),
        P("tensor", None),
        P(),
        P("dp", None),
    )
    out_specs = (
        P("dp", None),
        P("dp", "tensor"),
        P("tensor", "dp"),
        P("tensor", "dp"),
        P("dp"),
        P("dp"),
        P("dp", None, "tensor"),
        P(("tensor", "dp")),
        P(("tensor", "dp")),
        P("tensor", "dp"),
        P("dp"),
        P("dp"),
        P("dp"),
        P("dp", "tensor"),
        P(("tensor", "dp")),
        P("tensor", "dp"),
        P("dp"),
    )
    body = functools.partial(local, size=mesh.shape["dp"])
    return jax.shard_map(body, mesh=mesh, in_specs=in_specs, out_specs=out_specs, check_vma=False)
```

time: 985 us -> 490 us (0.50)
  waiting for transfers between devices: 655 us -> 285 us
  Pallas kernels: 0 us -> 123 us
  local copies, waits for them, and re-layouts: 122 us -> 7.92 us
  matrix products: 78.8 us -> 8.52 us
  blocking collectives: 68.1 us -> 0 us
  starting transfers between devices: 1.34 us -> 34.6 us
  between operations: 17.1 us -> 1.05 us
    reduce_scatter x6 -> x0, waiting for transfers between devices: 375 us -> none  [the longest x1 110 us: local(): lax.psum_scatter(fc2_grad, 'dp', scatter_dimension=1, tiled=True)]
    ppermute x0 -> x30, waiting for transfers between devices: none -> 285 us  [exchange(): return lax.ppermute(values, axis, [(i, i ^ bit) for i in range(size)])]
    psum x4 -> x0, waiting for transfers between devices: 279 us -> none  [the longest x1 104 us: local(): resid2 = resid1 + (lax.psum(matmul(hidden_act, w_fc2), 'tensor') + fc2_bias)]
    pallas_call x0 -> x15, Pallas kernels: none -> 123 us  [the longest x4 41 us: weight_grad(): pl.pallas_call(functools.partial(weight_grad_kernel, groups=tuple(groups)...]
    dot_general x24 -> x2, matrix products: 78.8 us -> 8.52 us  [nn(): lax.dot_general(left, right, (((1,), (0,)), ((), ())), preferred_element_...]
    unnamed x1 -> x0, blocking collectives: 68.1 us -> none
    ppermute x0 -> x30, starting transfers between devices: none -> 34.6 us  [exchange(): return lax.ppermute(values, axis, [(i, i ^ bit) for i in range(size)])]
    unnamed x122 -> x52, local copies, waits for them, and re-layouts: 32.3 us -> 1.33 us
  transfers between devices with their start and end apart: 10 -> 30, of which waited for: 8 -> 16; matrix products, arithmetic and copies ran while one was open for 10% -> 8% of each run, Pallas kernels for 0% -> 24%
where the time goes in v1:
time: 490 us; the launch traced here: 488 us
  waiting for transfers between devices  285 us (58%)
  Pallas kernels  123 us (25%)
  starting transfers between devices  34.6 us (7%)
  other arithmetic  27.1 us (6%)
  matrix products  8.52 us (2%)
  local copies, waits for them, and re-layouts  7.92 us (2%)
    ppermute x30, waiting for transfers between devices, exchange(): return lax.ppermute(values, axis, [(i, i ^ bit) for i in range(size)])  285 us
    pallas_call x4, Pallas kernels, weight_grad(): pl.pallas_call(functools.partial(weight_grad_kernel, groups=tuple(groups)...  41 us
    ppermute x30, starting transfers between devices, exchange(): return lax.ppermute(values, axis, [(i, i ^ bit) for i in range(size)])  34.6 us
    pallas_call x2, Pallas kernels, attn_backward(): pl.pallas_call(attn_backward_kernel, grid=(steps,), in_specs=[whole(gpart...  20 us
    pallas_call x2, Pallas kernels, mlp(): pl.pallas_call(mlp_kernel, grid=(hidden // tile,), in_specs=[whole(x0.sha...  19 us
    add x10, other arithmetic, halve(): kept = keep[block:] + recv[block:]  17.9 us
    pallas_call x2, Pallas kernels, attn_forward(): pl.pallas_call(attn_forward_kernel, grid=(steps,), in_specs=[whole(part.s...  14.6 us
    pallas_call x2, Pallas kernels, embed(): pl.pallas_call(functools.partial(embed_kernel, item=item), grid_spec=pltp...  13.1 us
  transfers between devices with their start and end apart: 30, of which 16 were waited for; matrix products, arithmetic and copies ran while one was open for 8% of the time, Pallas kernels for 24%

profile of v1, /device:TPU:0, one launch (start us, length us, event | category | flops | bytes accessed | tf_op | source)
XLA Modules:
  0.0 487.8 jit_solution(6365826658950618547)
XLA Ops:
  0.7 1.4 fusion.pick_ref
  2.1 6.5 %embed.2 = (f32[256,1024]{1,0:T(8,128)}, bf16[256,2048]{1,0:T(8,128)(2,1)}) custom-call(s32[2]{0:T(128)} %kinds.5, bf16[512,1664]{1,0:T(8,128)(2,1)} %pix_ref.3, bf16[1664,1024]{1,0:T(8,128)(2,1)} %wspec_ref.5, bf16[384,1024]{1,0:T(8,128)(2,1)} %wrgb_ref.5, bf16[1664,384]{1,0:T(8,128)(2,1)} %fusion.pick_ref), custom_call_target="tpu_custom_call" | custom-call | flops 872415232 | bytes 4456448 | tf_op jit(solution)/shard_map/embed/pallas_call | solution.py:90
  8.6 3.0 collective-permute-start
  11.7 6.6 %embed.3 = (f32[256,1024]{1,0:T(8,128)}, bf16[256,2048]{1,0:T(8,128)(2,1)}) custom-call(s32[2]{0:T(128)} %kinds.5, bf16[512,1664]{1,0:T(8,128)(2,1)} %pix_ref.3, bf16[1664,1024]{1,0:T(8,128)(2,1)} %wspec_ref.5, bf16[384,1024]{1,0:T(8,128)(2,1)} %wrgb_ref.5, bf16[1664,384]{1,0:T(8,128)(2,1)} %fusion.pick_ref), custom_call_target="tpu_custom_call" | custom-call | flops 872415232 | bytes 4456448 | tf_op jit(solution)/shard_map/embed/pallas_call | solution.py:90
  18.3 16.9 %collective-permute-done.recv_ref = f32[256,1024]{1,0:T(8,128)S(1)} collective-permute-done((f32[256,1024]{1,0:T(8,128)}, f32[256,1024]{1,0:T(8,128)S(1)}, u32[]{:S(2)}, u32[]{:S(2)}) %collective-permute-start) | collective-permute-done | bytes 1048608 | tf_op jit(solution)/shard_map/ppermute | solution.py:507
  35.2 1.7 collective-permute-start.1
  37.9 7.3 %attn_forward.2 = (f32[256,1024]{1,0:T(8,128)}, bf16[256,1024]{1,0:T(8,128)(2,1)}, bf16[3,256,512]{2,1,0:T(8,128)(2,1)}, bf16[256,512]{1,0:T(8,128)(2,1)}, f32[256,1024]{1,0:T(8,128)}) custom-call(f32[256,1024]{1,0:T(8,128)} %get-tuple-element.76.part_ref, f32[256,1024]{1,0:T(8,128)} %copy-done.23, f32[16,512]{1,0:T(8,128)} %get-tuple-element.161.table_ref, ...), custom_call_target="tpu_custom_call" | custom-call | flops 2147483648 | bytes 6291456 | tf_op jit(solution)/shard_map/attn_forward/pallas_call | solution.py:177
  45.1 14.8 %collective-permute-done.1.recv_ref = f32[256,1024]{1,0:T(8,128)S(1)} collective-permute-done((f32[256,1024]{1,0:T(8,128)}, f32[256,1024]{1,0:T(8,128)S(1)}, u32[]{:S(2)}, u32[]{:S(2)}) %collective-permute-start.1) | collective-permute-done | bytes 1048608 | tf_op jit(solution)/shard_map/ppermute | solution.py:507
  59.9 1.4 collective-permute-start.2
  61.4 7.3 %attn_forward.3 = (f32[256,1024]{1,0:T(8,128)}, bf16[256,1024]{1,0:T(8,128)(2,1)}, bf16[3,256,512]{2,1,0:T(8,128)(2,1)}, bf16[256,512]{1,0:T(8,128)(2,1)}, f32[256,1024]{1,0:T(8,128)}) custom-call(f32[256,1024]{1,0:T(8,128)} %get-tuple-element.80.part_ref, f32[256,1024]{1,0:T(8,128)} %copy-done.22, f32[16,512]{1,0:T(8,128)} %get-tuple-element.162.table_ref, ...), custom_call_target="tpu_custom_call" | custom-call | flops 2147483648 | bytes 6291456 | tf_op jit(solution)/shard_map/attn_forward/pallas_call | solution.py:177
  68.7 15.1 %collective-permute-done.2.orecv_ref = f32[256,1024]{1,0:T(8,128)S(1)} collective-permute-done((f32[256,1024]{1,0:T(8,128)}, f32[256,1024]{1,0:T(8,128)S(1)}, u32[]{:S(2)}, u32[]{:S(2)}) %collective-permute-start.2) | collective-permute-done | bytes 1048608 | tf_op jit(solution)/shard_map/ppermute | solution.py:507
  83.8 1.1 collective-permute-start.3
  84.9 9.4 %mlp.2 = (f32[256,1024]{1,0:T(8,128)}, bf16[256,1024]{1,0:T(8,128)(2,1)}, bf16[256,2048]{1,0:T(8,128)(2,1)}, bf16[256,2048]{1,0:T(8,128)(2,1)}, f32[256,1024]{1,0:T(8,128)}, /*index=5*/f32[1,2048]{1,0:T(1,128)}) custom-call(f32[256,1024]{1,0:T(8,128)} %get-tuple-element.77.x0_ref, f32[256,1024]{1,0:T(8,128)} %get-tuple-element.81.opart_ref, ...), custom_call_target="tpu_custom_call" | custom-call | flops 3221225472 | bytes 16777216 | tf_op jit(solution)/shard_map/mlp/pallas_call | solution.py:327
  94.3 12.8 %collective-permute-done.3.orecv_ref = f32[256,1024]{1,0:T(8,128)S(1)} collective-permute-done((f32[256,1024]{1,0:T(8,128)}, f32[256,1024]{1,0:T(8,128)S(1)}, u32[]{:S(2)}, u32[]{:S(2)}) %collective-permute-start.3) | collective-permute-done | bytes 1048608 | tf_op jit(solution)/shard_map/ppermute | solution.py:507
  107.1 1.1 collective-permute-start.4
  108.2 9.6 %mlp.3 = (f32[256,1024]{1,0:T(8,128)}, bf16[256,1024]{1,0:T(8,128)(2,1)}, bf16[256,2048]{1,0:T(8,128)(2,1)}, bf16[256,2048]{1,0:T(8,128)(2,1)}, f32[256,1024]{1,0:T(8,128)}, /*index=5*/f32[1,2048]{1,0:T(1,128)}) custom-call(f32[256,1024]{1,0:T(8,128)} %get-tuple-element.88.x0_ref, f32[256,1024]{1,0:T(8,128)} %get-tuple-element.85.opart_ref, ...), custom_call_target="tpu_custom_call" | custom-call | flops 3221225472 | bytes 16777216 | tf_op jit(solution)/shard_map/mlp/pallas_call | solution.py:327
  117.8 12.7 %collective-permute-done.4.grecv_ref = f32[256,1024]{1,0:T(8,128)S(1)} collective-permute-done((f32[256,1024]{1,0:T(8,128)}, f32[256,1024]{1,0:T(8,128)S(1)}, u32[]{:S(2)}, u32[]{:S(2)}) %collective-permute-start.4) | collective-permute-done | bytes 1048608 | tf_op jit(solution)/shard_map/ppermute | solution.py:507
  130.4 1.1 collective-permute-start.5
  132.1 1.1 fusion.20
  133.2 9.5 %fc2_grad.1 = (f32[8,64,2048]{2,1,0:T(8,128)}, f32[8,64,2048]{2,1,0:T(8,128)}) custom-call(s32[9]{0:T(128)} %pad_add_fusion.place, bf16[256,1024]{1,0:T(8,128)(2,1)} %get-tuple-element.160.refs_0_, bf16[256,1024]{1,0:T(8,128)(2,1)} %get-tuple-element.159.refs_1_, bf16[256,2048]{1,0:T(8,128)(2,1)} %get-tuple-element.83.refs_2_, ...), custom_call_target="tpu_custom_call" | custom-call | flops 2147483648 | bytes 8388608 | tf_op jit(solution)/shard_map/fc2_grad/pallas_call | solution.py:491
  142.7 10.1 %attn_backward.2 = (f32[256,1024]{1,0:T(8,128)}, bf16[256,1024]{1,0:T(8,128)(2,1)}, bf16[3,256,512]{2,1,0:T(8,128)(2,1)}, f32[256,1024]{1,0:T(8,128)}, f32[8,1024]{1,0:T(8,128)}, /*index=5*/f32[8,512]{1,0:T(8,128)}) custom-call(f32[256,1024]{1,0:T(8,128)} %get-tuple-element.87.gpart_ref, f32[256,1024]{1,0:T(8,128)} %copy-done.20, ...), custom_call_target="tpu_custom_call" | custom-call | flops 3221225472 | bytes 10485760 | tf_op jit(solution)/shard_map/attn_backward/pallas_call | solution.py:264
  152.8 1.0 collective-permute-start.6
  153.8 9.4 %fc1_grad.1 = (f32[8,64,2048]{2,1,0:T(8,128)}, f32[8,64,2048]{2,1,0:T(8,128)}) custom-call(s32[9]{0:T(128)} %pad_add_fusion.place, bf16[256,1024]{1,0:T(8,128)(2,1)} %get-tuple-element.127.refs_0_, bf16[256,1024]{1,0:T(8,128)(2,1)} %get-tuple-element.128.refs_1_, bf16[256,2048]{1,0:T(8,128)(2,1)} %get-tuple-element.129.refs_2_, ...), custom_call_target="tpu_custom_call" | custom-call | flops 2147483648 | bytes 8388608 | tf_op jit(solution)/shard_map/fc1_grad/pallas_call | solution.py:491
  163.4 9.9 %attn_backward.3 = (f32[256,1024]{1,0:T(8,128)}, bf16[256,1024]{1,0:T(8,128)(2,1)}, bf16[3,256,512]{2,1,0:T(8,128)(2,1)}, f32[256,1024]{1,0:T(8,128)}, f32[8,1024]{1,0:T(8,128)}, /*index=5*/f32[8,512]{1,0:T(8,128)}) custom-call(f32[256,1024]{1,0:T(8,128)} %get-tuple-element.90.gpart_ref, f32[256,1024]{1,0:T(8,128)} %copy-done.21, ...), custom_call_target="tpu_custom_call" | custom-call | flops 3221225472 | bytes 10485760 | tf_op jit(solution)/shard_map/attn_backward/pallas_call | solution.py:264
  173.3 5.1 %collective-permute-done.6.grecv_ref = f32[256,1024]{1,0:T(8,128)S(1)} collective-permute-done((f32[256,1024]{1,0:T(8,128)}, f32[256,1024]{1,0:T(8,128)S(1)}, u32[]{:S(2)}, u32[]{:S(2)}) %collective-permute-start.6) | collective-permute-done | bytes 1048608 | tf_op jit(solution)/shard_map/ppermute | solution.py:507
  178.5 0.9 collective-permute-start.7
  179.4 3.8 fusion.21
  183.9 12.5 %attn_grad.1 = (f32[8,256,512]{2,1,0:T(8,128)}, f32[8,256,512]{2,1,0:T(8,128)}) custom-call(s32[9]{0:T(128)} %pad_add_fusion.place, bf16[256,1024]{1,0:T(8,128)(2,1)} %get-tuple-element.117.refs_0_, bf16[256,1024]{1,0:T(8,128)(2,1)} %get-tuple-element.118.refs_1_, bf16[3,256,512]{2,1,0:T(8,128)(2,1)} %get-tuple-element.119.refs_2_.refs_4_.refs_6_, ...), custom_call_target="tpu_custom_call" | custom-call | flops 2147483648 | bytes 8388608 | tf_op jit(solution)/shard_map/attn_grad/pallas_call | solution.py:491
  196.4 4.4 first_norm_back.2
  200.8 2.4 collective-permute-done.7.grecv_ref
  203.2 1.0 copy-done.8
  204.2 4.4 first_norm_back.3
  209.5 9.6 %embed_grad.1 = (f32[8,64,2048]{2,1,0:T(8,128)}, f32[8,64,2048]{2,1,0:T(8,128)}) custom-call(s32[9]{0:T(128)} %pad_add_fusion.place, bf16[256,1024]{1,0:T(8,128)(2,1)} %get-tuple-element.102.da_ref.refs_0_, bf16[256,1024]{1,0:T(8,128)(2,1)} %get-tuple-element.104.db_ref.refs_1_, bf16[256,2048]{1,0:T(8,128)(2,1)} %get-tuple-element.105.refs_2_, ...), custom_call_target="tpu_custom_call" | custom-call | flops 2147483648 | bytes 8388608 | tf_op jit(solution)/shard_map/embed_grad/pallas_call | solution.py:491
  220.0 4.7 fusion.22
  224.7 1.2 collective-permute-done.14
  225.9 0.9 collective-permute-start.8
  226.9 1.1 collective-permute-start.15
  228.0 4.5 slice_add_fusion.1
  232.5 1.0 collective-permute-start.27
  234.2 4.3 slice_add_fusion.3
  238.6 2.8 collective-permute-start.17
  241.4 6.9 %pixel_grad.1 = bf16[512,1664]{1,0:T(8,128)(2,1)} custom-call(s32[2]{0:T(128)} %kinds.5, bf16[256,1024]{1,0:T(8,128)(2,1)} %get-tuple-element.102.da_ref.refs_0_, bf16[256,1024]{1,0:T(8,128)(2,1)} %get-tuple-element.104.db_ref.refs_1_, bf16[1664,1024]{1,0:T(8,128)(2,1)} %wspec_ref.5, bf16[384,1024]{1,0:T(8,128)(2,1)} %wrgb_ref.5, bf16[1664,384]{1,0:T(8,128)(2,1)} %fusion.pick_ref), custom_call_target="tpu_custom_call" | custom-call | flops 1744830464 | bytes 8519680 | tf_op jit(solution)/shard_map/pixel_grad/pallas_call | solution.py:416
  248.3 1.2 collective-permute-start.23
  251.5 1.3 collective-permute-start.9
  252.8 4.7 slice_add_fusion.5
  257.4 0.9 collective-permute-start.19
  258.4 3.0 slice_add_fusion.7
  261.4 1.2 collective-permute-start.11
  262.6 18.7 %collective-permute-done.27 = f32[4,64,2048]{2,1,0:T(8,128)S(1)} collective-permute-done((f32[4,64,2048]{2,1,0:T(8,128)}, f32[4,64,2048]{2,1,0:T(8,128)S(1)}, u32[]{:S(2)}, u32[]{:S(2)}) %collective-permute-start.27) | collective-permute-done | bytes 2097184 | tf_op jit(solution)/shard_map/ppermute | solution.py:507
  281.5 1.3 collective-permute-start.28
  283.1 2.0 add_convert_fusion.1
  285.1 1.0 pad_maximum_fusion
  286.1 40.0 %collective-permute-done.23 = f32[4,64,2048]{2,1,0:T(8,128)S(1)} collective-permute-done((f32[4,64,2048]{2,1,0:T(8,128)}, f32[4,64,2048]{2,1,0:T(8,128)S(1)}, u32[]{:S(2)}, u32[]{:S(2)}) %collective-permute-start.23) | collective-permute-done | bytes 2097184 | tf_op jit(solution)/shard_map/ppermute | solution.py:507
  326.5 1.3 collective-permute-start.24
  327.9 2.3 collective-permute-start.29
  330.2 40.9 %collective-permute-done.19 = f32[4,256,512]{2,1,0:T(8,128)S(1)} collective-permute-done((f32[4,256,512]{2,1,0:T(8,128)S(1)}, f32[4,256,512]{2,1,0:T(8,128)S(1)}, u32[]{:S(2)}, u32[]{:S(2)}) %collective-permute-start.19) | collective-permute-done | bytes 2097184 | tf_op jit(solution)/shard_map/ppermute | solution.py:507
  371.7 1.3 collective-permute-start.20
  373.0 41.9 %collective-permute-done.11 = f32[4,64,2048]{2,1,0:T(8,128)S(1)} collective-permute-done((f32[4,64,2048]{2,1,0:T(8,128)S(1)}, f32[4,64,2048]{2,1,0:T(8,128)S(1)}, u32[]{:S(2)}, u32[]{:S(2)}) %collective-permute-start.11) | collective-permute-done | bytes 2097184 | tf_op jit(solution)/shard_map/ppermute | solution.py:507
  415.2 1.3 collective-permute-start.12
  416.6 2.3 collective-permute-start.25
  418.9 0.9 fusion.2
  420.6 40.5 %collective-permute-done.12 = f32[2,64,2048]{2,1,0:T(8,128)S(1)} collective-permute-done((f32[2,64,2048]{2,1,0:T(8,128)S(1)}, f32[2,64,2048]{2,1,0:T(8,128)S(1)}, u32[]{:S(2)}, u32[]{:S(2)}) %collective-permute-start.12) | collective-permute-done | bytes 1048608 | tf_op jit(solution)/shard_map/ppermute | solution.py:507
  462.7 12.8 %collective-permute-done.21 = f32[1,256,512]{2,1,0:T(8,128)S(1)} collective-permute-done((f32[1,256,512]{2,1,0:T(8,128)S(1)}, f32[1,256,512]{2,1,0:T(8,128)S(1)}, u32[]{:S(2)}, u32[]{:S(2)}) %collective-permute-start.21) | collective-permute-done | bytes 524320 | tf_op jit(solution)/shard_map/ppermute | solution.py:507
  477.1 9.1 %collective-permute-done.13 = f32[1,64,2048]{2,1,0:T(8,128)S(1)} collective-permute-done((f32[1,64,2048]{2,1,0:T(8,128)S(1)}, f32[1,64,2048]{2,1,0:T(8,128)S(1)}, u32[]{:S(2)}, u32[]{:S(2)}) %collective-permute-start.13) | collective-permute-done | bytes 524320 | tf_op jit(solution)/shard_map/ppermute | solution.py:507
  (128 shorter events, 14.3 us)
Async XLA Ops:
  8.6 28.3 %copy-start.24 = (s32[2]{0:T(128)S(1)}, s32[2]{0:T(128)}, u32[]{:S(2)}) copy-start(s32[2]{0:T(128)} %param.22) | copy-start | bytes 28
  8.6 26.6 %collective-permute-start = (f32[256,1024]{1,0:T(8,128)}, f32[256,1024]{1,0:T(8,128)S(1)}, u32[]{:S(2)}, u32[]{:S(2)}) collective-permute-start(f32[256,1024]{1,0:T(8,128)} %get-tuple-element.76.part_ref), channel_id=1, source_target_pairs={{0,1},{1,0},{2,3},{3,2},{4,5},{5,4},{6,7},{7,6},{8,9},{9,8},{10,11... | collective-permute-start | bytes 3145736 | tf_op jit(solution)/shard_map/ppermute | solution.py:507
  35.2 2.7 copy-start.23
  35.2 24.7 %collective-permute-start.1 = (f32[256,1024]{1,0:T(8,128)}, f32[256,1024]{1,0:T(8,128)S(1)}, u32[]{:S(2)}, u32[]{:S(2)}) collective-permute-start(f32[256,1024]{1,0:T(8,128)} %get-tuple-element.80.part_ref), channel_id=1, source_target_pairs={{0,1},{1,0},{2,3},{3,2},{4,5},{5,4},{6,7},{7,6},{8,9},{9,8},{10,11... | collective-permute-start | bytes 3145736 | tf_op jit(solution)/shard_map/ppermute | solution.py:507
  59.9 1.4 copy-start.22
  59.9 23.8 %collective-permute-start.2 = (f32[256,1024]{1,0:T(8,128)}, f32[256,1024]{1,0:T(8,128)S(1)}, u32[]{:S(2)}, u32[]{:S(2)}) collective-permute-start(f32[256,1024]{1,0:T(8,128)} %get-tuple-element.81.opart_ref), channel_id=1, source_target_pairs={{0,1},{1,0},{2,3},{3,2},{4,5},{5,4},{6,7},{7,6},{8,9},{9,8},{10,11... | collective-permute-start | bytes 3145736 | tf_op jit(solution)/shard_map/ppermute | solution.py:507
  83.8 1.1 copy-start.10
  83.8 23.3 %collective-permute-start.3 = (f32[256,1024]{1,0:T(8,128)}, f32[256,1024]{1,0:T(8,128)S(1)}, u32[]{:S(2)}, u32[]{:S(2)}) collective-permute-start(f32[256,1024]{1,0:T(8,128)} %get-tuple-element.85.opart_ref), channel_id=1, source_target_pairs={{0,1},{1,0},{2,3},{3,2},{4,5},{5,4},{6,7},{7,6},{8,9},{9,8},{10,11... | collective-permute-start | bytes 3145736 | tf_op jit(solution)/shard_map/ppermute | solution.py:507
  107.1 1.1 copy-start.9
  107.1 23.3 %collective-permute-start.4 = (f32[256,1024]{1,0:T(8,128)}, f32[256,1024]{1,0:T(8,128)S(1)}, u32[]{:S(2)}, u32[]{:S(2)}) collective-permute-start(f32[256,1024]{1,0:T(8,128)} %get-tuple-element.87.gpart_ref), channel_id=1, source_target_pairs={{0,1},{1,0},{2,3},{3,2},{4,5},{5,4},{6,7},{7,6},{8,9},{9,8},{10,11... | collective-permute-start | bytes 3145736 | tf_op jit(solution)/shard_map/ppermute | solution.py:507
  108.2 23.3 %copy-start.25 = (s32[8]{0:T(128)S(1)}, s32[8]{0:T(128)}, u32[]{:S(2)}) copy-start(s32[8]{0:T(128)} %constant.68.clone) | copy-start | bytes 100
  108.2 23.9 %copy-start = (bf16[512,1024]{1,0:T(8,128)(2,1)S(1)}, bf16[512,1024]{1,0:T(8,128)(2,1)}, u32[]{:S(2)}) copy-start(bf16[512,1024]{1,0:T(8,128)(2,1)} %cot_ref.7) | copy-start | bytes 3145732
  130.4 12.3 %copy-start.20 = (f32[256,1024]{1,0:T(8,128)}, f32[256,1024]{1,0:T(8,128)S(1)}, u32[]{:S(2)}) copy-start(f32[256,1024]{1,0:T(8,128)S(1)} %collective-permute-done.4.grecv_ref) | copy-start | bytes 3145732
  130.4 22.4 %collective-permute-start.5 = (f32[256,1024]{1,0:T(8,128)}, f32[256,1024]{1,0:T(8,128)S(1)}, u32[]{:S(2)}, u32[]{:S(2)}) collective-permute-start(f32[256,1024]{1,0:T(8,128)} %get-tuple-element.90.gpart_ref), channel_id=1, source_target_pairs={{0,1},{1,0},{2,3},{3,2},{4,5},{5,4},{6,7},{7,6},{8,9},{9,8},{10,11... | collective-permute-start | bytes 3145736 | tf_op jit(solution)/shard_map/ppermute | solution.py:507
  142.7 84.2 %collective-permute-start.26 = (f32[8,64,2048]{2,1,0:T(8,128)}, f32[8,64,2048]{2,1,0:T(8,128)}, u32[]{:S(2)}, u32[]{:S(2)}) collective-permute-start(f32[8,64,2048]{2,1,0:T(8,128)} %get-tuple-element.134), channel_id=1, source_target_pairs={{0,2},{2,0},{4,6},{6,4},{8,10},{10,8},{12,14},{14,12},{16,18},{18,... | collective-permute-start | bytes 12582920 | tf_op jit(solution)/shard_map/ppermute | solution.py:507
  152.8 10.4 %copy-start.21 = (f32[256,1024]{1,0:T(8,128)}, f32[256,1024]{1,0:T(8,128)S(1)}, u32[]{:S(2)}) copy-start(f32[256,1024]{1,0:T(8,128)S(1)} %collective-permute-done.5.grecv_ref) | copy-start | bytes 3145732
  152.8 25.6 %collective-permute-start.6 = (f32[256,1024]{1,0:T(8,128)}, f32[256,1024]{1,0:T(8,128)S(1)}, u32[]{:S(2)}, u32[]{:S(2)}) collective-permute-start(f32[256,1024]{1,0:T(8,128)} %get-tuple-element.93.gpart_ref), channel_id=1, source_target_pairs={{0,1},{1,0},{2,3},{3,2},{4,5},{5,4},{6,7},{7,6},{8,9},{9,8},{10,11... | collective-permute-start | bytes 3145736 | tf_op jit(solution)/shard_map/ppermute | solution.py:507
  163.2 70.2 %collective-permute-start.22 = (f32[8,64,2048]{2,1,0:T(8,128)}, f32[8,64,2048]{2,1,0:T(8,128)}, u32[]{:S(2)}, u32[]{:S(2)}) collective-permute-start(f32[8,64,2048]{2,1,0:T(8,128)} %get-tuple-element.132), channel_id=1, source_target_pairs={{0,2},{2,0},{4,6},{6,4},{8,10},{10,8},{12,14},{14,12},{16,18},{18,... | collective-permute-start | bytes 12582920 | tf_op jit(solution)/shard_map/ppermute | solution.py:507
  178.5 4.8 copy-start.7
  178.5 24.8 %collective-permute-start.7 = (f32[256,1024]{1,0:T(8,128)}, f32[256,1024]{1,0:T(8,128)S(1)}, u32[]{:S(2)}, u32[]{:S(2)}) collective-permute-start(f32[256,1024]{1,0:T(8,128)} %get-tuple-element.97.gpart_ref), channel_id=1, source_target_pairs={{0,1},{1,0},{2,3},{3,2},{4,5},{5,4},{6,7},{7,6},{8,9},{9,8},{10,11... | collective-permute-start | bytes 3145736 | tf_op jit(solution)/shard_map/ppermute | solution.py:507
  179.4 3.9 copy-start.16
  179.4 3.9 copy-start.17
  179.4 3.9 copy-start.11
  179.4 3.9 copy-start.12
  179.4 4.1 copy-start.14
  179.4 4.0 copy-start.15
  196.4 56.4 %collective-permute-start.18 = (f32[8,256,512]{2,1,0:T(8,128)}, f32[8,256,512]{2,1,0:T(8,128)}, u32[]{:S(2)}, u32[]{:S(2)}) collective-permute-start(f32[8,256,512]{2,1,0:T(8,128)} %get-tuple-element.126), channel_id=1, source_target_pairs={{0,2},{2,0},{4,6},{6,4},{8,10},{10,8},{12,14},{14,12},{16,18},{18,... | collective-permute-start | bytes 12582920 | tf_op jit(solution)/shard_map/ppermute | solution.py:507
  203.2 1.0 copy-start.8
  204.2 4.4 copy-start.13
  209.5 10.4 %copy-start.19 = (bf16[256,2048]{1,0:T(8,128)(2,1)S(1)}, bf16[256,2048]{1,0:T(8,128)(2,1)}, u32[]{:S(2)}) copy-start(bf16[256,2048]{1,0:T(8,128)(2,1)} %get-tuple-element.99.refs_3_) | copy-start | bytes 3145732
  219.1 39.3 %collective-permute-start.10 = (f32[8,64,2048]{2,1,0:T(8,128)}, f32[8,64,2048]{2,1,0:T(8,128)}, u32[]{:S(2)}, u32[]{:S(2)}) collective-permute-start(f32[8,64,2048]{2,1,0:T(8,128)} %get-tuple-element.108), channel_id=1, source_target_pairs={{0,2},{2,0},{4,6},{6,4},{8,10},{10,8},{12,14},{14,12},{16,18},{18,... | collective-permute-start | bytes 12582920 | tf_op jit(solution)/shard_map/ppermute | solution.py:507
  219.4 8.6 %copy-start.2 = (f32[8,64,2048]{2,1,0:T(8,128)S(1)}, f32[8,64,2048]{2,1,0:T(8,128)}, u32[]{:S(2)}) copy-start(f32[8,64,2048]{2,1,0:T(8,128)} %get-tuple-element.133) | copy-start | bytes 12582916
  219.4 6.5 %collective-permute-start.14 = (f32[8,1,576]{2,1,0:T(1,128)S(1)}, f32[8,1,576]{2,1,0:T(1,128)S(1)}, u32[]{:S(2)}, u32[]{:S(2)}) collective-permute-start(f32[8,1,576]{2,1,0:T(1,128)S(1)} %get-tuple-element.166), channel_id=1, source_target_pairs={{0,2},{2,0},{4,6},{6,4},{8,10},{10,8},{12,14},{14,12},{16,18},{18,... | collective-permute-start | bytes 55304 | tf_op jit(solution)/shard_map/ppermute | solution.py:507
  225.9 25.5 %collective-permute-start.8 = (f32[256,1024]{1,0:T(8,128)S(1)}, f32[256,1024]{1,0:T(8,128)}, u32[]{:S(2)}, u32[]{:S(2)}) collective-permute-start(f32[256,1024]{1,0:T(8,128)S(1)} %fusion.21), channel_id=1, source_target_pairs={{0,1},{1,0},{2,3},{3,2},{4,5},{5,4},{6,7},{7,6},{8,9},{9,8},{10,11... | collective-permute-start | bytes 3145736 | tf_op jit(solution)/shard_map/ppermute | solution.py:507
  226.9 5.6 %collective-permute-start.15 = (f32[4,1,576]{2,1,0:T(1,128)S(1)}, f32[4,1,576]{2,1,0:T(1,128)S(1)}, u32[]{:S(2)}, u32[]{:S(2)}) collective-permute-start(f32[4,1,576]{2,1,0:T(1,128)S(1)} %get-tuple-element.164), channel_id=1, source_target_pairs={{0,4},{2,6},{4,0},{6,2},{8,12},{10,14},{12,8},{14,10},{16,20},{18,... | collective-permute-start | bytes 27656 | tf_op jit(solution)/shard_map/ppermute | solution.py:507
  228.0 6.2 %copy-start.1 = (f32[8,64,2048]{2,1,0:T(8,128)S(1)}, f32[8,64,2048]{2,1,0:T(8,128)}, u32[]{:S(2)}) copy-start(f32[8,64,2048]{2,1,0:T(8,128)} %get-tuple-element.131) | copy-start | bytes 12582916
  232.5 48.7 %collective-permute-start.27 = (f32[4,64,2048]{2,1,0:T(8,128)}, f32[4,64,2048]{2,1,0:T(8,128)S(1)}, u32[]{:S(2)}, u32[]{:S(2)}) collective-permute-start(f32[4,64,2048]{2,1,0:T(8,128)} %get-tuple-element.144), channel_id=1, source_target_pairs={{0,4},{2,6},{4,0},{6,2},{8,12},{10,14},{12,8},{14,10},{16,20},{18,... | collective-permute-start | bytes 6291464 | tf_op jit(solution)/shard_map/ppermute | solution.py:507
  233.5 5.1 %collective-permute-start.16 = (f32[2,1,576]{2,1,0:T(1,128)S(1)}, f32[2,1,576]{2,1,0:T(1,128)S(1)}, u32[]{:S(2)}, u32[]{:S(2)}) collective-permute-start(f32[2,1,576]{2,1,0:T(1,128)S(1)} %get-tuple-element.168), channel_id=1, source_target_pairs={{0,8},{2,10},{4,12},{6,14},{8,0},{10,2},{12,4},{14,6},{16,24},{18,... | collective-permute-start | bytes 13832 | tf_op jit(solution)/shard_map/ppermute | solution.py:507
  238.6 9.7 %collective-permute-start.17 = (f32[1,1,576]{2,1,0:T(1,128)S(1)}, f32[1,1,576]{2,1,0:T(1,128)S(1)}, u32[]{:S(2)}, u32[]{:S(2)}) collective-permute-start(f32[1,1,576]{2,1,0:T(1,128)S(1)} %slice_add_fusion.28), channel_id=1, source_target_pairs={{0,16},{2,18},{4,20},{6,22},{8,24},{10,26},{12,28},{14,30},{16,0},... | collective-permute-start | bytes 6920 | tf_op jit(solution)/shard_map/ppermute | solution.py:507
  248.3 77.9 %collective-permute-start.23 = (f32[4,64,2048]{2,1,0:T(8,128)}, f32[4,64,2048]{2,1,0:T(8,128)S(1)}, u32[]{:S(2)}, u32[]{:S(2)}) collective-permute-start(f32[4,64,2048]{2,1,0:T(8,128)} %get-tuple-element.146), channel_id=1, source_target_pairs={{0,4},{2,6},{4,0},{6,2},{8,12},{10,14},{12,8},{14,10},{16,20},{18,... | collective-permute-start | bytes 6291464 | tf_op jit(solution)/shard_map/ppermute | solution.py:507
  251.5 31.3 %collective-permute-start.9 = (f32[256,1024]{1,0:T(8,128)}, f32[256,1024]{1,0:T(8,128)S(1)}, u32[]{:S(2)}, u32[]{:S(2)}) collective-permute-start(f32[256,1024]{1,0:T(8,128)} %fusion.22), channel_id=1, source_target_pairs={{0,1},{1,0},{2,3},{3,2},{4,5},{5,4},{6,7},{7,6},{8,9},{9,8},{10,11... | collective-permute-start | bytes 3145736 | tf_op jit(solution)/shard_map/ppermute | solution.py:507
  252.8 5.6 %copy-start.3 = (f32[8,64,2048]{2,1,0:T(8,128)S(1)}, f32[8,64,2048]{2,1,0:T(8,128)}, u32[]{:S(2)}) copy-start(f32[8,64,2048]{2,1,0:T(8,128)} %get-tuple-element.107) | copy-start | bytes 12582916
  257.4 113.7 %collective-permute-start.19 = (f32[4,256,512]{2,1,0:T(8,128)S(1)}, f32[4,256,512]{2,1,0:T(8,128)S(1)}, u32[]{:S(2)}, u32[]{:S(2)}) collective-permute-start(f32[4,256,512]{2,1,0:T(8,128)S(1)} %get-tuple-element.148), channel_id=1, source_target_pairs={{0,4},{2,6},{4,0},{6,2},{8,12},{10,14},{12,8},{14,10},{16,20},{18,... | collective-permute-start | bytes 6291464 | tf_op jit(solution)/shard_map/ppermute | solution.py:507
  261.4 153.5 %collective-permute-start.11 = (f32[4,64,2048]{2,1,0:T(8,128)S(1)}, f32[4,64,2048]{2,1,0:T(8,128)S(1)}, u32[]{:S(2)}, u32[]{:S(2)}) collective-permute-start(f32[4,64,2048]{2,1,0:T(8,128)S(1)} %get-tuple-element.150), channel_id=1, source_target_pairs={{0,4},{2,6},{4,0},{6,2},{8,12},{10,14},{12,8},{14,10},{16,20},{18,... | collective-permute-start | bytes 6291464 | tf_op jit(solution)/shard_map/ppermute | solution.py:507
  281.2 1.6 copy-start.4
  281.2 1.6 copy-start.5
  281.2 1.9 copy-start.6
  281.2 1.9 copy-start.18
  281.5 46.3 %collective-permute-start.28 = (f32[2,64,2048]{2,1,0:T(8,128)S(1)}, f32[2,64,2048]{2,1,0:T(8,128)S(1)}, u32[]{:S(2)}, u32[]{:S(2)}) collective-permute-start(f32[2,64,2048]{2,1,0:T(8,128)S(1)} %get-tuple-element.152), channel_id=1, source_target_pairs={{0,8},{2,10},{4,12},{6,14},{8,0},{10,2},{12,4},{14,6},{16,24},{18,... | collective-permute-start | bytes 3145736 | tf_op jit(solution)/shard_map/ppermute | solution.py:507
  326.5 90.0 %collective-permute-start.24 = (f32[2,64,2048]{2,1,0:T(8,128)S(1)}, f32[2,64,2048]{2,1,0:T(8,128)S(1)}, u32[]{:S(2)}, u32[]{:S(2)}) collective-permute-start(f32[2,64,2048]{2,1,0:T(8,128)S(1)} %get-tuple-element.154), channel_id=1, source_target_pairs={{0,8},{2,10},{4,12},{6,14},{8,0},{10,2},{12,4},{14,6},{16,24},{18,... | collective-permute-start | bytes 3145736 | tf_op jit(solution)/shard_map/ppermute | solution.py:507
  327.9 91.0 %collective-permute-start.29 = (f32[1,64,2048]{2,1,0:T(8,128)S(1)}, f32[1,64,2048]{2,1,0:T(8,128)S(1)}, u32[]{:S(2)}, u32[]{:S(2)}) collective-permute-start(f32[1,64,2048]{2,1,0:T(8,128)S(1)} %slice_add_fusion.16), channel_id=1, source_target_pairs={{0,16},{2,18},{4,20},{6,22},{8,24},{10,26},{12,28},{14,30},{16,0},... | collective-permute-start | bytes 1572872 | tf_op jit(solution)/shard_map/ppermute | solution.py:507
  371.7 48.1 %collective-permute-start.20 = (f32[2,256,512]{2,1,0:T(8,128)S(1)}, f32[2,256,512]{2,1,0:T(8,128)S(1)}, u32[]{:S(2)}, u32[]{:S(2)}) collective-permute-start(f32[2,256,512]{2,1,0:T(8,128)S(1)} %get-tuple-element.156), channel_id=1, source_target_pairs={{0,8},{2,10},{4,12},{6,14},{8,0},{10,2},{12,4},{14,6},{16,24},{18,... | collective-permute-start | bytes 3145736 | tf_op jit(solution)/shard_map/ppermute | solution.py:507
  415.2 45.9 %collective-permute-start.12 = (f32[2,64,2048]{2,1,0:T(8,128)S(1)}, f32[2,64,2048]{2,1,0:T(8,128)S(1)}, u32[]{:S(2)}, u32[]{:S(2)}) collective-permute-start(f32[2,64,2048]{2,1,0:T(8,128)S(1)} %get-tuple-element.158), channel_id=1, source_target_pairs={{0,8},{2,10},{4,12},{6,14},{8,0},{10,2},{12,4},{14,6},{16,24},{18,... | collective-permute-start | bytes 3145736 | tf_op jit(solution)/shard_map/ppermute | solution.py:507
  416.6 45.3 %collective-permute-start.25 = (f32[1,64,2048]{2,1,0:T(8,128)S(1)}, f32[1,64,2048]{2,1,0:T(8,128)S(1)}, u32[]{:S(2)}, u32[]{:S(2)}) collective-permute-start(f32[1,64,2048]{2,1,0:T(8,128)S(1)} %slice_add_fusion.18), channel_id=1, source_target_pairs={{0,16},{2,18},{4,20},{6,22},{8,24},{10,26},{12,28},{14,30},{16,0},... | collective-permute-start | bytes 1572872 | tf_op jit(solution)/shard_map/ppermute | solution.py:507
  419.9 55.6 %collective-permute-start.21 = (f32[1,256,512]{2,1,0:T(8,128)S(1)}, f32[1,256,512]{2,1,0:T(8,128)S(1)}, u32[]{:S(2)}, u32[]{:S(2)}) collective-permute-start(f32[1,256,512]{2,1,0:T(8,128)S(1)} %slice_add_fusion.20), channel_id=1, source_target_pairs={{0,16},{2,18},{4,20},{6,22},{8,24},{10,26},{12,28},{14,30},{16,0},... | collective-permute-start | bytes 1572872 | tf_op jit(solution)/shard_map/ppermute | solution.py:507
  461.2 25.0 %collective-permute-start.13 = (f32[1,64,2048]{2,1,0:T(8,128)S(1)}, f32[1,64,2048]{2,1,0:T(8,128)S(1)}, u32[]{:S(2)}, u32[]{:S(2)}) collective-permute-start(f32[1,64,2048]{2,1,0:T(8,128)S(1)} %slice_add_fusion.22), channel_id=1, source_target_pairs={{0,16},{2,18},{4,20},{6,22},{8,24},{10,26},{12,28},{14,30},{16,0},... | collective-permute-start | bytes 1572872 | tf_op jit(solution)/shard_map/ppermute | solution.py:507

commit v2 on v1

--- a/solution.py
+++ b/solution.py
@@ -34,7 +34,11 @@
 
 
 def cost(flops, nbytes, trans=0):
-    return pl.CostEstimate(flops=int(flops), bytes_accessed=int(nbytes), transcendentals=int(trans))
+    return pl.CostEstimate(flops=1000, bytes_accessed=1000, transcendentals=0)
+
+
+def long_cost():
+    return pl.CostEstimate(flops=int(1e11), bytes_accessed=1000, transcendentals=0)
 
 
 def whole(shape):
@@ -203,7 +207,7 @@
             jax.ShapeDtypeStruct((rows, width), F32),
         ],
         compiler_params=params(),
-        cost_estimate=cost(8 * rows * width * heads_wide * 2, 12 * rows * width * 2, rows * rows * 8),
+        cost_estimate=long_cost(),
         name="attn_forward",
     )(part, recv, table, gain, bias, w_qkv, q_bias, v_bias, w_out)
 
@@ -291,7 +295,7 @@
             jax.ShapeDtypeStruct((8, heads_wide), F32),
         ],
         compiler_params=params(),
-        cost_estimate=cost(8 * rows * width * heads_wide * 3, 20 * rows * width * 2, rows * rows * 8),
+        cost_estimate=long_cost(),
         name="attn_backward",
     )(gpart, grecv, x1, cotangent, gain, w_out, qkv, w_qkv)
 
@@ -356,7 +360,7 @@
             jax.ShapeDtypeStruct((1, hidden), F32),
         ],
         compiler_params=params(),
-        cost_estimate=cost(6 * rows * width * hidden, 8 * width * hidden, 2 * rows * hidden),
+        cost_estimate=long_cost(),
         name="mlp",
     )(x0, opart, orecv, out_bias, gain, bias, w_fc1, fc1_bias, w_fc2, cotangent)
 
@@ -387,7 +391,7 @@
             jax.ShapeDtypeStruct((8, width), F32),
         ],
         compiler_params=params(),
-        cost_estimate=cost(20 * rows * width, 18 * rows * width),
+        cost_estimate=long_cost(),
         name="first_norm_back",
     )(gpart, grecv, x0, dx1, gain)
 
@@ -429,78 +433,118 @@
         ),
         out_shape=jax.ShapeDtypeStruct((2 * rows, wide), BF16),
         compiler_params=params(),
-        cost_estimate=cost(4 * rows * wide * width, 4 * wide * width + 4 * rows * wide),
+        cost_estimate=long_cost(),
         name="pixel_grad",
     )(kinds, grad_a, grad_b, w_spectral, w_rgb, pick)
 
 
-def weight_grad_kernel(place, *refs, groups):
-    count = sum(2 + 2 * g for g in groups)
-    send_ref, keep_ref = refs[count:]
-    half = send_ref.shape[1] // sum(groups)
-    core = place[8]
-    base = 0
-    cursor = 0
-    for planes in groups:
-        left_a, left_b = refs[cursor], refs[cursor + 1]
-        for plane in range(planes):
-            right_a = refs[cursor + 2 + 2 * plane]
-            right_b = refs[cursor + 3 + 2 * plane]
-            total = tn(left_a[...], right_a[...]) + tn(left_b[...], right_b[...])
-            low, high = total[:half], total[half:]
-            spot = slice(base, base + half)
-
-            @pl.when(core == 0)
-            def _(low=low, high=high, spot=spot):
-                keep_ref[0, spot, :] = low
-                send_ref[0, spot, :] = high
-
-            @pl.when(core != 0)
-            def _(low=low, high=high, spot=spot):
-                send_ref[0, spot, :] = low
-                keep_ref[0, spot, :] = high
-
-            base += half
-        cursor += 2 + 2 * planes
-
-
-def weight_grad(place, sides, name):
-    operands, specs, groups = [], [], []
-    flops = 0
-    for left_a, left_b, rights in sides:
-        rows, width = left_a.shape
-        groups.append(len(rights))
-        for left in (left_a, left_b):
-            operands.append(left)
-            specs.append(pl.BlockSpec((rows, LANES), lambda n, pr: (0, pr[n])))
-        for right_a, right_b, plane in rights:
-            for right in (right_a, right_b):
-                operands.append(right)
-                if plane is None:
-                    specs.append(pl.BlockSpec(right.shape, lambda n, pr: (0, 0)))
-                else:
-                    specs.append(
-                        pl.BlockSpec((None,) + right.shape[1:], lambda n, pr, q=plane: (q, 0, 0))
-                    )
-            columns = right_a.shape[-1]
-            flops += 4 * rows * width * columns
+def turn(place, left_refs, turned_ref):
+    chips = turned_ref.shape[0] // LANES
+    half = LANES // 2
+    core = place[chips]
+    for chip in range(chips):
+        lanes = pl.ds(pl.multiple_of(place[chip] * LANES, LANES), LANES)
+        for pos, left_ref in enumerate(left_refs):
+            rows = left_ref.shape[0]
+            block = left_ref[:, lanes].T
+            columns = slice(pos * rows, (pos + 1) * rows)
+            low = pl.multiple_of(core * (chips * half) + chip * half, half)
+            high = pl.multiple_of((1 - core) * (chips * half) + chip * half, half)
+            turned_ref[pl.ds(low, half), columns] = block[:half]
+            turned_ref[pl.ds(high, half), columns] = block[half:]
+
+
+def emit(turned_ref, right_refs, send_ref, keep_ref):
+    middle = turned_ref.shape[0] // 2
+    for out_ref, rows in ((send_ref, slice(middle, None)), (keep_ref, slice(0, middle))):
+        total = None
+        for pos, right_ref in enumerate(right_refs):
+            depth = right_ref.shape[0]
+            term = nn(turned_ref[rows, pos * depth : (pos + 1) * depth], right_ref[...])
+            total = term if total is None else total + term
+        out_ref[...] = total.reshape(out_ref.shape)
+
+
+def plain_grad_kernel(place, la_ref, lb_ref, ra_ref, rb_ref, send_ref, keep_ref, turned_ref):
+    @pl.when(pl.program_id(0) == 0)
+    def _():
+        turn(place, (la_ref, lb_ref), turned_ref)
+
+    emit(turned_ref, (ra_ref, rb_ref), send_ref, keep_ref)
+
+
+def plain_grad(place, left_a, left_b, right_a, right_b, name, skip=0, columns=None):
+    rows, width = left_a.shape
+    columns = columns or right_a.shape[1]
     chips = width // LANES
     half = LANES // 2
-    block = (1, half * sum(groups), columns)
-    shape = jax.ShapeDtypeStruct((chips,) + block[1:], F32)
+    tile = 256
+    base = skip // tile
+    right = pl.BlockSpec((rows, tile), lambda n, *_: (0, n + base))
+    out = pl.BlockSpec((chips, half, tile), lambda n, *_: (0, 0, n))
+    shape = jax.ShapeDtypeStruct((chips, half, columns), F32)
     return pl.pallas_call(
-        functools.partial(weight_grad_kernel, groups=tuple(groups)),
+        plain_grad_kernel,
         grid_spec=pltpu.PrefetchScalarGridSpec(
             num_scalar_prefetch=1,
-            grid=(chips,),
-            in_specs=specs,
-            out_specs=[pl.BlockSpec(block, lambda n, pr: (n, 0, 0))] * 2,
+            grid=(columns // tile,),
+            in_specs=[whole(left_a.shape), whole(left_b.shape), right, right],
+            out_specs=[out, out],
+            scratch_shapes=[pltpu.VMEM((width, 2 * rows), BF16)],
         ),
         out_shape=[shape, shape],
         compiler_params=params(),
-        cost_estimate=cost(flops, 8 * chips * block[1] * columns),
+        cost_estimate=cost(4 * rows * width * columns, 4 * width * columns),
         name=name,
-    )(place, *operands)
+    )(place, left_a, left_b, right_a, right_b)
+
+
+def attn_grad_kernel(
+    place, aa_ref, ab_ref, ya_ref, yb_ref, da_ref, db_ref, ma_ref, mb_ref,
+    send_ref, keep_ref, turned_a, turned_y,
+):
+    plane, step = pl.program_id(0), pl.program_id(1)
+
+    @pl.when((plane == 0) & (step == 0))
+    def _():
+        turn(place, (aa_ref, ab_ref), turned_a)
+        turn(place, (ya_ref, yb_ref), turned_y)
+
+    @pl.when(plane < 3)
+    def _():
+        emit(turned_a, (da_ref, db_ref), send_ref, keep_ref)
+
+    @pl.when(plane == 3)
+    def _():
+        emit(turned_y, (ma_ref, mb_ref), send_ref, keep_ref)
+
+
+def attn_grad(place, a1, dya, dqkv, mix):
+    rows, width = a1[0].shape
+    columns = mix[0].shape[1]
+    chips = width // LANES
+    half = LANES // 2
+    tile = 256
+    side = whole((rows, width))
+    plane = pl.BlockSpec((None, rows, tile), lambda p, n, *_: (jnp.minimum(p, 2), 0, n))
+    mixed = pl.BlockSpec((rows, tile), lambda p, n, *_: (0, n))
+    out = pl.BlockSpec((chips, half, tile), lambda p, n, *_: (0, p, n))
+    shape = jax.ShapeDtypeStruct((chips, 4 * half, columns), F32)
+    scratch = pltpu.VMEM((width, 2 * rows), BF16)
+    return pl.pallas_call(
+        attn_grad_kernel,
+        grid_spec=pltpu.PrefetchScalarGridSpec(
+            num_scalar_prefetch=1,
+            grid=(4, columns // tile),
+            in_specs=[side, side, side, side, plane, plane, mixed, mixed],
+            out_specs=[out, out],
+            scratch_shapes=[scratch, scratch],
+        ),
+        out_shape=[shape, shape],
+        compiler_params=params(),
+        cost_estimate=cost(16 * rows * width * columns, 16 * width * columns),
+        name="attn_grad",
+    )(place, *a1, *dya, *dqkv, *mix)
 
 
 def exchange(values, axis, bit, size):
@@ -515,28 +559,73 @@
     return lax.optimization_barrier((first, values))[1]
 
 
-def halve(send, keep, size):
-    recv = exchange(send, "dp", 1, size)
-    block = keep.shape[0]
-    bit = 2
-    while block > 1:
-        block //= 2
-        out = keep[:block] + recv[:block]
-        kept = keep[block:] + recv[block:]
-        recv = exchange(out, "dp", bit, size)
-        keep = kept
-        bit *= 2
-    return (keep + recv)[0]
-
-
-def places(size):
+X_FIRST = (2, 4, 8)
+Z_FIRST = (4, 2, 8)
+
+
+CORE_PIECES = 1
+
+
+class Halving:
+    def __init__(self, send, keep, bits, size, pieces=CORE_PIECES):
+        self.keep, self.bits, self.size = keep, bits, size
+        blocks = send.shape[0] // pieces
+        self.core = [
+            exchange(send[p * blocks : (p + 1) * blocks], "dp", 1, size) for p in range(pieces)
+        ]
+        self.recvs = []
+        self.at = 0
+
+    def from_core(self, first, count):
+        blocks = self.core[0].shape[0]
+        if count >= blocks:
+            return jnp.concatenate(self.core[first // blocks : (first + count) // blocks], 0)
+        start = first % blocks
+        return self.core[first // blocks][start : start + count]
+
+    def step(self, order=None):
+        if order is not None:
+            if self.recvs:
+                self.recvs[-1] = order.tie(self.recvs[-1])
+            else:
+                self.core = list(order.tie(tuple(self.core)))
+        left = self.keep.shape[0] >> self.at
+        if left == 1:
+            count = 1
+        else:
+            count = left // 2
+        total = self.keep.shape[0] - left
+        value = self.keep[total : total + count] + self.from_core(total, count)
+        for recv in self.recvs:
+            first = recv.shape[0] - left
+            value = value + recv[first : first + count]
+        if order is not None:
+            order.mark(value)
+        if left == 1:
+            return value[0]
+        self.recvs.append(exchange(value, "dp", self.bits[self.at], self.size))
+        self.at += 1
+        return None
+
+
+class Order:
+    def __init__(self):
+        self.last = None
+
+    def tie(self, values):
+        return values if self.last is None else after(self.last, values)
+
+    def mark(self, values):
+        self.last = values
+
+
+def places(bits):
     me = lax.axis_index("dp")
     chip = me // 2
     core = me % 2
     order = []
     for p in range(8):
-        b2, b1, b0 = (p >> 2) & 1, (p >> 1) & 1, p & 1
-        order.append((1 - b2) + 2 * (1 - b1) + 4 * (1 - b0))
+        order.append(sum((1 - ((p >> (2 - n)) & 1)) * (bits[n] // 2) for n in range(3)))
     flips = jnp.array(order, jnp.int32)
     return jnp.concatenate([chip ^ flips, core[None]]).astype(jnp.int32)
 
@@ -571,92 +660,137 @@
     angle = ratio[:, None, None] * spot[None, :, None] * frequency[None, None, :]
     tables = jnp.concatenate([jnp.sin(angle), jnp.cos(angle)], -1)
 
-    part, mixed = [None] * items, [None] * items
-    for i in range(items):
-        part[i], mixed[i] = embed(item_kinds, pixels, w_spectral, w_rgb, pick, i, rows)
-
+    def scatter(values):
+        return lax.psum_scatter(values, "dp", scatter_dimension=0, tiled=True)
+
+    def both(left, right):
+        return sum(tn(left[i], right[i]) for i in range(items))
+
+    order = Order()
     gate = None
 
-    def send(values):
+    def send(values, wait=True):
         nonlocal gate
         if gate is not None:
             values = after(gate, values)
         gate = swap(values)
         return gate
 
-    erecv = [send(part[i]) for i in range(items)]
-    fwd = []
-    orecv = []
+    if custom:
+        place_x, place_z = places(X_FIRST), places(Z_FIRST)
+
+    none = [None] * items
+    part, mixed, erecv, fwd, orecv, ffn, grecv, bwd, arecv, last, ycot = (list(none) for _ in range(11))
     for i in range(items):
-        fwd.append(attn_forward(part[i], erecv[i], tables[i], g1, c1, wqkv, qb, vb, w_out))
-        orecv.append(send(fwd[i][4]))
-    ffn = []
-    grecv = []
+        part[i], mixed[i] = embed(order.tie(item_kinds), pixels, w_spectral, w_rgb, pick, i, rows)
+        order.mark(part[i])
+        erecv[i] = send(part[i])
     for i in range(items):
-        ffn.append(
-            mlp(fwd[i][0], fwd[i][4], orecv[i], ob, g2, c2, w_fc1, b1, w_fc2, cotangent, i)
+        fwd[i] = attn_forward(
+            part[i], erecv[i], tables[i], order.tie(g1), c1, wqkv, qb, vb, w_out
         )
-        grecv.append(send(ffn[i][4]))
-    bwd = []
-    arecv = []
+        order.mark(fwd[i][4])
+        orecv[i] = send(fwd[i][4])
+    x0, a1, qkv, mix, _ = zip(*fwd)
+    cot = [cotangent[i * rows : (i + 1) * rows] for i in range(items)]
     for i in range(items):
-        bwd.append(
-            attn_backward(ffn[i][4], grecv[i], ffn[i][0], cotangent, g2, w_out, fwd[i][2], wqkv, i)
+        ffn[i] = mlp(
+            x0[i], fwd[i][4], orecv[i], order.tie(ob), g2, c2, w_fc1, b1, w_fc2, cotangent, i
         )
-        arecv.append(send(bwd[i][3]))
-    last = []
+        order.mark(ffn[i][4])
+        grecv[i] = send(ffn[i][4])
+        ycot[i] = nn(order.tie(ffn[i][2]), w_fc2)
+        order.mark(ycot[i])
+        if i == items - 1 and custom:
+            fc2_s = plain_grad(
+                order.tie(place_x), cot[0], cot[1], ffn[0][2], ffn[1][2], "fc2_grad"
+            )
+            order.mark(fc2_s[0])
+            fc2_h = Halving(*fc2_s, X_FIRST, size)
+    x1, a2, act, dpre, _, b1sum = zip(*ffn)
     for i in range(items):
-        last.append(first_norm_back(bwd[i][3], arecv[i], fwd[i][0], bwd[i][0], g1))
-
-    x0, a1, qkv, mix, _ = zip(*fwd)
-    x1, a2, act, dpre, _, b1sum = zip(*ffn)
+        bwd[i] = attn_backward(
+            ffn[i][4], grecv[i], x1[i], cotangent, order.tie(g2), w_out, qkv[i], wqkv, i
+        )
+        order.mark(bwd[i][3])
+        if custom and i == 0:
+            fc2_h.step(order)
+            fc1_s = plain_grad(order.tie(place_z), a2[0], a2[1], dpre[0], dpre[1], "fc1_grad")
+            order.mark(fc1_s[0])
+            fc1_h = Halving(*fc1_s, Z_FIRST, size)
+        if custom and i == items - 1:
+            fc1_h.step(order)
+            dqkv = [bwd[0][2], bwd[1][2]]
+            dya = [bwd[0][1], bwd[1][1]]
+            att_s = attn_grad(order.tie(place_x), a1, dya, dqkv, mix)
+            order.mark(att_s[0])
+            att_h = Halving(*att_s, X_FIRST, size)
+        arecv[i] = send(order.tie(bwd[i][3]))
     dx1, dya, dqkv, _, sums2, qvsum = zip(*bwd)
+    for i in range(items):
+        last[i] = first_norm_back(bwd[i][3], arecv[i], x0[i], dx1[i], order.tie(g1))
+        order.mark(last[i][0])
+        if custom and i == 0:
+            fc2_h.step(order)
+            fc1_h.step(order)
     dx0, sums1 = zip(*last)
-
-    cot = [cotangent[i * rows : (i + 1) * rows] for i in range(items)]
-    out_terms = [nn(act[i], w_fc2) for i in range(items)]
-    block_rows = []
-    for i in range(items):
-        got = send(out_terms[i])
-        block_rows.append((x1[i] + (out_terms[i] + got + fc2_bias)).astype(BF16))
-    block_out = jnp.concatenate(block_rows, 0)
-
-    pixels_grad = pixel_grad(item_kinds, dx0[0], dx0[1], w_spectral, w_rgb, pick)
+    if custom:
+        mid = mixed[0].shape[1] // 2
+        embx_s = plain_grad(
+            order.tie(place_x), dx0[0], dx0[1], mixed[0], mixed[1], "embed_grad_a", 0, mid
+        )
+        order.mark(embx_s[0])
+        embx_h = Halving(*embx_s, X_FIRST, size)
+        embz_s = plain_grad(
+            order.tie(place_z), dx0[0], dx0[1], mixed[0], mixed[1], "embed_grad_b", mid, mid
+        )
+        order.mark(embz_s[0])
+        embz_h = Halving(*embz_s, Z_FIRST, size)
+        fc2_h.step(order)
+        att_h.step(order)
+        fc1_h.step(order)
+
+    got = [send(order.tie(ycot[i])) for i in range(items)]
+    pixels_grad = pixel_grad(order.tie(item_kinds), dx0[0], dx0[1], w_spectral, w_rgb, pick)
+    order.mark(pixels_grad)
 
     vec2 = sums2[0] + sums2[1]
     vec1 = sums1[0] + sums1[1]
     qv = qvsum[0] + qvsum[1]
     b1s = b1sum[0] + b1sum[1]
-
+    pieces = [vec2[0], vec2[1], vec2[2], vec2[3], vec1[0], vec1[1], qv[0], qv[1], b1s[0]]
+    small = jnp.concatenate([v.reshape(size, -1) for v in pieces], 1)
     if custom:
-        place = places(size)
-        fc2_s = weight_grad(place, [(cot[0], cot[1], [(act[0], act[1], None)])], "fc2_grad")
-        fc1_s = weight_grad(place, [(a2[0], a2[1], [(dpre[0], dpre[1], None)])], "fc1_grad")
-        att_s = weight_grad(
-            place,
-            [
-                (a1[0], a1[1], [(dqkv[0], dqkv[1], p) for p in range(3)]),
-                (dya[0], dya[1], [(mix[0], mix[1], None)]),
-            ],
-            "attn_grad",
-        )
-        emb_s = weight_grad(place, [(dx0[0], dx0[1], [(mixed[0], mixed[1], None)])], "embed_grad")
-        fc2_g = halve(*fc2_s, size)
-        fc1_g = halve(*fc1_s, size)
-        att_g = halve(*att_s, size)
-        emb_g = halve(*emb_s, size)
-        shard = width // size
-        att_g = att_g.reshape(4, shard, -1)
+        cube = small.reshape(2, 2, 2, 2, -1)
+        chip, core = lax.axis_index("dp") // 2, place_x[8]
+        for axis, bit in ((0, 4), (1, 2), (2, 1)):
+            cube = jnp.where((chip & bit) == 0, jnp.flip(cube, axis), cube)
+        cube = jnp.transpose(cube, (2, 1, 0, 3, 4)).reshape(8, 2, 1, -1)
+        kept = jnp.where(core == 0, cube[:, 0], cube[:, 1])
+        gone = jnp.where(core == 0, cube[:, 1], cube[:, 0])
+        embx_h.step(order)
+        embz_h.step(order)
+        fc2_g = fc2_h.step(order)
+        small_h = Halving(order.tie(gone), kept, X_FIRST, size)
+        fc1_g = fc1_h.step(order)
+        small_h.step(order)
+        embz_h.step(order)
+        att_h.step(order)
+        small_h.step(order)
+        embx_h.step(order)
+        small_h.step(order)
+        embz_h.step(order)
+        att_h.step(order)
+        small = small_h.step(order)[0]
+        embx_h.step(order)
+        embz_g = embz_h.step(order)
+        att_g = att_h.step(order)
+        embx_g = embx_h.step(order)
+        emb_g = jnp.concatenate([embx_g, embz_g], 1)
+        att_g = att_g.reshape(4, width // size, -1)
         qkv_grad = jnp.transpose(att_g[:3], (1, 0, 2))
         out_grad = att_g[3].T
     else:
-
-        def scatter(values):
-            return lax.psum_scatter(values, "dp", scatter_dimension=0, tiled=True)
-
-        def both(left, right):
-            return sum(tn(left[i], right[i]) for i in range(items))
-
         fc2_g = scatter(both(cot, act))
         fc1_g = scatter(both(a2, dpre))
         emb_g = scatter(both(dx0, mixed))
@@ -669,20 +803,10 @@
             )
         )
         out_grad = scatter(both(dya, mix)).T
-
-    pieces = [vec2[0], vec2[1], vec2[2], vec2[3], vec1[0], vec1[1], qv[0], qv[1], b1s[0]]
-    small = jnp.concatenate([v.reshape(size, -1) for v in pieces], 1)
-    if custom:
-        cube = small.reshape(2, 2, 2, 2, -1)
-        chip, core = lax.axis_index("dp") // 2, place[8]
-        for axis, bit in ((0, 4), (1, 2), (2, 1)):
-            cube = jnp.where((chip & bit) == 0, jnp.flip(cube, axis), cube)
-        cube = jnp.transpose(cube, (2, 1, 0, 3, 4)).reshape(8, 2, 1, -1)
-        kept = jnp.where(core == 0, cube[:, 0], cube[:, 1])
-        gone = jnp.where(core == 0, cube[:, 1], cube[:, 0])
-        small = halve(gone, kept, size)[0]
-    else:
-        small = lax.psum_scatter(small, "dp", scatter_dimension=0, tiled=True)[0]
+        small = scatter(small)[0]
+    block_out = jnp.concatenate(
+        [(x1[i] + (ycot[i] + got[i] + fc2_bias)).astype(BF16) for i in range(items)], 0
+    )
     outs = []
     start = 0
     for v in pieces:

time: 490 us -> 397 us (0.81)
  waiting for transfers between devices: 285 us -> 165 us
  other arithmetic: 27.1 us -> 42.2 us
  starting transfers between devices: 34.6 us -> 41.1 us
    ppermute x30 -> x34, waiting for transfers between devices: 285 us -> 165 us  [exchange(): return lax.ppermute(values, axis, [(i, i ^ bit) for i in range(size)])]
    add x17 -> x23, other arithmetic: 18.3 us -> 33.7 us  [the longest x17 23.7 us: step(): value = value + recv[first:first + count]]
    ppermute x30 -> x34, starting transfers between devices: 34.6 us -> 41.1 us  [exchange(): return lax.ppermute(values, axis, [(i, i ^ bit) for i in range(size)])]
    pallas_call x4 -> x5, Pallas kernels: 41 us -> 44.6 us  [the longest x4 33.1 us: plain_grad(): pl.pallas_call(plain_grad_kernel, grid_spec=pltpu.PrefetchScalarGridSpec(...]
  transfers between devices with their start and end apart: 30 -> 34, of which waited for: 16 -> 14; matrix products, arithmetic and copies ran while one was open for 8% -> 14% of each run, Pallas kernels for 24% -> 30%
where the time goes in v2:
time: 397 us; the launch traced here: 396 us
  waiting for transfers between devices  165 us (42%)
  Pallas kernels  127 us (32%)
  other arithmetic  42.2 us (11%)
  starting transfers between devices  41.1 us (10%)
  local copies, waits for them, and re-layouts  11.6 us (3%)
  matrix products  6.99 us (2%)
    ppermute x34, waiting for transfers between devices, exchange(): return lax.ppermute(values, axis, [(i, i ^ bit) for i in range(size)])  165 us
    ppermute x34, starting transfers between devices, exchange(): return lax.ppermute(values, axis, [(i, i ^ bit) for i in range(size)])  41.1 us
    pallas_call x4, Pallas kernels, plain_grad(): pl.pallas_call(plain_grad_kernel, grid_spec=pltpu.PrefetchScalarGridSpec(...  33.1 us
    add x17, other arithmetic, step(): value = value + recv[first:first + count]  23.7 us
    pallas_call x2, Pallas kernels, attn_backward(): pl.pallas_call(attn_backward_kernel, grid=(steps,), in_specs=[whole(gpart...  19.9 us
    pallas_call x2, Pallas kernels, mlp(): pl.pallas_call(mlp_kernel, grid=(hidden // tile,), in_specs=[whole(x0.sha...  19.2 us
    pallas_call x2, Pallas kernels, attn_forward(): pl.pallas_call(attn_forward_kernel, grid=(steps,), in_specs=[whole(part.s...  14.5 us
    pallas_call x2, Pallas kernels, embed(): pl.pallas_call(functools.partial(embed_kernel, item=item), grid_spec=pltp...  13.6 us
  transfers between devices with their start and end apart: 34, of which 14 were waited for; matrix products, arithmetic and copies ran while one was open for 14% of the time, Pallas kernels for 30%

profile of v2, /device:TPU:0, one launch (start us, length us, event | category | flops | bytes accessed | tf_op | source)
XLA Modules:
  0.0 395.7 jit_solution(6959855013606325458)
XLA Ops:
  0.7 1.4 fusion.pick_ref
  2.1 6.8 %embed.2 = (f32[256,1024]{1,0:T(8,128)}, bf16[256,2048]{1,0:T(8,128)(2,1)}) custom-call(s32[2]{0:T(128)} %kinds.3, bf16[512,1664]{1,0:T(8,128)(2,1)} %pix_ref.3, bf16[1664,1024]{1,0:T(8,128)(2,1)} %wspec_ref.5, bf16[384,1024]{1,0:T(8,128)(2,1)} %wrgb_ref.5, bf16[1664,384]{1,0:T(8,128)(2,1)} %fusion.pick_ref), custom_call_target="tpu_custom_call" | custom-call | flops 1000 | bytes 1000 | tf_op jit(solution)/shard_map/embed/pallas_call | solution.py:94
  8.9 3.0 collective-permute-start
  13.1 6.8 %embed.3 = (f32[256,1024]{1,0:T(8,128)}, bf16[256,2048]{1,0:T(8,128)(2,1)}) custom-call(s32[2]{0:T(128)} %kinds.3, bf16[512,1664]{1,0:T(8,128)(2,1)} %pix_ref.3, bf16[1664,1024]{1,0:T(8,128)(2,1)} %wspec_ref.5, bf16[384,1024]{1,0:T(8,128)(2,1)} %wrgb_ref.5, bf16[1664,384]{1,0:T(8,128)(2,1)} %fusion.pick_ref), custom_call_target="tpu_custom_call" | custom-call | flops 1000 | bytes 1000 | tf_op jit(solution)/shard_map/embed/pallas_call | solution.py:94
  20.9 1.1 fusion.23
  21.9 13.3 %collective-permute-done.recv_ref = f32[256,1024]{1,0:T(8,128)S(1)} collective-permute-done((f32[256,1024]{1,0:T(8,128)}, f32[256,1024]{1,0:T(8,128)S(1)}, u32[]{:S(2)}, u32[]{:S(2)}) %collective-permute-start) | collective-permute-done | bytes 1048608 | tf_op jit(solution)/shard_map/ppermute | solution.py:551
  35.3 1.7 collective-permute-start.1
  37.0 7.2 %attn_forward.2 = (f32[256,1024]{1,0:T(8,128)}, bf16[256,1024]{1,0:T(8,128)(2,1)}, bf16[3,256,512]{2,1,0:T(8,128)(2,1)}, bf16[256,512]{1,0:T(8,128)(2,1)}, f32[256,1024]{1,0:T(8,128)}) custom-call(f32[256,1024]{1,0:T(8,128)} %get-tuple-element.124.part_ref, f32[256,1024]{1,0:T(8,128)} %copy-done.28, f32[16,512]{1,0:T(8,128)} %get-tuple-element.241.table_ref, ...), custom_call_target="tpu_custom_call" | custom-call | flops 99999997952 | bytes 1000 | tf_op jit(solution)/shard_map/attn_forward/pallas_call | solution.py:181
  44.3 15.6 %collective-permute-done.1.recv_ref = f32[256,1024]{1,0:T(8,128)S(1)} collective-permute-done((f32[256,1024]{1,0:T(8,128)}, f32[256,1024]{1,0:T(8,128)S(1)}, u32[]{:S(2)}, u32[]{:S(2)}) %collective-permute-start.1) | collective-permute-done | bytes 1048608 | tf_op jit(solution)/shard_map/ppermute | solution.py:551
  59.8 1.4 collective-permute-start.2
  61.2 7.2 %attn_forward.3 = (f32[256,1024]{1,0:T(8,128)}, bf16[256,1024]{1,0:T(8,128)(2,1)}, bf16[3,256,512]{2,1,0:T(8,128)(2,1)}, bf16[256,512]{1,0:T(8,128)(2,1)}, f32[256,1024]{1,0:T(8,128)}) custom-call(f32[256,1024]{1,0:T(8,128)} %get-tuple-element.130.part_ref, f32[256,1024]{1,0:T(8,128)} %copy-done.35, f32[16,512]{1,0:T(8,128)} %get-tuple-element.242.table_ref, ...), custom_call_target="tpu_custom_call" | custom-call | flops 99999997952 | bytes 1000 | tf_op jit(solution)/shard_map/attn_forward/pallas_call | solution.py:181
  68.5 15.0 %collective-permute-done.2.orecv_ref = f32[256,1024]{1,0:T(8,128)S(1)} collective-permute-done((f32[256,1024]{1,0:T(8,128)}, f32[256,1024]{1,0:T(8,128)S(1)}, u32[]{:S(2)}, u32[]{:S(2)}) %collective-permute-start.2) | collective-permute-done | bytes 1048608 | tf_op jit(solution)/shard_map/ppermute | solution.py:551
  83.4 1.1 collective-permute-start.3
  84.6 9.6 %mlp.2 = (f32[256,1024]{1,0:T(8,128)}, bf16[256,1024]{1,0:T(8,128)(2,1)}, bf16[256,2048]{1,0:T(8,128)(2,1)}, bf16[256,2048]{1,0:T(8,128)(2,1)}, f32[256,1024]{1,0:T(8,128)}, /*index=5*/f32[1,2048]{1,0:T(1,128)}) custom-call(f32[256,1024]{1,0:T(8,128)} %get-tuple-element.128.x0_ref, f32[256,1024]{1,0:T(8,128)} %get-tuple-element.131.opart_ref, ...), custom_call_target="tpu_custom_call" | custom-call | flops 99999997952 | bytes 1000 | tf_op jit(solution)/shard_map/mlp/pallas_call | solution.py:331
  94.2 3.5 fusion.24
  97.7 9.2 %collective-permute-done.3.orecv_ref = f32[256,1024]{1,0:T(8,128)S(1)} collective-permute-done((f32[256,1024]{1,0:T(8,128)}, f32[256,1024]{1,0:T(8,128)S(1)}, u32[]{:S(2)}, u32[]{:S(2)}) %collective-permute-start.3) | collective-permute-done | bytes 1048608 | tf_op jit(solution)/shard_map/ppermute | solution.py:551
  107.0 1.1 collective-permute-start.4
  108.1 9.6 %mlp.3 = (f32[256,1024]{1,0:T(8,128)}, bf16[256,1024]{1,0:T(8,128)(2,1)}, bf16[256,2048]{1,0:T(8,128)(2,1)}, bf16[256,2048]{1,0:T(8,128)(2,1)}, f32[256,1024]{1,0:T(8,128)}, /*index=5*/f32[1,2048]{1,0:T(1,128)}) custom-call(f32[256,1024]{1,0:T(8,128)} %get-tuple-element.141.x0_ref, f32[256,1024]{1,0:T(8,128)} %get-tuple-element.139.opart_ref, ...), custom_call_target="tpu_custom_call" | custom-call | flops 99999997952 | bytes 1000 | tf_op jit(solution)/shard_map/mlp/pallas_call | solution.py:331
  117.7 3.5 fusion.25
  121.2 10.2 %fc2_grad.1 = (f32[8,64,2048]{2,1,0:T(8,128)}, f32[8,64,2048]{2,1,0:T(8,128)}) custom-call(s32[9]{0:T(128)} %pad_add_fusion.place, bf16[256,1024]{1,0:T(8,128)(2,1)} %get-tuple-element.240.la_ref, bf16[256,1024]{1,0:T(8,128)(2,1)} %get-tuple-element.239.lb_ref, bf16[256,2048]{1,0:T(8,128)(2,1)} %get-tuple-element.138.ra_ref, ...), custom_call_target="tpu_custom_call" | custom-call | flops 1000 | bytes 1000 | tf_op jit(solution)/shard_map/fc2_grad/pallas_call | solution.py:486
  132.0 1.1 collective-permute-start.5
  133.1 10.0 %attn_backward.2 = (f32[256,1024]{1,0:T(8,128)}, bf16[256,1024]{1,0:T(8,128)(2,1)}, bf16[3,256,512]{2,1,0:T(8,128)(2,1)}, f32[256,1024]{1,0:T(8,128)}, f32[8,1024]{1,0:T(8,128)}, /*index=5*/f32[8,512]{1,0:T(8,128)}) custom-call(f32[256,1024]{1,0:T(8,128)} %get-tuple-element.140.gpart_ref, f32[256,1024]{1,0:T(8,128)} %copy-done.34, ...), custom_call_target="tpu_custom_call" | custom-call | flops 99999997952 | bytes 1000 | tf_op jit(solution)/shard_map/attn_backward/pallas_call | solution.py:268
  143.1 3.2 slice_add_fusion.2
  146.4 1.5 collective-permute-start.10
  147.9 9.9 %fc1_grad.1 = (f32[8,64,2048]{2,1,0:T(8,128)}, f32[8,64,2048]{2,1,0:T(8,128)}) custom-call(s32[9]{0:T(128)} %pad_add_fusion.1.place, bf16[256,1024]{1,0:T(8,128)(2,1)} %get-tuple-element.155.la_ref, bf16[256,1024]{1,0:T(8,128)(2,1)} %get-tuple-element.156.lb_ref, bf16[256,2048]{1,0:T(8,128)(2,1)} %get-tuple-element.157.ra_ref, ...), custom_call_target="tpu_custom_call" | custom-call | flops 1000 | bytes 1000 | tf_op jit(solution)/shard_map/fc1_grad/pallas_call | solution.py:486
  158.9 9.9 %attn_backward.3 = (f32[256,1024]{1,0:T(8,128)}, bf16[256,1024]{1,0:T(8,128)(2,1)}, bf16[3,256,512]{2,1,0:T(8,128)(2,1)}, f32[256,1024]{1,0:T(8,128)}, f32[8,1024]{1,0:T(8,128)}, /*index=5*/f32[8,512]{1,0:T(8,128)}) custom-call(f32[256,1024]{1,0:T(8,128)} %get-tuple-element.144.gpart_ref, f32[256,1024]{1,0:T(8,128)} %collective-permute-done.5.grecv_ref, ...), custom_call_target="tpu_custom_call" | custom-call | flops 99999997952 | bytes 1000 | tf_op jit(solution)/shard_map/attn_backward/pallas_call | solution.py:268
  174.5 2.6 slice_add_fusion.1
  177.0 1.3 collective-permute-start.11
  178.4 11.6 %attn_grad.1 = (f32[8,256,512]{2,1,0:T(8,128)}, f32[8,256,512]{2,1,0:T(8,128)}) custom-call(s32[9]{0:T(128)} %pad_add_fusion.place, bf16[256,1024]{1,0:T(8,128)(2,1)} %get-tuple-element.169.aa_ref, bf16[256,1024]{1,0:T(8,128)(2,1)} %get-tuple-element.170.ab_ref, bf16[256,1024]{1,0:T(8,128)(2,1)} %get-tuple-element.171.ya_ref, ...), custom_call_target="tpu_custom_call" | custom-call | flops 1000 | bytes 1000 | tf_op jit(solution)/shard_map/attn_grad/pallas_call | solution.py:534
  190.9 4.5 %first_norm_back.2 = (bf16[256,1024]{1,0:T(8,128)(2,1)}, f32[8,1024]{1,0:T(8,128)}) custom-call(f32[256,1024]{1,0:T(8,128)} %get-tuple-element.161.gpart_ref, f32[256,1024]{1,0:T(8,128)} %copy-done.31, f32[256,1024]{1,0:T(8,128)} %get-tuple-element.128.x0_ref, f32[256,1024]{1,0:T(8,128)} %get-tuple-element.180.dx1_ref, f32[1,1024]{1,0:T(1,128)} %bitcast.113), custom_call_target="tpu_custom_call" | custom-call | flops 99999997952 | bytes 1000 | tf_op jit(solution)/shard_map/first_norm_back/pallas_call | solution.py:384
  196.5 3.0 slice_add_fusion.7
  200.3 25.3 %collective-permute-done.11 = f32[4,64,2048]{2,1,0:T(8,128)S(1)} collective-permute-done((f32[4,64,2048]{2,1,0:T(8,128)S(1)}, f32[4,64,2048]{2,1,0:T(8,128)S(1)}, u32[]{:S(2)}, u32[]{:S(2)}) %collective-permute-start.11) | collective-permute-done | bytes 2097184 | tf_op jit(solution)/shard_map/ppermute | solution.py:551
  225.6 3.5 slice_add_fusion.6
  229.1 1.4 collective-permute-start.14
  231.5 4.4 %first_norm_back.3 = (bf16[256,1024]{1,0:T(8,128)(2,1)}, f32[8,1024]{1,0:T(8,128)}) custom-call(f32[256,1024]{1,0:T(8,128)} %get-tuple-element.179.gpart_ref, f32[256,1024]{1,0:T(8,128)} %copy-done.38, f32[256,1024]{1,0:T(8,128)} %get-tuple-element.141.x0_ref, f32[256,1024]{1,0:T(8,128)} %get-tuple-element.186.dx1_ref, f32[1,1024]{1,0:T(1,128)} %bitcast.114), custom_call_target="tpu_custom_call" | custom-call | flops 99999997952 | bytes 1000 | tf_op jit(solution)/shard_map/first_norm_back/pallas_call | solution.py:384
  236.0 6.7 %embed_grad_a.1 = (f32[8,64,1024]{2,1,0:T(8,128)}, f32[8,64,1024]{2,1,0:T(8,128)}) custom-call(s32[9]{0:T(128)} %pad_add_fusion.place, bf16[256,1024]{1,0:T(8,128)(2,1)} %get-tuple-element.182.la_ref.da_ref, bf16[256,1024]{1,0:T(8,128)(2,1)} %get-tuple-element.188.lb_ref.db_ref, bf16[256,2048]{1,0:T(8,128)(2,1)} %get-tuple-element.190.ra_ref, ...), custom_call_target="tpu_custom_call" | custom-call | flops 1000 | bytes 1000 | tf_op jit(solution)/shard_map/embed_grad_a/pallas_call | solution.py:486
  242.7 6.3 %embed_grad_b.1 = (f32[8,64,1024]{2,1,0:T(8,128)}, f32[8,64,1024]{2,1,0:T(8,128)}) custom-call(s32[9]{0:T(128)} %pad_add_fusion.1.place, bf16[256,1024]{1,0:T(8,128)(2,1)} %get-tuple-element.182.la_ref.da_ref, bf16[256,1024]{1,0:T(8,128)(2,1)} %get-tuple-element.188.lb_ref.db_ref, bf16[256,2048]{1,0:T(8,128)(2,1)} %get-tuple-element.190.ra_ref, ...), custom_call_target="tpu_custom_call" | custom-call | flops 1000 | bytes 1000 | tf_op jit(solution)/shard_map/embed_grad_b/pallas_call | solution.py:486
  250.0 1.6 slice_add_fusion.12
  251.7 2.5 collective-permute-start.19
  254.2 2.7 slice_add_fusion
  257.0 2.3 slice_add_fusion.11
  260.3 6.6 %pixel_grad.1 = bf16[512,1664]{1,0:T(8,128)(2,1)} custom-call(s32[2]{0:T(128)} %kinds.3, bf16[256,1024]{1,0:T(8,128)(2,1)} %get-tuple-element.182.la_ref.da_ref, bf16[256,1024]{1,0:T(8,128)(2,1)} %get-tuple-element.188.lb_ref.db_ref, bf16[1664,1024]{1,0:T(8,128)(2,1)} %wspec_ref.5, bf16[384,1024]{1,0:T(8,128)(2,1)} %wrgb_ref.5, bf16[1664,384]{1,0:T(8,128)(2,1)} %fusion.pick_ref), custom_call_target="tpu_custom_call" | custom-call | flops 99999997952 | bytes 1000 | tf_op jit(solution)/shard_map/pixel_grad/pallas_call | solution.py:420
  267.1 1.5 collective-permute-start.25
  268.6 1.4 slice_add_fusion.4
  270.0 1.8 collective-permute-start.22
  271.8 18.3 %collective-permute-done.19 = f32[1,64,2048]{2,1,0:T(8,128)} collective-permute-done((f32[1,64,2048]{2,1,0:T(8,128)S(1)}, f32[1,64,2048]{2,1,0:T(8,128)}, u32[]{:S(2)}, u32[]{:S(2)}) %collective-permute-start.19) | collective-permute-done | bytes 524320 | tf_op jit(solution)/shard_map/ppermute | solution.py:551
  291.1 2.6 add_add_fusion.1
  293.7 6.7 %collective-permute-done.20 = f32[1,64,2048]{2,1,0:T(8,128)} collective-permute-done((f32[1,64,2048]{2,1,0:T(8,128)}, f32[1,64,2048]{2,1,0:T(8,128)}, u32[]{:S(2)}, u32[]{:S(2)}) %collective-permute-start.20) | collective-permute-done | bytes 524320 | tf_op jit(solution)/shard_map/ppermute | solution.py:551
  300.4 2.4 add_add_fusion.2
  303.6 12.2 %collective-permute-done.22 = f32[4,64,1024]{2,1,0:T(8,128)S(1)} collective-permute-done((f32[4,64,1024]{2,1,0:T(8,128)S(1)}, f32[4,64,1024]{2,1,0:T(8,128)S(1)}, u32[]{:S(2)}, u32[]{:S(2)}) %collective-permute-start.22) | collective-permute-done | bytes 1048608 | tf_op jit(solution)/shard_map/ppermute | solution.py:551
  316.7 1.1 slice_add_fusion.10
  317.9 1.5 collective-permute-start.27
  319.4 1.9 slice_add_fusion.3
  321.4 9.6 %collective-permute-done.24 = f32[4,1,576]{2,1,0:T(1,128)S(1)} collective-permute-done((f32[4,1,576]{2,1,0:T(1,128)S(1)}, f32[4,1,576]{2,1,0:T(1,128)S(1)}, u32[]{:S(2)}, u32[]{:S(2)}) %collective-permute-start.24) | collective-permute-done | bytes 9248 | tf_op jit(solution)/shard_map/ppermute | solution.py:551
  331.0 1.6 collective-permute-start.26
  333.2 6.2 %collective-permute-done.16 = f32[256,1024]{1,0:T(8,128)S(1)} collective-permute-done((f32[256,1024]{1,0:T(8,128)S(1)}, f32[256,1024]{1,0:T(8,128)S(1)}, u32[]{:S(2)}, u32[]{:S(2)}) %collective-permute-start.16) | collective-permute-done | bytes 1048608 | tf_op jit(solution)/shard_map/ppermute | solution.py:551
  341.3 6.3 %collective-permute-done.26 = f32[2,1,576]{2,1,0:T(1,128)S(1)} collective-permute-done((f32[2,1,576]{2,1,0:T(1,128)S(1)}, f32[2,1,576]{2,1,0:T(1,128)S(1)}, u32[]{:S(2)}, u32[]{:S(2)}) %collective-permute-start.26) | collective-permute-done | bytes 4640 | tf_op jit(solution)/shard_map/ppermute | solution.py:551
  347.6 7.6 %collective-permute-start.29 = (f32[1,1,576]{2,1,0:T(1,128)S(1)}, f32[1,1,576]{2,1,0:T(1,128)S(1)}, u32[]{:S(2)}, u32[]{:S(2)}) collective-permute-start(f32[1,1,576]{2,1,0:T(1,128)S(1)} %fusion.12), channel_id=1, source_target_pairs={{0,16},{2,18},{4,20},{6,22},{8,24},{10,26},{12,28},{14,30},{16,0},... | collective-permute-start | bytes 6920 | tf_op jit(solution)/shard_map/ppermute | solution.py:551
  356.3 1.4 slice_add_fusion.8
  357.7 3.0 collective-permute-start.32
  361.3 3.7 collective-permute-done.30
  366.3 16.4 %collective-permute-done.31 = f32[1,64,1024]{2,1,0:T(8,128)S(1)} collective-permute-done((f32[1,64,1024]{2,1,0:T(8,128)S(1)}, f32[1,64,1024]{2,1,0:T(8,128)S(1)}, u32[]{:S(2)}, u32[]{:S(2)}) %collective-permute-start.31) | collective-permute-done | bytes 262176 | tf_op jit(solution)/shard_map/ppermute | solution.py:551
  384.4 7.4 %collective-permute-done.32 = f32[1,256,512]{2,1,0:T(8,128)S(1)} collective-permute-done((f32[1,256,512]{2,1,0:T(8,128)S(1)}, f32[1,256,512]{2,1,0:T(8,128)S(1)}, u32[]{:S(2)}, u32[]{:S(2)}) %collective-permute-start.32) | collective-permute-done | bytes 524320 | tf_op jit(solution)/shard_map/ppermute | solution.py:551
  391.8 1.5 add_add_fusion
  (170 shorter events, 28.0 us)
Async XLA Ops:
  2.1 9.8 %copy-start.24 = (s32[8]{0:T(128)S(1)}, s32[8]{0:T(128)}, u32[]{:S(2)}) copy-start(s32[8]{0:T(128)} %constant.75.clone) | copy-start | bytes 100
  2.1 9.8 %copy-start.25 = (s32[8]{0:T(128)S(1)}, s32[8]{0:T(128)}, u32[]{:S(2)}) copy-start(s32[8]{0:T(128)} %constant.74.clone) | copy-start | bytes 100
  8.9 26.3 %collective-permute-start = (f32[256,1024]{1,0:T(8,128)}, f32[256,1024]{1,0:T(8,128)S(1)}, u32[]{:S(2)}, u32[]{:S(2)}) collective-permute-start(f32[256,1024]{1,0:T(8,128)} %get-tuple-element.124.part_ref), channel_id=1, source_target_pairs={{0,1},{1,0},{2,3},{3,2},{4,5},{5,4},{6,7},{7,6},{8,9},{9,8},{10,11... | collective-permute-start | bytes 3145736 | tf_op jit(solution)/shard_map/ppermute | solution.py:551
  13.1 7.8 %copy-start.9 = (bf16[512,1024]{1,0:T(8,128)(2,1)S(1)}, bf16[512,1024]{1,0:T(8,128)(2,1)}, u32[]{:S(2)}) copy-start(bf16[512,1024]{1,0:T(8,128)(2,1)} %cot_ref.7) | copy-start | bytes 3145732
  35.3 24.6 %collective-permute-start.1 = (f32[256,1024]{1,0:T(8,128)}, f32[256,1024]{1,0:T(8,128)S(1)}, u32[]{:S(2)}, u32[]{:S(2)}) collective-permute-start(f32[256,1024]{1,0:T(8,128)} %get-tuple-element.130.part_ref), channel_id=1, source_target_pairs={{0,1},{1,0},{2,3},{3,2},{4,5},{5,4},{6,7},{7,6},{8,9},{9,8},{10,11... | collective-permute-start | bytes 3145736 | tf_op jit(solution)/shard_map/ppermute | solution.py:551
  59.8 23.6 %collective-permute-start.2 = (f32[256,1024]{1,0:T(8,128)}, f32[256,1024]{1,0:T(8,128)S(1)}, u32[]{:S(2)}, u32[]{:S(2)}) collective-permute-start(f32[256,1024]{1,0:T(8,128)} %get-tuple-element.131.opart_ref), channel_id=1, source_target_pairs={{0,1},{1,0},{2,3},{3,2},{4,5},{5,4},{6,7},{7,6},{8,9},{9,8},{10,11... | collective-permute-start | bytes 3145736 | tf_op jit(solution)/shard_map/ppermute | solution.py:551
  83.4 23.5 %collective-permute-start.3 = (f32[256,1024]{1,0:T(8,128)}, f32[256,1024]{1,0:T(8,128)S(1)}, u32[]{:S(2)}, u32[]{:S(2)}) collective-permute-start(f32[256,1024]{1,0:T(8,128)} %get-tuple-element.139.opart_ref), channel_id=1, source_target_pairs={{0,1},{1,0},{2,3},{3,2},{4,5},{5,4},{6,7},{7,6},{8,9},{9,8},{10,11... | collective-permute-start | bytes 3145736 | tf_op jit(solution)/shard_map/ppermute | solution.py:551
  84.6 9.6 %copy-start.26 = (bf16[2048,1024]{1,0:T(8,128)(2,1)S(1)}, bf16[2048,1024]{1,0:T(8,128)(2,1)}, u32[]{:S(2)}) copy-start(bf16[2048,1024]{1,0:T(8,128)(2,1)} %wfc2_ref.3) | copy-start | bytes 12582916
  94.2 12.8 %copy-start.33 = (f32[256,1024]{1,0:T(8,128)S(1)}, f32[256,1024]{1,0:T(8,128)}, u32[]{:S(2)}) copy-start(f32[256,1024]{1,0:T(8,128)} %get-tuple-element.140.gpart_ref) | copy-start | bytes 3145732
  107.0 25.0 %collective-permute-start.4 = (f32[256,1024]{1,0:T(8,128)S(1)}, f32[256,1024]{1,0:T(8,128)S(1)}, u32[]{:S(2)}, u32[]{:S(2)}) collective-permute-start(f32[256,1024]{1,0:T(8,128)S(1)} %copy-done.33), channel_id=1, source_target_pairs={{0,1},{1,0},{2,3},{3,2},{4,5},{5,4},{6,7},{7,6},{8,9},{9,8},{10,11... | collective-permute-start | bytes 3145736 | tf_op jit(solution)/shard_map/ppermute | solution.py:551
  108.1 9.6 %copy-start.27 = (bf16[2048,1024]{1,0:T(8,128)(2,1)S(1)}, bf16[2048,1024]{1,0:T(8,128)(2,1)}, u32[]{:S(2)}) copy-start(bf16[2048,1024]{1,0:T(8,128)(2,1)} %wfc2_ref.3) | copy-start | bytes 12582916
  121.2 10.2 %copy-start.21 = (f32[1,2048]{1,0:T(1,128)S(1)}, f32[1,2048]{1,0:T(1,128)}, u32[]{:S(2)}) copy-start(f32[1,2048]{1,0:T(1,128)} %get-tuple-element.211) | copy-start | bytes 24580
  121.2 10.2 %copy-start.22 = (f32[1,2048]{1,0:T(1,128)S(1)}, f32[1,2048]{1,0:T(1,128)}, u32[]{:S(2)}) copy-start(f32[1,2048]{1,0:T(1,128)} %get-tuple-element.212) | copy-start | bytes 24580
  121.2 10.8 %copy-start.32 = (f32[256,1024]{1,0:T(8,128)S(1)}, f32[256,1024]{1,0:T(8,128)}, u32[]{:S(2)}) copy-start(f32[256,1024]{1,0:T(8,128)} %get-tuple-element.144.gpart_ref) | copy-start | bytes 3145732
  131.4 11.7 %collective-permute-start.6 = (f32[8,64,2048]{2,1,0:T(8,128)}, f32[8,64,2048]{2,1,0:T(8,128)}, u32[]{:S(2)}, u32[]{:S(2)}) collective-permute-start(f32[8,64,2048]{2,1,0:T(8,128)} %get-tuple-element.149), channel_id=1, source_target_pairs={{0,2},{2,0},{4,6},{6,4},{8,10},{10,8},{12,14},{14,12},{16,18},{18,... | collective-permute-start | bytes 12582920 | tf_op jit(solution)/shard_map/ppermute | solution.py:551
  132.0 25.9 %collective-permute-start.5 = (f32[256,1024]{1,0:T(8,128)S(1)}, f32[256,1024]{1,0:T(8,128)}, u32[]{:S(2)}, u32[]{:S(2)}) collective-permute-start(f32[256,1024]{1,0:T(8,128)S(1)} %copy-done.32), channel_id=1, source_target_pairs={{0,1},{1,0},{2,3},{3,2},{4,5},{5,4},{6,7},{7,6},{8,9},{9,8},{10,11... | collective-permute-start | bytes 3145736 | tf_op jit(solution)/shard_map/ppermute | solution.py:551
  133.1 10.0 %copy-start.1 = (f32[8,64,2048]{2,1,0:T(8,128)S(1)}, f32[8,64,2048]{2,1,0:T(8,128)}, u32[]{:S(2)}) copy-start(f32[8,64,2048]{2,1,0:T(8,128)} %get-tuple-element.148) | copy-start | bytes 12582916
  146.4 11.5 %copy-start.29 = (f32[256,1024]{1,0:T(8,128)S(1)}, f32[256,1024]{1,0:T(8,128)}, u32[]{:S(2)}) copy-start(f32[256,1024]{1,0:T(8,128)} %get-tuple-element.161.gpart_ref) | copy-start | bytes 3145732
  146.4 49.1 %collective-permute-start.10 = (f32[4,64,2048]{2,1,0:T(8,128)}, f32[4,64,2048]{2,1,0:T(8,128)}, u32[]{:S(2)}, u32[]{:S(2)}) collective-permute-start(f32[4,64,2048]{2,1,0:T(8,128)} %slice_add_fusion.2), channel_id=1, source_target_pairs={{0,4},{2,6},{4,0},{6,2},{8,12},{10,14},{12,8},{14,10},{16,20},{18,... | collective-permute-start | bytes 6291464 | tf_op jit(solution)/shard_map/ppermute | solution.py:551
  157.8 16.7 %collective-permute-start.8 = (f32[8,64,2048]{2,1,0:T(8,128)}, f32[8,64,2048]{2,1,0:T(8,128)}, u32[]{:S(2)}, u32[]{:S(2)}) collective-permute-start(f32[8,64,2048]{2,1,0:T(8,128)} %get-tuple-element.159), channel_id=1, source_target_pairs={{0,2},{2,0},{4,6},{6,4},{8,10},{10,8},{12,14},{14,12},{16,18},{18,... | collective-permute-start | bytes 12582920 | tf_op jit(solution)/shard_map/ppermute | solution.py:551
  157.9 32.1 %collective-permute-start.7 = (f32[256,1024]{1,0:T(8,128)S(1)}, f32[256,1024]{1,0:T(8,128)S(1)}, u32[]{:S(2)}, u32[]{:S(2)}) collective-permute-start(f32[256,1024]{1,0:T(8,128)S(1)} %copy-done.29), channel_id=1, source_target_pairs={{0,1},{1,0},{2,3},{3,2},{4,5},{5,4},{6,7},{7,6},{8,9},{9,8},{10,11... | collective-permute-start | bytes 3145736 | tf_op jit(solution)/shard_map/ppermute | solution.py:551
  158.9 9.9 %copy-start.18 = (f32[8,1024]{1,0:T(8,128)S(1)}, f32[8,1024]{1,0:T(8,128)}, u32[]{:S(2)}) copy-start(f32[8,1024]{1,0:T(8,128)} %get-tuple-element.205) | copy-start | bytes 98308
  158.9 11.4 %copy-start.20 = (f32[8,512]{1,0:T(8,128)S(1)}, f32[8,512]{1,0:T(8,128)}, u32[]{:S(2)}) copy-start(f32[8,512]{1,0:T(8,128)} %get-tuple-element.209) | copy-start | bytes 49156
  177.0 48.5 %collective-permute-start.11 = (f32[4,64,2048]{2,1,0:T(8,128)S(1)}, f32[4,64,2048]{2,1,0:T(8,128)S(1)}, u32[]{:S(2)}, u32[]{:S(2)}) collective-permute-start(f32[4,64,2048]{2,1,0:T(8,128)S(1)} %slice_add_fusion.1), channel_id=1, source_target_pairs={{0,8},{2,10},{4,12},{6,14},{8,0},{10,2},{12,4},{14,6},{16,24},{18,... | collective-permute-start | bytes 6291464 | tf_op jit(solution)/shard_map/ppermute | solution.py:551
  189.9 64.3 %collective-permute-start.13 = (f32[8,256,512]{2,1,0:T(8,128)}, f32[8,256,512]{2,1,0:T(8,128)}, u32[]{:S(2)}, u32[]{:S(2)}) collective-permute-start(f32[8,256,512]{2,1,0:T(8,128)} %get-tuple-element.177), channel_id=1, source_target_pairs={{0,2},{2,0},{4,6},{6,4},{8,10},{10,8},{12,14},{14,12},{16,18},{18,... | collective-permute-start | bytes 12582920 | tf_op jit(solution)/shard_map/ppermute | solution.py:551
  195.4 35.0 %collective-permute-start.9 = (f32[256,1024]{1,0:T(8,128)S(1)}, f32[256,1024]{1,0:T(8,128)S(1)}, u32[]{:S(2)}, u32[]{:S(2)}) collective-permute-start(f32[256,1024]{1,0:T(8,128)S(1)} %copy-done.30), channel_id=1, source_target_pairs={{0,1},{1,0},{2,3},{3,2},{4,5},{5,4},{6,7},{7,6},{8,9},{9,8},{10,11... | collective-permute-start | bytes 3145736 | tf_op jit(solution)/shard_map/ppermute | solution.py:551
  199.5 50.5 %collective-permute-start.12 = (f32[2,64,2048]{2,1,0:T(8,128)}, f32[2,64,2048]{2,1,0:T(8,128)}, u32[]{:S(2)}, u32[]{:S(2)}) collective-permute-start(f32[2,64,2048]{2,1,0:T(8,128)} %slice_add_fusion.7), channel_id=1, source_target_pairs={{0,8},{2,10},{4,12},{6,14},{8,0},{10,2},{12,4},{14,6},{16,24},{18,... | collective-permute-start | bytes 3145736 | tf_op jit(solution)/shard_map/ppermute | solution.py:551
  225.6 10.3 %copy-start.4 = (f32[4,64,2048]{2,1,0:T(8,128)}, f32[4,64,2048]{2,1,0:T(8,128)S(1)}, u32[]{:S(2)}) copy-start(f32[4,64,2048]{2,1,0:T(8,128)S(1)} %collective-permute-done.11) | copy-start | bytes 6291460
  229.1 27.9 %collective-permute-start.14 = (f32[2,64,2048]{2,1,0:T(8,128)}, f32[2,64,2048]{2,1,0:T(8,128)S(1)}, u32[]{:S(2)}, u32[]{:S(2)}) collective-permute-start(f32[2,64,2048]{2,1,0:T(8,128)} %slice_add_fusion.6), channel_id=1, source_target_pairs={{0,4},{2,6},{4,0},{6,2},{8,12},{10,14},{12,8},{14,10},{16,20},{18,... | collective-permute-start | bytes 3145736 | tf_op jit(solution)/shard_map/ppermute | solution.py:551
  235.9 13.0 %copy-start.17 = (f32[8,1024]{1,0:T(8,128)S(1)}, f32[8,1024]{1,0:T(8,128)}, u32[]{:S(2)}) copy-start(f32[8,1024]{1,0:T(8,128)} %get-tuple-element.207) | copy-start | bytes 98308
  235.9 13.0 %copy-start.19 = (f32[8,1024]{1,0:T(8,128)S(1)}, f32[8,1024]{1,0:T(8,128)}, u32[]{:S(2)}) copy-start(f32[8,1024]{1,0:T(8,128)} %get-tuple-element.208) | copy-start | bytes 98308
  235.9 13.2 %copy-start.10 = (f32[1,2048]{1,0:T(1,128)S(1)}, f32[1,2048]{1,0:T(1,128)}, u32[]{:S(2)}) copy-start(f32[1,2048]{1,0:T(1,128)} %add.275) | copy-start | bytes 24580
  235.9 13.2 %copy-start.11 = (f32[2,2,2,2,32]{4,3,2,1,0:T(2,128)S(1)}, f32[2,2,2,2,32]{4,3,2,1,0:T(2,128)}, u32[]{:S(2)}) copy-start(f32[2,2,2,2,32]{4,3,2,1,0:T(2,128)} %concatenate.48) | copy-start | bytes 6148
  235.9 13.2 %copy-start.12 = (f32[2,2,2,2,32]{4,3,2,1,0:T(2,128)S(1)}, f32[2,2,2,2,32]{4,3,2,1,0:T(2,128)}, u32[]{:S(2)}) copy-start(f32[2,2,2,2,32]{4,3,2,1,0:T(2,128)} %concatenate.47) | copy-start | bytes 6148
  236.0 13.2 %copy-start.13 = (f32[2,2,2,2,64]{4,3,2,1,0:T(2,128)S(1)}, f32[2,2,2,2,64]{4,3,2,1,0:T(2,128)}, u32[]{:S(2)}) copy-start(f32[2,2,2,2,64]{4,3,2,1,0:T(2,128)} %concatenate.44) | copy-start | bytes 12292
  236.0 13.2 %copy-start.14 = (f32[2,2,2,2,64]{4,3,2,1,0:T(2,128)S(1)}, f32[2,2,2,2,64]{4,3,2,1,0:T(2,128)}, u32[]{:S(2)}) copy-start(f32[2,2,2,2,64]{4,3,2,1,0:T(2,128)} %concatenate.43) | copy-start | bytes 12292
  236.0 13.2 %copy-start.15 = (f32[2,2,2,2,64]{4,3,2,1,0:T(2,128)S(1)}, f32[2,2,2,2,64]{4,3,2,1,0:T(2,128)}, u32[]{:S(2)}) copy-start(f32[2,2,2,2,64]{4,3,2,1,0:T(2,128)} %concatenate.42) | copy-start | bytes 12292
  236.0 13.2 %copy-start.16 = (f32[2,2,2,2,64]{4,3,2,1,0:T(2,128)S(1)}, f32[2,2,2,2,64]{4,3,2,1,0:T(2,128)}, u32[]{:S(2)}) copy-start(f32[2,2,2,2,64]{4,3,2,1,0:T(2,128)} %concatenate.41) | copy-start | bytes 12292
  242.7 24.3 %collective-permute-start.17 = (f32[8,64,1024]{2,1,0:T(8,128)}, f32[8,64,1024]{2,1,0:T(8,128)S(1)}, u32[]{:S(2)}, u32[]{:S(2)}) collective-permute-start(f32[8,64,1024]{2,1,0:T(8,128)} %get-tuple-element.192), channel_id=1, source_target_pairs={{0,2},{2,0},{4,6},{6,4},{8,10},{10,8},{12,14},{14,12},{16,18},{18,... | collective-permute-start | bytes 6291464 | tf_op jit(solution)/shard_map/ppermute | solution.py:551
  249.5 19.1 %collective-permute-start.18 = (f32[8,64,1024]{2,1,0:T(8,128)}, f32[8,64,1024]{2,1,0:T(8,128)}, u32[]{:S(2)}, u32[]{:S(2)}) collective-permute-start(f32[8,64,1024]{2,1,0:T(8,128)} %get-tuple-element.194), channel_id=1, source_target_pairs={{0,2},{2,0},{4,6},{6,4},{8,10},{10,8},{12,14},{14,12},{16,18},{18,... | collective-permute-start | bytes 6291464 | tf_op jit(solution)/shard_map/ppermute | solution.py:551
  251.7 38.4 %collective-permute-start.19 = (f32[1,64,2048]{2,1,0:T(8,128)S(1)}, f32[1,64,2048]{2,1,0:T(8,128)}, u32[]{:S(2)}, u32[]{:S(2)}) collective-permute-start(f32[1,64,2048]{2,1,0:T(8,128)S(1)} %slice_add_fusion.12), channel_id=1, source_target_pairs={{0,16},{2,18},{4,20},{6,22},{8,24},{10,26},{12,28},{14,30},{16,0},... | collective-permute-start | bytes 1572872 | tf_op jit(solution)/shard_map/ppermute | solution.py:551
  259.2 7.7 %copy-start.2 = (f32[8,64,1024]{2,1,0:T(8,128)S(1)}, f32[8,64,1024]{2,1,0:T(8,128)}, u32[]{:S(2)}) copy-start(f32[8,64,1024]{2,1,0:T(8,128)} %get-tuple-element.203) | copy-start | bytes 6291460
  259.2 41.2 %collective-permute-start.20 = (f32[1,64,2048]{2,1,0:T(8,128)}, f32[1,64,2048]{2,1,0:T(8,128)}, u32[]{:S(2)}, u32[]{:S(2)}) collective-permute-start(f32[1,64,2048]{2,1,0:T(8,128)} %slice_add_fusion.11), channel_id=1, source_target_pairs={{0,16},{2,18},{4,20},{6,22},{8,24},{10,26},{12,28},{14,30},{16,0},... | collective-permute-start | bytes 1572872 | tf_op jit(solution)/shard_map/ppermute | solution.py:551
  259.7 59.7 %collective-permute-start.23 = (f32[4,256,512]{2,1,0:T(8,128)S(1)}, f32[4,256,512]{2,1,0:T(8,128)}, u32[]{:S(2)}, u32[]{:S(2)}) collective-permute-start(f32[4,256,512]{2,1,0:T(8,128)S(1)} %slice_add_fusion), channel_id=1, source_target_pairs={{0,4},{2,6},{4,0},{6,2},{8,12},{10,14},{12,8},{14,10},{16,20},{18,... | collective-permute-start | bytes 6291464 | tf_op jit(solution)/shard_map/ppermute | solution.py:551
  267.0 23.1 %copy-start.6 = (f32[256,1024]{1,0:T(8,128)S(1)}, f32[256,1024]{1,0:T(8,128)}, u32[]{:S(2)}) copy-start(f32[256,1024]{1,0:T(8,128)} %fusion.24) | copy-start | bytes 3145732
  267.1 65.5 %collective-permute-start.25 = (f32[4,64,1024]{2,1,0:T(8,128)S(1)}, f32[4,64,1024]{2,1,0:T(8,128)S(1)}, u32[]{:S(2)}, u32[]{:S(2)}) collective-permute-start(f32[4,64,1024]{2,1,0:T(8,128)S(1)} %slice_add_fusion.5), channel_id=1, source_target_pairs={{0,4},{2,6},{4,0},{6,2},{8,12},{10,14},{12,8},{14,10},{16,20},{18,... | collective-permute-start | bytes 3145736 | tf_op jit(solution)/shard_map/ppermute | solution.py:551
  270.0 45.8 %copy-start.8 = (f32[256,1024]{1,0:T(8,128)S(1)}, f32[256,1024]{1,0:T(8,128)}, u32[]{:S(2)}) copy-start(f32[256,1024]{1,0:T(8,128)} %fusion.25) | copy-start | bytes 3145732
  270.0 45.7 %collective-permute-start.22 = (f32[4,64,1024]{2,1,0:T(8,128)S(1)}, f32[4,64,1024]{2,1,0:T(8,128)S(1)}, u32[]{:S(2)}, u32[]{:S(2)}) collective-permute-start(f32[4,64,1024]{2,1,0:T(8,128)S(1)} %slice_add_fusion.4), channel_id=1, source_target_pairs={{0,8},{2,10},{4,12},{6,14},{8,0},{10,2},{12,4},{14,6},{16,24},{18,... | collective-permute-start | bytes 3145736 | tf_op jit(solution)/shard_map/ppermute | solution.py:551
  290.1 25.6 %collective-permute-start.15 = (f32[256,1024]{1,0:T(8,128)S(1)}, f32[256,1024]{1,0:T(8,128)S(1)}, u32[]{:S(2)}, u32[]{:S(2)}) collective-permute-start(f32[256,1024]{1,0:T(8,128)S(1)} %copy-done.6), channel_id=1, source_target_pairs={{0,1},{1,0},{2,3},{3,2},{4,5},{5,4},{6,7},{7,6},{8,9},{9,8},{10,11... | collective-permute-start | bytes 3145736 | tf_op jit(solution)/shard_map/ppermute | solution.py:551
  293.7 25.7 %copy-start = (f32[8,256,512]{2,1,0:T(8,128)S(1)}, f32[8,256,512]{2,1,0:T(8,128)}, u32[]{:S(2)}) copy-start(f32[8,256,512]{2,1,0:T(8,128)} %get-tuple-element.185) | copy-start | bytes 12582916
  300.4 2.4 collective-permute-start.21
  302.9 28.1 %collective-permute-start.24 = (f32[4,1,576]{2,1,0:T(1,128)S(1)}, f32[4,1,576]{2,1,0:T(1,128)S(1)}, u32[]{:S(2)}, u32[]{:S(2)}) collective-permute-start(f32[4,1,576]{2,1,0:T(1,128)S(1)} %fusion.7), channel_id=1, source_target_pairs={{0,4},{2,6},{4,0},{6,2},{8,12},{10,14},{12,8},{14,10},{16,20},{18,... | collective-permute-start | bytes 27656 | tf_op jit(solution)/shard_map/ppermute | solution.py:551
  315.8 23.7 %collective-permute-start.16 = (f32[256,1024]{1,0:T(8,128)S(1)}, f32[256,1024]{1,0:T(8,128)S(1)}, u32[]{:S(2)}, u32[]{:S(2)}) collective-permute-start(f32[256,1024]{1,0:T(8,128)S(1)} %copy-done.8), channel_id=1, source_target_pairs={{0,1},{1,0},{2,3},{3,2},{4,5},{5,4},{6,7},{7,6},{8,9},{9,8},{10,11... | collective-permute-start | bytes 3145736 | tf_op jit(solution)/shard_map/ppermute | solution.py:551
  317.9 21.6 %copy-start.5 = (f32[256,1024]{1,0:T(8,128)S(1)}, f32[256,1024]{1,0:T(8,128)}, u32[]{:S(2)}) copy-start(f32[256,1024]{1,0:T(8,128)} %get-tuple-element.135.x1_ref) | copy-start | bytes 3145732
  317.9 21.6 %copy-start.7 = (f32[256,1024]{1,0:T(8,128)S(1)}, f32[256,1024]{1,0:T(8,128)}, u32[]{:S(2)}) copy-start(f32[256,1024]{1,0:T(8,128)} %get-tuple-element.163.x1_ref) | copy-start | bytes 3145732
  317.9 21.6 %copy-start.23 = (f32[1024]{0:T(1024)S(1)}, f32[1024]{0:T(1024)}, u32[]{:S(2)}) copy-start(f32[1024]{0:T(1024)} %param.38) | copy-start | bytes 12292
  317.9 37.3 %collective-permute-start.27 = (f32[2,64,1024]{2,1,0:T(8,128)S(1)}, f32[2,64,1024]{2,1,0:T(8,128)S(1)}, u32[]{:S(2)}, u32[]{:S(2)}) collective-permute-start(f32[2,64,1024]{2,1,0:T(8,128)S(1)} %slice_add_fusion.10), channel_id=1, source_target_pairs={{0,4},{2,6},{4,0},{6,2},{8,12},{10,14},{12,8},{14,10},{16,20},{18,... | collective-permute-start | bytes 1572872 | tf_op jit(solution)/shard_map/ppermute | solution.py:551
  321.3 35.0 %collective-permute-start.28 = (f32[2,256,512]{2,1,0:T(8,128)S(1)}, f32[2,256,512]{2,1,0:T(8,128)S(1)}, u32[]{:S(2)}, u32[]{:S(2)}) collective-permute-start(f32[2,256,512]{2,1,0:T(8,128)S(1)} %slice_add_fusion.3), channel_id=1, source_target_pairs={{0,8},{2,10},{4,12},{6,14},{8,0},{10,2},{12,4},{14,6},{16,24},{18,... | collective-permute-start | bytes 3145736 | tf_op jit(solution)/shard_map/ppermute | solution.py:551
  331.0 16.6 %collective-permute-start.26 = (f32[2,1,576]{2,1,0:T(1,128)S(1)}, f32[2,1,576]{2,1,0:T(1,128)S(1)}, u32[]{:S(2)}, u32[]{:S(2)}) collective-permute-start(f32[2,1,576]{2,1,0:T(1,128)S(1)} %fusion.9), channel_id=1, source_target_pairs={{0,8},{2,10},{4,12},{6,14},{8,0},{10,2},{12,4},{14,6},{16,24},{18,... | collective-permute-start | bytes 13832 | tf_op jit(solution)/shard_map/ppermute | solution.py:551
  332.7 32.3 %collective-permute-start.30 = (f32[2,64,1024]{2,1,0:T(8,128)S(1)}, f32[2,64,1024]{2,1,0:T(8,128)S(1)}, u32[]{:S(2)}, u32[]{:S(2)}) collective-permute-start(f32[2,64,1024]{2,1,0:T(8,128)S(1)} %slice_add_fusion.9), channel_id=1, source_target_pairs={{0,8},{2,10},{4,12},{6,14},{8,0},{10,2},{12,4},{14,6},{16,24},{18,... | collective-permute-start | bytes 1572872 | tf_op jit(solution)/shard_map/ppermute | solution.py:551
  347.6 13.1 %collective-permute-start.29 = (f32[1,1,576]{2,1,0:T(1,128)S(1)}, f32[1,1,576]{2,1,0:T(1,128)S(1)}, u32[]{:S(2)}, u32[]{:S(2)}) collective-permute-start(f32[1,1,576]{2,1,0:T(1,128)S(1)} %fusion.12), channel_id=1, source_target_pairs={{0,16},{2,18},{4,20},{6,22},{8,24},{10,26},{12,28},{14,30},{16,0},... | collective-permute-start | bytes 6920 | tf_op jit(solution)/shard_map/ppermute | solution.py:551
  356.2 26.5 %collective-permute-start.31 = (f32[1,64,1024]{2,1,0:T(8,128)S(1)}, f32[1,64,1024]{2,1,0:T(8,128)S(1)}, u32[]{:S(2)}, u32[]{:S(2)}) collective-permute-start(f32[1,64,1024]{2,1,0:T(8,128)S(1)} %slice_add_fusion.14), channel_id=1, source_target_pairs={{0,16},{2,18},{4,20},{6,22},{8,24},{10,26},{12,28},{14,30},{16,0},... | collective-permute-start | bytes 786440 | tf_op jit(solution)/shard_map/ppermute | solution.py:551
  357.7 34.1 %collective-permute-start.32 = (f32[1,256,512]{2,1,0:T(8,128)S(1)}, f32[1,256,512]{2,1,0:T(8,128)S(1)}, u32[]{:S(2)}, u32[]{:S(2)}) collective-permute-start(f32[1,256,512]{2,1,0:T(8,128)S(1)} %slice_add_fusion.8), channel_id=1, source_target_pairs={{0,16},{2,18},{4,20},{6,22},{8,24},{10,26},{12,28},{14,30},{16,0},... | collective-permute-start | bytes 1572872 | tf_op jit(solution)/shard_map/ppermute | solution.py:551
  366.3 28.5 %collective-permute-start.33 = (f32[1,64,1024]{2,1,0:T(8,128)S(1)}, f32[1,64,1024]{2,1,0:T(8,128)S(1)}, u32[]{:S(2)}, u32[]{:S(2)}) collective-permute-start(f32[1,64,1024]{2,1,0:T(8,128)S(1)} %slice_add_fusion.13), channel_id=1, source_target_pairs={{0,16},{2,18},{4,20},{6,22},{8,24},{10,26},{12,28},{14,30},{16,0},... | collective-permute-start | bytes 786440 | tf_op jit(solution)/shard_map/ppermute | solution.py:551
  (10 other events, 21.5 us)

commit v3 on v2

--- a/solution.py
+++ b/solution.py
@@ -13,8 +13,9 @@
 F32 = jnp.float32
 BF16 = jnp.bfloat16
 LANES = 128
-VMEM_LIMIT = 56 * 1024 * 1024
+MIB = 1024 * 1024
 QUAD = 256
+PART = 256
 
 
 def nn(left, right):
@@ -29,11 +30,11 @@
     return lax.dot_general(left, right, (((0,), (0,)), ((), ())), preferred_element_type=F32)
 
 
-def params(**extra):
-    return pltpu.CompilerParams(vmem_limit_bytes=VMEM_LIMIT, **extra)
-
-
-def cost(flops, nbytes, trans=0):
+def params(mib):
+    return pltpu.CompilerParams(vmem_limit_bytes=mib * MIB)
+
+
+def short_cost():
     return pl.CostEstimate(flops=1000, bytes_accessed=1000, transcendentals=0)
 
 
@@ -61,6 +62,104 @@
 
 def column_sum(values):
     return jnp.sum(values, 0, keepdims=True)
+
+
+def turn(place, source_ref, turned_ref, columns):
+    chips = turned_ref.shape[0] // LANES
+    half = LANES // 2
+    core = place[chips]
+    low = pl.multiple_of(core * (chips * half), half)
+    high = pl.multiple_of((1 - core) * (chips * half), half)
+    for chip in range(chips):
+        lanes = pl.ds(pl.multiple_of(place[chip] * LANES, LANES), LANES)
+        block = source_ref[:, lanes].T
+        turned_ref[pl.ds(low + chip * half, half), columns] = block[:half]
+        turned_ref[pl.ds(high + chip * half, half), columns] = block[half:]
+
+
+def spread(turned_ref, keep_ref, gone_ref, first=0):
+    middle = turned_ref.shape[0] // 2
+    keep_ref[...] = turned_ref[:middle, :]
+    for part in range(2):
+        start = middle + part * PART
+        gone_ref[first + part] = turned_ref[start : start + PART, :].astype(F32)
+
+
+def turn_cot_kernel(place, cot_ref, keep_ref, gone_ref, turned_ref):
+    turn(place, cot_ref, turned_ref, slice(None))
+    spread(turned_ref, keep_ref, gone_ref)
+
+
+def turn_cot(place, cotangent, rows):
+    width = cotangent.shape[1]
+    items = cotangent.shape[0] // rows
+    return pl.pallas_call(
+        turn_cot_kernel,
+        grid_spec=pltpu.PrefetchScalarGridSpec(
+            num_scalar_prefetch=1,
+            grid=(items,),
+            in_specs=[pl.BlockSpec((rows, width), lambda i, *_: (i, 0))],
+            out_specs=[
+                pl.BlockSpec((None, width // 2, rows), lambda i, *_: (i, 0, 0)),
+                pl.BlockSpec((2, PART, rows), lambda i, *_: (i, 0, 0)),
+            ],
+            scratch_shapes=[pltpu.VMEM((width, rows), BF16)],
+        ),
+        out_shape=[
+            jax.ShapeDtypeStruct((items, width // 2, rows), BF16),
+            jax.ShapeDtypeStruct((2 * items, PART, rows), F32),
+        ],
+        compiler_params=params(12),
+        cost_estimate=short_cost(),
+        name="turn_cotangent",
+    )(place, cotangent)
+
+
+def pack_kernel(values_ref, out_ref):
+    out_ref[0] = values_ref[...].astype(F32)
+
+
+def pack(values):
+    rows, columns = values.shape
+    return pl.pallas_call(
+        pack_kernel,
+        grid=(columns // PART,),
+        in_specs=[pl.BlockSpec((rows, PART), lambda n: (0, n))],
+        out_specs=pl.BlockSpec((1, rows, PART), lambda n: (n, 0, 0)),
+        out_shape=jax.ShapeDtypeStruct((columns // PART, rows, PART), F32),
+        compiler_params=params(8),
+        cost_estimate=short_cost(),
+        name="pack_pixels",
+    )(values)
+
+
+def pack_attn_kernel(place, a1_ref, o_ref, keep_ref, gone_ref, turned_ref):
+    turn(place, a1_ref, turned_ref, slice(None))
+    spread(turned_ref, keep_ref, gone_ref)
+    for part in range(o_ref.shape[1] // PART):
+        gone_ref[2 + part] = o_ref[:, part * PART : (part + 1) * PART].astype(F32)
+
+
+def pack_attn(place, a1, mix):
+    rows, width = a1.shape
+    parts = 2 + mix.shape[1] // PART
+    return pl.pallas_call(
+        pack_attn_kernel,
+        grid_spec=pltpu.PrefetchScalarGridSpec(
+            num_scalar_prefetch=1,
+            grid=(1,),
+            in_specs=[whole(a1.shape), whole(mix.shape)],
+            out_specs=[whole((width // 2, rows)), whole((parts, PART, rows))],
+            scratch_shapes=[pltpu.VMEM((width, rows), BF16)],
+        ),
+        out_shape=[
+            jax.ShapeDtypeStruct((width // 2, rows), BF16),
+            jax.ShapeDtypeStruct((parts, PART, rows), F32),
+        ],
+        compiler_params=params(12),
+        cost_estimate=short_cost(),
+        name="pack_attn",
+    )(place, a1, mix)
 
 
 def embed_kernel(kinds, pix_ref, wspec_ref, wrgb_ref, pick_ref, part_ref, mixed_ref, *, item):
@@ -111,8 +210,8 @@
             jax.ShapeDtypeStruct((rows, width), F32),
             jax.ShapeDtypeStruct((rows, wide + narrow), BF16),
         ],
-        compiler_params=params(),
-        cost_estimate=cost(2 * rows * wide * width, 2 * wide * width + 4 * rows * width),
+        compiler_params=params(16),
+        cost_estimate=short_cost(),
         name="embed",
     )(kinds, pixels, w_spectral, w_rgb, pick)
 
@@ -206,15 +305,15 @@
             jax.ShapeDtypeStruct((rows, heads_wide), BF16),
             jax.ShapeDtypeStruct((rows, width), F32),
         ],
-        compiler_params=params(),
+        compiler_params=params(24),
         cost_estimate=long_cost(),
         name="attn_forward",
     )(part, recv, table, gain, bias, w_qkv, q_bias, v_bias, w_out)
 
 
 def attn_backward_kernel(
-    gpart_ref, grecv_ref, x1_ref, cot_ref, gain_ref, wout_ref, qkv_ref, wqkv_ref,
-    dx1_ref, dya_ref, dqkv_ref, da1_ref, sums_ref, qvsum_ref,
+    place, gpart_ref, grecv_ref, x1_ref, cot_ref, gain_ref, wout_ref, qkv_ref, wqkv_ref,
+    dx1_ref, dya_ref, dqkv_ref, da1_ref, sums_ref, qvsum_ref, keep_ref, gone_ref, turned_ref,
 ):
     quad = pl.program_id(0)
     rows = x1_ref.shape[0]
@@ -234,6 +333,8 @@
         sums_ref[2:3, :] = column_sum(dya.astype(F32))
         sums_ref[3:4, :] = column_sum(cot)
         sums_ref[4:8, :] = jnp.zeros((4, sums_ref.shape[1]), F32)
+        turn(place, dya_ref, turned_ref, slice(None))
+        spread(turned_ref, keep_ref, gone_ref)
 
     dmix = nt(dya_ref[...], wout_ref[...]).astype(BF16)
     scale = HEAD_DIM**-0.5
@@ -256,36 +357,45 @@
     da1_ref[...] += (
         nt(dqkv_ref[0], wqkv_ref[0]) + nt(dqkv_ref[1], wqkv_ref[1]) + nt(dqkv_ref[2], wqkv_ref[2])
     )
+    steps = pl.num_programs(0)
+    for plane in range(3):
+        gone_ref[2 + plane * steps + quad] = dqkv_ref[plane].astype(F32)
     qvsum_ref[0:1, :] = column_sum(dqkv_ref[0].astype(F32))
     qvsum_ref[1:2, :] = column_sum(dqkv_ref[2].astype(F32))
     qvsum_ref[2:8, :] = jnp.zeros((6, qvsum_ref.shape[1]), F32)
 
 
-def attn_backward(gpart, grecv, x1, cotangent, gain, w_out, qkv, w_qkv, item):
+def attn_backward(place, gpart, grecv, x1, cotangent, gain, w_out, qkv, w_qkv, item):
     rows, width = x1.shape
     heads_wide = w_out.shape[0]
     steps = heads_wide // QUAD
     return pl.pallas_call(
         attn_backward_kernel,
-        grid=(steps,),
-        in_specs=[
-            whole(gpart.shape),
-            whole(grecv.shape),
-            whole(x1.shape),
-            pl.BlockSpec((rows, width), lambda n: (item, 0)),
-            whole(gain.shape),
-            pl.BlockSpec((QUAD, width), lambda n: (n, 0)),
-            pl.BlockSpec((3, rows, QUAD), lambda n: (0, 0, n)),
-            pl.BlockSpec((3, width, QUAD), lambda n: (0, 0, n)),
-        ],
-        out_specs=[
-            whole((rows, width)),
-            whole((rows, width)),
-            pl.BlockSpec((3, rows, QUAD), lambda n: (0, 0, n)),
-            whole((rows, width)),
-            whole((8, width)),
-            pl.BlockSpec((8, QUAD), lambda n: (0, n)),
-        ],
+        grid_spec=pltpu.PrefetchScalarGridSpec(
+            num_scalar_prefetch=1,
+            grid=(steps,),
+            in_specs=[
+                whole(gpart.shape),
+                whole(grecv.shape),
+                whole(x1.shape),
+                pl.BlockSpec((rows, width), lambda n, *_: (item, 0)),
+                whole(gain.shape),
+                pl.BlockSpec((QUAD, width), lambda n, *_: (n, 0)),
+                pl.BlockSpec((3, rows, QUAD), lambda n, *_: (0, 0, n)),
+                pl.BlockSpec((3, width, QUAD), lambda n, *_: (0, 0, n)),
+            ],
+            out_specs=[
+                whole((rows, width)),
+                whole((rows, width)),
+                pl.BlockSpec((3, rows, QUAD), lambda n, *_: (0, 0, n)),
+                whole((rows, width)),
+                whole((8, width)),
+                pl.BlockSpec((8, QUAD), lambda n, *_: (0, n)),
+                whole((width // 2, rows)),
+                whole((2 + 3 * steps, PART, rows)),
+            ],
+            scratch_shapes=[pltpu.VMEM((width, rows), BF16)],
+        ),
         out_shape=[
             jax.ShapeDtypeStruct((rows, width), F32),
             jax.ShapeDtypeStruct((rows, width), BF16),
@@ -293,16 +403,18 @@
             jax.ShapeDtypeStruct((rows, width), F32),
             jax.ShapeDtypeStruct((8, width), F32),
             jax.ShapeDtypeStruct((8, heads_wide), F32),
+            jax.ShapeDtypeStruct((width // 2, rows), BF16),
+            jax.ShapeDtypeStruct((2 + 3 * steps, PART, rows), F32),
         ],
-        compiler_params=params(),
+        compiler_params=params(32),
         cost_estimate=long_cost(),
         name="attn_backward",
-    )(gpart, grecv, x1, cotangent, gain, w_out, qkv, w_qkv)
+    )(place, gpart, grecv, x1, cotangent, gain, w_out, qkv, w_qkv)
 
 
 def mlp_kernel(
-    x0_ref, opart_ref, orecv_ref, obias_ref, gain_ref, bias_ref, wfc1_ref, b1_ref, wfc2_ref, cot_ref,
-    x1_ref, a2_ref, act_ref, dpre_ref, da2_ref, b1sum_ref,
+    place, x0_ref, opart_ref, orecv_ref, obias_ref, gain_ref, bias_ref, wfc1_ref, b1_ref, wfc2_ref, cot_ref,
+    x1_ref, a2_ref, act_ref, dpre_ref, da2_ref, b1sum_ref, keep_ref, gact_ref, gpre_ref, turned_ref,
 ):
     step = pl.program_id(0)
 
@@ -312,45 +424,62 @@
         normed, _inv = norm_parts(x1_ref[...])
         a2_ref[...] = (normed * gain_ref[...] + bias_ref[...]).astype(BF16)
         da2_ref[...] = jnp.zeros_like(da2_ref)
+        turn(place, a2_ref, turned_ref, slice(None))
+        spread(turned_ref, keep_ref, gpre_ref)
 
     pre = nn(a2_ref[...], wfc1_ref[...]) + b1_ref[...]
     dact = nt(cot_ref[...], wfc2_ref[...])
     cdf = 0.5 * (1.0 + lax.erf(pre * (2.0**-0.5)))
-    act_ref[...] = (pre * cdf).astype(BF16)
+    act = (pre * cdf).astype(BF16)
+    act_ref[...] = act
     density = jnp.exp(-0.5 * pre * pre) * 0.3989422804014327
     dpre = (dact * (cdf + pre * density)).astype(BF16)
     dpre_ref[...] = dpre
+    for part in range(act.shape[1] // PART):
+        columns = slice(part * PART, (part + 1) * PART)
+        gact_ref[part] = act[:, columns].astype(F32)
+        gpre_ref[2 + step * (act.shape[1] // PART) + part] = dpre[:, columns].astype(F32)
     b1sum_ref[...] = column_sum(dpre.astype(F32))
     da2_ref[...] += nt(dpre, wfc1_ref[...])
 
 
-def mlp(x0, opart, orecv, out_bias, gain, bias, w_fc1, fc1_bias, w_fc2, cotangent, item):
+def mlp(place, x0, opart, orecv, out_bias, gain, bias, w_fc1, fc1_bias, w_fc2, cotangent, item):
     rows, width = x0.shape
     hidden = w_fc1.shape[1]
     tile = 512
+    parts = tile // PART
+    row_tile = pl.BlockSpec((rows, tile), lambda n, *_: (0, n))
+    gone = pl.BlockSpec((parts, rows, PART), lambda n, *_: (n, 0, 0))
     return pl.pallas_call(
         mlp_kernel,
-        grid=(hidden // tile,),
-        in_specs=[
-            whole(x0.shape),
-            whole(opart.shape),
-            whole(orecv.shape),
-            whole(out_bias.shape),
-            whole(gain.shape),
-            whole(bias.shape),
-            pl.BlockSpec((width, tile), lambda n: (0, n)),
-            pl.BlockSpec((1, tile), lambda n: (0, n)),
-            pl.BlockSpec((tile, width), lambda n: (n, 0)),
-            pl.BlockSpec((rows, width), lambda n: (item, 0)),
-        ],
-        out_specs=[
-            whole((rows, width)),
-            whole((rows, width)),
-            pl.BlockSpec((rows, tile), lambda n: (0, n)),
-            pl.BlockSpec((rows, tile), lambda n: (0, n)),
-            whole((rows, width)),
-            pl.BlockSpec((1, tile), lambda n: (0, n)),
-        ],
+        grid_spec=pltpu.PrefetchScalarGridSpec(
+            num_scalar_prefetch=1,
+            grid=(hidden // tile,),
+            in_specs=[
+                whole(x0.shape),
+                whole(opart.shape),
+                whole(orecv.shape),
+                whole(out_bias.shape),
+                whole(gain.shape),
+                whole(bias.shape),
+                pl.BlockSpec((width, tile), lambda n, *_: (0, n)),
+                pl.BlockSpec((1, tile), lambda n, *_: (0, n)),
+                pl.BlockSpec((tile, width), lambda n, *_: (n, 0)),
+                pl.BlockSpec((rows, width), lambda n, *_: (item, 0)),
+            ],
+            out_specs=[
+                whole((rows, width)),
+                whole((rows, width)),
+                row_tile,
+                row_tile,
+                whole((rows, width)),
+                pl.BlockSpec((1, tile), lambda n, *_: (0, n)),
+                whole((width // 2, rows)),
+                gone,
+                whole((2 + hidden // PART, rows, PART)),
+            ],
+            scratch_shapes=[pltpu.VMEM((width, rows), BF16)],
+        ),
         out_shape=[
             jax.ShapeDtypeStruct((rows, width), F32),
             jax.ShapeDtypeStruct((rows, width), BF16),
@@ -358,15 +487,44 @@
             jax.ShapeDtypeStruct((rows, hidden), BF16),
             jax.ShapeDtypeStruct((rows, width), F32),
             jax.ShapeDtypeStruct((1, hidden), F32),
+            jax.ShapeDtypeStruct((width // 2, rows), BF16),
+            jax.ShapeDtypeStruct((hidden // PART, rows, PART), F32),
+            jax.ShapeDtypeStruct((2 + hidden // PART, rows, PART), F32),
         ],
-        compiler_params=params(),
+        compiler_params=params(32),
         cost_estimate=long_cost(),
         name="mlp",
-    )(x0, opart, orecv, out_bias, gain, bias, w_fc1, fc1_bias, w_fc2, cotangent)
-
-
-def first_norm_back_kernel(gpart_ref, grecv_ref, x0_ref, dx1_ref, gain_ref, dx0_ref, sums_ref):
-    @pl.when(pl.program_id(0) == 0)
+    )(place, x0, opart, orecv, out_bias, gain, bias, w_fc1, fc1_bias, w_fc2, cotangent)
+
+
+def mlp_out_kernel(act_ref, wfc2_ref, out_ref):
+    out_ref[...] = nn(act_ref[...], wfc2_ref[...])
+
+
+def mlp_out(act, w_fc2):
+    rows, hidden = act.shape
+    width = w_fc2.shape[1]
+    tile = 512
+    return pl.pallas_call(
+        mlp_out_kernel,
+        grid=(width // tile,),
+        in_specs=[whole(act.shape), pl.BlockSpec((hidden, tile), lambda n: (0, n))],
+        out_specs=pl.BlockSpec((rows, tile), lambda n: (0, n)),
+        out_shape=jax.ShapeDtypeStruct((rows, width), F32),
+        compiler_params=params(16),
+        cost_estimate=long_cost(),
+        name="mlp_out",
+    )(act, w_fc2)
+
+
+def first_norm_back_kernel(
+    place, gpart_ref, grecv_ref, x0_ref, dx1_ref, gain_ref, dx0_ref, sums_ref, keep_ref, gone_ref,
+    turned_ref,
+):
+    step = pl.program_id(0)
+    tile = x0_ref.shape[0]
+
+    @pl.when(step == 0)
     def _():
         sums_ref[...] = jnp.zeros_like(sums_ref)
 
@@ -375,25 +533,41 @@
     dx0_ref[...] = (dx1_ref[...] + norm_back(normed, inverse, grad, gain_ref[...])).astype(BF16)
     sums_ref[0:1, :] += column_sum(grad * normed)
     sums_ref[1:2, :] += column_sum(grad)
-
-
-def first_norm_back(gpart, grecv, x0, dx1, gain):
+    turn(place, dx0_ref, turned_ref, pl.ds(pl.multiple_of(step * tile, tile), tile))
+
+    @pl.when(step == pl.num_programs(0) - 1)
+    def _():
+        spread(turned_ref, keep_ref, gone_ref)
+
+
+def first_norm_back(place, gpart, grecv, x0, dx1, gain):
     rows, width = x0.shape
-    tile = 64
-    block = pl.BlockSpec((tile, width), lambda n: (n, 0))
+    tile = 128
+    block = pl.BlockSpec((tile, width), lambda n, *_: (n, 0))
     return pl.pallas_call(
         first_norm_back_kernel,
-        grid=(rows // tile,),
-        in_specs=[block, block, block, block, whole(gain.shape)],
-        out_specs=[block, whole((8, width))],
+        grid_spec=pltpu.PrefetchScalarGridSpec(
+            num_scalar_prefetch=1,
+            grid=(rows // tile,),
+            in_specs=[block, block, block, block, whole(gain.shape)],
+            out_specs=[
+                block,
+                whole((8, width)),
+                whole((width // 2, rows)),
+                whole((2, PART, rows)),
+            ],
+            scratch_shapes=[pltpu.VMEM((width, rows), BF16)],
+        ),
         out_shape=[
             jax.ShapeDtypeStruct((rows, width), BF16),
             jax.ShapeDtypeStruct((8, width), F32),
+            jax.ShapeDtypeStruct((width // 2, rows), BF16),
+            jax.ShapeDtypeStruct((2, PART, rows), F32),
         ],
-        compiler_params=params(),
-        cost_estimate=long_cost(),
+        compiler_params=params(14),
+        cost_estimate=short_cost(),
         name="first_norm_back",
-    )(gpart, grecv, x0, dx1, gain)
+    )(place, gpart, grecv, x0, dx1, gain)
 
 
 def pixel_grad_kernel(kinds, da_ref, db_ref, wspec_ref, wrgb_ref, pick_ref, out_ref):
@@ -432,119 +606,122 @@
             out_specs=pl.BlockSpec((rows, wide), lambda i, *_: (i, 0)),
         ),
         out_shape=jax.ShapeDtypeStruct((2 * rows, wide), BF16),
-        compiler_params=params(),
+        compiler_params=params(20),
         cost_estimate=long_cost(),
         name="pixel_grad",
     )(kinds, grad_a, grad_b, w_spectral, w_rgb, pick)
 
 
-def turn(place, left_refs, turned_ref):
-    chips = turned_ref.shape[0] // LANES
+def gather_left(keep_refs, gone_refs, first, left_ref):
+    rows = keep_refs[0].shape[-1]
+    for pos, keep_ref in enumerate(keep_refs):
+        left_ref[:, pos * rows : (pos + 1) * rows] = keep_ref[...]
+    base = len(keep_refs) * rows
+    for pos, gone_ref in enumerate(gone_refs):
+        columns = slice(base + pos * rows, base + (pos + 1) * rows)
+        for part in range(2):
+            left_ref[part * PART : (part + 1) * PART, columns] = gone_ref[first + part].astype(BF16)
+
+
+def emit(left_ref, rights, send_ref, keep_ref, moves):
+    right = jnp.concatenate([r.astype(BF16) for r in rights], 0)
+    total = nn(left_ref[...], right)
     half = LANES // 2
-    core = place[chips]
-    for chip in range(chips):
-        lanes = pl.ds(pl.multiple_of(place[chip] * LANES, LANES), LANES)
-        for pos, left_ref in enumerate(left_refs):
-            rows = left_ref.shape[0]
-            block = left_ref[:, lanes].T
-            columns = slice(pos * rows, (pos + 1) * rows)
-            low = pl.multiple_of(core * (chips * half) + chip * half, half)
-            high = pl.multiple_of((1 - core) * (chips * half) + chip * half, half)
-            turned_ref[pl.ds(low, half), columns] = block[:half]
-            turned_ref[pl.ds(high, half), columns] = block[half:]
-
-
-def emit(turned_ref, right_refs, send_ref, keep_ref):
-    middle = turned_ref.shape[0] // 2
-    for out_ref, rows in ((send_ref, slice(middle, None)), (keep_ref, slice(0, middle))):
-        total = None
-        for pos, right_ref in enumerate(right_refs):
-            depth = right_ref.shape[0]
-            term = nn(turned_ref[rows, pos * depth : (pos + 1) * depth], right_ref[...])
-            total = term if total is None else total + term
-        out_ref[...] = total.reshape(out_ref.shape)
-
-
-def plain_grad_kernel(place, la_ref, lb_ref, ra_ref, rb_ref, send_ref, keep_ref, turned_ref):
+    for pos, block in enumerate(moves):
+        out_ref = send_ref if pos < 4 else keep_ref
+        out_ref[pos % 4] = total[block * half : (block + 1) * half]
+
+
+def plain_grad_kernel(
+    ka_ref, kb_ref, la_ref, lb_ref, ra_ref, rb_ref, oa_ref, ob_ref, send_ref, keep_ref, left_ref,
+    *, moves,
+):
     @pl.when(pl.program_id(0) == 0)
     def _():
-        turn(place, (la_ref, lb_ref), turned_ref)
-
-    emit(turned_ref, (ra_ref, rb_ref), send_ref, keep_ref)
-
-
-def plain_grad(place, left_a, left_b, right_a, right_b, name, skip=0, columns=None):
-    rows, width = left_a.shape
-    columns = columns or right_a.shape[1]
-    chips = width // LANES
+        gather_left((ka_ref, kb_ref), (la_ref, lb_ref), 0, left_ref)
+
+    rights = (ra_ref[...], rb_ref[...], oa_ref[0], ob_ref[0])
+    emit(left_ref, rights, send_ref, keep_ref, moves)
+
+
+def plain_grad(keeps, lefts, rights, others, moves, name, skip=0, columns=None, lead=0):
+    half_width, rows = keeps[0][0].shape[-2:]
+    columns = columns or rights[0].shape[1]
+    base = skip // PART
     half = LANES // 2
-    tile = 256
-    base = skip // tile
-    right = pl.BlockSpec((rows, tile), lambda n, *_: (0, n + base))
-    out = pl.BlockSpec((chips, half, tile), lambda n, *_: (0, 0, n))
-    shape = jax.ShapeDtypeStruct((chips, half, columns), F32)
-    return pl.pallas_call(
-        plain_grad_kernel,
-        grid_spec=pltpu.PrefetchScalarGridSpec(
-            num_scalar_prefetch=1,
-            grid=(columns // tile,),
-            in_specs=[whole(left_a.shape), whole(left_b.shape), right, right],
-            out_specs=[out, out],
-            scratch_shapes=[pltpu.VMEM((width, 2 * rows), BF16)],
-        ),
+
+    def keep_spec(array, item):
+        if array.ndim == 2:
+            return whole(array.shape)
+        return pl.BlockSpec((None,) + array.shape[1:], lambda n: (item, 0, 0))
+
+    right = pl.BlockSpec((rows, PART), lambda n: (0, n + base))
+    other = pl.BlockSpec((1, rows, PART), lambda n: (n + base + lead, 0, 0))
+    out = pl.BlockSpec((4, half, PART), lambda n: (0, 0, n))
+    shape = jax.ShapeDtypeStruct((4, half, columns), F32)
+    return pl.pallas_call(
+        functools.partial(plain_grad_kernel, moves=moves),
+        grid=(columns // PART,),
+        in_specs=[keep_spec(*k) for k in keeps]
+        + [pl.BlockSpec((2, PART, rows), lambda n, q=i: (q, 0, 0)) for _, i in lefts]
+        + [right, right, other, other],
+        out_specs=[out, out],
+        scratch_shapes=[pltpu.VMEM((half_width, 4 * rows), BF16)],
         out_shape=[shape, shape],
-        compiler_params=params(),
-        cost_estimate=cost(4 * rows * width * columns, 4 * width * columns),
+        compiler_params=params(16),
+        cost_estimate=short_cost(),
         name=name,
-    )(place, left_a, left_b, right_a, right_b)
+    )(*[k for k, _ in keeps], *[v for v, _ in lefts], *rights, *others)
 
 
 def attn_grad_kernel(
-    place, aa_ref, ab_ref, ya_ref, yb_ref, da_ref, db_ref, ma_ref, mb_ref,
-    send_ref, keep_ref, turned_a, turned_y,
+    aa_ref, ab_ref, ya_ref, yb_ref, fa_ref, fb_ref, ba_ref, bb_ref, da_ref, db_ref, ma_ref, mb_ref,
+    send_ref, keep_ref, left_ref, *, moves,
 ):
     plane, step = pl.program_id(0), pl.program_id(1)
+    steps = pl.num_programs(1)
 
     @pl.when((plane == 0) & (step == 0))
     def _():
-        turn(place, (aa_ref, ab_ref), turned_a)
-        turn(place, (ya_ref, yb_ref), turned_y)
+        gather_left((aa_ref, ab_ref), (fa_ref, fb_ref), 0, left_ref)
+
+    @pl.when((plane == 3) & (step == 0))
+    def _():
+        gather_left((ya_ref, yb_ref), (ba_ref, bb_ref), 0, left_ref)
 
     @pl.when(plane < 3)
     def _():
-        emit(turned_a, (da_ref, db_ref), send_ref, keep_ref)
+        spot = 2 + plane * steps + step
+        emit(left_ref, (da_ref[...], db_ref[...], ba_ref[spot], bb_ref[spot]), send_ref, keep_ref, moves)
 
     @pl.when(plane == 3)
     def _():
-        emit(turned_y, (ma_ref, mb_ref), send_ref, keep_ref)
-
-
-def attn_grad(place, a1, dya, dqkv, mix):
-    rows, width = a1[0].shape
+        spot = 2 + step
+        emit(left_ref, (ma_ref[...], mb_ref[...], fa_ref[spot], fb_ref[spot]), send_ref, keep_ref, moves)
+
+
+def attn_grad(keep_a1, keep_dya, other_f, other_b, dqkv, mix, moves):
+    half_width, rows = keep_a1[0].shape
     columns = mix[0].shape[1]
-    chips = width // LANES
     half = LANES // 2
-    tile = 256
-    side = whole((rows, width))
-    plane = pl.BlockSpec((None, rows, tile), lambda p, n, *_: (jnp.minimum(p, 2), 0, n))
-    mixed = pl.BlockSpec((rows, tile), lambda p, n, *_: (0, n))
-    out = pl.BlockSpec((chips, half, tile), lambda p, n, *_: (0, p, n))
-    shape = jax.ShapeDtypeStruct((chips, 4 * half, columns), F32)
-    scratch = pltpu.VMEM((width, 2 * rows), BF16)
-    return pl.pallas_call(
-        attn_grad_kernel,
-        grid_spec=pltpu.PrefetchScalarGridSpec(
-            num_scalar_prefetch=1,
-            grid=(4, columns // tile),
-            in_specs=[side, side, side, side, plane, plane, mixed, mixed],
-            out_specs=[out, out],
-            scratch_shapes=[scratch, scratch],
-        ),
+    side = whole((half_width, rows))
+    plane = pl.BlockSpec((None, rows, PART), lambda p, n: (jnp.minimum(p, 2), 0, n))
+    mixed = pl.BlockSpec((rows, PART), lambda p, n: (0, n))
+    out = pl.BlockSpec((4, half, PART), lambda p, n: (0, p, n))
+    shape = jax.ShapeDtypeStruct((4, 4 * half, columns), F32)
+    return pl.pallas_call(
+        functools.partial(attn_grad_kernel, moves=moves),
+        grid=(4, columns // PART),
+        in_specs=[side, side, side, side]
+        + [whole(v.shape) for v in (*other_f, *other_b)]
+        + [plane, plane, mixed, mixed],
+        out_specs=[out, out],
+        scratch_shapes=[pltpu.VMEM((half_width, 4 * rows), BF16)],
         out_shape=[shape, shape],
-        compiler_params=params(),
-        cost_estimate=cost(16 * rows * width * columns, 16 * width * columns),
+        compiler_params=params(24),
+        cost_estimate=short_cost(),
         name="attn_grad",
-    )(place, *a1, *dya, *dqkv, *mix)
+    )(*keep_a1, *keep_dya, *other_f, *other_b, *dqkv, *mix)
 
 
 def exchange(values, axis, bit, size):
@@ -563,48 +740,42 @@
 Z_FIRST = (4, 2, 8)
 
 
-CORE_PIECES = 1
+def block_flips(bits):
+    return [sum((1 - ((p >> (2 - n)) & 1)) * (bits[n] // 2) for n in range(3)) for p in range(8)]
+
+
+def block_moves(bits):
+    stands = block_flips(X_FIRST)
+    return tuple(stands.index(f) for f in block_flips(bits))
+
+
+def places():
+    me = lax.axis_index("dp")
+    flips = jnp.array(block_flips(X_FIRST), jnp.int32)
+    return jnp.concatenate([(me // 2) ^ flips, (me % 2)[None]]).astype(jnp.int32)
 
 
 class Halving:
-    def __init__(self, send, keep, bits, size, pieces=CORE_PIECES):
+    def __init__(self, send, keep, bits, size):
         self.keep, self.bits, self.size = keep, bits, size
-        blocks = send.shape[0] // pieces
-        self.core = [
-            exchange(send[p * blocks : (p + 1) * blocks], "dp", 1, size) for p in range(pieces)
-        ]
-        self.recvs = []
-        self.at = 0
-
-    def from_core(self, first, count):
-        blocks = self.core[0].shape[0]
-        if count >= blocks:
-            return jnp.concatenate(self.core[first // blocks : (first + count) // blocks], 0)
-        start = first % blocks
-        return self.core[first // blocks][start : start + count]
-
-    def step(self, order=None):
-        if order is not None:
-            if self.recvs:
-                self.recvs[-1] = order.tie(self.recvs[-1])
-            else:
-                self.core = list(order.tie(tuple(self.core)))
-        left = self.keep.shape[0] >> self.at
-        if left == 1:
-            count = 1
-        else:
-            count = left // 2
+        self.recvs = [exchange(send, "dp", bits[0], size)]
+        self.left = keep.shape[0]
+        self.sent = send
+
+    def step(self, order):
+        self.recvs[-1] = order.tie(self.recvs[-1])
+        left = self.left
+        count = max(left // 2, 1)
         total = self.keep.shape[0] - left
-        value = self.keep[total : total + count] + self.from_core(total, count)
+        value = self.keep[total : total + count]
         for recv in self.recvs:
             first = recv.shape[0] - left
             value = value + recv[first : first + count]
-        if order is not None:
-            order.mark(value)
+        order.mark(value)
         if left == 1:
             return value[0]
-        self.recvs.append(exchange(value, "dp", self.bits[self.at], self.size))
-        self.at += 1
+        self.recvs.append(exchange(value, "dp", self.bits[len(self.recvs)], self.size))
+        self.left = left // 2
         return None
 
 
@@ -617,17 +788,6 @@
 
     def mark(self, values):
         self.last = values
-
-
-def places(bits):
-    me = lax.axis_index("dp")
-    chip = me // 2
-    core = me % 2
-    order = []
-    for p in range(8):
-        order.append(sum((1 - ((p >> (2 - n)) & 1)) * (bits[n] // 2) for n in range(3)))
-    flips = jnp.array(order, jnp.int32)
-    return jnp.concatenate([chip ^ flips, core[None]]).astype(jnp.int32)
 
 
 def local(
@@ -676,84 +836,123 @@
         gate = swap(values)
         return gate
 
-    if custom:
-        place_x, place_z = places(X_FIRST), places(Z_FIRST)
+    place = places() if custom else jnp.arange(9, dtype=jnp.int32) % 8
+    move_x, move_z = block_moves(X_FIRST), block_moves(Z_FIRST)
+
+    def other(values):
+        return exchange(values, "dp", 1, size) if custom else values
+
+    def settle(values):
+        values = order.tie(values)
+        order.mark(jax.tree.leaves(values)[0])
+        return values
 
     none = [None] * items
     part, mixed, erecv, fwd, orecv, ffn, grecv, bwd, arecv, last, ycot = (list(none) for _ in range(11))
+    gmix, pk, gfwd, gact, gpre, gbwd, gdx0 = (list(none) for _ in range(7))
+
     for i in range(items):
         part[i], mixed[i] = embed(order.tie(item_kinds), pixels, w_spectral, w_rgb, pick, i, rows)
         order.mark(part[i])
         erecv[i] = send(part[i])
+    keep_cot, gone_cot = turn_cot(order.tie(place), cotangent, rows)
+    order.mark(gone_cot)
+    gone_mix = []
+    for i in range(items):
+        gone_mix.append(pack(order.tie(mixed[i])))
+        order.mark(gone_mix[i])
+    gcot = other(gone_cot)
+    gmix = [other(v) for v in gone_mix]
     for i in range(items):
         fwd[i] = attn_forward(
             part[i], erecv[i], tables[i], order.tie(g1), c1, wqkv, qb, vb, w_out
         )
         order.mark(fwd[i][4])
         orecv[i] = send(fwd[i][4])
+        if i == 0:
+            gcot = settle(gcot)
+        else:
+            gmix = [settle(v) for v in gmix]
+        pk[i] = pack_attn(order.tie(place), fwd[i][1], fwd[i][3])
+        order.mark(pk[i][1])
+        gfwd[i] = other(pk[i][1])
     x0, a1, qkv, mix, _ = zip(*fwd)
-    cot = [cotangent[i * rows : (i + 1) * rows] for i in range(items)]
     for i in range(items):
         ffn[i] = mlp(
-            x0[i], fwd[i][4], orecv[i], order.tie(ob), g2, c2, w_fc1, b1, w_fc2, cotangent, i
+            place, x0[i], fwd[i][4], orecv[i], order.tie(ob), g2, c2, w_fc1, b1, w_fc2, cotangent, i
         )
         order.mark(ffn[i][4])
-        grecv[i] = send(ffn[i][4])
-        ycot[i] = nn(order.tie(ffn[i][2]), w_fc2)
-        order.mark(ycot[i])
-        if i == items - 1 and custom:
-            fc2_s = plain_grad(
-                order.tie(place_x), cot[0], cot[1], ffn[0][2], ffn[1][2], "fc2_grad"
-            )
-            order.mark(fc2_s[0])
-            fc2_h = Halving(*fc2_s, X_FIRST, size)
-    x1, a2, act, dpre, _, b1sum = zip(*ffn)
+        if i == 0:
+            grecv[i] = send(ffn[i][4])
+        gact[i] = other(ffn[i][7])
+        gpre[i] = other(ffn[i][8])
+        if i == 0:
+            gfwd = [settle(v) for v in gfwd]
+        else:
+            gact[0], gpre[0] = settle((gact[0], gpre[0]))
+            ycot[1] = mlp_out(order.tie(ffn[1][2]), w_fc2)
+            order.mark(ycot[1])
+    x1, a2, act, dpre, _, b1sum, ka2 = list(zip(*ffn))[:7]
+    if custom:
+        gact[1] = order.tie(gact[1])
+        fc2_h = Halving(
+            *plain_grad(
+                [(keep_cot, 0), (keep_cot, 1)], [(gcot, 0), (gcot, 1)], act, gact, move_x, "fc2_grad"
+            ),
+            X_FIRST, size,
+        )
+        order.mark(fc2_h.sent)
+        gpre[1] = order.tie(gpre[1])
+        fc1_h = Halving(
+            *plain_grad(
+                [(ka2[0], 0), (ka2[1], 0)], [(gpre[0], 0), (gpre[1], 0)], dpre, gpre, move_z, "fc1_grad", lead=2
+            ),
+            Z_FIRST, size,
+        )
+        order.mark(fc1_h.sent)
+    grecv[1] = send(order.tie(ffn[1][4]))
     for i in range(items):
         bwd[i] = attn_backward(
-            ffn[i][4], grecv[i], x1[i], cotangent, order.tie(g2), w_out, qkv[i], wqkv, i
+            place, ffn[i][4], grecv[i], x1[i], cotangent, order.tie(g2), w_out, qkv[i], wqkv, i
         )
         order.mark(bwd[i][3])
-        if custom and i == 0:
-            fc2_h.step(order)
-            fc1_s = plain_grad(order.tie(place_z), a2[0], a2[1], dpre[0], dpre[1], "fc1_grad")
-            order.mark(fc1_s[0])
-            fc1_h = Halving(*fc1_s, Z_FIRST, size)
-        if custom and i == items - 1:
-            fc1_h.step(order)
-            dqkv = [bwd[0][2], bwd[1][2]]
-            dya = [bwd[0][1], bwd[1][1]]
-            att_s = attn_grad(order.tie(place_x), a1, dya, dqkv, mix)
-            order.mark(att_s[0])
-            att_h = Halving(*att_s, X_FIRST, size)
-        arecv[i] = send(order.tie(bwd[i][3]))
-    dx1, dya, dqkv, _, sums2, qvsum = zip(*bwd)
+        if i == 0:
+            arecv[i] = send(bwd[i][3])
+        if i == items - 1:
+            gbwd = [other(order.tie(bwd[0][7])), other(bwd[1][7])]
+            ycot[0] = mlp_out(order.tie(ffn[0][2]), w_fc2)
+            order.mark(ycot[0])
+    dx1, dya, dqkv, _, sums2, qvsum, kdya = list(zip(*bwd))[:7]
+    if custom:
+        gbwd = [order.tie(v) for v in gbwd]
+        att_h = Halving(
+            *attn_grad([v[0] for v in pk], kdya, gfwd, gbwd, dqkv, mix, move_x), X_FIRST, size
+        )
+        order.mark(att_h.sent)
+    arecv[1] = send(order.tie(bwd[1][3]))
     for i in range(items):
-        last[i] = first_norm_back(bwd[i][3], arecv[i], x0[i], dx1[i], order.tie(g1))
+        last[i] = first_norm_back(place, bwd[i][3], arecv[i], x0[i], dx1[i], order.tie(g1))
         order.mark(last[i][0])
+        gdx0[i] = other(last[i][3])
         if custom and i == 0:
             fc2_h.step(order)
             fc1_h.step(order)
-    dx0, sums1 = zip(*last)
+    dx0, sums1, kdx0, _ = zip(*last)
+    pixels_grad = pixel_grad(order.tie(item_kinds), dx0[0], dx0[1], w_spectral, w_rgb, pick)
+    order.mark(pixels_grad)
     if custom:
         mid = mixed[0].shape[1] // 2
-        embx_s = plain_grad(
-            order.tie(place_x), dx0[0], dx0[1], mixed[0], mixed[1], "embed_grad_a", 0, mid
-        )
-        order.mark(embx_s[0])
-        embx_h = Halving(*embx_s, X_FIRST, size)
-        embz_s = plain_grad(
-            order.tie(place_z), dx0[0], dx0[1], mixed[0], mixed[1], "embed_grad_b", mid, mid
-        )
-        order.mark(embz_s[0])
-        embz_h = Halving(*embz_s, Z_FIRST, size)
+        gdx0 = [order.tie(v) for v in gdx0]
+        sides = ([(kdx0[0], 0), (kdx0[1], 0)], [(gdx0[0], 0), (gdx0[1], 0)], mixed, gmix)
+        embx_h = Halving(*plain_grad(*sides, move_x, "embed_grad_a", 0, mid), X_FIRST, size)
+        order.mark(embx_h.sent)
+        sides[3][1] = order.tie(gmix[1])
+        embz_h = Halving(*plain_grad(*sides, move_z, "embed_grad_b", mid, mid), Z_FIRST, size)
+        order.mark(embz_h.sent)
         fc2_h.step(order)
-        att_h.step(order)
-        fc1_h.step(order)
 
     got = [send(order.tie(ycot[i])) for i in range(items)]
-    pixels_grad = pixel_grad(order.tie(item_kinds), dx0[0], dx0[1], w_spectral, w_rgb, pick)
-    order.mark(pixels_grad)
-
+    sums2, sums1, qvsum, b1sum = order.tie((sums2, sums1, qvsum, b1sum))
     vec2 = sums2[0] + sums2[1]
     vec1 = sums1[0] + sums1[1]
     qv = qvsum[0] + qvsum[1]
@@ -762,28 +961,28 @@
     small = jnp.concatenate([v.reshape(size, -1) for v in pieces], 1)
     if custom:
         cube = small.reshape(2, 2, 2, 2, -1)
-        chip, core = lax.axis_index("dp") // 2, place_x[8]
+        chip, core = lax.axis_index("dp") // 2, lax.axis_index("dp") % 2
         for axis, bit in ((0, 4), (1, 2), (2, 1)):
             cube = jnp.where((chip & bit) == 0, jnp.flip(cube, axis), cube)
         cube = jnp.transpose(cube, (2, 1, 0, 3, 4)).reshape(8, 2, 1, -1)
         kept = jnp.where(core == 0, cube[:, 0], cube[:, 1])
         gone = jnp.where(core == 0, cube[:, 1], cube[:, 0])
-        embx_h.step(order)
+        gone = exchange(gone, "dp", 1, size)
+        fc2_g = fc2_h.step(order)
+        gone = order.tie(gone)
+        small_h = Halving(kept[:4] + gone[:4], kept[4:] + gone[4:], X_FIRST, size)
         embz_h.step(order)
-        fc2_g = fc2_h.step(order)
-        small_h = Halving(order.tie(gone), kept, X_FIRST, size)
-        fc1_g = fc1_h.step(order)
+        fc1_h.step(order)
+        small_h.step(order)
+        att_h.step(order)
         small_h.step(order)
         embz_h.step(order)
+        fc1_g = fc1_h.step(order)
+        small = small_h.step(order)[0]
         att_h.step(order)
-        small_h.step(order)
-        embx_h.step(order)
-        small_h.step(order)
-        embz_h.step(order)
-        att_h.step(order)
-        small = small_h.step(order)[0]
         embx_h.step(order)
         embz_g = embz_h.step(order)
+        embx_h.step(order)
         att_g = att_h.step(order)
         embx_g = embx_h.step(order)
         emb_g = jnp.concatenate([embx_g, embz_g], 1)
@@ -791,6 +990,7 @@
         qkv_grad = jnp.transpose(att_g[:3], (1, 0, 2))
         out_grad = att_g[3].T
     else:
+        cot = [cotangent[i * rows : (i + 1) * rows] for i in range(items)]
         fc2_g = scatter(both(cot, act))
         fc1_g = scatter(both(a2, dpre))
         emb_g = scatter(both(dx0, mixed))

time: 397 us -> 400 us (level)
  waiting for transfers between devices: 165 us -> 196 us
  Pallas kernels: 127 us -> 98.6 us
  local copies, waits for them, and re-layouts: 11.6 us -> 39.7 us
  other arithmetic: 42.2 us -> 24.8 us
  matrix products: 6.99 us -> 0 us
    unnamed x80 -> x186, local copies, waits for them, and re-layouts: 2.18 us -> 35 us
    ppermute x34 -> x42, waiting for transfers between devices: 165 us -> 196 us  [exchange(): return lax.ppermute(values, axis, [(i, i ^ bit) for i in range(size)])]
    pallas_call x11 -> x18, Pallas kernels: 92.6 us -> 77.9 us  [the longest x4 21.2 us: plain_grad(): pl.pallas_call(functools.partial(plain_grad_kernel, moves=moves), grid=(c...]
    add x6 -> x1, other arithmetic: 10 us -> 0.02 us  [local(): small_h = Halving(kept[:4] + gone[:4], kept[4:] + gone[4:], X_FIRST, size)]
    dot_general x2 -> x0, matrix products: 6.99 us -> none  [nn(): lax.dot_general(left, right, (((1,), (0,)), ((), ())), preferred_element_...]
    pallas_call x2, Pallas kernels: 13.6 us -> 6.77 us  [embed(): pl.pallas_call(functools.partial(embed_kernel, item=item), grid_spec=pltp...]
    pallas_call x2, Pallas kernels: 14.5 us -> 10.2 us  [attn_forward(): pl.pallas_call(attn_forward_kernel, grid=(steps,), in_specs=[whole(part.s...]
    ppermute x34 -> x42, starting transfers between devices: 41.1 us -> 38.3 us  [exchange(): return lax.ppermute(values, axis, [(i, i ^ bit) for i in range(size)])]
  transfers between devices with their start and end apart: 34 -> 42, of which waited for: 14 -> 17; matrix products, arithmetic and copies ran while one was open for 14% -> 7% of each run, Pallas kernels for 30% -> 24%
where the time goes in v3:
time: 400 us; the launch traced here: 399 us
  waiting for transfers between devices  196 us (49%)
  Pallas kernels  98.6 us (25%)
  local copies, waits for them, and re-layouts  39.7 us (10%)
  starting transfers between devices  38.3 us (10%)
  other arithmetic  24.8 us (6%)
    ppermute x42, waiting for transfers between devices, exchange(): return lax.ppermute(values, axis, [(i, i ^ bit) for i in range(size)])  196 us
    ppermute x42, starting transfers between devices, exchange(): return lax.ppermute(values, axis, [(i, i ^ bit) for i in range(size)])  38.3 us
    unnamed x186, local copies, waits for them, and re-layouts  35 us
    pallas_call x4, Pallas kernels, plain_grad(): pl.pallas_call(functools.partial(plain_grad_kernel, moves=moves), grid=(c...  21.2 us
    add x17, other arithmetic, step(): value = value + recv[first:first + count]  20.2 us
    pallas_call x2, Pallas kernels, attn_backward(): pl.pallas_call(attn_backward_kernel, grid_spec=pltpu.PrefetchScalarGridSp...  16.3 us
    pallas_call x2, Pallas kernels, mlp(): pl.pallas_call(mlp_kernel, grid_spec=pltpu.PrefetchScalarGridSpec(num_sca...  15.2 us
    pallas_call x2, Pallas kernels, attn_forward(): pl.pallas_call(attn_forward_kernel, grid=(steps,), in_specs=[whole(part.s...  10.2 us
  transfers between devices with their start and end apart: 42, of which 17 were waited for; matrix products, arithmetic and copies ran while one was open for 7% of the time, Pallas kernels for 24%

profile of v3, /device:TPU:0, one launch (start us, length us, event | category | flops | bytes accessed | tf_op | source)
XLA Modules:
  0.0 398.9 jit_solution(11861540130972032739)
XLA Ops:
  1.1 2.0 copy-done
  3.0 1.5 copy-done.10
  6.3 3.8 embed.2
  11.0 3.0 collective-permute-start
  15.4 1.5 copy-done.11
  18.0 3.0 embed.3
  21.0 1.9 turn_cotangent.1
  22.9 3.2 pack_pixels.2
  26.6 3.1 pack_pixels.3
  30.2 7.3 %collective-permute-done.recv_ref = f32[256,1024]{1,0:T(8,128)} collective-permute-done((f32[256,1024]{1,0:T(8,128)}, f32[256,1024]{1,0:T(8,128)}, u32[]{:S(2)}, u32[]{:S(2)}) %collective-permute-start) | collective-permute-done | bytes 1048608 | tf_op jit(solution)/shard_map/ppermute | solution.py:728
  37.4 1.7 collective-permute-start.1
  39.2 1.9 copy-done.63
  42.3 5.9 %attn_forward.2 = (f32[256,1024]{1,0:T(8,128)S(1)}, bf16[256,1024]{1,0:T(8,128)(2,1)S(1)}, bf16[3,256,512]{2,1,0:T(8,128)(2,1)S(1)}, bf16[256,512]{1,0:T(8,128)(2,1)S(1)}, f32[256,1024]{1,0:T(8,128)S(1)}) custom-call(f32[256,1024]{1,0:T(8,128)} %get-tuple-element.157.part_ref, f32[256,1024]{1,0:T(8,128)} %collective-permute-done.recv_ref, ...), custom_call_target="tpu_custom_call" | custom-call | flops 99999997952 | bytes 1000 | tf_op jit(solution)/shard_map/attn_forward/pallas_call | solution.py:280
  49.1 1.8 pack_attn.2
  51.6 10.4 %collective-permute-done.1.recv_ref = f32[256,1024]{1,0:T(8,128)S(1)} collective-permute-done((f32[256,1024]{1,0:T(8,128)}, f32[256,1024]{1,0:T(8,128)S(1)}, u32[]{:S(2)}, u32[]{:S(2)}) %collective-permute-start.1) | collective-permute-done | bytes 1048608 | tf_op jit(solution)/shard_map/ppermute | solution.py:728
  62.0 1.4 collective-permute-start.2
  63.5 4.3 %attn_forward.3 = (f32[256,1024]{1,0:T(8,128)S(1)}, bf16[256,1024]{1,0:T(8,128)(2,1)S(1)}, bf16[3,256,512]{2,1,0:T(8,128)(2,1)S(1)}, bf16[256,512]{1,0:T(8,128)(2,1)S(1)}, f32[256,1024]{1,0:T(8,128)S(1)}) custom-call(f32[256,1024]{1,0:T(8,128)S(1)} %copy-done.73, f32[256,1024]{1,0:T(8,128)S(1)} %collective-permute-done.1.recv_ref, ...), custom_call_target="tpu_custom_call" | custom-call | flops 99999997952 | bytes 1000 | tf_op jit(solution)/shard_map/attn_forward/pallas_call | solution.py:280
  68.7 16.6 %collective-permute-done.2.orecv_ref = f32[256,1024]{1,0:T(8,128)S(1)} collective-permute-done((f32[256,1024]{1,0:T(8,128)S(1)}, f32[256,1024]{1,0:T(8,128)S(1)}, u32[]{:S(2)}, u32[]{:S(2)}) %collective-permute-start.2) | collective-permute-done | bytes 1048608 | tf_op jit(solution)/shard_map/ppermute | solution.py:728
  86.8 8.1 %mlp.2 = (f32[256,1024]{1,0:T(8,128)S(1)}, bf16[256,1024]{1,0:T(8,128)(2,1)}, bf16[256,2048]{1,0:T(8,128)(2,1)S(1)}, bf16[256,2048]{1,0:T(8,128)(2,1)S(1)}, f32[...) custom-call(s32[9]{0:T(128)S(1)} %pad_add_fusion.place, ...), custom_call_target="tpu_custom_call" | custom-call | flops 99999997952 | bytes 1000 | tf_op jit(solution)/shard_map/mlp/pallas_call | solution.py:453
  99.6 8.3 %collective-permute-done.6.orecv_ref = f32[256,1024]{1,0:T(8,128)S(1)} collective-permute-done((f32[256,1024]{1,0:T(8,128)S(1)}, f32[256,1024]{1,0:T(8,128)S(1)}, u32[]{:S(2)}, u32[]{:S(2)}) %collective-permute-start.6) | collective-permute-done | bytes 1048608 | tf_op jit(solution)/shard_map/ppermute | solution.py:728
  109.0 2.2 copy-done.59
  111.1 2.2 copy-done.61
  115.8 7.1 %mlp.3 = (f32[256,1024]{1,0:T(8,128)S(1)}, bf16[256,1024]{1,0:T(8,128)(2,1)}, bf16[256,2048]{1,0:T(8,128)(2,1)S(1)}, bf16[256,2048]{1,0:T(8,128)(2,1)S(1)}, f32[...) custom-call(s32[9]{0:T(128)S(1)} %pad_add_fusion.place, ...), custom_call_target="tpu_custom_call" | custom-call | flops 99999997952 | bytes 1000 | tf_op jit(solution)/shard_map/mlp/pallas_call | solution.py:453
  125.4 1.8 mlp_out.2
  128.3 6.5 %fc2_grad.1 = (f32[4,64,2048]{2,1,0:T(8,128)}, f32[4,64,2048]{2,1,0:T(8,128)S(1)}) custom-call(bf16[2,512,256]{2,1,0:T(8,128)(2,1)S(1)} %copy-done.16, bf16[2,512,256]{2,1,0:T(8,128)(2,1)S(1)} %copy-done.16, f32[4,256,256]{2,1,0:T(8,128)} %collective-permute-done.3.la_ref.lb_ref, f32[4,256,256]{2,1,0:T(8,128)} %collective-permute-done.3.la_ref.lb_ref, ...), custom_call_target="tpu_custom_call" | custom-call | flops 1000 | bytes 1000 | tf_op jit(solution)/shard_map/fc2_grad/pallas_call | solution.py:662
  134.8 1.5 collective-permute-start.19
  136.3 5.4 %fc1_grad.1 = (f32[4,64,2048]{2,1,0:T(8,128)}, f32[4,64,2048]{2,1,0:T(8,128)S(1)}) custom-call(bf16[512,256]{1,0:T(8,128)(2,1)S(1)} %get-tuple-element.194.ka_ref, bf16[512,256]{1,0:T(8,128)(2,1)S(1)} %get-tuple-element.195.kb_ref, f32[10,256,256]{2,1,0:T(8,128)S(1)} %collective-permute-done.11.la_ref.oa_ref, ...), custom_call_target="tpu_custom_call" | custom-call | flops 1000 | bytes 1000 | tf_op jit(solution)/shard_map/fc1_grad/pallas_call | solution.py:662
  141.8 1.6 collective-permute-start.20
  143.3 6.3 %collective-permute-done.9.grecv_ref = f32[256,1024]{1,0:T(8,128)S(1)} collective-permute-done((f32[256,1024]{1,0:T(8,128)}, f32[256,1024]{1,0:T(8,128)S(1)}, u32[]{:S(2)}, u32[]{:S(2)}) %collective-permute-start.9) | collective-permute-done | bytes 1048608 | tf_op jit(solution)/shard_map/ppermute | solution.py:728
  150.7 1.9 copy-done.64
  152.6 7.7 %attn_backward.2 = (f32[256,1024]{1,0:T(8,128)S(1)}, bf16[256,1024]{1,0:T(8,128)(2,1)}, bf16[3,256,512]{2,1,0:T(8,128)(2,1)S(1)}, f32[256,1024]{1,0:T(8,128)S(1)...) custom-call(s32[9]{0:T(128)S(1)} %pad_add_fusion.place, ...), custom_call_target="tpu_custom_call" | custom-call | flops 99999997952 | bytes 1000 | tf_op jit(solution)/shard_map/attn_backward/pallas_call | solution.py:372
  160.3 13.6 %collective-permute-done.14.grecv_ref = f32[256,1024]{1,0:T(8,128)S(1)} collective-permute-done((f32[256,1024]{1,0:T(8,128)S(1)}, f32[256,1024]{1,0:T(8,128)S(1)}, u32[]{:S(2)}, u32[]{:S(2)}) %collective-permute-start.14) | collective-permute-done | bytes 1048608 | tf_op jit(solution)/shard_map/ppermute | solution.py:728
  174.0 8.6 %attn_backward.3 = (f32[256,1024]{1,0:T(8,128)S(1)}, bf16[256,1024]{1,0:T(8,128)(2,1)}, bf16[3,256,512]{2,1,0:T(8,128)(2,1)S(1)}, f32[256,1024]{1,0:T(8,128)S(1)...) custom-call(s32[9]{0:T(128)S(1)} %pad_add_fusion.place, ...), custom_call_target="tpu_custom_call" | custom-call | flops 99999997952 | bytes 1000 | tf_op jit(solution)/shard_map/attn_backward/pallas_call | solution.py:372
  184.1 2.2 copy-done.62
  186.3 1.8 mlp_out.3
  189.7 7.2 %attn_grad.1 = (f32[4,256,512]{2,1,0:T(8,128)}, f32[4,256,512]{2,1,0:T(8,128)S(1)}) custom-call(bf16[512,256]{1,0:T(8,128)(2,1)S(1)} %get-tuple-element.223.aa_ref, bf16[512,256]{1,0:T(8,128)(2,1)S(1)} %get-tuple-element.224.ab_ref, bf16[512,256]{1,0:T(8,128)(2,1)S(1)} %get-tuple-element.225.ya_ref, bf16[512,256]{1,0:T(8,128)(2,1)S(1)} %get-tuple-element.226.yb_ref, ...), custom_call_target="tpu_custom_call" | custom-call | flops 1000 | bytes 1000 | tf_op jit(solution)/shard_map/attn_grad/pallas_call | solution.py:712
  196.9 11.3 %collective-permute-done.15.grecv_ref = f32[256,1024]{1,0:T(8,128)S(1)} collective-permute-done((f32[256,1024]{1,0:T(8,128)S(1)}, f32[256,1024]{1,0:T(8,128)S(1)}, u32[]{:S(2)}, u32[]{:S(2)}) %collective-permute-start.15) | collective-permute-done | bytes 1048608 | tf_op jit(solution)/shard_map/ppermute | solution.py:728
  208.2 1.8 first_norm_back.2
  212.6 1.6 collective-permute-start.23
  214.2 2.4 slice_add_fusion.1
  216.5 1.5 collective-permute-start.29
  218.6 15.9 %collective-permute-done.18.grecv_ref = f32[256,1024]{1,0:T(8,128)S(1)} collective-permute-done((f32[256,1024]{1,0:T(8,128)S(1)}, f32[256,1024]{1,0:T(8,128)S(1)}, u32[]{:S(2)}, u32[]{:S(2)}) %collective-permute-start.18) | collective-permute-done | bytes 1048608 | tf_op jit(solution)/shard_map/ppermute | solution.py:728
  234.4 1.8 first_norm_back.3
  236.4 3.8 pixel_grad.1
  240.2 4.6 %embed_grad_a.1 = (f32[4,64,1024]{2,1,0:T(8,128)}, f32[4,64,1024]{2,1,0:T(8,128)S(1)}) custom-call(bf16[512,256]{1,0:T(8,128)(2,1)S(1)} %get-tuple-element.242.ka_ref, bf16[512,256]{1,0:T(8,128)(2,1)S(1)} %get-tuple-element.247.kb_ref, f32[2,256,256]{2,1,0:T(8,128)S(1)} %collective-permute-done.21.la_ref, f32[2,256,256]{2,1,0:T(8,128)S(1)} %collective-permute-done.22.lb_ref, ...), custom_call_target="tpu_custom_call" | custom-call | flops 1000 | bytes 1000 | tf_op jit(solution)/shard_map/embed_grad_a/pallas_call | solution.py:662
  246.7 4.6 %embed_grad_b.1 = (f32[4,64,1024]{2,1,0:T(8,128)}, f32[4,64,1024]{2,1,0:T(8,128)S(1)}) custom-call(bf16[512,256]{1,0:T(8,128)(2,1)S(1)} %get-tuple-element.242.ka_ref, bf16[512,256]{1,0:T(8,128)(2,1)S(1)} %get-tuple-element.247.kb_ref, f32[2,256,256]{2,1,0:T(8,128)S(1)} %collective-permute-done.21.la_ref, f32[2,256,256]{2,1,0:T(8,128)S(1)} %collective-permute-done.22.lb_ref, ...), custom_call_target="tpu_custom_call" | custom-call | flops 1000 | bytes 1000 | tf_op jit(solution)/shard_map/embed_grad_b/pallas_call | solution.py:662
  251.3 1.8 collective-permute-start.28
  253.2 1.5 slice_add_fusion.7
  254.7 2.5 collective-permute-start.26
  258.3 28.8 %collective-permute-done.26 = f32[1,64,2048]{2,1,0:T(8,128)S(1)} collective-permute-done((f32[1,64,2048]{2,1,0:T(8,128)S(1)}, f32[1,64,2048]{2,1,0:T(8,128)S(1)}, u32[]{:S(2)}, u32[]{:S(2)}) %collective-permute-start.26) | collective-permute-done | bytes 524320 | tf_op jit(solution)/shard_map/ppermute | solution.py:728
  287.1 2.4 add_add_fusion.2
  289.6 1.6 collective-permute-start.24
  293.0 1.5 collective-permute-start.33
  295.8 14.7 %collective-permute-done.30 = f32[4,1,576]{2,1,0:T(1,128)S(1)} collective-permute-done((f32[4,1,576]{2,1,0:T(1,128)S(1)}, f32[4,1,576]{2,1,0:T(1,128)S(1)}, u32[]{:S(2)}, u32[]{:S(2)}) %collective-permute-start.30) | collective-permute-done | bytes 9248 | tf_op jit(solution)/shard_map/ppermute | solution.py:728
  310.5 2.6 collective-permute-start.34
  313.6 1.4 slice_add_fusion
  315.1 3.6 collective-permute-start.36
  318.7 3.1 collective-permute-done.32
  323.5 8.5 %collective-permute-done.34 = f32[1,64,2048]{2,1,0:T(8,128)S(1)} collective-permute-done((f32[1,64,2048]{2,1,0:T(8,128)S(1)}, f32[1,64,2048]{2,1,0:T(8,128)S(1)}, u32[]{:S(2)}, u32[]{:S(2)}) %collective-permute-start.34) | collective-permute-done | bytes 524320 | tf_op jit(solution)/shard_map/ppermute | solution.py:728
  332.0 2.1 add_add_fusion.1
  334.1 10.1 %collective-permute-done.35 = f32[1,1,576]{2,1,0:T(1,128)S(1)} collective-permute-done((f32[1,1,576]{2,1,0:T(1,128)S(1)}, f32[1,1,576]{2,1,0:T(1,128)S(1)}, u32[]{:S(2)}, u32[]{:S(2)}) %collective-permute-start.35) | collective-permute-done | bytes 2336 | tf_op jit(solution)/shard_map/ppermute | solution.py:728
  346.0 12.3 %collective-permute-done.36 = f32[2,256,512]{2,1,0:T(8,128)S(1)} collective-permute-done((f32[2,256,512]{2,1,0:T(8,128)S(1)}, f32[2,256,512]{2,1,0:T(8,128)S(1)}, u32[]{:S(2)}, u32[]{:S(2)}) %collective-permute-start.36) | collective-permute-done | bytes 1048608 | tf_op jit(solution)/shard_map/ppermute | solution.py:728
  365.1 21.8 %collective-permute-done.39 = f32[2,64,1024]{2,1,0:T(8,128)S(1)} collective-permute-done((f32[2,64,1024]{2,1,0:T(8,128)S(1)}, f32[2,64,1024]{2,1,0:T(8,128)S(1)}, u32[]{:S(2)}, u32[]{:S(2)}) %collective-permute-start.39) | collective-permute-done | bytes 524320 | tf_op jit(solution)/shard_map/ppermute | solution.py:728
  390.7 6.4 %collective-permute-done.41 = f32[1,64,1024]{2,1,0:T(8,128)S(1)} collective-permute-done((f32[1,64,1024]{2,1,0:T(8,128)S(1)}, f32[1,64,1024]{2,1,0:T(8,128)S(1)}, u32[]{:S(2)}, u32[]{:S(2)}) %collective-permute-start.41) | collective-permute-done | bytes 262176 | tf_op jit(solution)/shard_map/ppermute | solution.py:728
  (290 shorter events, 53.2 us)
Async XLA Ops:
  11.0 26.4 %collective-permute-start = (f32[256,1024]{1,0:T(8,128)}, f32[256,1024]{1,0:T(8,128)}, u32[]{:S(2)}, u32[]{:S(2)}) collective-permute-start(f32[256,1024]{1,0:T(8,128)} %get-tuple-element.157.part_ref), channel_id=1, source_target_pairs={{0,1},{1,0},{2,3},{3,2},{4,5},{5,4},{6,7},{7,6},{8,9},{9,8},{10,11... | collective-permute-start | bytes 3145736 | tf_op jit(solution)/shard_map/ppermute | solution.py:728
  22.9 26.2 %collective-permute-start.3 = (f32[4,256,256]{2,1,0:T(8,128)}, f32[4,256,256]{2,1,0:T(8,128)}, u32[]{:S(2)}, u32[]{:S(2)}) collective-permute-start(f32[4,256,256]{2,1,0:T(8,128)} %get-tuple-element.161), channel_id=1, source_target_pairs={{0,2},{2,0},{4,6},{6,4},{8,10},{10,8},{12,14},{14,12},{16,18},{18,... | collective-permute-start | bytes 3145736 | tf_op jit(solution)/shard_map/ppermute | solution.py:728
  26.2 41.7 %collective-permute-start.4 = (f32[8,256,256]{2,1,0:T(8,128)}, f32[8,256,256]{2,1,0:T(8,128)}, u32[]{:S(2)}, u32[]{:S(2)}) collective-permute-start(f32[8,256,256]{2,1,0:T(8,128)} %pack_pixels.2), channel_id=1, source_target_pairs={{0,2},{2,0},{4,6},{6,4},{8,10},{10,8},{12,14},{14,12},{16,18},{18,... | collective-permute-start | bytes 6291464 | tf_op jit(solution)/shard_map/ppermute | solution.py:728
  29.8 38.1 %collective-permute-start.5 = (f32[8,256,256]{2,1,0:T(8,128)}, f32[8,256,256]{2,1,0:T(8,128)}, u32[]{:S(2)}, u32[]{:S(2)}) collective-permute-start(f32[8,256,256]{2,1,0:T(8,128)} %pack_pixels.3), channel_id=1, source_target_pairs={{0,2},{2,0},{4,6},{6,4},{8,10},{10,8},{12,14},{14,12},{16,18},{18,... | collective-permute-start | bytes 6291464 | tf_op jit(solution)/shard_map/ppermute | solution.py:728
  37.4 24.5 %collective-permute-start.1 = (f32[256,1024]{1,0:T(8,128)}, f32[256,1024]{1,0:T(8,128)S(1)}, u32[]{:S(2)}, u32[]{:S(2)}) collective-permute-start(f32[256,1024]{1,0:T(8,128)} %copy-done.72), channel_id=1, source_target_pairs={{0,1},{1,0},{2,3},{3,2},{4,5},{5,4},{6,7},{7,6},{8,9},{9,8},{10,11... | collective-permute-start | bytes 3145736 | tf_op jit(solution)/shard_map/ppermute | solution.py:728
  49.1 37.6 %copy-start.31 = (f32[256,1024]{1,0:T(8,128)}, f32[256,1024]{1,0:T(8,128)S(1)}, u32[]{:S(2)}) copy-start(f32[256,1024]{1,0:T(8,128)S(1)} %get-tuple-element.167.x0_ref) | copy-start | bytes 3145732
  51.6 46.5 %collective-permute-start.7 = (f32[4,256,256]{2,1,0:T(8,128)}, f32[4,256,256]{2,1,0:T(8,128)}, u32[]{:S(2)}, u32[]{:S(2)}) collective-permute-start(f32[4,256,256]{2,1,0:T(8,128)} %get-tuple-element.175), channel_id=1, source_target_pairs={{0,2},{2,0},{4,6},{6,4},{8,10},{10,8},{12,14},{14,12},{16,18},{18,... | collective-permute-start | bytes 3145736 | tf_op jit(solution)/shard_map/ppermute | solution.py:728
  62.0 23.4 %collective-permute-start.2 = (f32[256,1024]{1,0:T(8,128)S(1)}, f32[256,1024]{1,0:T(8,128)S(1)}, u32[]{:S(2)}, u32[]{:S(2)}) collective-permute-start(f32[256,1024]{1,0:T(8,128)S(1)} %get-tuple-element.170.opart_ref), channel_id=1, source_target_pairs={{0,1},{1,0},{2,3},{3,2},{4,5},{5,4},{6,7},{7,6},{8,9},{9,8},{10,11... | collective-permute-start | bytes 3145736 | tf_op jit(solution)/shard_map/ppermute | solution.py:728
  63.4 23.3 %copy-start.45 = (bf16[512,1024]{1,0:T(8,128)(2,1)S(1)}, bf16[512,1024]{1,0:T(8,128)(2,1)}, u32[]{:S(2)}) copy-start(bf16[512,1024]{1,0:T(8,128)(2,1)} %cot_ref.9) | copy-start | bytes 3145732
  63.4 23.3 %copy-start.58 = (bf16[1024,2048]{1,0:T(8,128)(2,1)S(1)}, bf16[1024,2048]{1,0:T(8,128)(2,1)}, u32[]{:S(2)}) copy-start(bf16[1024,2048]{1,0:T(8,128)(2,1)} %wfc1_ref.3) | copy-start | bytes 12582916
  63.4 23.3 %copy-start.60 = (bf16[2048,1024]{1,0:T(8,128)(2,1)S(1)}, bf16[2048,1024]{1,0:T(8,128)(2,1)}, u32[]{:S(2)}) copy-start(bf16[2048,1024]{1,0:T(8,128)(2,1)} %wfc2_ref.7) | copy-start | bytes 12582916
  63.4 23.3 %copy-start.78 = (f32[2048]{0:T(1024)S(1)}, f32[2048]{0:T(1024)}, u32[]{:S(2)}) copy-start(f32[2048]{0:T(1024)} %param.35) | copy-start | bytes 24580
  63.4 23.3 %copy-start.80 = (f32[1024]{0:T(1024)S(1)}, f32[1024]{0:T(1024)}, u32[]{:S(2)}) copy-start(f32[1024]{0:T(1024)} %param.31) | copy-start | bytes 12292
  63.5 23.3 %copy-start.81 = (f32[1024]{0:T(1024)S(1)}, f32[1024]{0:T(1024)}, u32[]{:S(2)}) copy-start(f32[1024]{0:T(1024)} %param.33) | copy-start | bytes 12292
  67.8 27.1 %copy-start.74 = (f32[256,1024]{1,0:T(8,128)}, f32[256,1024]{1,0:T(8,128)S(1)}, u32[]{:S(2)}) copy-start(f32[256,1024]{1,0:T(8,128)S(1)} %get-tuple-element.187.opart_ref) | copy-start | bytes 3145732
  67.8 27.1 %copy-start.87 = (bf16[3,256,512]{2,1,0:T(8,128)(2,1)}, bf16[3,256,512]{2,1,0:T(8,128)(2,1)S(1)}, u32[]{:S(2)}) copy-start(bf16[3,256,512]{2,1,0:T(8,128)(2,1)S(1)} %get-tuple-element.219.qkv_ref) | copy-start | bytes 2359300
  68.7 29.4 %collective-permute-start.8 = (f32[4,256,256]{2,1,0:T(8,128)S(1)}, f32[4,256,256]{2,1,0:T(8,128)S(1)}, u32[]{:S(2)}, u32[]{:S(2)}) collective-permute-start(f32[4,256,256]{2,1,0:T(8,128)S(1)} %get-tuple-element.183), channel_id=1, source_target_pairs={{0,2},{2,0},{4,6},{6,4},{8,10},{10,8},{12,14},{14,12},{16,18},{18,... | collective-permute-start | bytes 3145736 | tf_op jit(solution)/shard_map/ppermute | solution.py:728
  85.4 22.5 %collective-permute-start.6 = (f32[256,1024]{1,0:T(8,128)S(1)}, f32[256,1024]{1,0:T(8,128)S(1)}, u32[]{:S(2)}, u32[]{:S(2)}) collective-permute-start(f32[256,1024]{1,0:T(8,128)S(1)} %get-tuple-element.187.opart_ref), channel_id=1, source_target_pairs={{0,1},{1,0},{2,3},{3,2},{4,5},{5,4},{6,7},{7,6},{8,9},{9,8},{10,11... | collective-permute-start | bytes 3145736 | tf_op jit(solution)/shard_map/ppermute | solution.py:728
  98.1 52.7 %copy-start.22 = (f32[256,1024]{1,0:T(8,128)}, f32[256,1024]{1,0:T(8,128)S(1)}, u32[]{:S(2)}) copy-start(f32[256,1024]{1,0:T(8,128)S(1)} %get-tuple-element.185.x1_ref) | copy-start | bytes 3145732
  99.1 26.3 %collective-permute-start.11 = (f32[10,256,256]{2,1,0:T(8,128)}, f32[10,256,256]{2,1,0:T(8,128)S(1)}, u32[]{:S(2)}, u32[]{:S(2)}) collective-permute-start(f32[10,256,256]{2,1,0:T(8,128)} %get-tuple-element.197), channel_id=1, source_target_pairs={{0,2},{2,0},{4,6},{6,4},{8,10},{10,8},{12,14},{14,12},{16,18},{18,... | collective-permute-start | bytes 7864328 | tf_op jit(solution)/shard_map/ppermute | solution.py:728
  99.1 26.3 %collective-permute-start.10 = (f32[8,256,256]{2,1,0:T(8,128)}, f32[8,256,256]{2,1,0:T(8,128)S(1)}, u32[]{:S(2)}, u32[]{:S(2)}) collective-permute-start(f32[8,256,256]{2,1,0:T(8,128)} %get-tuple-element.196), channel_id=1, source_target_pairs={{0,2},{2,0},{4,6},{6,4},{8,10},{10,8},{12,14},{14,12},{16,18},{18,... | collective-permute-start | bytes 6291464 | tf_op jit(solution)/shard_map/ppermute | solution.py:728
  123.8 50.1 %copy-start.24 = (f32[256,1024]{1,0:T(8,128)}, f32[256,1024]{1,0:T(8,128)S(1)}, u32[]{:S(2)}) copy-start(f32[256,1024]{1,0:T(8,128)S(1)} %get-tuple-element.214.x1_ref) | copy-start | bytes 3145732
  123.8 4.4 %collective-permute-start.12 = (f32[8,256,256]{2,1,0:T(8,128)S(1)}, f32[8,256,256]{2,1,0:T(8,128)S(1)}, u32[]{:S(2)}, u32[]{:S(2)}) collective-permute-start(f32[8,256,256]{2,1,0:T(8,128)S(1)} %get-tuple-element.204), channel_id=1, source_target_pairs={{0,2},{2,0},{4,6},{6,4},{8,10},{10,8},{12,14},{14,12},{16,18},{18,... | collective-permute-start | bytes 6291464 | tf_op jit(solution)/shard_map/ppermute | solution.py:728
  123.8 12.5 %collective-permute-start.13 = (f32[10,256,256]{2,1,0:T(8,128)S(1)}, f32[10,256,256]{2,1,0:T(8,128)S(1)}, u32[]{:S(2)}, u32[]{:S(2)}) collective-permute-start(f32[10,256,256]{2,1,0:T(8,128)S(1)} %get-tuple-element.207), channel_id=1, source_target_pairs={{0,2},{2,0},{4,6},{6,4},{8,10},{10,8},{12,14},{14,12},{16,18},{18,... | collective-permute-start | bytes 7864328 | tf_op jit(solution)/shard_map/ppermute | solution.py:728
  124.4 25.3 %collective-permute-start.9 = (f32[256,1024]{1,0:T(8,128)}, f32[256,1024]{1,0:T(8,128)S(1)}, u32[]{:S(2)}, u32[]{:S(2)}) collective-permute-start(f32[256,1024]{1,0:T(8,128)} %copy-done.68), channel_id=1, source_target_pairs={{0,1},{1,0},{2,3},{3,2},{4,5},{5,4},{6,7},{7,6},{8,9},{9,8},{10,11... | collective-permute-start | bytes 3145736 | tf_op jit(solution)/shard_map/ppermute | solution.py:728
  134.8 118.4 %copy-start.21 = (f32[4,64,2048]{2,1,0:T(8,128)}, f32[4,64,2048]{2,1,0:T(8,128)S(1)}, u32[]{:S(2)}) copy-start(f32[4,64,2048]{2,1,0:T(8,128)S(1)} %get-tuple-element.237) | copy-start | bytes 6291460
  134.8 75.3 %collective-permute-start.19 = (f32[4,64,2048]{2,1,0:T(8,128)}, f32[4,64,2048]{2,1,0:T(8,128)}, u32[]{:S(2)}, u32[]{:S(2)}) collective-permute-start(f32[4,64,2048]{2,1,0:T(8,128)} %get-tuple-element.206), channel_id=1, source_target_pairs={{0,4},{2,6},{4,0},{6,2},{8,12},{10,14},{12,8},{14,10},{16,20},{18,... | collective-permute-start | bytes 6291464 | tf_op jit(solution)/shard_map/ppermute | solution.py:728
  141.8 72.4 %copy-start.19 = (f32[4,64,2048]{2,1,0:T(8,128)}, f32[4,64,2048]{2,1,0:T(8,128)S(1)}, u32[]{:S(2)}) copy-start(f32[4,64,2048]{2,1,0:T(8,128)S(1)} %get-tuple-element.244) | copy-start | bytes 6291460
  141.8 72.4 %collective-permute-start.20 = (f32[4,64,2048]{2,1,0:T(8,128)}, f32[4,64,2048]{2,1,0:T(8,128)}, u32[]{:S(2)}, u32[]{:S(2)}) collective-permute-start(f32[4,64,2048]{2,1,0:T(8,128)} %get-tuple-element.211), channel_id=1, source_target_pairs={{0,8},{2,10},{4,12},{6,14},{8,0},{10,2},{12,4},{14,6},{16,24},{18,... | collective-permute-start | bytes 6291464 | tf_op jit(solution)/shard_map/ppermute | solution.py:728
  149.6 24.3 %collective-permute-start.14 = (f32[256,1024]{1,0:T(8,128)S(1)}, f32[256,1024]{1,0:T(8,128)S(1)}, u32[]{:S(2)}, u32[]{:S(2)}) collective-permute-start(f32[256,1024]{1,0:T(8,128)S(1)} %copy-done.71), channel_id=1, source_target_pairs={{0,1},{1,0},{2,3},{3,2},{4,5},{5,4},{6,7},{7,6},{8,9},{9,8},{10,11... | collective-permute-start | bytes 3145736 | tf_op jit(solution)/shard_map/ppermute | solution.py:728
  182.5 6.6 %collective-permute-start.17 = (f32[8,256,256]{2,1,0:T(8,128)}, f32[8,256,256]{2,1,0:T(8,128)S(1)}, u32[]{:S(2)}, u32[]{:S(2)}) collective-permute-start(f32[8,256,256]{2,1,0:T(8,128)} %get-tuple-element.230), channel_id=1, source_target_pairs={{0,2},{2,0},{4,6},{6,4},{8,10},{10,8},{12,14},{14,12},{16,18},{18,... | collective-permute-start | bytes 6291464 | tf_op jit(solution)/shard_map/ppermute | solution.py:728
  182.6 7.1 %collective-permute-start.16 = (f32[8,256,256]{2,1,0:T(8,128)S(1)}, f32[8,256,256]{2,1,0:T(8,128)S(1)}, u32[]{:S(2)}, u32[]{:S(2)}) collective-permute-start(f32[8,256,256]{2,1,0:T(8,128)S(1)} %get-tuple-element.228), channel_id=1, source_target_pairs={{0,2},{2,0},{4,6},{6,4},{8,10},{10,8},{12,14},{14,12},{16,18},{18,... | collective-permute-start | bytes 6291464 | tf_op jit(solution)/shard_map/ppermute | solution.py:728
  183.1 25.1 %collective-permute-start.15 = (f32[256,1024]{1,0:T(8,128)S(1)}, f32[256,1024]{1,0:T(8,128)S(1)}, u32[]{:S(2)}, u32[]{:S(2)}) collective-permute-start(f32[256,1024]{1,0:T(8,128)S(1)} %get-tuple-element.222.gpart_ref), channel_id=1, source_target_pairs={{0,1},{1,0},{2,3},{3,2},{4,5},{5,4},{6,7},{7,6},{8,9},{9,8},{10,11... | collective-permute-start | bytes 3145736 | tf_op jit(solution)/shard_map/ppermute | solution.py:728
  210.1 24.4 %collective-permute-start.18 = (f32[256,1024]{1,0:T(8,128)S(1)}, f32[256,1024]{1,0:T(8,128)S(1)}, u32[]{:S(2)}, u32[]{:S(2)}) collective-permute-start(f32[256,1024]{1,0:T(8,128)S(1)} %get-tuple-element.236.gpart_ref), channel_id=1, source_target_pairs={{0,1},{1,0},{2,3},{3,2},{4,5},{5,4},{6,7},{7,6},{8,9},{9,8},{10,11... | collective-permute-start | bytes 3145736 | tf_op jit(solution)/shard_map/ppermute | solution.py:728
  212.6 40.6 %collective-permute-start.23 = (f32[2,64,2048]{2,1,0:T(8,128)S(1)}, f32[2,64,2048]{2,1,0:T(8,128)S(1)}, u32[]{:S(2)}, u32[]{:S(2)}) collective-permute-start(f32[2,64,2048]{2,1,0:T(8,128)S(1)} %slice_add_fusion.2), channel_id=1, source_target_pairs={{0,8},{2,10},{4,12},{6,14},{8,0},{10,2},{12,4},{14,6},{16,24},{18,... | collective-permute-start | bytes 3145736 | tf_op jit(solution)/shard_map/ppermute | solution.py:728
  216.5 76.5 %collective-permute-start.29 = (f32[2,64,2048]{2,1,0:T(8,128)}, f32[2,64,2048]{2,1,0:T(8,128)}, u32[]{:S(2)}, u32[]{:S(2)}) collective-permute-start(f32[2,64,2048]{2,1,0:T(8,128)} %slice_add_fusion.1), channel_id=1, source_target_pairs={{0,4},{2,6},{4,0},{6,2},{8,12},{10,14},{12,8},{14,10},{16,20},{18,... | collective-permute-start | bytes 3145736 | tf_op jit(solution)/shard_map/ppermute | solution.py:728
  218.1 95.0 %collective-permute-start.31 = (f32[4,256,512]{2,1,0:T(8,128)}, f32[4,256,512]{2,1,0:T(8,128)}, u32[]{:S(2)}, u32[]{:S(2)}) collective-permute-start(f32[4,256,512]{2,1,0:T(8,128)} %get-tuple-element.234), channel_id=1, source_target_pairs={{0,4},{2,6},{4,0},{6,2},{8,12},{10,14},{12,8},{14,10},{16,20},{18,... | collective-permute-start | bytes 6291464 | tf_op jit(solution)/shard_map/ppermute | solution.py:728
  218.6 21.6 %collective-permute-start.21 = (f32[2,256,256]{2,1,0:T(8,128)S(1)}, f32[2,256,256]{2,1,0:T(8,128)S(1)}, u32[]{:S(2)}, u32[]{:S(2)}) collective-permute-start(f32[2,256,256]{2,1,0:T(8,128)S(1)} %get-tuple-element.250), channel_id=1, source_target_pairs={{0,2},{2,0},{4,6},{6,4},{8,10},{10,8},{12,14},{14,12},{16,18},{18,... | collective-permute-start | bytes 1572872 | tf_op jit(solution)/shard_map/ppermute | solution.py:728
  236.3 3.9 collective-permute-start.22
  245.8 113.9 %collective-permute-start.37 = (f32[4,64,1024]{2,1,0:T(8,128)}, f32[4,64,1024]{2,1,0:T(8,128)}, u32[]{:S(2)}, u32[]{:S(2)}) collective-permute-start(f32[4,64,1024]{2,1,0:T(8,128)} %get-tuple-element.254), channel_id=1, source_target_pairs={{0,4},{2,6},{4,0},{6,2},{8,12},{10,14},{12,8},{14,10},{16,20},{18,... | collective-permute-start | bytes 3145736 | tf_op jit(solution)/shard_map/ppermute | solution.py:728
  251.3 39.9 %collective-permute-start.28 = (f32[4,64,1024]{2,1,0:T(8,128)}, f32[4,64,1024]{2,1,0:T(8,128)}, u32[]{:S(2)}, u32[]{:S(2)}) collective-permute-start(f32[4,64,1024]{2,1,0:T(8,128)} %get-tuple-element.256), channel_id=1, source_target_pairs={{0,8},{2,10},{4,12},{6,14},{8,0},{10,2},{12,4},{14,6},{16,24},{18,... | collective-permute-start | bytes 3145736 | tf_op jit(solution)/shard_map/ppermute | solution.py:728
  254.7 34.9 %copy-start.29 = (f32[256,1024]{1,0:T(8,128)S(1)}, f32[256,1024]{1,0:T(8,128)}, u32[]{:S(2)}) copy-start(f32[256,1024]{1,0:T(8,128)} %copy-done.28) | copy-start | bytes 3145732
  254.7 32.4 %collective-permute-start.26 = (f32[1,64,2048]{2,1,0:T(8,128)S(1)}, f32[1,64,2048]{2,1,0:T(8,128)S(1)}, u32[]{:S(2)}, u32[]{:S(2)}) collective-permute-start(f32[1,64,2048]{2,1,0:T(8,128)S(1)} %slice_add_fusion.7), channel_id=1, source_target_pairs={{0,16},{2,18},{4,20},{6,22},{8,24},{10,26},{12,28},{14,30},{16,0},... | collective-permute-start | bytes 1572872 | tf_op jit(solution)/shard_map/ppermute | solution.py:728
  258.2 33.8 %copy-start.43 = (f32[4,64,1024]{2,1,0:T(8,128)S(1)}, f32[4,64,1024]{2,1,0:T(8,128)}, u32[]{:S(2)}) copy-start(f32[4,64,1024]{2,1,0:T(8,128)} %copy-done.42) | copy-start | bytes 3145732
  287.1 2.4 collective-permute-start.27
  289.5 24.1 %copy-start.18 = (f32[4,256,512]{2,1,0:T(8,128)S(1)}, f32[4,256,512]{2,1,0:T(8,128)}, u32[]{:S(2)}) copy-start(f32[4,256,512]{2,1,0:T(8,128)} %copy-done.17) | copy-start | bytes 6291460
  289.6 25.5 %collective-permute-start.24 = (f32[256,1024]{1,0:T(8,128)S(1)}, f32[256,1024]{1,0:T(8,128)S(1)}, u32[]{:S(2)}, u32[]{:S(2)}) collective-permute-start(f32[256,1024]{1,0:T(8,128)S(1)} %copy-done.29), channel_id=1, source_target_pairs={{0,1},{1,0},{2,3},{3,2},{4,5},{5,4},{6,7},{7,6},{8,9},{9,8},{10,11... | collective-permute-start | bytes 3145736 | tf_op jit(solution)/shard_map/ppermute | solution.py:728
  291.2 19.3 %collective-permute-start.30 = (f32[4,1,576]{2,1,0:T(1,128)S(1)}, f32[4,1,576]{2,1,0:T(1,128)S(1)}, u32[]{:S(2)}, u32[]{:S(2)}) collective-permute-start(f32[4,1,576]{2,1,0:T(1,128)S(1)} %get-tuple-element.307), channel_id=1, source_target_pairs={{0,4},{2,6},{4,0},{6,2},{8,12},{10,14},{12,8},{14,10},{16,20},{18,... | collective-permute-start | bytes 27656 | tf_op jit(solution)/shard_map/ppermute | solution.py:728
  293.0 28.7 %collective-permute-start.33 = (f32[2,64,1024]{2,1,0:T(8,128)S(1)}, f32[2,64,1024]{2,1,0:T(8,128)S(1)}, u32[]{:S(2)}, u32[]{:S(2)}) collective-permute-start(f32[2,64,1024]{2,1,0:T(8,128)S(1)} %slice_add_fusion.6), channel_id=1, source_target_pairs={{0,4},{2,6},{4,0},{6,2},{8,12},{10,14},{12,8},{14,10},{16,20},{18,... | collective-permute-start | bytes 1572872 | tf_op jit(solution)/shard_map/ppermute | solution.py:728
  295.8 26.0 %copy-start.27 = (f32[256,1024]{1,0:T(8,128)S(1)}, f32[256,1024]{1,0:T(8,128)}, u32[]{:S(2)}) copy-start(f32[256,1024]{1,0:T(8,128)} %copy-done.26) | copy-start | bytes 3145732
  310.5 21.5 %collective-permute-start.34 = (f32[1,64,2048]{2,1,0:T(8,128)S(1)}, f32[1,64,2048]{2,1,0:T(8,128)S(1)}, u32[]{:S(2)}, u32[]{:S(2)}) collective-permute-start(f32[1,64,2048]{2,1,0:T(8,128)S(1)} %slice_add_fusion.5), channel_id=1, source_target_pairs={{0,16},{2,18},{4,20},{6,22},{8,24},{10,26},{12,28},{14,30},{16,0},... | collective-permute-start | bytes 1572872 | tf_op jit(solution)/shard_map/ppermute | solution.py:728
  313.1 8.7 %collective-permute-start.32 = (f32[2,1,576]{2,1,0:T(1,128)S(1)}, f32[2,1,576]{2,1,0:T(1,128)S(1)}, u32[]{:S(2)}, u32[]{:S(2)}) collective-permute-start(f32[2,1,576]{2,1,0:T(1,128)S(1)} %slice_add_fusion.10), channel_id=1, source_target_pairs={{0,8},{2,10},{4,12},{6,14},{8,0},{10,2},{12,4},{14,6},{16,24},{18,... | collective-permute-start | bytes 13832 | tf_op jit(solution)/shard_map/ppermute | solution.py:728
  315.1 43.3 %collective-permute-start.36 = (f32[2,256,512]{2,1,0:T(8,128)S(1)}, f32[2,256,512]{2,1,0:T(8,128)S(1)}, u32[]{:S(2)}, u32[]{:S(2)}) collective-permute-start(f32[2,256,512]{2,1,0:T(8,128)S(1)} %slice_add_fusion), channel_id=1, source_target_pairs={{0,8},{2,10},{4,12},{6,14},{8,0},{10,2},{12,4},{14,6},{16,24},{18,... | collective-permute-start | bytes 3145736 | tf_op jit(solution)/shard_map/ppermute | solution.py:728
  321.8 39.8 %collective-permute-start.25 = (f32[256,1024]{1,0:T(8,128)S(1)}, f32[256,1024]{1,0:T(8,128)S(1)}, u32[]{:S(2)}, u32[]{:S(2)}) collective-permute-start(f32[256,1024]{1,0:T(8,128)S(1)} %copy-done.27), channel_id=1, source_target_pairs={{0,1},{1,0},{2,3},{3,2},{4,5},{5,4},{6,7},{7,6},{8,9},{9,8},{10,11... | collective-permute-start | bytes 3145736 | tf_op jit(solution)/shard_map/ppermute | solution.py:728
  321.8 22.5 %collective-permute-start.35 = (f32[1,1,576]{2,1,0:T(1,128)S(1)}, f32[1,1,576]{2,1,0:T(1,128)S(1)}, u32[]{:S(2)}, u32[]{:S(2)}) collective-permute-start(f32[1,1,576]{2,1,0:T(1,128)S(1)} %fusion.9), channel_id=1, source_target_pairs={{0,16},{2,18},{4,20},{6,22},{8,24},{10,26},{12,28},{14,30},{16,0},... | collective-permute-start | bytes 6920 | tf_op jit(solution)/shard_map/ppermute | solution.py:728
  323.5 36.2 %copy-start.41 = (f32[4,64,1024]{2,1,0:T(8,128)S(1)}, f32[4,64,1024]{2,1,0:T(8,128)}, u32[]{:S(2)}) copy-start(f32[4,64,1024]{2,1,0:T(8,128)} %copy-done.40) | copy-start | bytes 3145732
  332.0 29.6 %collective-permute-start.38 = (f32[1,64,1024]{2,1,0:T(8,128)S(1)}, f32[1,64,1024]{2,1,0:T(8,128)S(1)}, u32[]{:S(2)}, u32[]{:S(2)}) collective-permute-start(f32[1,64,1024]{2,1,0:T(8,128)S(1)} %slice_add_fusion.9), channel_id=1, source_target_pairs={{0,16},{2,18},{4,20},{6,22},{8,24},{10,26},{12,28},{14,30},{16,0},... | collective-permute-start | bytes 786440 | tf_op jit(solution)/shard_map/ppermute | solution.py:728
  334.1 27.5 %copy-start.23 = (f32[256,1024]{1,0:T(8,128)S(1)}, f32[256,1024]{1,0:T(8,128)}, u32[]{:S(2)}) copy-start(f32[256,1024]{1,0:T(8,128)} %copy-done.22) | copy-start | bytes 3145732
  334.1 27.5 %copy-start.25 = (f32[256,1024]{1,0:T(8,128)S(1)}, f32[256,1024]{1,0:T(8,128)}, u32[]{:S(2)}) copy-start(f32[256,1024]{1,0:T(8,128)} %copy-done.24) | copy-start | bytes 3145732
  334.1 27.5 %copy-start.30 = (f32[256,1024]{1,0:T(8,128)S(1)}, f32[256,1024]{1,0:T(8,128)}, u32[]{:S(2)}) copy-start(f32[256,1024]{1,0:T(8,128)} %copy-done.28) | copy-start | bytes 3145732
  334.1 27.5 %copy-start.90 = (f32[1024]{0:T(1024)S(1)}, f32[1024]{0:T(1024)}, u32[]{:S(2)}) copy-start(f32[1024]{0:T(1024)} %param.37) | copy-start | bytes 12292
  359.6 28.4 %collective-permute-start.40 = (f32[1,256,512]{2,1,0:T(8,128)S(1)}, f32[1,256,512]{2,1,0:T(8,128)S(1)}, u32[]{:S(2)}, u32[]{:S(2)}) collective-permute-start(f32[1,256,512]{2,1,0:T(8,128)S(1)} %slice_add_fusion.4), channel_id=1, source_target_pairs={{0,16},{2,18},{4,20},{6,22},{8,24},{10,26},{12,28},{14,30},{16,0},... | collective-permute-start | bytes 1572872 | tf_op jit(solution)/shard_map/ppermute | solution.py:728
  360.8 26.1 %collective-permute-start.39 = (f32[2,64,1024]{2,1,0:T(8,128)S(1)}, f32[2,64,1024]{2,1,0:T(8,128)S(1)}, u32[]{:S(2)}, u32[]{:S(2)}) collective-permute-start(f32[2,64,1024]{2,1,0:T(8,128)S(1)} %slice_add_fusion.3), channel_id=1, source_target_pairs={{0,8},{2,10},{4,12},{6,14},{8,0},{10,2},{12,4},{14,6},{16,24},{18,... | collective-permute-start | bytes 1572872 | tf_op jit(solution)/shard_map/ppermute | solution.py:728
  387.9 9.2 %collective-permute-start.41 = (f32[1,64,1024]{2,1,0:T(8,128)S(1)}, f32[1,64,1024]{2,1,0:T(8,128)S(1)}, u32[]{:S(2)}, u32[]{:S(2)}) collective-permute-start(f32[1,64,1024]{2,1,0:T(8,128)S(1)} %slice_add_fusion.8), channel_id=1, source_target_pairs={{0,16},{2,18},{4,20},{6,22},{8,24},{10,26},{12,28},{14,30},{16,0},... | collective-permute-start | bytes 786440 | tf_op jit(solution)/shard_map/ppermute | solution.py:728
  (71 other events, 454.0 us)

commit v4 on v3

--- a/solution.py
+++ b/solution.py
@@ -2,6 +2,8 @@
 
 import jax
 import jax.numpy as jnp
+import ml_dtypes
+import numpy as np
 from jax import lax
 from jax.experimental import pallas as pl
 from jax.experimental.pallas import tpu as pltpu
@@ -16,6 +18,7 @@
 MIB = 1024 * 1024
 QUAD = 256
 PART = 256
+WIDE = 2
 
 
 def nn(left, right):
@@ -43,7 +46,7 @@
 
 
 def whole(shape):
-    return pl.BlockSpec(shape, lambda *_: (0,) * len(shape))
+    return pl.BlockSpec(shape, lambda *_: (0,) * len(shape), pipeline_mode=pl.Buffered(1))
 
 
 def norm_parts(values):
@@ -109,7 +112,7 @@
             jax.ShapeDtypeStruct((items, width // 2, rows), BF16),
             jax.ShapeDtypeStruct((2 * items, PART, rows), F32),
         ],
-        compiler_params=params(12),
+        compiler_params=params(4),
         cost_estimate=short_cost(),
         name="turn_cotangent",
     )(place, cotangent)
@@ -127,7 +130,7 @@
         in_specs=[pl.BlockSpec((rows, PART), lambda n: (0, n))],
         out_specs=pl.BlockSpec((1, rows, PART), lambda n: (n, 0, 0)),
         out_shape=jax.ShapeDtypeStruct((columns // PART, rows, PART), F32),
-        compiler_params=params(8),
+        compiler_params=params(4),
         cost_estimate=short_cost(),
         name="pack_pixels",
     )(values)
@@ -156,61 +159,108 @@
             jax.ShapeDtypeStruct((width // 2, rows), BF16),
             jax.ShapeDtypeStruct((parts, PART, rows), F32),
         ],
-        compiler_params=params(12),
+        compiler_params=params(4),
         cost_estimate=short_cost(),
         name="pack_attn",
     )(place, a1, mix)
 
 
-def embed_kernel(kinds, pix_ref, wspec_ref, wrgb_ref, pick_ref, part_ref, mixed_ref, *, item):
-    step = pl.program_id(0)
-    wide = pix_ref.shape[1]
+def pieces_of(length):
+    third = length // 3 // LANES * LANES
+    return [(0, third), (third, third), (2 * third, length - 2 * third)]
+
+
+def embed_kernel(
+    kinds, pix_ref, wspec_ref, wrgb_ref, pick_ref, part_ref, mixed_ref,
+    pix_buf, wspec_buf, wrgb_buf, pick_buf, pix_sem, big_sem, small_sem, *, item,
+):
+    rows, wide = pix_buf.shape
     spectral = kinds[item] == 1
+    pieces = pieces_of(wide)
+    own_rows = pl.ds(item * rows, rows)
 
     @pl.when(spectral)
     def _():
-        @pl.when(step == 0)
-        def _():
-            mixed_ref[:, :wide] = pix_ref[...]
-            mixed_ref[:, wide:] = jnp.zeros((pix_ref.shape[0], wrgb_ref.shape[0]), BF16)
-
-        part_ref[...] = nn(pix_ref[...], wspec_ref[...])
+        copies = []
+        for n, (first, size) in enumerate(pieces):
+            span = pl.ds(first, size)
+            copies.append(
+                (
+                    pltpu.make_async_copy(
+                        pix_ref.at[own_rows, span], mixed_ref.at[:, span], pix_sem.at[n]
+                    ),
+                    pltpu.make_async_copy(wspec_ref.at[span], wspec_buf.at[span], big_sem.at[n]),
+                )
+            )
+        for pair in copies:
+            for copy in pair:
+                copy.start()
+        mixed_ref[:, wide:] = jnp.zeros((rows, wrgb_buf.shape[0]), BF16)
+        for n, (first, size) in enumerate(pieces):
+            for copy in copies[n]:
+                copy.wait()
+            term = nn(mixed_ref[:, first : first + size], wspec_buf[first : first + size, :])
+            if n == 0:
+                part_ref[...] = term
+            else:
+                part_ref[...] += term
 
     @pl.when(jnp.logical_not(spectral))
     def _():
-        @pl.when(step == 0)
-        def _():
-            mixed_ref[:, :wide] = jnp.zeros(pix_ref.shape, BF16)
-            mixed_ref[:, wide:] = nn(pix_ref[...], pick_ref[...]).astype(BF16)
-
-        part_ref[...] = nn(mixed_ref[:, wide:], wrgb_ref[...])
+        copies = []
+        for n, (first, size) in enumerate(pieces):
+            span = pl.ds(first, size)
+            copies.append(
+                (
+                    pltpu.make_async_copy(
+                        pix_ref.at[own_rows, span], pix_buf.at[:, span], pix_sem.at[n]
+                    ),
+                    pltpu.make_async_copy(pick_ref.at[span], pick_buf.at[span], big_sem.at[n]),
+                )
+            )
+        for pair in copies:
+            for copy in pair:
+                copy.start()
+        weights = pltpu.make_async_copy(wrgb_ref, wrgb_buf, small_sem)
+        weights.start()
+        mixed_ref[:, :wide] = jnp.zeros((rows, wide), BF16)
+        total = None
+        for n, (first, size) in enumerate(pieces):
+            for copy in copies[n]:
+                copy.wait()
+            term = nn(pix_buf[:, first : first + size], pick_buf[first : first + size, :])
+            total = term if total is None else total + term
+        mixed_ref[:, wide:] = total.astype(BF16)
+        weights.wait()
+        part_ref[...] = nn(mixed_ref[:, wide:], wrgb_buf[...])
 
 
 def embed(kinds, pixels, w_spectral, w_rgb, pick, item, rows):
     wide, width = w_spectral.shape
     narrow = w_rgb.shape[0]
-    tile = 256
+    far = pl.BlockSpec(memory_space=pltpu.HBM)
     return pl.pallas_call(
         functools.partial(embed_kernel, item=item),
         grid_spec=pltpu.PrefetchScalarGridSpec(
             num_scalar_prefetch=1,
-            grid=(width // tile,),
-            in_specs=[
-                pl.BlockSpec((rows, wide), lambda n, *_: (item, 0)),
-                pl.BlockSpec((wide, tile), lambda n, *_: (0, n)),
-                pl.BlockSpec((narrow, tile), lambda n, *_: (0, n)),
-                whole((wide, narrow)),
-            ],
-            out_specs=[
-                pl.BlockSpec((rows, tile), lambda n, *_: (0, n)),
-                whole((rows, wide + narrow)),
+            grid=(1,),
+            in_specs=[far, far, far, far],
+            out_specs=[whole((rows, width)), whole((rows, wide + narrow))],
+            scratch_shapes=[
+                pltpu.VMEM((rows, wide), BF16),
+                pltpu.VMEM((wide, width), BF16),
+                pltpu.VMEM((narrow, width), BF16),
+                pltpu.VMEM((wide, narrow), BF16),
+                pltpu.SemaphoreType.DMA((3,)),
+                pltpu.SemaphoreType.DMA((3,)),
+                pltpu.SemaphoreType.DMA(()),
             ],
         ),
         out_shape=[
             jax.ShapeDtypeStruct((rows, width), F32),
             jax.ShapeDtypeStruct((rows, wide + narrow), BF16),
         ],
-        compiler_params=params(16),
+        compiler_params=params(58),
         cost_estimate=short_cost(),
         name="embed",
     )(kinds, pixels, w_spectral, w_rgb, pick)
@@ -305,29 +355,46 @@
             jax.ShapeDtypeStruct((rows, heads_wide), BF16),
             jax.ShapeDtypeStruct((rows, width), F32),
         ],
-        compiler_params=params(24),
+        compiler_params=params(10),
         cost_estimate=long_cost(),
         name="attn_forward",
     )(part, recv, table, gain, bias, w_qkv, q_bias, v_bias, w_out)
 
 
-def attn_backward_kernel(
-    place, gpart_ref, grecv_ref, x1_ref, cot_ref, gain_ref, wout_ref, qkv_ref, wqkv_ref,
-    dx1_ref, dya_ref, dqkv_ref, da1_ref, sums_ref, qvsum_ref, keep_ref, gone_ref, turned_ref,
-):
+def put_rows(refs, values, add):
+    first = 0
+    for ref in refs:
+        rows = ref.shape[0]
+        if add:
+            ref[...] += values[first : first + rows]
+        else:
+            ref[...] = values[first : first + rows]
+        first += rows
+
+
+def joined(refs):
+    values = [ref[...] for ref in refs]
+    return values[0] if len(values) == 1 else jnp.concatenate(values, 0)
+
+
+def attn_backward_kernel(place, *refs, parts):
+    gpart_refs, refs = refs[: parts[0]], refs[parts[0] :]
+    grecv_refs, refs = refs[: parts[1]], refs[parts[1] :]
+    x1_ref, cot_ref, gain_ref, wout_ref, qkv_ref, wqkv_ref, *refs = refs
+    dx1_ref, dya_ref, dqkv_ref, sums_ref, qvsum_ref, keep_ref, gone_ref, *da1_refs = refs[:-1]
+    turned_ref = refs[-1]
     quad = pl.program_id(0)
     rows = x1_ref.shape[0]
 
     @pl.when(quad == 0)
     def _():
         normed, inverse = norm_parts(x1_ref[...])
-        grad = gpart_ref[...] + grecv_ref[...]
+        grad = joined(gpart_refs) + joined(grecv_refs)
         cot = cot_ref[...].astype(F32)
         dx1 = cot + norm_back(normed, inverse, grad, gain_ref[...])
         dx1_ref[...] = dx1
         dya = dx1.astype(BF16)
         dya_ref[...] = dya
-        da1_ref[...] = jnp.zeros_like(da1_ref)
         sums_ref[0:1, :] = column_sum(grad * normed)
         sums_ref[1:2, :] = column_sum(grad)
         sums_ref[2:3, :] = column_sum(dya.astype(F32))
@@ -354,9 +421,16 @@
         dqkv_ref[0, :, span] = (totals[0] * scale).astype(BF16)
         dqkv_ref[1, :, span] = (totals[1] * scale).astype(BF16)
         dqkv_ref[2, :, span] = totals[2].astype(BF16)
-    da1_ref[...] += (
-        nt(dqkv_ref[0], wqkv_ref[0]) + nt(dqkv_ref[1], wqkv_ref[1]) + nt(dqkv_ref[2], wqkv_ref[2])
-    )
+    da1 = nt(dqkv_ref[0], wqkv_ref[0]) + nt(dqkv_ref[1], wqkv_ref[1]) + nt(dqkv_ref[2], wqkv_ref[2])
+
+    @pl.when(quad == 0)
+    def _():
+        put_rows(da1_refs, da1, False)
+
+    @pl.when(quad != 0)
+    def _():
+        put_rows(da1_refs, da1, True)
+
     steps = pl.num_programs(0)
     for plane in range(3):
         gone_ref[2 + plane * steps + quad] = dqkv_ref[plane].astype(F32)
@@ -365,18 +439,17 @@
     qvsum_ref[2:8, :] = jnp.zeros((6, qvsum_ref.shape[1]), F32)
 
 
-def attn_backward(place, gpart, grecv, x1, cotangent, gain, w_out, qkv, w_qkv, item):
+def attn_backward(place, gparts, grecvs, x1, cotangent, gain, w_out, qkv, w_qkv, item, cuts):
     rows, width = x1.shape
     heads_wide = w_out.shape[0]
     steps = heads_wide // QUAD
     return pl.pallas_call(
-        attn_backward_kernel,
+        functools.partial(attn_backward_kernel, parts=(len(gparts), len(grecvs))),
         grid_spec=pltpu.PrefetchScalarGridSpec(
             num_scalar_prefetch=1,
             grid=(steps,),
             in_specs=[
-                whole(gpart.shape),
-                whole(grecv.shape),
+                *[whole(v.shape) for v in (*gparts, *grecvs)],
                 whole(x1.shape),
                 pl.BlockSpec((rows, width), lambda n, *_: (item, 0)),
                 whole(gain.shape),
@@ -388,11 +461,11 @@
                 whole((rows, width)),
                 whole((rows, width)),
                 pl.BlockSpec((3, rows, QUAD), lambda n, *_: (0, 0, n)),
-                whole((rows, width)),
                 whole((8, width)),
                 pl.BlockSpec((8, QUAD), lambda n, *_: (0, n)),
                 whole((width // 2, rows)),
                 whole((2 + 3 * steps, PART, rows)),
+                *[whole((cut, width)) for cut in cuts],
             ],
             scratch_shapes=[pltpu.VMEM((width, rows), BF16)],
         ),
@@ -400,22 +473,23 @@
             jax.ShapeDtypeStruct((rows, width), F32),
             jax.ShapeDtypeStruct((rows, width), BF16),
             jax.ShapeDtypeStruct((3, rows, heads_wide), BF16),
-            jax.ShapeDtypeStruct((rows, width), F32),
             jax.ShapeDtypeStruct((8, width), F32),
             jax.ShapeDtypeStruct((8, heads_wide), F32),
             jax.ShapeDtypeStruct((width // 2, rows), BF16),
             jax.ShapeDtypeStruct((2 + 3 * steps, PART, rows), F32),
+            *[jax.ShapeDtypeStruct((cut, width), F32) for cut in cuts],
         ],
-        compiler_params=params(32),
+        compiler_params=params(16),
         cost_estimate=long_cost(),
         name="attn_backward",
-    )(place, gpart, grecv, x1, cotangent, gain, w_out, qkv, w_qkv)
+    )(place, *gparts, *grecvs, x1, cotangent, gain, w_out, qkv, w_qkv)
 
 
 def mlp_kernel(
     place, x0_ref, opart_ref, orecv_ref, obias_ref, gain_ref, bias_ref, wfc1_ref, b1_ref, wfc2_ref, cot_ref,
-    x1_ref, a2_ref, act_ref, dpre_ref, da2_ref, b1sum_ref, keep_ref, gact_ref, gpre_ref, turned_ref,
+    x1_ref, a2_ref, act_ref, dpre_ref, b1sum_ref, keep_ref, gact_ref, gpre_ref, *refs,
 ):
+    da2_refs, turned_ref = refs[:-1], refs[-1]
     step = pl.program_id(0)
 
     @pl.when(step == 0)
@@ -423,7 +497,6 @@
         x1_ref[...] = x0_ref[...] + (opart_ref[...] + orecv_ref[...] + obias_ref[...])
         normed, _inv = norm_parts(x1_ref[...])
         a2_ref[...] = (normed * gain_ref[...] + bias_ref[...]).astype(BF16)
-        da2_ref[...] = jnp.zeros_like(da2_ref)
         turn(place, a2_ref, turned_ref, slice(None))
         spread(turned_ref, keep_ref, gpre_ref)
 
@@ -440,10 +513,20 @@
         gact_ref[part] = act[:, columns].astype(F32)
         gpre_ref[2 + step * (act.shape[1] // PART) + part] = dpre[:, columns].astype(F32)
     b1sum_ref[...] = column_sum(dpre.astype(F32))
-    da2_ref[...] += nt(dpre, wfc1_ref[...])
-
-
-def mlp(place, x0, opart, orecv, out_bias, gain, bias, w_fc1, fc1_bias, w_fc2, cotangent, item):
+    da2 = nt(dpre, wfc1_ref[...])
+
+    @pl.when(step == 0)
+    def _():
+        put_rows(da2_refs, da2, False)
+
+    @pl.when(step != 0)
+    def _():
+        put_rows(da2_refs, da2, True)
+
+
+def mlp(
+    place, x0, opart, orecv, out_bias, gain, bias, w_fc1, fc1_bias, w_fc2, cotangent, item, cuts
+):
     rows, width = x0.shape
     hidden = w_fc1.shape[1]
     tile = 512
@@ -472,11 +555,11 @@
                 whole((rows, width)),
                 row_tile,
                 row_tile,
-                whole((rows, width)),
                 pl.BlockSpec((1, tile), lambda n, *_: (0, n)),
                 whole((width // 2, rows)),
                 gone,
                 whole((2 + hidden // PART, rows, PART)),
+                *[whole((cut, width)) for cut in cuts],
             ],
             scratch_shapes=[pltpu.VMEM((width, rows), BF16)],
         ),
@@ -485,13 +568,13 @@
             jax.ShapeDtypeStruct((rows, width), BF16),
             jax.ShapeDtypeStruct((rows, hidden), BF16),
             jax.ShapeDtypeStruct((rows, hidden), BF16),
-            jax.ShapeDtypeStruct((rows, width), F32),
             jax.ShapeDtypeStruct((1, hidden), F32),
             jax.ShapeDtypeStruct((width // 2, rows), BF16),
             jax.ShapeDtypeStruct((hidden // PART, rows, PART), F32),
             jax.ShapeDtypeStruct((2 + hidden // PART, rows, PART), F32),
+            *[jax.ShapeDtypeStruct((cut, width), F32) for cut in cuts],
         ],
-        compiler_params=params(32),
+        compiler_params=params(14),
         cost_estimate=long_cost(),
         name="mlp",
     )(place, x0, opart, orecv, out_bias, gain, bias, w_fc1, fc1_bias, w_fc2, cotangent)
@@ -511,63 +594,49 @@
         in_specs=[whole(act.shape), pl.BlockSpec((hidden, tile), lambda n: (0, n))],
         out_specs=pl.BlockSpec((rows, tile), lambda n: (0, n)),
         out_shape=jax.ShapeDtypeStruct((rows, width), F32),
-        compiler_params=params(16),
+        compiler_params=params(6),
         cost_estimate=long_cost(),
         name="mlp_out",
     )(act, w_fc2)
 
 
-def first_norm_back_kernel(
-    place, gpart_ref, grecv_ref, x0_ref, dx1_ref, gain_ref, dx0_ref, sums_ref, keep_ref, gone_ref,
-    turned_ref,
-):
-    step = pl.program_id(0)
-    tile = x0_ref.shape[0]
-
-    @pl.when(step == 0)
-    def _():
-        sums_ref[...] = jnp.zeros_like(sums_ref)
-
+def first_norm_back_kernel(place, *refs, parts):
+    gpart_refs, refs = refs[: parts[0]], refs[parts[0] :]
+    grecv_refs, refs = refs[: parts[1]], refs[parts[1] :]
+    x0_ref, dx1_ref, gain_ref, dx0_ref, sums_ref, keep_ref, gone_ref, turned_ref = refs
     normed, inverse = norm_parts(x0_ref[...])
-    grad = gpart_ref[...] + grecv_ref[...]
+    grad = joined(gpart_refs) + joined(grecv_refs)
     dx0_ref[...] = (dx1_ref[...] + norm_back(normed, inverse, grad, gain_ref[...])).astype(BF16)
-    sums_ref[0:1, :] += column_sum(grad * normed)
-    sums_ref[1:2, :] += column_sum(grad)
-    turn(place, dx0_ref, turned_ref, pl.ds(pl.multiple_of(step * tile, tile), tile))
-
-    @pl.when(step == pl.num_programs(0) - 1)
-    def _():
-        spread(turned_ref, keep_ref, gone_ref)
-
-
-def first_norm_back(place, gpart, grecv, x0, dx1, gain):
+    sums_ref[0:1, :] = column_sum(grad * normed)
+    sums_ref[1:2, :] = column_sum(grad)
+    sums_ref[2:8, :] = jnp.zeros((6, sums_ref.shape[1]), F32)
+    turn(place, dx0_ref, turned_ref, slice(None))
+    spread(turned_ref, keep_ref, gone_ref)
+
+
+def first_norm_back(place, gparts, grecvs, x0, dx1, gain, estimate):
     rows, width = x0.shape
-    tile = 128
-    block = pl.BlockSpec((tile, width), lambda n, *_: (n, 0))
+    operands = (*gparts, *grecvs, x0, dx1, gain)
+    shapes = [
+        jax.ShapeDtypeStruct((rows, width), BF16),
+        jax.ShapeDtypeStruct((8, width), F32),
+        jax.ShapeDtypeStruct((width // 2, rows), BF16),
+        jax.ShapeDtypeStruct((2, PART, rows), F32),
+    ]
     return pl.pallas_call(
-        first_norm_back_kernel,
+        functools.partial(first_norm_back_kernel, parts=(len(gparts), len(grecvs))),
         grid_spec=pltpu.PrefetchScalarGridSpec(
             num_scalar_prefetch=1,
-            grid=(rows // tile,),
-            in_specs=[block, block, block, block, whole(gain.shape)],
-            out_specs=[
-                block,
-                whole((8, width)),
-                whole((width // 2, rows)),
-                whole((2, PART, rows)),
-            ],
+            grid=(1,),
+            in_specs=[whole(v.shape) for v in operands],
+            out_specs=[whole(v.shape) for v in shapes],
             scratch_shapes=[pltpu.VMEM((width, rows), BF16)],
         ),
-        out_shape=[
-            jax.ShapeDtypeStruct((rows, width), BF16),
-            jax.ShapeDtypeStruct((8, width), F32),
-            jax.ShapeDtypeStruct((width // 2, rows), BF16),
-            jax.ShapeDtypeStruct((2, PART, rows), F32),
-        ],
-        compiler_params=params(14),
-        cost_estimate=short_cost(),
+        out_shape=shapes,
+        compiler_params=params(10),
+        cost_estimate=estimate,
         name="first_norm_back",
-    )(place, gpart, grecv, x0, dx1, gain)
+    )(place, *operands)
 
 
 def pixel_grad_kernel(kinds, da_ref, db_ref, wspec_ref, wrgb_ref, pick_ref, out_ref):
@@ -606,7 +675,7 @@
             out_specs=pl.BlockSpec((rows, wide), lambda i, *_: (i, 0)),
         ),
         out_shape=jax.ShapeDtypeStruct((2 * rows, wide), BF16),
-        compiler_params=params(20),
+        compiler_params=params(8),
         cost_estimate=long_cost(),
         name="pixel_grad",
     )(kinds, grad_a, grad_b, w_spectral, w_rgb, pick)
@@ -623,13 +692,13 @@
             left_ref[part * PART : (part + 1) * PART, columns] = gone_ref[first + part].astype(BF16)
 
 
-def emit(left_ref, rights, send_ref, keep_ref, moves):
+def emit(left_ref, rights, send_ref, keep_ref, moves, columns=slice(None)):
     right = jnp.concatenate([r.astype(BF16) for r in rights], 0)
     total = nn(left_ref[...], right)
     half = LANES // 2
     for pos, block in enumerate(moves):
         out_ref = send_ref if pos < 4 else keep_ref
-        out_ref[pos % 4] = total[block * half : (block + 1) * half]
+        out_ref[pos % 4, :, columns] = total[block * half : (block + 1) * half]
 
 
 def plain_grad_kernel(
@@ -640,14 +709,17 @@
     def _():
         gather_left((ka_ref, kb_ref), (la_ref, lb_ref), 0, left_ref)
 
-    rights = (ra_ref[...], rb_ref[...], oa_ref[0], ob_ref[0])
-    emit(left_ref, rights, send_ref, keep_ref, moves)
+    for part in range(oa_ref.shape[0]):
+        columns = slice(part * PART, (part + 1) * PART)
+        rights = (ra_ref[:, columns], rb_ref[:, columns], oa_ref[part], ob_ref[part])
+        emit(left_ref, rights, send_ref, keep_ref, moves, columns)
 
 
 def plain_grad(keeps, lefts, rights, others, moves, name, skip=0, columns=None, lead=0):
     half_width, rows = keeps[0][0].shape[-2:]
     columns = columns or rights[0].shape[1]
-    base = skip // PART
+    wide = WIDE
+    base = skip // (wide * PART)
     half = LANES // 2
 
     def keep_spec(array, item):
@@ -655,20 +727,20 @@
             return whole(array.shape)
         return pl.BlockSpec((None,) + array.shape[1:], lambda n: (item, 0, 0))
 
-    right = pl.BlockSpec((rows, PART), lambda n: (0, n + base))
-    other = pl.BlockSpec((1, rows, PART), lambda n: (n + base + lead, 0, 0))
-    out = pl.BlockSpec((4, half, PART), lambda n: (0, 0, n))
+    right = pl.BlockSpec((rows, wide * PART), lambda n: (0, n + base))
+    other = pl.BlockSpec((wide, rows, PART), lambda n: (n + base + lead // wide, 0, 0))
+    out = pl.BlockSpec((4, half, wide * PART), lambda n: (0, 0, n))
     shape = jax.ShapeDtypeStruct((4, half, columns), F32)
     return pl.pallas_call(
         functools.partial(plain_grad_kernel, moves=moves),
-        grid=(columns // PART,),
+        grid=(columns // (wide * PART),),
         in_specs=[keep_spec(*k) for k in keeps]
         + [pl.BlockSpec((2, PART, rows), lambda n, q=i: (q, 0, 0)) for _, i in lefts]
         + [right, right, other, other],
         out_specs=[out, out],
         scratch_shapes=[pltpu.VMEM((half_width, 4 * rows), BF16)],
         out_shape=[shape, shape],
-        compiler_params=params(16),
+        compiler_params=params(14),
         cost_estimate=short_cost(),
         name=name,
     )(*[k for k, _ in keeps], *[v for v, _ in lefts], *rights, *others)
@@ -718,7 +790,7 @@
         out_specs=[out, out],
         scratch_shapes=[pltpu.VMEM((half_width, 4 * rows), BF16)],
         out_shape=[shape, shape],
-        compiler_params=params(24),
+        compiler_params=params(8),
         cost_estimate=short_cost(),
         name="attn_grad",
     )(*keep_a1, *keep_dya, *other_f, *other_b, *dqkv, *mix)
@@ -809,9 +881,9 @@
     qb, vb, ob, b1 = row(q_bias), row(v_bias), row(out_bias), row(fc1_bias)
     wqkv = jnp.transpose(w_qkv, (1, 0, 2))
 
-    source = lax.broadcasted_iota(jnp.int32, (wide, narrow), 0)
-    target = lax.broadcasted_iota(jnp.int32, (wide, narrow), 1)
-    pick = (source == (target // 3) * bands + target % 3).astype(BF16)
+    source = np.arange(wide)[:, None]
+    target = np.arange(narrow)[None, :]
+    pick = jnp.asarray((source == (target // 3) * bands + target % 3).astype(ml_dtypes.bfloat16))
 
     ratio = (gsd_codes.astype(F32) + 1.0) / 4.0
     quarter = width // 4
@@ -842,6 +914,9 @@
     def other(values):
         return exchange(values, "dp", 1, size) if custom else values
 
+    cut = rows * 3 // 8 // 8 * 8
+    cuts = [(cut, rows - cut)] + [(rows,)] * (items - 1)
+
     def settle(values):
         values = order.tie(values)
         order.mark(jax.tree.leaves(values)[0])
@@ -849,7 +924,7 @@
 
     none = [None] * items
     part, mixed, erecv, fwd, orecv, ffn, grecv, bwd, arecv, last, ycot = (list(none) for _ in range(11))
-    gmix, pk, gfwd, gact, gpre, gbwd, gdx0 = (list(none) for _ in range(7))
+    gmix, pk, gfwd, gact, gpre, gbwd, gdx0, da1, da2 = (list(none) for _ in range(9))
 
     for i in range(items):
         part[i], mixed[i] = embed(order.tie(item_kinds), pixels, w_spectral, w_rgb, pick, i, rows)
@@ -879,20 +954,23 @@
     x0, a1, qkv, mix, _ = zip(*fwd)
     for i in range(items):
         ffn[i] = mlp(
-            place, x0[i], fwd[i][4], orecv[i], order.tie(ob), g2, c2, w_fc1, b1, w_fc2, cotangent, i
+            place, x0[i], fwd[i][4], orecv[i], order.tie(ob), g2, c2, w_fc1, b1, w_fc2, cotangent, i,
+            cuts[i],
         )
-        order.mark(ffn[i][4])
+        da2[i] = ffn[i][8:]
+        order.mark(da2[i][0])
         if i == 0:
-            grecv[i] = send(ffn[i][4])
-        gact[i] = other(ffn[i][7])
-        gpre[i] = other(ffn[i][8])
+            grecv[i] = [send(v) for v in da2[i]]
+        gact[i] = other(ffn[i][6])
+        gpre[i] = other(ffn[i][7])
         if i == 0:
             gfwd = [settle(v) for v in gfwd]
         else:
+            grecv[0][0] = settle(grecv[0][0])
             gact[0], gpre[0] = settle((gact[0], gpre[0]))
             ycot[1] = mlp_out(order.tie(ffn[1][2]), w_fc2)
             order.mark(ycot[1])
-    x1, a2, act, dpre, _, b1sum, ka2 = list(zip(*ffn))[:7]
+    x1, a2, act, dpre, b1sum, ka2 = list(zip(*[v[:6] for v in ffn]))
     if custom:
         gact[1] = order.tie(gact[1])
         fc2_h = Halving(
@@ -910,33 +988,36 @@
             Z_FIRST, size,
         )
         order.mark(fc1_h.sent)
-    grecv[1] = send(order.tie(ffn[1][4]))
+    grecv[1] = [send(order.tie(da2[1][0]))]
     for i in range(items):
         bwd[i] = attn_backward(
-            place, ffn[i][4], grecv[i], x1[i], cotangent, order.tie(g2), w_out, qkv[i], wqkv, i
+            place, da2[i], grecv[i], x1[i], cotangent, order.tie(g2), w_out, qkv[i], wqkv, i, cuts[i]
         )
-        order.mark(bwd[i][3])
+        da1[i] = bwd[i][7:]
+        order.mark(da1[i][0])
         if i == 0:
-            arecv[i] = send(bwd[i][3])
-        if i == items - 1:
-            gbwd = [other(order.tie(bwd[0][7])), other(bwd[1][7])]
+            arecv[i] = [send(v) for v in da1[i]]
+        else:
+            arecv[0][0] = settle(arecv[0][0])
+            gbwd = [other(order.tie(bwd[0][6])), other(bwd[1][6])]
             ycot[0] = mlp_out(order.tie(ffn[0][2]), w_fc2)
             order.mark(ycot[0])
-    dx1, dya, dqkv, _, sums2, qvsum, kdya = list(zip(*bwd))[:7]
+    dx1, dya, dqkv, sums2, qvsum, kdya = list(zip(*[v[:6] for v in bwd]))
     if custom:
+        fc2_h.step(order)
         gbwd = [order.tie(v) for v in gbwd]
         att_h = Halving(
             *attn_grad([v[0] for v in pk], kdya, gfwd, gbwd, dqkv, mix, move_x), X_FIRST, size
         )
         order.mark(att_h.sent)
-    arecv[1] = send(order.tie(bwd[1][3]))
+        fc1_h.step(order)
+    arecv[1] = [send(order.tie(da1[1][0]))]
     for i in range(items):
-        last[i] = first_norm_back(place, bwd[i][3], arecv[i], x0[i], dx1[i], order.tie(g1))
+        estimate = long_cost() if i == 0 else short_cost()
+        last[i] = first_norm_back(place, da1[i], arecv[i], x0[i], dx1[i], order.tie(g1), estimate)
         order.mark(last[i][0])
-        gdx0[i] = other(last[i][3])
-        if custom and i == 0:
-            fc2_h.step(order)
-            fc1_h.step(order)
+    summed = list(none)
+    gdx0 = [other(order.tie(last[0][3])), other(last[1][3])]
     dx0, sums1, kdx0, _ = zip(*last)
     pixels_grad = pixel_grad(order.tie(item_kinds), dx0[0], dx0[1], w_spectral, w_rgb, pick)
     order.mark(pixels_grad)
@@ -950,8 +1031,10 @@
         embz_h = Halving(*plain_grad(*sides, move_z, "embed_grad_b", mid, mid), Z_FIRST, size)
         order.mark(embz_h.sent)
         fc2_h.step(order)
-
-    got = [send(order.tie(ycot[i])) for i in range(items)]
+    summed[0] = send(order.tie(ycot[0]))
+    if custom:
+        fc1_h.step(order)
+
     sums2, sums1, qvsum, b1sum = order.tie((sums2, sums1, qvsum, b1sum))
     vec2 = sums2[0] + sums2[1]
     vec1 = sums1[0] + sums1[1]
@@ -967,22 +1050,27 @@
         cube = jnp.transpose(cube, (2, 1, 0, 3, 4)).reshape(8, 2, 1, -1)
         kept = jnp.where(core == 0, cube[:, 0], cube[:, 1])
         gone = jnp.where(core == 0, cube[:, 1], cube[:, 0])
-        gone = exchange(gone, "dp", 1, size)
+        order.mark(gone)
         fc2_g = fc2_h.step(order)
+        embz_h.step(order)
+    summed[0] = settle(summed[0])
+    summed[1] = send(order.tie(ycot[1]))
+    if custom:
+        gone = exchange(order.tie(gone), "dp", 1, size)
+        fc1_g = fc1_h.step(order)
         gone = order.tie(gone)
         small_h = Halving(kept[:4] + gone[:4], kept[4:] + gone[4:], X_FIRST, size)
-        embz_h.step(order)
-        fc1_h.step(order)
-        small_h.step(order)
+        order.mark(small_h.sent)
         att_h.step(order)
         small_h.step(order)
+        embx_h.step(order)
+        summed[1] = settle(summed[1])
+        small_h.step(order)
         embz_h.step(order)
-        fc1_g = fc1_h.step(order)
         small = small_h.step(order)[0]
         att_h.step(order)
         embx_h.step(order)
         embz_g = embz_h.step(order)
-        embx_h.step(order)
         att_g = att_h.step(order)
         embx_g = embx_h.step(order)
         emb_g = jnp.concatenate([embx_g, embz_g], 1)
@@ -1005,7 +1093,7 @@
         out_grad = scatter(both(dya, mix)).T
         small = scatter(small)[0]
     block_out = jnp.concatenate(
-        [(x1[i] + (ycot[i] + got[i] + fc2_bias)).astype(BF16) for i in range(items)], 0
+        [(x1[i] + (ycot[i] + summed[i] + fc2_bias)).astype(BF16) for i in range(items)], 0
     )
     outs = []
     start = 0

time: 400 us -> 364 us (0.910)
  local copies, waits for them, and re-layouts: 39.7 us -> 11 us
  waiting for transfers between devices: 196 us -> 187 us
    unnamed x186 -> x98, local copies, waits for them, and re-layouts: 35 us -> 6.28 us
    ppermute x42 -> x44, waiting for transfers between devices: 196 us -> 187 us  [exchange(): return lax.ppermute(values, axis, [(i, i ^ bit) for i in range(size)])]
    pallas_call x4, Pallas kernels: 21.2 us -> 15.2 us  [plain_grad(): pl.pallas_call(functools.partial(plain_grad_kernel, moves=moves), grid=(c...]
    ppermute x42 -> x44, starting transfers between devices: 38.3 us -> 38.2 us  [exchange(): return lax.ppermute(values, axis, [(i, i ^ bit) for i in range(size)])]
  transfers between devices with their start and end apart: 42 -> 44, of which waited for: 17 -> 19; matrix products, arithmetic and copies ran while one was open for 7% -> 8% of each run, Pallas kernels for 24% -> 25%
where the time goes in v4:
time: 364 us; the launch traced here: 360 us
  waiting for transfers between devices  187 us (51%)
  Pallas kernels  95.1 us (26%)
  starting transfers between devices  38.2 us (10%)
  other arithmetic  26.4 us (7%)
  local copies, waits for them, and re-layouts  11 us (3%)
    ppermute x44, waiting for transfers between devices, exchange(): return lax.ppermute(values, axis, [(i, i ^ bit) for i in range(size)])  187 us
    ppermute x44, starting transfers between devices, exchange(): return lax.ppermute(values, axis, [(i, i ^ bit) for i in range(size)])  38.2 us
    add x17, other arithmetic, step(): value = value + recv[first:first + count]  21.6 us
    pallas_call x2, Pallas kernels, attn_backward(): pl.pallas_call(functools.partial(attn_backward_kernel, parts=(len(gparts)...  16.1 us
    pallas_call x4, Pallas kernels, plain_grad(): pl.pallas_call(functools.partial(plain_grad_kernel, moves=moves), grid=(c...  15.2 us
    pallas_call x2, Pallas kernels, mlp(): pl.pallas_call(mlp_kernel, grid_spec=pltpu.PrefetchScalarGridSpec(num_sca...  15 us
    pallas_call x2, Pallas kernels, attn_forward(): pl.pallas_call(attn_forward_kernel, grid=(steps,), in_specs=[whole(part.s...  9.81 us
    pallas_call x2, Pallas kernels, embed(): pl.pallas_call(functools.partial(embed_kernel, item=item), grid_spec=pltp...  9.62 us
  transfers between devices with their start and end apart: 44, of which 19 were waited for; matrix products, arithmetic and copies ran while one was open for 8% of the time, Pallas kernels for 25%

profile of v4, /device:TPU:0, one launch (start us, length us, event | category | flops | bytes accessed | tf_op | source)
XLA Modules:
  0.0 359.8 jit_solution(13426483151127052108)
XLA Ops:
  0.7 4.7 %embed.2 = (f32[256,1024]{1,0:T(8,128)}, bf16[256,2048]{1,0:T(8,128)(2,1)}) custom-call(s32[2]{0:T(128)} %kinds.3, bf16[512,1664]{1,0:T(8,128)(2,1)} %pix_ref.3, bf16[1664,1024]{1,0:T(8,128)(2,1)} %wspec_ref.5, bf16[384,1024]{1,0:T(8,128)(2,1)} %wrgb_ref.5, bf16[1664,384]{1,0:T(8,128)(2,1)} %constant.53.clone.pick_ref), custom_call_target="tpu_custom_call" | custom-call | flops 1000 | bytes 1000 | tf_op jit(solution)/shard_map/embed/pallas_call | solution.py:242
  5.4 3.0 collective-permute-start
  8.5 4.9 %embed.3 = (f32[256,1024]{1,0:T(8,128)}, bf16[256,2048]{1,0:T(8,128)(2,1)}) custom-call(s32[2]{0:T(128)} %kinds.3, bf16[512,1664]{1,0:T(8,128)(2,1)} %pix_ref.3, bf16[1664,1024]{1,0:T(8,128)(2,1)} %wspec_ref.5, bf16[384,1024]{1,0:T(8,128)(2,1)} %wrgb_ref.5, bf16[1664,384]{1,0:T(8,128)(2,1)} %constant.53.clone.pick_ref), custom_call_target="tpu_custom_call" | custom-call | flops 1000 | bytes 1000 | tf_op jit(solution)/shard_map/embed/pallas_call | solution.py:242
  13.4 1.9 turn_cotangent.1
  15.4 3.1 pack_pixels.2
  19.1 3.2 pack_pixels.3
  22.7 9.5 %collective-permute-done.recv_ref = f32[256,1024]{1,0:T(8,128)} collective-permute-done((f32[256,1024]{1,0:T(8,128)}, f32[256,1024]{1,0:T(8,128)}, u32[]{:S(2)}, u32[]{:S(2)}) %collective-permute-start) | collective-permute-done | bytes 1048608 | tf_op jit(solution)/shard_map/ppermute | solution.py:800
  32.2 1.7 collective-permute-start.1
  33.9 1.9 copy-done.30
  35.8 1.2 copy-done.35
  37.0 5.5 %attn_forward.2 = (f32[256,1024]{1,0:T(8,128)S(1)}, bf16[256,1024]{1,0:T(8,128)(2,1)S(1)}, bf16[3,256,512]{2,1,0:T(8,128)(2,1)S(1)}, bf16[256,512]{1,0:T(8,128)(2,1)S(1)}, f32[256,1024]{1,0:T(8,128)S(1)}) custom-call(f32[256,1024]{1,0:T(8,128)S(1)} %copy-done.35, f32[256,1024]{1,0:T(8,128)} %collective-permute-done.recv_ref, ...), custom_call_target="tpu_custom_call" | custom-call | flops 99999997952 | bytes 1000 | tf_op jit(solution)/shard_map/attn_forward/pallas_call | solution.py:330
  42.6 1.8 pack_attn.2
  44.4 12.7 %collective-permute-done.1.recv_ref = f32[256,1024]{1,0:T(8,128)S(1)} collective-permute-done((f32[256,1024]{1,0:T(8,128)}, f32[256,1024]{1,0:T(8,128)S(1)}, u32[]{:S(2)}, u32[]{:S(2)}) %collective-permute-start.1) | collective-permute-done | bytes 1048608 | tf_op jit(solution)/shard_map/ppermute | solution.py:800
  57.0 1.4 collective-permute-start.2
  58.5 4.3 %attn_forward.3 = (f32[256,1024]{1,0:T(8,128)S(1)}, bf16[256,1024]{1,0:T(8,128)(2,1)S(1)}, bf16[3,256,512]{2,1,0:T(8,128)(2,1)S(1)}, bf16[256,512]{1,0:T(8,128)(2,1)S(1)}, f32[256,1024]{1,0:T(8,128)S(1)}) custom-call(f32[256,1024]{1,0:T(8,128)S(1)} %copy-done.36, f32[256,1024]{1,0:T(8,128)S(1)} %collective-permute-done.1.recv_ref, ...), custom_call_target="tpu_custom_call" | custom-call | flops 99999997952 | bytes 1000 | tf_op jit(solution)/shard_map/attn_forward/pallas_call | solution.py:330
  63.8 17.0 %collective-permute-done.2.orecv_ref = f32[256,1024]{1,0:T(8,128)S(1)} collective-permute-done((f32[256,1024]{1,0:T(8,128)S(1)}, f32[256,1024]{1,0:T(8,128)S(1)}, u32[]{:S(2)}, u32[]{:S(2)}) %collective-permute-start.2) | collective-permute-done | bytes 1048608 | tf_op jit(solution)/shard_map/ppermute | solution.py:800
  81.9 7.5 %mlp.2 = (f32[256,1024]{1,0:T(8,128)S(1)}, bf16[256,1024]{1,0:T(8,128)(2,1)}, bf16[256,2048]{1,0:T(8,128)(2,1)S(1)}, bf16[256,2048]{1,0:T(8,128)(2,1)S(1)}, f32[...) custom-call(s32[9]{0:T(128)S(1)} %pad_add_fusion.place, ...), custom_call_target="tpu_custom_call" | custom-call | flops 99999997952 | bytes 1000 | tf_op jit(solution)/shard_map/mlp/pallas_call | solution.py:536
  91.0 13.1 %collective-permute-done.6.orecv_ref = f32[256,1024]{1,0:T(8,128)S(1)} collective-permute-done((f32[256,1024]{1,0:T(8,128)S(1)}, f32[256,1024]{1,0:T(8,128)S(1)}, u32[]{:S(2)}, u32[]{:S(2)}) %collective-permute-start.6) | collective-permute-done | bytes 1048608 | tf_op jit(solution)/shard_map/ppermute | solution.py:800
  105.2 7.5 %mlp.3 = (f32[256,1024]{1,0:T(8,128)S(1)}, bf16[256,1024]{1,0:T(8,128)(2,1)}, bf16[256,2048]{1,0:T(8,128)(2,1)S(1)}, bf16[256,2048]{1,0:T(8,128)(2,1)S(1)}, f32[...) custom-call(s32[9]{0:T(128)S(1)} %pad_add_fusion.place, ...), custom_call_target="tpu_custom_call" | custom-call | flops 99999997952 | bytes 1000 | tf_op jit(solution)/shard_map/mlp/pallas_call | solution.py:536
  114.2 1.8 mlp_out.2
  116.9 4.1 %fc2_grad.1 = (f32[4,64,2048]{2,1,0:T(8,128)}, f32[4,64,2048]{2,1,0:T(8,128)S(1)}) custom-call(bf16[2,512,256]{2,1,0:T(8,128)(2,1)S(1)} %get-tuple-element.212.ka_ref.kb_ref, bf16[2,512,256]{2,1,0:T(8,128)(2,1)S(1)} %get-tuple-element.212.ka_ref.kb_ref, f32[4,256,256]{2,1,0:T(8,128)S(1)} %collective-permute-done.3.la_ref.lb_ref, ...), custom_call_target="tpu_custom_call" | custom-call | flops 1000 | bytes 1000 | tf_op jit(solution)/shard_map/fc2_grad/pallas_call | solution.py:734
  120.9 1.5 collective-permute-start.18
  122.4 4.4 %fc1_grad.1 = (f32[4,64,2048]{2,1,0:T(8,128)}, f32[4,64,2048]{2,1,0:T(8,128)S(1)}) custom-call(bf16[512,256]{1,0:T(8,128)(2,1)S(1)} %get-tuple-element.206.ka_ref, bf16[512,256]{1,0:T(8,128)(2,1)S(1)} %get-tuple-element.207.kb_ref, f32[10,256,256]{2,1,0:T(8,128)S(1)} %collective-permute-done.12.la_ref.oa_ref, ...), custom_call_target="tpu_custom_call" | custom-call | flops 1000 | bytes 1000 | tf_op jit(solution)/shard_map/fc1_grad/pallas_call | solution.py:734
  127.8 2.1 collective-permute-done.10.refs_3_
  130.8 8.1 %attn_backward.2 = (f32[256,1024]{1,0:T(8,128)S(1)}, bf16[256,1024]{1,0:T(8,128)(2,1)}, bf16[3,256,512]{2,1,0:T(8,128)(2,1)S(1)}, f32[8,1024]{1,0:T(8,128)S(1)},...) custom-call(s32[9]{0:T(128)S(1)} %pad_add_fusion.place, ...), custom_call_target="tpu_custom_call" | custom-call | flops 99999997952 | bytes 1000 | tf_op jit(solution)/shard_map/attn_backward/pallas_call | solution.py:446
  138.9 15.3 %collective-permute-done.15.refs_1_ = f32[256,1024]{1,0:T(8,128)S(1)} collective-permute-done((f32[256,1024]{1,0:T(8,128)S(1)}, f32[256,1024]{1,0:T(8,128)S(1)}, u32[]{:S(2)}, u32[]{:S(2)}) %collective-permute-start.15) | collective-permute-done | bytes 1048608 | tf_op jit(solution)/shard_map/ppermute | solution.py:800
  155.1 8.0 %attn_backward.3 = (f32[256,1024]{1,0:T(8,128)S(1)}, bf16[256,1024]{1,0:T(8,128)(2,1)}, bf16[3,256,512]{2,1,0:T(8,128)(2,1)S(1)}, f32[8,1024]{1,0:T(8,128)S(1)},...) custom-call(s32[9]{0:T(128)S(1)} %pad_add_fusion.place, ...), custom_call_target="tpu_custom_call" | custom-call | flops 99999997952 | bytes 1000 | tf_op jit(solution)/shard_map/attn_backward/pallas_call | solution.py:446
  163.7 2.5 mlp_out.3
  167.3 1.7 collective-permute-done.18
  168.9 2.4 slice_add_fusion.2
  172.0 7.3 %attn_grad.1 = (f32[4,256,512]{2,1,0:T(8,128)}, f32[4,256,512]{2,1,0:T(8,128)S(1)}) custom-call(bf16[512,256]{1,0:T(8,128)(2,1)S(1)} %get-tuple-element.241.aa_ref, bf16[512,256]{1,0:T(8,128)(2,1)S(1)} %get-tuple-element.242.ab_ref, bf16[512,256]{1,0:T(8,128)(2,1)S(1)} %get-tuple-element.243.ya_ref, bf16[512,256]{1,0:T(8,128)(2,1)S(1)} %get-tuple-element.244.yb_ref, ...), custom_call_target="tpu_custom_call" | custom-call | flops 1000 | bytes 1000 | tf_op jit(solution)/shard_map/attn_grad/pallas_call | solution.py:784
  179.4 2.4 slice_add_fusion.1
  181.8 1.7 collective-permute-start.26
  184.4 1.7 first_norm_back.2
  186.0 22.1 %collective-permute-done.22.refs_1_ = f32[256,1024]{1,0:T(8,128)S(1)} collective-permute-done((f32[256,1024]{1,0:T(8,128)S(1)}, f32[256,1024]{1,0:T(8,128)S(1)}, u32[]{:S(2)}, u32[]{:S(2)}) %collective-permute-start.22) | collective-permute-done | bytes 1048608 | tf_op jit(solution)/shard_map/ppermute | solution.py:800
  208.2 1.7 first_norm_back.3
  210.4 3.6 %pixel_grad.1 = bf16[512,1664]{1,0:T(8,128)(2,1)} custom-call(s32[2]{0:T(128)S(1)} %copy-done.27, bf16[256,1024]{1,0:T(8,128)(2,1)S(1)} %get-tuple-element.261.da_ref, bf16[256,1024]{1,0:T(8,128)(2,1)S(1)} %get-tuple-element.264.db_ref, bf16[1664,1024]{1,0:T(8,128)(2,1)S(1)} %copy-done, bf16[384,1024]{1,0:T(8,128)(2,1)S(1)} %copy-done.6, ...), custom_call_target="tpu_custom_call" | custom-call | flops 99999997952 | bytes 1000 | tf_op jit(solution)/shard_map/pixel_grad/pallas_call | solution.py:663
  214.1 3.0 embed_grad_a.1
  219.1 3.7 %embed_grad_b.1 = (f32[4,64,1024]{2,1,0:T(8,128)}, f32[4,64,1024]{2,1,0:T(8,128)S(1)}) custom-call(bf16[512,256]{1,0:T(8,128)(2,1)S(1)} %get-tuple-element.257.ka_ref, bf16[512,256]{1,0:T(8,128)(2,1)S(1)} %get-tuple-element.263.kb_ref, f32[2,256,256]{2,1,0:T(8,128)S(1)} %collective-permute-done.23.la_ref, f32[2,256,256]{2,1,0:T(8,128)S(1)} %collective-permute-done.24.lb_ref, ...), custom_call_target="tpu_custom_call" | custom-call | flops 1000 | bytes 1000 | tf_op jit(solution)/shard_map/embed_grad_b/pallas_call | solution.py:734
  222.7 2.6 slice_add_fusion.7
  225.3 2.5 collective-permute-start.27
  227.8 1.5 collective-permute-start.28
  229.6 2.2 slice_add_fusion.6
  233.4 19.2 %collective-permute-done.27 = f32[1,64,2048]{2,1,0:T(8,128)} collective-permute-done((f32[1,64,2048]{2,1,0:T(8,128)}, f32[1,64,2048]{2,1,0:T(8,128)}, u32[]{:S(2)}, u32[]{:S(2)}) %collective-permute-start.27) | collective-permute-done | bytes 524320 | tf_op jit(solution)/shard_map/ppermute | solution.py:800
  252.6 1.3 collective-permute-start.34
  253.9 2.4 add_add_fusion.2
  256.3 18.5 %collective-permute-done.28 = f32[4,64,1024]{2,1,0:T(8,128)} collective-permute-done((f32[4,64,1024]{2,1,0:T(8,128)}, f32[4,64,1024]{2,1,0:T(8,128)}, u32[]{:S(2)}, u32[]{:S(2)}) %collective-permute-start.28) | collective-permute-done | bytes 1048608 | tf_op jit(solution)/shard_map/ppermute | solution.py:800
  275.9 1.6 collective-permute-start.37
  278.0 2.4 add_add_fusion.1
  280.4 1.1 collective-permute-start.33
  281.6 1.4 slice_add_fusion
  283.1 5.8 %collective-permute-done.33 = f32[4,1,576]{2,1,0:T(1,128)S(1)} collective-permute-done((f32[4,1,576]{2,1,0:T(1,128)S(1)}, f32[4,1,576]{2,1,0:T(1,128)S(1)}, u32[]{:S(2)}, u32[]{:S(2)}) %collective-permute-start.33) | collective-permute-done | bytes 9248 | tf_op jit(solution)/shard_map/ppermute | solution.py:800
  289.1 2.0 collective-permute-start.40
  291.1 10.2 %collective-permute-done.35 = f32[256,1024]{1,0:T(8,128)S(1)} collective-permute-done((f32[256,1024]{1,0:T(8,128)S(1)}, f32[256,1024]{1,0:T(8,128)S(1)}, u32[]{:S(2)}, u32[]{:S(2)}) %collective-permute-start.35) | collective-permute-done | bytes 1048608 | tf_op jit(solution)/shard_map/ppermute | solution.py:800
  301.4 7.8 %collective-permute-done.36 = f32[2,1,576]{2,1,0:T(1,128)S(1)} collective-permute-done((f32[2,1,576]{2,1,0:T(1,128)S(1)}, f32[2,1,576]{2,1,0:T(1,128)S(1)}, u32[]{:S(2)}, u32[]{:S(2)}) %collective-permute-start.36) | collective-permute-done | bytes 4640 | tf_op jit(solution)/shard_map/ppermute | solution.py:800
  310.2 3.0 collective-permute-start.41
  313.2 2.3 add_convert_fusion.1
  316.6 1.4 collective-permute-done.38
  319.8 1.2 slice_add_fusion.3
  320.9 3.4 collective-permute-start.42
  324.4 1.4 collective-permute-done.40
  327.6 25.7 %collective-permute-done.42 = f32[1,256,512]{2,1,0:T(8,128)S(1)} collective-permute-done((f32[1,256,512]{2,1,0:T(8,128)S(1)}, f32[1,256,512]{2,1,0:T(8,128)S(1)}, u32[]{:S(2)}, u32[]{:S(2)}) %collective-permute-start.42) | collective-permute-done | bytes 524320 | tf_op jit(solution)/shard_map/ppermute | solution.py:800
  353.2 1.3 add_add_fusion
  356.0 2.6 collective-permute-done.43
  (201 shorter events, 28.2 us)
Async XLA Ops:
  5.4 26.8 %collective-permute-start = (f32[256,1024]{1,0:T(8,128)}, f32[256,1024]{1,0:T(8,128)}, u32[]{:S(2)}, u32[]{:S(2)}) collective-permute-start(f32[256,1024]{1,0:T(8,128)} %get-tuple-element.167.part_ref), channel_id=1, source_target_pairs={{0,1},{1,0},{2,3},{3,2},{4,5},{5,4},{6,7},{7,6},{8,9},{9,8},{10,11... | collective-permute-start | bytes 3145736 | tf_op jit(solution)/shard_map/ppermute | solution.py:800
  15.3 27.2 %collective-permute-start.3 = (f32[4,256,256]{2,1,0:T(8,128)}, f32[4,256,256]{2,1,0:T(8,128)S(1)}, u32[]{:S(2)}, u32[]{:S(2)}) collective-permute-start(f32[4,256,256]{2,1,0:T(8,128)} %get-tuple-element.171), channel_id=1, source_target_pairs={{0,2},{2,0},{4,6},{6,4},{8,10},{10,8},{12,14},{14,12},{16,18},{18,... | collective-permute-start | bytes 3145736 | tf_op jit(solution)/shard_map/ppermute | solution.py:800
  18.6 44.3 %collective-permute-start.4 = (f32[8,256,256]{2,1,0:T(8,128)}, f32[8,256,256]{2,1,0:T(8,128)}, u32[]{:S(2)}, u32[]{:S(2)}) collective-permute-start(f32[8,256,256]{2,1,0:T(8,128)} %pack_pixels.2), channel_id=1, source_target_pairs={{0,2},{2,0},{4,6},{6,4},{8,10},{10,8},{12,14},{14,12},{16,18},{18,... | collective-permute-start | bytes 6291464 | tf_op jit(solution)/shard_map/ppermute | solution.py:800
  22.2 40.6 %collective-permute-start.5 = (f32[8,256,256]{2,1,0:T(8,128)}, f32[8,256,256]{2,1,0:T(8,128)}, u32[]{:S(2)}, u32[]{:S(2)}) collective-permute-start(f32[8,256,256]{2,1,0:T(8,128)} %pack_pixels.3), channel_id=1, source_target_pairs={{0,2},{2,0},{4,6},{6,4},{8,10},{10,8},{12,14},{14,12},{16,18},{18,... | collective-permute-start | bytes 6291464 | tf_op jit(solution)/shard_map/ppermute | solution.py:800
  32.2 24.9 %collective-permute-start.1 = (f32[256,1024]{1,0:T(8,128)}, f32[256,1024]{1,0:T(8,128)S(1)}, u32[]{:S(2)}, u32[]{:S(2)}) collective-permute-start(f32[256,1024]{1,0:T(8,128)} %get-tuple-element.179.part_ref), channel_id=1, source_target_pairs={{0,1},{1,0},{2,3},{3,2},{4,5},{5,4},{6,7},{7,6},{8,9},{9,8},{10,11... | collective-permute-start | bytes 3145736 | tf_op jit(solution)/shard_map/ppermute | solution.py:800
  37.0 21.4 %copy-start.36 = (f32[256,1024]{1,0:T(8,128)S(1)}, f32[256,1024]{1,0:T(8,128)}, u32[]{:S(2)}) copy-start(f32[256,1024]{1,0:T(8,128)} %get-tuple-element.179.part_ref) | copy-start | bytes 3145732
  42.5 15.9 %copy-start.21 = (bf16[256,512]{1,0:T(8,128)(2,1)}, bf16[256,512]{1,0:T(8,128)(2,1)S(1)}, u32[]{:S(2)}) copy-start(bf16[256,512]{1,0:T(8,128)(2,1)S(1)} %get-tuple-element.184.o_ref.ma_ref) | copy-start | bytes 786436
  42.5 39.3 %copy-start.44 = (f32[256,1024]{1,0:T(8,128)}, f32[256,1024]{1,0:T(8,128)S(1)}, u32[]{:S(2)}) copy-start(f32[256,1024]{1,0:T(8,128)S(1)} %get-tuple-element.177.x0_ref.refs_4_) | copy-start | bytes 3145732
  44.4 45.1 %collective-permute-start.7 = (f32[4,256,256]{2,1,0:T(8,128)}, f32[4,256,256]{2,1,0:T(8,128)}, u32[]{:S(2)}, u32[]{:S(2)}) collective-permute-start(f32[4,256,256]{2,1,0:T(8,128)} %get-tuple-element.185), channel_id=1, source_target_pairs={{0,2},{2,0},{4,6},{6,4},{8,10},{10,8},{12,14},{14,12},{16,18},{18,... | collective-permute-start | bytes 3145736 | tf_op jit(solution)/shard_map/ppermute | solution.py:800
  57.0 23.7 %collective-permute-start.2 = (f32[256,1024]{1,0:T(8,128)S(1)}, f32[256,1024]{1,0:T(8,128)S(1)}, u32[]{:S(2)}, u32[]{:S(2)}) collective-permute-start(f32[256,1024]{1,0:T(8,128)S(1)} %get-tuple-element.180.opart_ref), channel_id=1, source_target_pairs={{0,1},{1,0},{2,3},{3,2},{4,5},{5,4},{6,7},{7,6},{8,9},{9,8},{10,11... | collective-permute-start | bytes 3145736 | tf_op jit(solution)/shard_map/ppermute | solution.py:800
  58.5 23.4 %copy-start.20 = (bf16[512,1024]{1,0:T(8,128)(2,1)S(1)}, bf16[512,1024]{1,0:T(8,128)(2,1)}, u32[]{:S(2)}) copy-start(bf16[512,1024]{1,0:T(8,128)(2,1)} %refs_3_.1) | copy-start | bytes 3145732
  58.5 23.4 %copy-start.28 = (bf16[1024,2048]{1,0:T(8,128)(2,1)S(1)}, bf16[1024,2048]{1,0:T(8,128)(2,1)}, u32[]{:S(2)}) copy-start(bf16[1024,2048]{1,0:T(8,128)(2,1)} %wfc1_ref.3) | copy-start | bytes 12582916
  58.5 23.4 %copy-start.29 = (bf16[2048,1024]{1,0:T(8,128)(2,1)S(1)}, bf16[2048,1024]{1,0:T(8,128)(2,1)}, u32[]{:S(2)}) copy-start(bf16[2048,1024]{1,0:T(8,128)(2,1)} %wfc2_ref.7) | copy-start | bytes 12582916
  58.5 23.4 %copy-start.37 = (f32[2048]{0:T(1024)S(1)}, f32[2048]{0:T(1024)}, u32[]{:S(2)}) copy-start(f32[2048]{0:T(1024)} %param.36) | copy-start | bytes 24580
  58.5 23.4 %copy-start.39 = (f32[1024]{0:T(1024)S(1)}, f32[1024]{0:T(1024)}, u32[]{:S(2)}) copy-start(f32[1024]{0:T(1024)} %param.32) | copy-start | bytes 12292
  58.5 23.4 %copy-start.40 = (f32[1024]{0:T(1024)S(1)}, f32[1024]{0:T(1024)}, u32[]{:S(2)}) copy-start(f32[1024]{0:T(1024)} %param.34) | copy-start | bytes 12292
  58.5 23.4 %copy-start.41 = (f32[1024]{0:T(1024)S(1)}, f32[1024]{0:T(1024)}, u32[]{:S(2)}) copy-start(f32[1024]{0:T(1024)} %param.33) | copy-start | bytes 12292
  62.9 19.0 %copy-start.23 = (bf16[256,512]{1,0:T(8,128)(2,1)}, bf16[256,512]{1,0:T(8,128)(2,1)S(1)}, u32[]{:S(2)}) copy-start(bf16[256,512]{1,0:T(8,128)(2,1)S(1)} %get-tuple-element.192.o_ref.mb_ref) | copy-start | bytes 786436
  63.7 25.8 %collective-permute-start.8 = (f32[4,256,256]{2,1,0:T(8,128)S(1)}, f32[4,256,256]{2,1,0:T(8,128)S(1)}, u32[]{:S(2)}, u32[]{:S(2)}) collective-permute-start(f32[4,256,256]{2,1,0:T(8,128)S(1)} %get-tuple-element.193), channel_id=1, source_target_pairs={{0,2},{2,0},{4,6},{6,4},{8,10},{10,8},{12,14},{14,12},{16,18},{18,... | collective-permute-start | bytes 3145736 | tf_op jit(solution)/shard_map/ppermute | solution.py:800
  80.8 23.3 %collective-permute-start.6 = (f32[256,1024]{1,0:T(8,128)S(1)}, f32[256,1024]{1,0:T(8,128)S(1)}, u32[]{:S(2)}, u32[]{:S(2)}) collective-permute-start(f32[256,1024]{1,0:T(8,128)S(1)} %get-tuple-element.197.opart_ref), channel_id=1, source_target_pairs={{0,1},{1,0},{2,3},{3,2},{4,5},{5,4},{6,7},{7,6},{8,9},{9,8},{10,11... | collective-permute-start | bytes 3145736 | tf_op jit(solution)/shard_map/ppermute | solution.py:800
  89.5 41.3 %copy-start.9 = (f32[256,1024]{1,0:T(8,128)}, f32[256,1024]{1,0:T(8,128)S(1)}, u32[]{:S(2)}) copy-start(f32[256,1024]{1,0:T(8,128)S(1)} %get-tuple-element.195.refs_4_) | copy-start | bytes 3145732
  90.5 23.7 %collective-permute-start.12 = (f32[10,256,256]{2,1,0:T(8,128)S(1)}, f32[10,256,256]{2,1,0:T(8,128)S(1)}, u32[]{:S(2)}, u32[]{:S(2)}) collective-permute-start(f32[10,256,256]{2,1,0:T(8,128)S(1)} %get-tuple-element.210), channel_id=1, source_target_pairs={{0,2},{2,0},{4,6},{6,4},{8,10},{10,8},{12,14},{14,12},{16,18},{18,... | collective-permute-start | bytes 7864328 | tf_op jit(solution)/shard_map/ppermute | solution.py:800
  90.5 23.7 %collective-permute-start.11 = (f32[8,256,256]{2,1,0:T(8,128)S(1)}, f32[8,256,256]{2,1,0:T(8,128)S(1)}, u32[]{:S(2)}, u32[]{:S(2)}) collective-permute-start(f32[8,256,256]{2,1,0:T(8,128)S(1)} %get-tuple-element.209), channel_id=1, source_target_pairs={{0,2},{2,0},{4,6},{6,4},{8,10},{10,8},{12,14},{14,12},{16,18},{18,... | collective-permute-start | bytes 6291464 | tf_op jit(solution)/shard_map/ppermute | solution.py:800
  104.1 9.1 %collective-permute-start.9 = (f32[96,1024]{1,0:T(8,128)S(1)}, f32[96,1024]{1,0:T(8,128)S(1)}, u32[]{:S(2)}, u32[]{:S(2)}) collective-permute-start(f32[96,1024]{1,0:T(8,128)S(1)} %get-tuple-element.203.refs_0_), channel_id=1, source_target_pairs={{0,1},{1,0},{2,3},{3,2},{4,5},{5,4},{6,7},{7,6},{8,9},{9,8},{10,11... | collective-permute-start | bytes 1179656 | tf_op jit(solution)/shard_map/ppermute | solution.py:800
  112.7 42.4 %copy-start.11 = (f32[256,1024]{1,0:T(8,128)}, f32[256,1024]{1,0:T(8,128)S(1)}, u32[]{:S(2)}) copy-start(f32[256,1024]{1,0:T(8,128)S(1)} %get-tuple-element.227.refs_2_) | copy-start | bytes 3145732
  112.7 4.2 %collective-permute-start.13 = (f32[8,256,256]{2,1,0:T(8,128)S(1)}, f32[8,256,256]{2,1,0:T(8,128)S(1)}, u32[]{:S(2)}, u32[]{:S(2)}) collective-permute-start(f32[8,256,256]{2,1,0:T(8,128)S(1)} %get-tuple-element.217), channel_id=1, source_target_pairs={{0,2},{2,0},{4,6},{6,4},{8,10},{10,8},{12,14},{14,12},{16,18},{18,... | collective-permute-start | bytes 6291464 | tf_op jit(solution)/shard_map/ppermute | solution.py:800
  112.7 9.7 %collective-permute-start.14 = (f32[10,256,256]{2,1,0:T(8,128)S(1)}, f32[10,256,256]{2,1,0:T(8,128)S(1)}, u32[]{:S(2)}, u32[]{:S(2)}) collective-permute-start(f32[10,256,256]{2,1,0:T(8,128)S(1)} %get-tuple-element.220), channel_id=1, source_target_pairs={{0,2},{2,0},{4,6},{6,4},{8,10},{10,8},{12,14},{14,12},{16,18},{18,... | collective-permute-start | bytes 7864328 | tf_op jit(solution)/shard_map/ppermute | solution.py:800
  113.2 16.6 %collective-permute-start.10 = (f32[160,1024]{1,0:T(8,128)S(1)}, f32[160,1024]{1,0:T(8,128)S(1)}, u32[]{:S(2)}, u32[]{:S(2)}) collective-permute-start(f32[160,1024]{1,0:T(8,128)S(1)} %get-tuple-element.205.refs_1_), channel_id=1, source_target_pairs={{0,1},{1,0},{2,3},{3,2},{4,5},{5,4},{6,7},{7,6},{8,9},{9,8},{10,11... | collective-permute-start | bytes 1966088 | tf_op jit(solution)/shard_map/ppermute | solution.py:800
  120.9 48.0 %copy-start.8 = (f32[4,64,2048]{2,1,0:T(8,128)}, f32[4,64,2048]{2,1,0:T(8,128)S(1)}, u32[]{:S(2)}) copy-start(f32[4,64,2048]{2,1,0:T(8,128)S(1)} %get-tuple-element.245) | copy-start | bytes 6291460
  120.9 48.0 %collective-permute-start.18 = (f32[4,64,2048]{2,1,0:T(8,128)}, f32[4,64,2048]{2,1,0:T(8,128)}, u32[]{:S(2)}, u32[]{:S(2)}) collective-permute-start(f32[4,64,2048]{2,1,0:T(8,128)} %get-tuple-element.219), channel_id=1, source_target_pairs={{0,4},{2,6},{4,0},{6,2},{8,12},{10,14},{12,8},{14,10},{16,20},{18,... | collective-permute-start | bytes 6291464 | tf_op jit(solution)/shard_map/ppermute | solution.py:800
  126.8 52.6 %copy-start.7 = (f32[4,64,2048]{2,1,0:T(8,128)}, f32[4,64,2048]{2,1,0:T(8,128)S(1)}, u32[]{:S(2)}) copy-start(f32[4,64,2048]{2,1,0:T(8,128)S(1)} %get-tuple-element.240) | copy-start | bytes 6291460
  126.8 52.5 %collective-permute-start.21 = (f32[4,64,2048]{2,1,0:T(8,128)}, f32[4,64,2048]{2,1,0:T(8,128)}, u32[]{:S(2)}, u32[]{:S(2)}) collective-permute-start(f32[4,64,2048]{2,1,0:T(8,128)} %get-tuple-element.224), channel_id=1, source_target_pairs={{0,8},{2,10},{4,12},{6,14},{8,0},{10,2},{12,4},{14,6},{16,24},{18,... | collective-permute-start | bytes 6291464 | tf_op jit(solution)/shard_map/ppermute | solution.py:800
  129.9 24.3 %collective-permute-start.15 = (f32[256,1024]{1,0:T(8,128)S(1)}, f32[256,1024]{1,0:T(8,128)S(1)}, u32[]{:S(2)}, u32[]{:S(2)}) collective-permute-start(f32[256,1024]{1,0:T(8,128)S(1)} %get-tuple-element.226.refs_0_), channel_id=1, source_target_pairs={{0,1},{1,0},{2,3},{3,2},{4,5},{5,4},{6,7},{7,6},{8,9},{9,8},{10,11... | collective-permute-start | bytes 3145736 | tf_op jit(solution)/shard_map/ppermute | solution.py:800
  154.2 9.5 %collective-permute-start.16 = (f32[96,1024]{1,0:T(8,128)S(1)}, f32[96,1024]{1,0:T(8,128)S(1)}, u32[]{:S(2)}, u32[]{:S(2)}) collective-permute-start(f32[96,1024]{1,0:T(8,128)S(1)} %get-tuple-element.234.refs_0_), channel_id=1, source_target_pairs={{0,1},{1,0},{2,3},{3,2},{4,5},{5,4},{6,7},{7,6},{8,9},{9,8},{10,11... | collective-permute-start | bytes 1179656 | tf_op jit(solution)/shard_map/ppermute | solution.py:800
  163.2 8.8 %collective-permute-start.20 = (f32[8,256,256]{2,1,0:T(8,128)S(1)}, f32[8,256,256]{2,1,0:T(8,128)S(1)}, u32[]{:S(2)}, u32[]{:S(2)}) collective-permute-start(f32[8,256,256]{2,1,0:T(8,128)S(1)} %get-tuple-element.250), channel_id=1, source_target_pairs={{0,2},{2,0},{4,6},{6,4},{8,10},{10,8},{12,14},{14,12},{16,18},{18,... | collective-permute-start | bytes 6291464 | tf_op jit(solution)/shard_map/ppermute | solution.py:800
  163.6 8.4 %collective-permute-start.19 = (f32[8,256,256]{2,1,0:T(8,128)S(1)}, f32[8,256,256]{2,1,0:T(8,128)S(1)}, u32[]{:S(2)}, u32[]{:S(2)}) collective-permute-start(f32[8,256,256]{2,1,0:T(8,128)S(1)} %get-tuple-element.248), channel_id=1, source_target_pairs={{0,2},{2,0},{4,6},{6,4},{8,10},{10,8},{12,14},{14,12},{16,18},{18,... | collective-permute-start | bytes 6291464 | tf_op jit(solution)/shard_map/ppermute | solution.py:800
  166.2 17.7 %collective-permute-start.17 = (f32[160,1024]{1,0:T(8,128)S(1)}, f32[160,1024]{1,0:T(8,128)S(1)}, u32[]{:S(2)}, u32[]{:S(2)}) collective-permute-start(f32[160,1024]{1,0:T(8,128)S(1)} %get-tuple-element.238.refs_1_), channel_id=1, source_target_pairs={{0,1},{1,0},{2,3},{3,2},{4,5},{5,4},{6,7},{7,6},{8,9},{9,8},{10,11... | collective-permute-start | bytes 1966088 | tf_op jit(solution)/shard_map/ppermute | solution.py:800
  171.3 51.4 %collective-permute-start.25 = (f32[2,64,2048]{2,1,0:T(8,128)}, f32[2,64,2048]{2,1,0:T(8,128)}, u32[]{:S(2)}, u32[]{:S(2)}) collective-permute-start(f32[2,64,2048]{2,1,0:T(8,128)} %slice_add_fusion.2), channel_id=1, source_target_pairs={{0,8},{2,10},{4,12},{6,14},{8,0},{10,2},{12,4},{14,6},{16,24},{18,... | collective-permute-start | bytes 3145736 | tf_op jit(solution)/shard_map/ppermute | solution.py:800
  181.8 47.8 %collective-permute-start.26 = (f32[2,64,2048]{2,1,0:T(8,128)}, f32[2,64,2048]{2,1,0:T(8,128)}, u32[]{:S(2)}, u32[]{:S(2)}) collective-permute-start(f32[2,64,2048]{2,1,0:T(8,128)} %slice_add_fusion.1), channel_id=1, source_target_pairs={{0,4},{2,6},{4,0},{6,2},{8,12},{10,14},{12,8},{14,10},{16,20},{18,... | collective-permute-start | bytes 3145736 | tf_op jit(solution)/shard_map/ppermute | solution.py:800
  183.6 98.0 %collective-permute-start.32 = (f32[4,256,512]{2,1,0:T(8,128)}, f32[4,256,512]{2,1,0:T(8,128)}, u32[]{:S(2)}, u32[]{:S(2)}) collective-permute-start(f32[4,256,512]{2,1,0:T(8,128)} %get-tuple-element.254), channel_id=1, source_target_pairs={{0,4},{2,6},{4,0},{6,2},{8,12},{10,14},{12,8},{14,10},{16,20},{18,... | collective-permute-start | bytes 6291464 | tf_op jit(solution)/shard_map/ppermute | solution.py:800
  183.9 24.3 %collective-permute-start.22 = (f32[256,1024]{1,0:T(8,128)S(1)}, f32[256,1024]{1,0:T(8,128)S(1)}, u32[]{:S(2)}, u32[]{:S(2)}) collective-permute-start(f32[256,1024]{1,0:T(8,128)S(1)} %get-tuple-element.259.refs_0_), channel_id=1, source_target_pairs={{0,1},{1,0},{2,3},{3,2},{4,5},{5,4},{6,7},{7,6},{8,9},{9,8},{10,11... | collective-permute-start | bytes 3145736 | tf_op jit(solution)/shard_map/ppermute | solution.py:800
  184.4 26.0 %copy-start.5 = (bf16[1664,384]{1,0:T(8,128)(2,1)S(1)}, bf16[1664,384]{1,0:T(8,128)(2,1)}, u32[]{:S(2)}) copy-start(bf16[1664,384]{1,0:T(8,128)(2,1)} %constant.53.clone.pick_ref) | copy-start | bytes 3833860
  209.8 4.2 %collective-permute-start.24 = (f32[2,256,256]{2,1,0:T(8,128)S(1)}, f32[2,256,256]{2,1,0:T(8,128)S(1)}, u32[]{:S(2)}, u32[]{:S(2)}) collective-permute-start(f32[2,256,256]{2,1,0:T(8,128)S(1)} %get-tuple-element.269), channel_id=1, source_target_pairs={{0,2},{2,0},{4,6},{6,4},{8,10},{10,8},{12,14},{14,12},{16,18},{18,... | collective-permute-start | bytes 1572872 | tf_op jit(solution)/shard_map/ppermute | solution.py:800
  209.9 4.1 %collective-permute-start.23 = (f32[2,256,256]{2,1,0:T(8,128)S(1)}, f32[2,256,256]{2,1,0:T(8,128)S(1)}, u32[]{:S(2)}, u32[]{:S(2)}) collective-permute-start(f32[2,256,256]{2,1,0:T(8,128)S(1)} %get-tuple-element.267), channel_id=1, source_target_pairs={{0,2},{2,0},{4,6},{6,4},{8,10},{10,8},{12,14},{14,12},{16,18},{18,... | collective-permute-start | bytes 1572872 | tf_op jit(solution)/shard_map/ppermute | solution.py:800
  225.3 27.3 %collective-permute-start.27 = (f32[1,64,2048]{2,1,0:T(8,128)}, f32[1,64,2048]{2,1,0:T(8,128)}, u32[]{:S(2)}, u32[]{:S(2)}) collective-permute-start(f32[1,64,2048]{2,1,0:T(8,128)} %slice_add_fusion.7), channel_id=1, source_target_pairs={{0,16},{2,18},{4,20},{6,22},{8,24},{10,26},{12,28},{14,30},{16,0},... | collective-permute-start | bytes 1572872 | tf_op jit(solution)/shard_map/ppermute | solution.py:800
  227.8 46.9 %collective-permute-start.28 = (f32[4,64,1024]{2,1,0:T(8,128)}, f32[4,64,1024]{2,1,0:T(8,128)}, u32[]{:S(2)}, u32[]{:S(2)}) collective-permute-start(f32[4,64,1024]{2,1,0:T(8,128)} %get-tuple-element.274), channel_id=1, source_target_pairs={{0,8},{2,10},{4,12},{6,14},{8,0},{10,2},{12,4},{14,6},{16,24},{18,... | collective-permute-start | bytes 3145736 | tf_op jit(solution)/shard_map/ppermute | solution.py:800
  229.3 46.6 %collective-permute-start.29 = (f32[256,1024]{1,0:T(8,128)}, f32[256,1024]{1,0:T(8,128)}, u32[]{:S(2)}, u32[]{:S(2)}) collective-permute-start(f32[256,1024]{1,0:T(8,128)} %mlp_out.3), channel_id=1, source_target_pairs={{0,1},{1,0},{2,3},{3,2},{4,5},{5,4},{6,7},{7,6},{8,9},{9,8},{10,11... | collective-permute-start | bytes 3145736 | tf_op jit(solution)/shard_map/ppermute | solution.py:800
  231.8 46.1 %collective-permute-start.30 = (f32[1,64,2048]{2,1,0:T(8,128)}, f32[1,64,2048]{2,1,0:T(8,128)}, u32[]{:S(2)}, u32[]{:S(2)}) collective-permute-start(f32[1,64,2048]{2,1,0:T(8,128)} %slice_add_fusion.6), channel_id=1, source_target_pairs={{0,16},{2,18},{4,20},{6,22},{8,24},{10,26},{12,28},{14,30},{16,0},... | collective-permute-start | bytes 1572872 | tf_op jit(solution)/shard_map/ppermute | solution.py:800
  233.3 41.5 %copy-start.18 = (f32[4,64,1024]{2,1,0:T(8,128)S(1)}, f32[4,64,1024]{2,1,0:T(8,128)}, u32[]{:S(2)}) copy-start(f32[4,64,1024]{2,1,0:T(8,128)} %copy-done.17) | copy-start | bytes 3145732
  252.6 36.4 %collective-permute-start.34 = (f32[4,64,1024]{2,1,0:T(8,128)}, f32[4,64,1024]{2,1,0:T(8,128)S(1)}, u32[]{:S(2)}, u32[]{:S(2)}) collective-permute-start(f32[4,64,1024]{2,1,0:T(8,128)} %copy-done.34), channel_id=1, source_target_pairs={{0,4},{2,6},{4,0},{6,2},{8,12},{10,14},{12,8},{14,10},{16,20},{18,... | collective-permute-start | bytes 3145736 | tf_op jit(solution)/shard_map/ppermute | solution.py:800
  275.9 33.3 %collective-permute-start.37 = (f32[2,64,1024]{2,1,0:T(8,128)S(1)}, f32[2,64,1024]{2,1,0:T(8,128)S(1)}, u32[]{:S(2)}, u32[]{:S(2)}) collective-permute-start(f32[2,64,1024]{2,1,0:T(8,128)S(1)} %slice_add_fusion.5), channel_id=1, source_target_pairs={{0,4},{2,6},{4,0},{6,2},{8,12},{10,14},{12,8},{14,10},{16,20},{18,... | collective-permute-start | bytes 1572872 | tf_op jit(solution)/shard_map/ppermute | solution.py:800
  277.5 23.9 %collective-permute-start.35 = (f32[256,1024]{1,0:T(8,128)S(1)}, f32[256,1024]{1,0:T(8,128)S(1)}, u32[]{:S(2)}, u32[]{:S(2)}) collective-permute-start(f32[256,1024]{1,0:T(8,128)S(1)} %mlp_out.2), channel_id=1, source_target_pairs={{0,1},{1,0},{2,3},{3,2},{4,5},{5,4},{6,7},{7,6},{8,9},{9,8},{10,11... | collective-permute-start | bytes 3145736 | tf_op jit(solution)/shard_map/ppermute | solution.py:800
  278.0 2.4 collective-permute-start.31
  280.4 8.5 %collective-permute-start.33 = (f32[4,1,576]{2,1,0:T(1,128)S(1)}, f32[4,1,576]{2,1,0:T(1,128)S(1)}, u32[]{:S(2)}, u32[]{:S(2)}) collective-permute-start(f32[4,1,576]{2,1,0:T(1,128)S(1)} %get-tuple-element.327), channel_id=1, source_target_pairs={{0,4},{2,6},{4,0},{6,2},{8,12},{10,14},{12,8},{14,10},{16,20},{18,... | collective-permute-start | bytes 27656 | tf_op jit(solution)/shard_map/ppermute | solution.py:800
  283.0 30.2 %copy-start.10 = (f32[256,1024]{1,0:T(8,128)S(1)}, f32[256,1024]{1,0:T(8,128)}, u32[]{:S(2)}) copy-start(f32[256,1024]{1,0:T(8,128)} %copy-done.9) | copy-start | bytes 3145732
  283.0 30.2 %copy-start.12 = (f32[256,1024]{1,0:T(8,128)S(1)}, f32[256,1024]{1,0:T(8,128)}, u32[]{:S(2)}) copy-start(f32[256,1024]{1,0:T(8,128)} %copy-done.11) | copy-start | bytes 3145732
  283.0 30.2 %copy-start.46 = (f32[1024]{0:T(1024)S(1)}, f32[1024]{0:T(1024)}, u32[]{:S(2)}) copy-start(f32[1024]{0:T(1024)} %param.38) | copy-start | bytes 12292
  283.0 36.7 %collective-permute-start.39 = (f32[2,256,512]{2,1,0:T(8,128)S(1)}, f32[2,256,512]{2,1,0:T(8,128)S(1)}, u32[]{:S(2)}, u32[]{:S(2)}) collective-permute-start(f32[2,256,512]{2,1,0:T(8,128)S(1)} %slice_add_fusion), channel_id=1, source_target_pairs={{0,8},{2,10},{4,12},{6,14},{8,0},{10,2},{12,4},{14,6},{16,24},{18,... | collective-permute-start | bytes 3145736 | tf_op jit(solution)/shard_map/ppermute | solution.py:800
  288.9 20.3 %collective-permute-start.36 = (f32[2,1,576]{2,1,0:T(1,128)S(1)}, f32[2,1,576]{2,1,0:T(1,128)S(1)}, u32[]{:S(2)}, u32[]{:S(2)}) collective-permute-start(f32[2,1,576]{2,1,0:T(1,128)S(1)} %slice_add_fusion.10), channel_id=1, source_target_pairs={{0,8},{2,10},{4,12},{6,14},{8,0},{10,2},{12,4},{14,6},{16,24},{18,... | collective-permute-start | bytes 13832 | tf_op jit(solution)/shard_map/ppermute | solution.py:800
  289.1 36.6 %collective-permute-start.40 = (f32[2,64,1024]{2,1,0:T(8,128)S(1)}, f32[2,64,1024]{2,1,0:T(8,128)S(1)}, u32[]{:S(2)}, u32[]{:S(2)}) collective-permute-start(f32[2,64,1024]{2,1,0:T(8,128)S(1)} %slice_add_fusion.4), channel_id=1, source_target_pairs={{0,8},{2,10},{4,12},{6,14},{8,0},{10,2},{12,4},{14,6},{16,24},{18,... | collective-permute-start | bytes 1572872 | tf_op jit(solution)/shard_map/ppermute | solution.py:800
  309.2 8.8 %collective-permute-start.38 = (f32[1,1,576]{2,1,0:T(1,128)S(1)}, f32[1,1,576]{2,1,0:T(1,128)S(1)}, u32[]{:S(2)}, u32[]{:S(2)}) collective-permute-start(f32[1,1,576]{2,1,0:T(1,128)S(1)} %fusion.8), channel_id=1, source_target_pairs={{0,16},{2,18},{4,20},{6,22},{8,24},{10,26},{12,28},{14,30},{16,0},... | collective-permute-start | bytes 6920 | tf_op jit(solution)/shard_map/ppermute | solution.py:800
  310.2 15.6 %collective-permute-start.41 = (f32[1,64,1024]{2,1,0:T(8,128)S(1)}, f32[1,64,1024]{2,1,0:T(8,128)S(1)}, u32[]{:S(2)}, u32[]{:S(2)}) collective-permute-start(f32[1,64,1024]{2,1,0:T(8,128)S(1)} %slice_add_fusion.9), channel_id=1, source_target_pairs={{0,16},{2,18},{4,20},{6,22},{8,24},{10,26},{12,28},{14,30},{16,0},... | collective-permute-start | bytes 786440 | tf_op jit(solution)/shard_map/ppermute | solution.py:800
  320.9 32.3 %collective-permute-start.42 = (f32[1,256,512]{2,1,0:T(8,128)S(1)}, f32[1,256,512]{2,1,0:T(8,128)S(1)}, u32[]{:S(2)}, u32[]{:S(2)}) collective-permute-start(f32[1,256,512]{2,1,0:T(8,128)S(1)} %slice_add_fusion.3), channel_id=1, source_target_pairs={{0,16},{2,18},{4,20},{6,22},{8,24},{10,26},{12,28},{14,30},{16,0},... | collective-permute-start | bytes 1572872 | tf_op jit(solution)/shard_map/ppermute | solution.py:800
  325.8 32.7 %collective-permute-start.43 = (f32[1,64,1024]{2,1,0:T(8,128)S(1)}, f32[1,64,1024]{2,1,0:T(8,128)S(1)}, u32[]{:S(2)}, u32[]{:S(2)}) collective-permute-start(f32[1,64,1024]{2,1,0:T(8,128)S(1)} %slice_add_fusion.8), channel_id=1, source_target_pairs={{0,16},{2,18},{4,20},{6,22},{8,24},{10,26},{12,28},{14,30},{16,0},... | collective-permute-start | bytes 786440 | tf_op jit(solution)/shard_map/ppermute | solution.py:800
  (29 other events, 188.8 us)

commit v5 on v4

--- a/solution.py
+++ b/solution.py
@@ -1016,6 +1016,8 @@
         estimate = long_cost() if i == 0 else short_cost()
         last[i] = first_norm_back(place, da1[i], arecv[i], x0[i], dx1[i], order.tie(g1), estimate)
         order.mark(last[i][0])
+        if custom and i == 0:
+            fc2_h.step(order)
     summed = list(none)
     gdx0 = [other(order.tie(last[0][3])), other(last[1][3])]
     dx0, sums1, kdx0, _ = zip(*last)
@@ -1030,9 +1032,6 @@
         sides[3][1] = order.tie(gmix[1])
         embz_h = Halving(*plain_grad(*sides, move_z, "embed_grad_b", mid, mid), Z_FIRST, size)
         order.mark(embz_h.sent)
-        fc2_h.step(order)
-    summed[0] = send(order.tie(ycot[0]))
-    if custom:
         fc1_h.step(order)
 
     sums2, sums1, qvsum, b1sum = order.tie((sums2, sums1, qvsum, b1sum))
@@ -1051,27 +1050,29 @@
         kept = jnp.where(core == 0, cube[:, 0], cube[:, 1])
         gone = jnp.where(core == 0, cube[:, 1], cube[:, 0])
         order.mark(gone)
+        embz_h.step(order)
+        att_h.step(order)
         fc2_g = fc2_h.step(order)
-        embz_h.step(order)
+        fc1_g = fc1_h.step(order)
+    summed[0] = send(order.tie(ycot[0]))
+    if custom:
+        gone = exchange(order.tie(gone), "dp", 1, size)
+        embx_h.step(order)
+        gone = order.tie(gone)
+        small_h = Halving(kept[:4] + gone[:4], kept[4:] + gone[4:], X_FIRST, size)
+        order.mark(small_h.sent)
     summed[0] = settle(summed[0])
     summed[1] = send(order.tie(ycot[1]))
     if custom:
-        gone = exchange(order.tie(gone), "dp", 1, size)
-        fc1_g = fc1_h.step(order)
-        gone = order.tie(gone)
-        small_h = Halving(kept[:4] + gone[:4], kept[4:] + gone[4:], X_FIRST, size)
-        order.mark(small_h.sent)
         att_h.step(order)
         small_h.step(order)
+        embz_h.step(order)
+        small_h.step(order)
         embx_h.step(order)
+        small = small_h.step(order)[0]
         summed[1] = settle(summed[1])
-        small_h.step(order)
-        embz_h.step(order)
-        small = small_h.step(order)[0]
-        att_h.step(order)
-        embx_h.step(order)
+        att_g = att_h.step(order)
         embz_g = embz_h.step(order)
-        att_g = att_h.step(order)
         embx_g = embx_h.step(order)
         emb_g = jnp.concatenate([embx_g, embz_g], 1)
         att_g = att_g.reshape(4, width // size, -1)

time: 364 us -> 352 us (0.967)
  waiting for transfers between devices: 187 us -> 168 us
  starting transfers between devices: 38.2 us -> 43.2 us
    ppermute x44, waiting for transfers between devices: 187 us -> 168 us  [exchange(): return lax.ppermute(values, axis, [(i, i ^ bit) for i in range(size)])]
    ppermute x44, starting transfers between devices: 38.2 us -> 43.2 us  [exchange(): return lax.ppermute(values, axis, [(i, i ^ bit) for i in range(size)])]
    unnamed x98 -> x110, local copies, waits for them, and re-layouts: 6.28 us -> 8.29 us
  transfers between devices with their start and end apart: 44 -> 44, of which waited for: 19 -> 17; matrix products, arithmetic and copies ran while one was open for 8% -> 8% of each run, Pallas kernels for 25% -> 26%
where the time goes in v5:
time: 352 us; the launch traced here: 348 us
  waiting for transfers between devices  168 us (48%)
  Pallas kernels  95.4 us (27%)
  starting transfers between devices  43.2 us (12%)
  other arithmetic  26.7 us (8%)
  local copies, waits for them, and re-layouts  13 us (4%)
    ppermute x44, waiting for transfers between devices, exchange(): return lax.ppermute(values, axis, [(i, i ^ bit) for i in range(size)])  168 us
    ppermute x44, starting transfers between devices, exchange(): return lax.ppermute(values, axis, [(i, i ^ bit) for i in range(size)])  43.2 us
    add x17, other arithmetic, step(): value = value + recv[first:first + count]  22.5 us
    pallas_call x2, Pallas kernels, attn_backward(): pl.pallas_call(functools.partial(attn_backward_kernel, parts=(len(gparts)...  16.1 us
    pallas_call x4, Pallas kernels, plain_grad(): pl.pallas_call(functools.partial(plain_grad_kernel, moves=moves), grid=(c...  15.7 us
    pallas_call x2, Pallas kernels, mlp(): pl.pallas_call(mlp_kernel, grid_spec=pltpu.PrefetchScalarGridSpec(num_sca...  15.1 us
    pallas_call x2, Pallas kernels, attn_forward(): pl.pallas_call(attn_forward_kernel, grid=(steps,), in_specs=[whole(part.s...  9.87 us
    pallas_call x2, Pallas kernels, embed(): pl.pallas_call(functools.partial(embed_kernel, item=item), grid_spec=pltp...  9.86 us
  transfers between devices with their start and end apart: 44, of which 17 were waited for; matrix products, arithmetic and copies ran while one was open for 8% of the time, Pallas kernels for 26%

profile of v5, /device:TPU:0, one launch (start us, length us, event | category | flops | bytes accessed | tf_op | source)
XLA Modules:
  0.0 348.1 jit_solution(14603110980206007754)
XLA Ops:
  0.7 5.0 %embed.2 = (f32[256,1024]{1,0:T(8,128)}, bf16[256,2048]{1,0:T(8,128)(2,1)}) custom-call(s32[2]{0:T(128)} %kinds.3, bf16[512,1664]{1,0:T(8,128)(2,1)} %pix_ref.3, bf16[1664,1024]{1,0:T(8,128)(2,1)} %wspec_ref.5, bf16[384,1024]{1,0:T(8,128)(2,1)} %wrgb_ref.5, bf16[1664,384]{1,0:T(8,128)(2,1)} %constant.53.clone.pick_ref), custom_call_target="tpu_custom_call" | custom-call | flops 1000 | bytes 1000 | tf_op jit(solution)/shard_map/embed/pallas_call | solution.py:242
  5.7 3.0 collective-permute-start
  8.8 4.9 %embed.3 = (f32[256,1024]{1,0:T(8,128)}, bf16[256,2048]{1,0:T(8,128)(2,1)}) custom-call(s32[2]{0:T(128)} %kinds.3, bf16[512,1664]{1,0:T(8,128)(2,1)} %pix_ref.3, bf16[1664,1024]{1,0:T(8,128)(2,1)} %wspec_ref.5, bf16[384,1024]{1,0:T(8,128)(2,1)} %wrgb_ref.5, bf16[1664,384]{1,0:T(8,128)(2,1)} %constant.53.clone.pick_ref), custom_call_target="tpu_custom_call" | custom-call | flops 1000 | bytes 1000 | tf_op jit(solution)/shard_map/embed/pallas_call | solution.py:242
  13.7 1.9 turn_cotangent.1
  15.6 3.1 pack_pixels.2
  19.3 3.1 pack_pixels.3
  22.7 9.4 %collective-permute-done.recv_ref = f32[256,1024]{1,0:T(8,128)} collective-permute-done((f32[256,1024]{1,0:T(8,128)}, f32[256,1024]{1,0:T(8,128)}, u32[]{:S(2)}, u32[]{:S(2)}) %collective-permute-start) | collective-permute-done | bytes 1048608 | tf_op jit(solution)/shard_map/ppermute | solution.py:800
  32.2 1.7 collective-permute-start.1
  33.9 1.9 copy-done.34
  35.8 1.2 copy-done.36
  37.0 1.2 copy-done.39
  38.3 5.5 %attn_forward.2 = (f32[256,1024]{1,0:T(8,128)S(1)}, bf16[256,1024]{1,0:T(8,128)(2,1)S(1)}, bf16[3,256,512]{2,1,0:T(8,128)(2,1)S(1)}, bf16[256,512]{1,0:T(8,128)(2,1)S(1)}, f32[256,1024]{1,0:T(8,128)S(1)}) custom-call(f32[256,1024]{1,0:T(8,128)S(1)} %copy-done.39, f32[256,1024]{1,0:T(8,128)} %collective-permute-done.recv_ref, ...), custom_call_target="tpu_custom_call" | custom-call | flops 99999997952 | bytes 1000 | tf_op jit(solution)/shard_map/attn_forward/pallas_call | solution.py:330
  43.9 1.8 pack_attn.2
  45.7 11.1 %collective-permute-done.1.recv_ref = f32[256,1024]{1,0:T(8,128)S(1)} collective-permute-done((f32[256,1024]{1,0:T(8,128)}, f32[256,1024]{1,0:T(8,128)S(1)}, u32[]{:S(2)}, u32[]{:S(2)}) %collective-permute-start.1) | collective-permute-done | bytes 1048608 | tf_op jit(solution)/shard_map/ppermute | solution.py:800
  56.7 1.4 collective-permute-start.2
  58.2 4.3 %attn_forward.3 = (f32[256,1024]{1,0:T(8,128)S(1)}, bf16[256,1024]{1,0:T(8,128)(2,1)S(1)}, bf16[3,256,512]{2,1,0:T(8,128)(2,1)S(1)}, bf16[256,512]{1,0:T(8,128)(2,1)S(1)}, f32[256,1024]{1,0:T(8,128)S(1)}) custom-call(f32[256,1024]{1,0:T(8,128)S(1)} %copy-done.40, f32[256,1024]{1,0:T(8,128)S(1)} %collective-permute-done.1.recv_ref, ...), custom_call_target="tpu_custom_call" | custom-call | flops 99999997952 | bytes 1000 | tf_op jit(solution)/shard_map/attn_forward/pallas_call | solution.py:330
  64.1 16.0 %collective-permute-done.2.orecv_ref = f32[256,1024]{1,0:T(8,128)S(1)} collective-permute-done((f32[256,1024]{1,0:T(8,128)S(1)}, f32[256,1024]{1,0:T(8,128)S(1)}, u32[]{:S(2)}, u32[]{:S(2)}) %collective-permute-start.2) | collective-permute-done | bytes 1048608 | tf_op jit(solution)/shard_map/ppermute | solution.py:800
  80.2 1.3 collective-permute-start.6
  81.5 7.5 %mlp.2 = (f32[256,1024]{1,0:T(8,128)S(1)}, bf16[256,1024]{1,0:T(8,128)(2,1)}, bf16[256,2048]{1,0:T(8,128)(2,1)S(1)}, bf16[256,2048]{1,0:T(8,128)(2,1)S(1)}, f32[...) custom-call(s32[9]{0:T(128)S(1)} %pad_add_fusion.place, ...), custom_call_target="tpu_custom_call" | custom-call | flops 99999997952 | bytes 1000 | tf_op jit(solution)/shard_map/mlp/pallas_call | solution.py:536
  90.7 12.8 %collective-permute-done.6.orecv_ref = f32[256,1024]{1,0:T(8,128)S(1)} collective-permute-done((f32[256,1024]{1,0:T(8,128)S(1)}, f32[256,1024]{1,0:T(8,128)S(1)}, u32[]{:S(2)}, u32[]{:S(2)}) %collective-permute-start.6) | collective-permute-done | bytes 1048608 | tf_op jit(solution)/shard_map/ppermute | solution.py:800
  103.5 1.3 collective-permute-start.9
  104.8 7.5 %mlp.3 = (f32[256,1024]{1,0:T(8,128)S(1)}, bf16[256,1024]{1,0:T(8,128)(2,1)}, bf16[256,2048]{1,0:T(8,128)(2,1)S(1)}, bf16[256,2048]{1,0:T(8,128)(2,1)S(1)}, f32[...) custom-call(s32[9]{0:T(128)S(1)} %pad_add_fusion.place, ...), custom_call_target="tpu_custom_call" | custom-call | flops 99999997952 | bytes 1000 | tf_op jit(solution)/shard_map/mlp/pallas_call | solution.py:536
  113.5 1.8 mlp_out.2
  116.5 4.1 %fc2_grad.1 = (f32[4,64,2048]{2,1,0:T(8,128)}, f32[4,64,2048]{2,1,0:T(8,128)S(1)}) custom-call(bf16[2,512,256]{2,1,0:T(8,128)(2,1)S(1)} %get-tuple-element.212.ka_ref.kb_ref, bf16[2,512,256]{2,1,0:T(8,128)(2,1)S(1)} %get-tuple-element.212.ka_ref.kb_ref, f32[4,256,256]{2,1,0:T(8,128)S(1)} %collective-permute-done.3.la_ref.lb_ref, ...), custom_call_target="tpu_custom_call" | custom-call | flops 1000 | bytes 1000 | tf_op jit(solution)/shard_map/fc2_grad/pallas_call | solution.py:734
  120.6 1.5 collective-permute-start.17
  122.1 4.3 %fc1_grad.1 = (f32[4,64,2048]{2,1,0:T(8,128)}, f32[4,64,2048]{2,1,0:T(8,128)S(1)}) custom-call(bf16[512,256]{1,0:T(8,128)(2,1)S(1)} %get-tuple-element.206.ka_ref, bf16[512,256]{1,0:T(8,128)(2,1)S(1)} %get-tuple-element.207.kb_ref, f32[10,256,256]{2,1,0:T(8,128)S(1)} %collective-permute-done.12.la_ref.oa_ref, ...), custom_call_target="tpu_custom_call" | custom-call | flops 1000 | bytes 1000 | tf_op jit(solution)/shard_map/fc1_grad/pallas_call | solution.py:734
  127.4 2.1 collective-permute-done.10.refs_3_
  130.2 8.1 %attn_backward.2 = (f32[256,1024]{1,0:T(8,128)S(1)}, bf16[256,1024]{1,0:T(8,128)(2,1)}, bf16[3,256,512]{2,1,0:T(8,128)(2,1)S(1)}, f32[8,1024]{1,0:T(8,128)S(1)},...) custom-call(s32[9]{0:T(128)S(1)} %pad_add_fusion.place, ...), custom_call_target="tpu_custom_call" | custom-call | flops 99999997952 | bytes 1000 | tf_op jit(solution)/shard_map/attn_backward/pallas_call | solution.py:446
  138.2 15.6 %collective-permute-done.15.refs_1_ = f32[256,1024]{1,0:T(8,128)S(1)} collective-permute-done((f32[256,1024]{1,0:T(8,128)S(1)}, f32[256,1024]{1,0:T(8,128)S(1)}, u32[]{:S(2)}, u32[]{:S(2)}) %collective-permute-start.15) | collective-permute-done | bytes 1048608 | tf_op jit(solution)/shard_map/ppermute | solution.py:800
  154.5 8.0 %attn_backward.3 = (f32[256,1024]{1,0:T(8,128)S(1)}, bf16[256,1024]{1,0:T(8,128)(2,1)}, bf16[3,256,512]{2,1,0:T(8,128)(2,1)S(1)}, f32[8,1024]{1,0:T(8,128)S(1)},...) custom-call(s32[9]{0:T(128)S(1)} %pad_add_fusion.place, ...), custom_call_target="tpu_custom_call" | custom-call | flops 99999997952 | bytes 1000 | tf_op jit(solution)/shard_map/attn_backward/pallas_call | solution.py:446
  163.3 1.8 mlp_out.3
  166.3 2.3 collective-permute-done.17
  168.6 1.4 slice_add_fusion.2
  170.0 2.0 collective-permute-start.23
  172.0 7.3 %attn_grad.1 = (f32[4,256,512]{2,1,0:T(8,128)}, f32[4,256,512]{2,1,0:T(8,128)S(1)}) custom-call(bf16[512,256]{1,0:T(8,128)(2,1)S(1)} %get-tuple-element.238.aa_ref, bf16[512,256]{1,0:T(8,128)(2,1)S(1)} %get-tuple-element.239.ab_ref, bf16[512,256]{1,0:T(8,128)(2,1)S(1)} %get-tuple-element.240.ya_ref, bf16[512,256]{1,0:T(8,128)(2,1)S(1)} %get-tuple-element.241.yb_ref, ...), custom_call_target="tpu_custom_call" | custom-call | flops 1000 | bytes 1000 | tf_op jit(solution)/shard_map/attn_grad/pallas_call | solution.py:784
  179.4 2.5 slice_add_fusion.1
  182.5 1.5 collective-permute-start.28
  184.5 1.7 first_norm_back.2
  186.1 10.4 %collective-permute-done.23 = f32[2,64,2048]{2,1,0:T(8,128)S(1)} collective-permute-done((f32[2,64,2048]{2,1,0:T(8,128)S(1)}, f32[2,64,2048]{2,1,0:T(8,128)S(1)}, u32[]{:S(2)}, u32[]{:S(2)}) %collective-permute-start.23) | collective-permute-done | bytes 1048608 | tf_op jit(solution)/shard_map/ppermute | solution.py:800
  196.5 2.3 slice_add_fusion.7
  198.8 3.0 collective-permute-start.29
  201.8 5.7 %collective-permute-done.22.refs_1_ = f32[256,1024]{1,0:T(8,128)S(1)} collective-permute-done((f32[256,1024]{1,0:T(8,128)S(1)}, f32[256,1024]{1,0:T(8,128)S(1)}, u32[]{:S(2)}, u32[]{:S(2)}) %collective-permute-start.22) | collective-permute-done | bytes 1048608 | tf_op jit(solution)/shard_map/ppermute | solution.py:800
  207.5 1.7 first_norm_back.3
  209.8 3.8 %pixel_grad.1 = bf16[512,1664]{1,0:T(8,128)(2,1)} custom-call(s32[2]{0:T(128)S(1)} %copy-done.31, bf16[256,1024]{1,0:T(8,128)(2,1)S(1)} %get-tuple-element.261.da_ref, bf16[256,1024]{1,0:T(8,128)(2,1)S(1)} %get-tuple-element.265.db_ref, bf16[1664,1024]{1,0:T(8,128)(2,1)S(1)} %copy-done, bf16[384,1024]{1,0:T(8,128)(2,1)S(1)} %copy-done.6, ...), custom_call_target="tpu_custom_call" | custom-call | flops 99999997952 | bytes 1000 | tf_op jit(solution)/shard_map/pixel_grad/pallas_call | solution.py:663
  213.6 3.7 %embed_grad_a.1 = (f32[4,64,1024]{2,1,0:T(8,128)}, f32[4,64,1024]{2,1,0:T(8,128)S(1)}) custom-call(bf16[512,256]{1,0:T(8,128)(2,1)S(1)} %get-tuple-element.257.ka_ref, bf16[512,256]{1,0:T(8,128)(2,1)S(1)} %get-tuple-element.264.kb_ref, f32[2,256,256]{2,1,0:T(8,128)S(1)} %collective-permute-done.24.la_ref, f32[2,256,256]{2,1,0:T(8,128)S(1)} %collective-permute-done.25.lb_ref, ...), custom_call_target="tpu_custom_call" | custom-call | flops 1000 | bytes 1000 | tf_op jit(solution)/shard_map/embed_grad_a/pallas_call | solution.py:734
  219.3 3.6 %embed_grad_b.1 = (f32[4,64,1024]{2,1,0:T(8,128)}, f32[4,64,1024]{2,1,0:T(8,128)S(1)}) custom-call(bf16[512,256]{1,0:T(8,128)(2,1)S(1)} %get-tuple-element.257.ka_ref, bf16[512,256]{1,0:T(8,128)(2,1)S(1)} %get-tuple-element.264.kb_ref, f32[2,256,256]{2,1,0:T(8,128)S(1)} %collective-permute-done.24.la_ref, f32[2,256,256]{2,1,0:T(8,128)S(1)} %collective-permute-done.25.lb_ref, ...), custom_call_target="tpu_custom_call" | custom-call | flops 1000 | bytes 1000 | tf_op jit(solution)/shard_map/embed_grad_b/pallas_call | solution.py:734
  225.0 2.2 slice_add_fusion.6
  227.2 3.4 collective-permute-start.30
  231.7 28.7 %collective-permute-done.27 = f32[4,64,1024]{2,1,0:T(8,128)} collective-permute-done((f32[4,64,1024]{2,1,0:T(8,128)}, f32[4,64,1024]{2,1,0:T(8,128)}, u32[]{:S(2)}, u32[]{:S(2)}) %collective-permute-start.27) | collective-permute-done | bytes 1048608 | tf_op jit(solution)/shard_map/ppermute | solution.py:800
  260.4 1.3 slice_add_fusion.5
  261.7 1.4 slice_add_fusion
  263.2 2.4 add_add_fusion.1
  265.6 2.4 add_add_fusion.2
  269.5 6.3 %collective-permute-done.31 = f32[4,64,1024]{2,1,0:T(8,128)} collective-permute-done((f32[4,64,1024]{2,1,0:T(8,128)}, f32[4,64,1024]{2,1,0:T(8,128)}, u32[]{:S(2)}, u32[]{:S(2)}) %collective-permute-start.31) | collective-permute-done | bytes 1048608 | tf_op jit(solution)/shard_map/ppermute | solution.py:800
  277.0 1.5 collective-permute-start.35
  278.6 13.5 %collective-permute-done.33 = f32[256,1024]{1,0:T(8,128)S(1)} collective-permute-done((f32[256,1024]{1,0:T(8,128)S(1)}, f32[256,1024]{1,0:T(8,128)S(1)}, u32[]{:S(2)}, u32[]{:S(2)}) %collective-permute-start.33) | collective-permute-done | bytes 1048608 | tf_op jit(solution)/shard_map/ppermute | solution.py:800
  292.6 2.1 collective-permute-done.34
  294.6 1.2 slice_add_fusion.3
  295.8 2.6 collective-permute-start.41
  298.5 2.1 collective-permute-start.37
  301.6 13.1 %collective-permute-done.37 = f32[2,1,576]{2,1,0:T(1,128)S(1)} collective-permute-done((f32[2,1,576]{2,1,0:T(1,128)S(1)}, f32[2,1,576]{2,1,0:T(1,128)S(1)}, u32[]{:S(2)}, u32[]{:S(2)}) %collective-permute-start.37) | collective-permute-done | bytes 4640 | tf_op jit(solution)/shard_map/ppermute | solution.py:800
  314.8 5.0 %collective-permute-start.39 = (f32[1,1,576]{2,1,0:T(1,128)S(1)}, f32[1,1,576]{2,1,0:T(1,128)S(1)}, u32[]{:S(2)}, u32[]{:S(2)}) collective-permute-start(f32[1,1,576]{2,1,0:T(1,128)S(1)} %fusion.8), channel_id=1, source_target_pairs={{0,16},{2,18},{4,20},{6,22},{8,24},{10,26},{12,28},{14,30},{16,0},... | collective-permute-start | bytes 6920 | tf_op jit(solution)/shard_map/ppermute | solution.py:800
  320.9 16.9 %collective-permute-done.39 = f32[1,1,576]{2,1,0:T(1,128)S(1)} collective-permute-done((f32[1,1,576]{2,1,0:T(1,128)S(1)}, f32[1,1,576]{2,1,0:T(1,128)S(1)}, u32[]{:S(2)}, u32[]{:S(2)}) %collective-permute-start.39) | collective-permute-done | bytes 2336 | tf_op jit(solution)/shard_map/ppermute | solution.py:800
  339.6 1.3 add_add_fusion
  (213 shorter events, 31.4 us)
Async XLA Ops:
  5.7 26.5 %collective-permute-start = (f32[256,1024]{1,0:T(8,128)}, f32[256,1024]{1,0:T(8,128)}, u32[]{:S(2)}, u32[]{:S(2)}) collective-permute-start(f32[256,1024]{1,0:T(8,128)} %get-tuple-element.167.part_ref), channel_id=1, source_target_pairs={{0,1},{1,0},{2,3},{3,2},{4,5},{5,4},{6,7},{7,6},{8,9},{9,8},{10,11... | collective-permute-start | bytes 3145736 | tf_op jit(solution)/shard_map/ppermute | solution.py:800
  15.6 28.3 %collective-permute-start.3 = (f32[4,256,256]{2,1,0:T(8,128)}, f32[4,256,256]{2,1,0:T(8,128)S(1)}, u32[]{:S(2)}, u32[]{:S(2)}) collective-permute-start(f32[4,256,256]{2,1,0:T(8,128)} %get-tuple-element.171), channel_id=1, source_target_pairs={{0,2},{2,0},{4,6},{6,4},{8,10},{10,8},{12,14},{14,12},{16,18},{18,... | collective-permute-start | bytes 3145736 | tf_op jit(solution)/shard_map/ppermute | solution.py:800
  18.7 15.3 %copy-start.42 = (f32[1024]{0:T(1024)S(1)}, f32[1024]{0:T(1024)}, u32[]{:S(2)}) copy-start(f32[1024]{0:T(1024)} %param.27) | copy-start | bytes 12292
  18.7 15.3 %copy-start.46 = (f32[512]{0:T(512)S(1)}, f32[512]{0:T(512)}, u32[]{:S(2)}) copy-start(f32[512]{0:T(512)} %param.29) | copy-start | bytes 6148
  18.7 43.9 %collective-permute-start.4 = (f32[8,256,256]{2,1,0:T(8,128)}, f32[8,256,256]{2,1,0:T(8,128)}, u32[]{:S(2)}, u32[]{:S(2)}) collective-permute-start(f32[8,256,256]{2,1,0:T(8,128)} %pack_pixels.2), channel_id=1, source_target_pairs={{0,2},{2,0},{4,6},{6,4},{8,10},{10,8},{12,14},{14,12},{16,18},{18,... | collective-permute-start | bytes 6291464 | tf_op jit(solution)/shard_map/ppermute | solution.py:800
  22.4 40.2 %collective-permute-start.5 = (f32[8,256,256]{2,1,0:T(8,128)}, f32[8,256,256]{2,1,0:T(8,128)}, u32[]{:S(2)}, u32[]{:S(2)}) collective-permute-start(f32[8,256,256]{2,1,0:T(8,128)} %pack_pixels.3), channel_id=1, source_target_pairs={{0,2},{2,0},{4,6},{6,4},{8,10},{10,8},{12,14},{14,12},{16,18},{18,... | collective-permute-start | bytes 6291464 | tf_op jit(solution)/shard_map/ppermute | solution.py:800
  32.2 24.6 %collective-permute-start.1 = (f32[256,1024]{1,0:T(8,128)}, f32[256,1024]{1,0:T(8,128)S(1)}, u32[]{:S(2)}, u32[]{:S(2)}) collective-permute-start(f32[256,1024]{1,0:T(8,128)} %get-tuple-element.179.part_ref), channel_id=1, source_target_pairs={{0,1},{1,0},{2,3},{3,2},{4,5},{5,4},{6,7},{7,6},{8,9},{9,8},{10,11... | collective-permute-start | bytes 3145736 | tf_op jit(solution)/shard_map/ppermute | solution.py:800
  38.3 19.9 %copy-start.37 = (bf16[512,1024]{1,0:T(8,128)(2,1)S(1)}, bf16[512,1024]{1,0:T(8,128)(2,1)}, u32[]{:S(2)}) copy-start(bf16[512,1024]{1,0:T(8,128)(2,1)} %refs_5_.3) | copy-start | bytes 3145732
  38.3 19.9 %copy-start.40 = (f32[256,1024]{1,0:T(8,128)S(1)}, f32[256,1024]{1,0:T(8,128)}, u32[]{:S(2)}) copy-start(f32[256,1024]{1,0:T(8,128)} %get-tuple-element.179.part_ref) | copy-start | bytes 3145732
  43.8 37.6 %copy-start.48 = (f32[256,1024]{1,0:T(8,128)}, f32[256,1024]{1,0:T(8,128)S(1)}, u32[]{:S(2)}) copy-start(f32[256,1024]{1,0:T(8,128)S(1)} %get-tuple-element.177.x0_ref.refs_4_) | copy-start | bytes 3145732
  45.7 43.4 %collective-permute-start.7 = (f32[4,256,256]{2,1,0:T(8,128)}, f32[4,256,256]{2,1,0:T(8,128)}, u32[]{:S(2)}, u32[]{:S(2)}) collective-permute-start(f32[4,256,256]{2,1,0:T(8,128)} %get-tuple-element.185), channel_id=1, source_target_pairs={{0,2},{2,0},{4,6},{6,4},{8,10},{10,8},{12,14},{14,12},{16,18},{18,... | collective-permute-start | bytes 3145736 | tf_op jit(solution)/shard_map/ppermute | solution.py:800
  56.7 23.4 %collective-permute-start.2 = (f32[256,1024]{1,0:T(8,128)S(1)}, f32[256,1024]{1,0:T(8,128)S(1)}, u32[]{:S(2)}, u32[]{:S(2)}) collective-permute-start(f32[256,1024]{1,0:T(8,128)S(1)} %get-tuple-element.180.opart_ref), channel_id=1, source_target_pairs={{0,1},{1,0},{2,3},{3,2},{4,5},{5,4},{6,7},{7,6},{8,9},{9,8},{10,11... | collective-permute-start | bytes 3145736 | tf_op jit(solution)/shard_map/ppermute | solution.py:800
  58.2 23.3 %copy-start.24 = (bf16[512,1024]{1,0:T(8,128)(2,1)S(1)}, bf16[512,1024]{1,0:T(8,128)(2,1)}, u32[]{:S(2)}) copy-start(bf16[512,1024]{1,0:T(8,128)(2,1)} %refs_3_.1) | copy-start | bytes 3145732
  58.2 23.3 %copy-start.32 = (bf16[1024,2048]{1,0:T(8,128)(2,1)S(1)}, bf16[1024,2048]{1,0:T(8,128)(2,1)}, u32[]{:S(2)}) copy-start(bf16[1024,2048]{1,0:T(8,128)(2,1)} %wfc1_ref.3) | copy-start | bytes 12582916
  58.2 23.3 %copy-start.33 = (bf16[2048,1024]{1,0:T(8,128)(2,1)S(1)}, bf16[2048,1024]{1,0:T(8,128)(2,1)}, u32[]{:S(2)}) copy-start(bf16[2048,1024]{1,0:T(8,128)(2,1)} %wfc2_ref.7) | copy-start | bytes 12582916
  58.2 23.3 %copy-start.41 = (f32[2048]{0:T(1024)S(1)}, f32[2048]{0:T(1024)}, u32[]{:S(2)}) copy-start(f32[2048]{0:T(1024)} %param.36) | copy-start | bytes 24580
  58.2 23.3 %copy-start.43 = (f32[1024]{0:T(1024)S(1)}, f32[1024]{0:T(1024)}, u32[]{:S(2)}) copy-start(f32[1024]{0:T(1024)} %param.32) | copy-start | bytes 12292
  58.2 23.3 %copy-start.44 = (f32[1024]{0:T(1024)S(1)}, f32[1024]{0:T(1024)}, u32[]{:S(2)}) copy-start(f32[1024]{0:T(1024)} %param.34) | copy-start | bytes 12292
  58.2 23.3 %copy-start.45 = (f32[1024]{0:T(1024)S(1)}, f32[1024]{0:T(1024)}, u32[]{:S(2)}) copy-start(f32[1024]{0:T(1024)} %param.33) | copy-start | bytes 12292
  62.6 42.2 %copy-start.15 = (f32[256,1024]{1,0:T(8,128)}, f32[256,1024]{1,0:T(8,128)S(1)}, u32[]{:S(2)}) copy-start(f32[256,1024]{1,0:T(8,128)S(1)} %get-tuple-element.196.x0_ref.refs_2_) | copy-start | bytes 3145732
  64.1 25.0 %collective-permute-start.8 = (f32[4,256,256]{2,1,0:T(8,128)S(1)}, f32[4,256,256]{2,1,0:T(8,128)S(1)}, u32[]{:S(2)}, u32[]{:S(2)}) collective-permute-start(f32[4,256,256]{2,1,0:T(8,128)S(1)} %get-tuple-element.193), channel_id=1, source_target_pairs={{0,2},{2,0},{4,6},{6,4},{8,10},{10,8},{12,14},{14,12},{16,18},{18,... | collective-permute-start | bytes 3145736 | tf_op jit(solution)/shard_map/ppermute | solution.py:800
  80.2 23.3 %collective-permute-start.6 = (f32[256,1024]{1,0:T(8,128)S(1)}, f32[256,1024]{1,0:T(8,128)S(1)}, u32[]{:S(2)}, u32[]{:S(2)}) collective-permute-start(f32[256,1024]{1,0:T(8,128)S(1)} %get-tuple-element.197.opart_ref), channel_id=1, source_target_pairs={{0,1},{1,0},{2,3},{3,2},{4,5},{5,4},{6,7},{7,6},{8,9},{9,8},{10,11... | collective-permute-start | bytes 3145736 | tf_op jit(solution)/shard_map/ppermute | solution.py:800
  89.1 41.1 %copy-start.9 = (f32[256,1024]{1,0:T(8,128)}, f32[256,1024]{1,0:T(8,128)S(1)}, u32[]{:S(2)}) copy-start(f32[256,1024]{1,0:T(8,128)S(1)} %get-tuple-element.195.refs_4_) | copy-start | bytes 3145732
  90.2 23.4 %collective-permute-start.12 = (f32[10,256,256]{2,1,0:T(8,128)S(1)}, f32[10,256,256]{2,1,0:T(8,128)S(1)}, u32[]{:S(2)}, u32[]{:S(2)}) collective-permute-start(f32[10,256,256]{2,1,0:T(8,128)S(1)} %get-tuple-element.210), channel_id=1, source_target_pairs={{0,2},{2,0},{4,6},{6,4},{8,10},{10,8},{12,14},{14,12},{16,18},{18,... | collective-permute-start | bytes 7864328 | tf_op jit(solution)/shard_map/ppermute | solution.py:800
  90.2 23.4 %collective-permute-start.11 = (f32[8,256,256]{2,1,0:T(8,128)S(1)}, f32[8,256,256]{2,1,0:T(8,128)S(1)}, u32[]{:S(2)}, u32[]{:S(2)}) collective-permute-start(f32[8,256,256]{2,1,0:T(8,128)S(1)} %get-tuple-element.209), channel_id=1, source_target_pairs={{0,2},{2,0},{4,6},{6,4},{8,10},{10,8},{12,14},{14,12},{16,18},{18,... | collective-permute-start | bytes 6291464 | tf_op jit(solution)/shard_map/ppermute | solution.py:800
  103.5 9.4 %collective-permute-start.9 = (f32[96,1024]{1,0:T(8,128)S(1)}, f32[96,1024]{1,0:T(8,128)S(1)}, u32[]{:S(2)}, u32[]{:S(2)}) collective-permute-start(f32[96,1024]{1,0:T(8,128)S(1)} %get-tuple-element.203.refs_0_), channel_id=1, source_target_pairs={{0,1},{1,0},{2,3},{3,2},{4,5},{5,4},{6,7},{7,6},{8,9},{9,8},{10,11... | collective-permute-start | bytes 1179656 | tf_op jit(solution)/shard_map/ppermute | solution.py:800
  112.3 42.2 %copy-start.11 = (f32[256,1024]{1,0:T(8,128)}, f32[256,1024]{1,0:T(8,128)S(1)}, u32[]{:S(2)}) copy-start(f32[256,1024]{1,0:T(8,128)S(1)} %get-tuple-element.227.refs_2_) | copy-start | bytes 3145732
  112.3 4.2 %collective-permute-start.13 = (f32[8,256,256]{2,1,0:T(8,128)S(1)}, f32[8,256,256]{2,1,0:T(8,128)S(1)}, u32[]{:S(2)}, u32[]{:S(2)}) collective-permute-start(f32[8,256,256]{2,1,0:T(8,128)S(1)} %get-tuple-element.217), channel_id=1, source_target_pairs={{0,2},{2,0},{4,6},{6,4},{8,10},{10,8},{12,14},{14,12},{16,18},{18,... | collective-permute-start | bytes 6291464 | tf_op jit(solution)/shard_map/ppermute | solution.py:800
  112.3 9.7 %collective-permute-start.14 = (f32[10,256,256]{2,1,0:T(8,128)S(1)}, f32[10,256,256]{2,1,0:T(8,128)S(1)}, u32[]{:S(2)}, u32[]{:S(2)}) collective-permute-start(f32[10,256,256]{2,1,0:T(8,128)S(1)} %get-tuple-element.220), channel_id=1, source_target_pairs={{0,2},{2,0},{4,6},{6,4},{8,10},{10,8},{12,14},{14,12},{16,18},{18,... | collective-permute-start | bytes 7864328 | tf_op jit(solution)/shard_map/ppermute | solution.py:800
  112.9 16.6 %collective-permute-start.10 = (f32[160,1024]{1,0:T(8,128)S(1)}, f32[160,1024]{1,0:T(8,128)S(1)}, u32[]{:S(2)}, u32[]{:S(2)}) collective-permute-start(f32[160,1024]{1,0:T(8,128)S(1)} %get-tuple-element.205.refs_1_), channel_id=1, source_target_pairs={{0,1},{1,0},{2,3},{3,2},{4,5},{5,4},{6,7},{7,6},{8,9},{9,8},{10,11... | collective-permute-start | bytes 1966088 | tf_op jit(solution)/shard_map/ppermute | solution.py:800
  120.6 75.9 %copy-start.7 = (f32[4,64,2048]{2,1,0:T(8,128)}, f32[4,64,2048]{2,1,0:T(8,128)S(1)}, u32[]{:S(2)}) copy-start(f32[4,64,2048]{2,1,0:T(8,128)S(1)} %get-tuple-element.242) | copy-start | bytes 6291460
  120.6 48.0 %collective-permute-start.17 = (f32[4,64,2048]{2,1,0:T(8,128)}, f32[4,64,2048]{2,1,0:T(8,128)}, u32[]{:S(2)}, u32[]{:S(2)}) collective-permute-start(f32[4,64,2048]{2,1,0:T(8,128)} %get-tuple-element.219), channel_id=1, source_target_pairs={{0,4},{2,6},{4,0},{6,2},{8,12},{10,14},{12,8},{14,10},{16,20},{18,... | collective-permute-start | bytes 6291464 | tf_op jit(solution)/shard_map/ppermute | solution.py:800
  126.4 53.0 %copy-start.8 = (f32[4,64,2048]{2,1,0:T(8,128)}, f32[4,64,2048]{2,1,0:T(8,128)S(1)}, u32[]{:S(2)}) copy-start(f32[4,64,2048]{2,1,0:T(8,128)S(1)} %get-tuple-element.237) | copy-start | bytes 6291460
  126.4 53.0 %collective-permute-start.20 = (f32[4,64,2048]{2,1,0:T(8,128)}, f32[4,64,2048]{2,1,0:T(8,128)}, u32[]{:S(2)}, u32[]{:S(2)}) collective-permute-start(f32[4,64,2048]{2,1,0:T(8,128)} %get-tuple-element.224), channel_id=1, source_target_pairs={{0,8},{2,10},{4,12},{6,14},{8,0},{10,2},{12,4},{14,6},{16,24},{18,... | collective-permute-start | bytes 6291464 | tf_op jit(solution)/shard_map/ppermute | solution.py:800
  129.5 24.3 %collective-permute-start.15 = (f32[256,1024]{1,0:T(8,128)S(1)}, f32[256,1024]{1,0:T(8,128)S(1)}, u32[]{:S(2)}, u32[]{:S(2)}) collective-permute-start(f32[256,1024]{1,0:T(8,128)S(1)} %get-tuple-element.226.refs_0_), channel_id=1, source_target_pairs={{0,1},{1,0},{2,3},{3,2},{4,5},{5,4},{6,7},{7,6},{8,9},{9,8},{10,11... | collective-permute-start | bytes 3145736 | tf_op jit(solution)/shard_map/ppermute | solution.py:800
  153.8 9.5 %collective-permute-start.16 = (f32[96,1024]{1,0:T(8,128)S(1)}, f32[96,1024]{1,0:T(8,128)S(1)}, u32[]{:S(2)}, u32[]{:S(2)}) collective-permute-start(f32[96,1024]{1,0:T(8,128)S(1)} %get-tuple-element.234.refs_0_), channel_id=1, source_target_pairs={{0,1},{1,0},{2,3},{3,2},{4,5},{5,4},{6,7},{7,6},{8,9},{9,8},{10,11... | collective-permute-start | bytes 1179656 | tf_op jit(solution)/shard_map/ppermute | solution.py:800
  162.5 9.5 %collective-permute-start.19 = (f32[8,256,256]{2,1,0:T(8,128)S(1)}, f32[8,256,256]{2,1,0:T(8,128)S(1)}, u32[]{:S(2)}, u32[]{:S(2)}) collective-permute-start(f32[8,256,256]{2,1,0:T(8,128)S(1)} %get-tuple-element.247), channel_id=1, source_target_pairs={{0,2},{2,0},{4,6},{6,4},{8,10},{10,8},{12,14},{14,12},{16,18},{18,... | collective-permute-start | bytes 6291464 | tf_op jit(solution)/shard_map/ppermute | solution.py:800
  163.3 8.7 %collective-permute-start.18 = (f32[8,256,256]{2,1,0:T(8,128)S(1)}, f32[8,256,256]{2,1,0:T(8,128)S(1)}, u32[]{:S(2)}, u32[]{:S(2)}) collective-permute-start(f32[8,256,256]{2,1,0:T(8,128)S(1)} %get-tuple-element.245), channel_id=1, source_target_pairs={{0,2},{2,0},{4,6},{6,4},{8,10},{10,8},{12,14},{14,12},{16,18},{18,... | collective-permute-start | bytes 6291464 | tf_op jit(solution)/shard_map/ppermute | solution.py:800
  165.1 18.8 %collective-permute-start.21 = (f32[160,1024]{1,0:T(8,128)S(1)}, f32[160,1024]{1,0:T(8,128)S(1)}, u32[]{:S(2)}, u32[]{:S(2)}) collective-permute-start(f32[160,1024]{1,0:T(8,128)S(1)} %get-tuple-element.254.refs_1_), channel_id=1, source_target_pairs={{0,1},{1,0},{2,3},{3,2},{4,5},{5,4},{6,7},{7,6},{8,9},{9,8},{10,11... | collective-permute-start | bytes 1966088 | tf_op jit(solution)/shard_map/ppermute | solution.py:800
  170.0 26.5 %collective-permute-start.23 = (f32[2,64,2048]{2,1,0:T(8,128)S(1)}, f32[2,64,2048]{2,1,0:T(8,128)S(1)}, u32[]{:S(2)}, u32[]{:S(2)}) collective-permute-start(f32[2,64,2048]{2,1,0:T(8,128)S(1)} %slice_add_fusion.2), channel_id=1, source_target_pairs={{0,8},{2,10},{4,12},{6,14},{8,0},{10,2},{12,4},{14,6},{16,24},{18,... | collective-permute-start | bytes 3145736 | tf_op jit(solution)/shard_map/ppermute | solution.py:800
  181.9 43.0 %collective-permute-start.26 = (f32[2,64,2048]{2,1,0:T(8,128)}, f32[2,64,2048]{2,1,0:T(8,128)}, u32[]{:S(2)}, u32[]{:S(2)}) collective-permute-start(f32[2,64,2048]{2,1,0:T(8,128)} %slice_add_fusion.1), channel_id=1, source_target_pairs={{0,4},{2,6},{4,0},{6,2},{8,12},{10,14},{12,8},{14,10},{16,20},{18,... | collective-permute-start | bytes 3145736 | tf_op jit(solution)/shard_map/ppermute | solution.py:800
  182.5 79.3 %collective-permute-start.28 = (f32[4,256,512]{2,1,0:T(8,128)}, f32[4,256,512]{2,1,0:T(8,128)}, u32[]{:S(2)}, u32[]{:S(2)}) collective-permute-start(f32[4,256,512]{2,1,0:T(8,128)} %get-tuple-element.251), channel_id=1, source_target_pairs={{0,4},{2,6},{4,0},{6,2},{8,12},{10,14},{12,8},{14,10},{16,20},{18,... | collective-permute-start | bytes 6291464 | tf_op jit(solution)/shard_map/ppermute | solution.py:800
  184.0 23.5 %collective-permute-start.22 = (f32[256,1024]{1,0:T(8,128)S(1)}, f32[256,1024]{1,0:T(8,128)S(1)}, u32[]{:S(2)}, u32[]{:S(2)}) collective-permute-start(f32[256,1024]{1,0:T(8,128)S(1)} %get-tuple-element.259.refs_0_), channel_id=1, source_target_pairs={{0,1},{1,0},{2,3},{3,2},{4,5},{5,4},{6,7},{7,6},{8,9},{9,8},{10,11... | collective-permute-start | bytes 3145736 | tf_op jit(solution)/shard_map/ppermute | solution.py:800
  184.5 25.3 %copy-start.5 = (bf16[1664,384]{1,0:T(8,128)(2,1)S(1)}, bf16[1664,384]{1,0:T(8,128)(2,1)}, u32[]{:S(2)}) copy-start(bf16[1664,384]{1,0:T(8,128)(2,1)} %constant.53.clone.pick_ref) | copy-start | bytes 3833860
  186.1 21.4 %copy-start.16 = (f32[256,1024]{1,0:T(8,128)S(1)}, f32[256,1024]{1,0:T(8,128)}, u32[]{:S(2)}) copy-start(f32[256,1024]{1,0:T(8,128)} %copy-done.15) | copy-start | bytes 3145732
  198.8 64.4 %collective-permute-start.29 = (f32[1,64,2048]{2,1,0:T(8,128)}, f32[1,64,2048]{2,1,0:T(8,128)}, u32[]{:S(2)}, u32[]{:S(2)}) collective-permute-start(f32[1,64,2048]{2,1,0:T(8,128)} %slice_add_fusion.7), channel_id=1, source_target_pairs={{0,16},{2,18},{4,20},{6,22},{8,24},{10,26},{12,28},{14,30},{16,0},... | collective-permute-start | bytes 1572872 | tf_op jit(solution)/shard_map/ppermute | solution.py:800
  209.2 4.4 %collective-permute-start.25 = (f32[2,256,256]{2,1,0:T(8,128)S(1)}, f32[2,256,256]{2,1,0:T(8,128)S(1)}, u32[]{:S(2)}, u32[]{:S(2)}) collective-permute-start(f32[2,256,256]{2,1,0:T(8,128)S(1)} %get-tuple-element.270), channel_id=1, source_target_pairs={{0,2},{2,0},{4,6},{6,4},{8,10},{10,8},{12,14},{14,12},{16,18},{18,... | collective-permute-start | bytes 1572872 | tf_op jit(solution)/shard_map/ppermute | solution.py:800
  209.3 4.3 %collective-permute-start.24 = (f32[2,256,256]{2,1,0:T(8,128)S(1)}, f32[2,256,256]{2,1,0:T(8,128)S(1)}, u32[]{:S(2)}, u32[]{:S(2)}) collective-permute-start(f32[2,256,256]{2,1,0:T(8,128)S(1)} %get-tuple-element.268), channel_id=1, source_target_pairs={{0,2},{2,0},{4,6},{6,4},{8,10},{10,8},{12,14},{14,12},{16,18},{18,... | collective-permute-start | bytes 1572872 | tf_op jit(solution)/shard_map/ppermute | solution.py:800
  218.2 57.5 %collective-permute-start.31 = (f32[4,64,1024]{2,1,0:T(8,128)}, f32[4,64,1024]{2,1,0:T(8,128)}, u32[]{:S(2)}, u32[]{:S(2)}) collective-permute-start(f32[4,64,1024]{2,1,0:T(8,128)} %get-tuple-element.272), channel_id=1, source_target_pairs={{0,4},{2,6},{4,0},{6,2},{8,12},{10,14},{12,8},{14,10},{16,20},{18,... | collective-permute-start | bytes 3145736 | tf_op jit(solution)/shard_map/ppermute | solution.py:800
  223.9 36.4 %collective-permute-start.27 = (f32[4,64,1024]{2,1,0:T(8,128)}, f32[4,64,1024]{2,1,0:T(8,128)}, u32[]{:S(2)}, u32[]{:S(2)}) collective-permute-start(f32[4,64,1024]{2,1,0:T(8,128)} %get-tuple-element.274), channel_id=1, source_target_pairs={{0,8},{2,10},{4,12},{6,14},{8,0},{10,2},{12,4},{14,6},{16,24},{18,... | collective-permute-start | bytes 3145736 | tf_op jit(solution)/shard_map/ppermute | solution.py:800
  227.2 38.4 %collective-permute-start.30 = (f32[1,64,2048]{2,1,0:T(8,128)}, f32[1,64,2048]{2,1,0:T(8,128)}, u32[]{:S(2)}, u32[]{:S(2)}) collective-permute-start(f32[1,64,2048]{2,1,0:T(8,128)} %slice_add_fusion.6), channel_id=1, source_target_pairs={{0,16},{2,18},{4,20},{6,22},{8,24},{10,26},{12,28},{14,30},{16,0},... | collective-permute-start | bytes 1572872 | tf_op jit(solution)/shard_map/ppermute | solution.py:800
  268.0 32.5 %copy-start.22 = (f32[4,64,1024]{2,1,0:T(8,128)S(1)}, f32[4,64,1024]{2,1,0:T(8,128)}, u32[]{:S(2)}) copy-start(f32[4,64,1024]{2,1,0:T(8,128)} %copy-done.21) | copy-start | bytes 3145732
  268.0 24.0 %collective-permute-start.33 = (f32[256,1024]{1,0:T(8,128)S(1)}, f32[256,1024]{1,0:T(8,128)S(1)}, u32[]{:S(2)}, u32[]{:S(2)}) collective-permute-start(f32[256,1024]{1,0:T(8,128)S(1)} %copy-done.14), channel_id=1, source_target_pairs={{0,1},{1,0},{2,3},{3,2},{4,5},{5,4},{6,7},{7,6},{8,9},{9,8},{10,11... | collective-permute-start | bytes 3145736 | tf_op jit(solution)/shard_map/ppermute | solution.py:800
  268.5 26.1 %collective-permute-start.34 = (f32[2,256,512]{2,1,0:T(8,128)S(1)}, f32[2,256,512]{2,1,0:T(8,128)S(1)}, u32[]{:S(2)}, u32[]{:S(2)}) collective-permute-start(f32[2,256,512]{2,1,0:T(8,128)S(1)} %slice_add_fusion), channel_id=1, source_target_pairs={{0,8},{2,10},{4,12},{6,14},{8,0},{10,2},{12,4},{14,6},{16,24},{18,... | collective-permute-start | bytes 3145736 | tf_op jit(solution)/shard_map/ppermute | solution.py:800
  268.5 32.0 %collective-permute-start.36 = (f32[2,64,1024]{2,1,0:T(8,128)S(1)}, f32[2,64,1024]{2,1,0:T(8,128)S(1)}, u32[]{:S(2)}, u32[]{:S(2)}) collective-permute-start(f32[2,64,1024]{2,1,0:T(8,128)S(1)} %slice_add_fusion.5), channel_id=1, source_target_pairs={{0,4},{2,6},{4,0},{6,2},{8,12},{10,14},{12,8},{14,10},{16,20},{18,... | collective-permute-start | bytes 1572872 | tf_op jit(solution)/shard_map/ppermute | solution.py:800
  269.5 7.5 %collective-permute-start.32 = (f32[8,1,576]{2,1,0:T(1,128)S(1)}, f32[8,1,576]{2,1,0:T(1,128)S(1)}, u32[]{:S(2)}, u32[]{:S(2)}) collective-permute-start(f32[8,1,576]{2,1,0:T(1,128)S(1)} %get-tuple-element.300), channel_id=1, source_target_pairs={{0,2},{2,0},{4,6},{6,4},{8,10},{10,8},{12,14},{14,12},{16,18},{18,... | collective-permute-start | bytes 55304 | tf_op jit(solution)/shard_map/ppermute | solution.py:800
  276.9 43.0 %collective-permute-start.38 = (f32[2,64,1024]{2,1,0:T(8,128)S(1)}, f32[2,64,1024]{2,1,0:T(8,128)S(1)}, u32[]{:S(2)}, u32[]{:S(2)}) collective-permute-start(f32[2,64,1024]{2,1,0:T(8,128)S(1)} %slice_add_fusion.4), channel_id=1, source_target_pairs={{0,8},{2,10},{4,12},{6,14},{8,0},{10,2},{12,4},{14,6},{16,24},{18,... | collective-permute-start | bytes 1572872 | tf_op jit(solution)/shard_map/ppermute | solution.py:800
  277.0 21.4 %collective-permute-start.35 = (f32[4,1,576]{2,1,0:T(1,128)S(1)}, f32[4,1,576]{2,1,0:T(1,128)S(1)}, u32[]{:S(2)}, u32[]{:S(2)}) collective-permute-start(f32[4,1,576]{2,1,0:T(1,128)S(1)} %get-tuple-element.327), channel_id=1, source_target_pairs={{0,4},{2,6},{4,0},{6,2},{8,12},{10,14},{12,8},{14,10},{16,20},{18,... | collective-permute-start | bytes 27656 | tf_op jit(solution)/shard_map/ppermute | solution.py:800
  292.1 47.6 %collective-permute-start.40 = (f32[256,1024]{1,0:T(8,128)S(1)}, f32[256,1024]{1,0:T(8,128)S(1)}, u32[]{:S(2)}, u32[]{:S(2)}) collective-permute-start(f32[256,1024]{1,0:T(8,128)S(1)} %mlp_out.2), channel_id=1, source_target_pairs={{0,1},{1,0},{2,3},{3,2},{4,5},{5,4},{6,7},{7,6},{8,9},{9,8},{10,11... | collective-permute-start | bytes 3145736 | tf_op jit(solution)/shard_map/ppermute | solution.py:800
  295.8 43.8 %collective-permute-start.41 = (f32[1,256,512]{2,1,0:T(8,128)S(1)}, f32[1,256,512]{2,1,0:T(8,128)S(1)}, u32[]{:S(2)}, u32[]{:S(2)}) collective-permute-start(f32[1,256,512]{2,1,0:T(8,128)S(1)} %slice_add_fusion.3), channel_id=1, source_target_pairs={{0,16},{2,18},{4,20},{6,22},{8,24},{10,26},{12,28},{14,30},{16,0},... | collective-permute-start | bytes 1572872 | tf_op jit(solution)/shard_map/ppermute | solution.py:800
  298.5 16.3 %collective-permute-start.37 = (f32[2,1,576]{2,1,0:T(1,128)S(1)}, f32[2,1,576]{2,1,0:T(1,128)S(1)}, u32[]{:S(2)}, u32[]{:S(2)}) collective-permute-start(f32[2,1,576]{2,1,0:T(1,128)S(1)} %slice_add_fusion.10), channel_id=1, source_target_pairs={{0,8},{2,10},{4,12},{6,14},{8,0},{10,2},{12,4},{14,6},{16,24},{18,... | collective-permute-start | bytes 13832 | tf_op jit(solution)/shard_map/ppermute | solution.py:800
  301.6 40.8 %collective-permute-start.42 = (f32[1,64,1024]{2,1,0:T(8,128)S(1)}, f32[1,64,1024]{2,1,0:T(8,128)S(1)}, u32[]{:S(2)}, u32[]{:S(2)}) collective-permute-start(f32[1,64,1024]{2,1,0:T(8,128)S(1)} %slice_add_fusion.9), channel_id=1, source_target_pairs={{0,16},{2,18},{4,20},{6,22},{8,24},{10,26},{12,28},{14,30},{16,0},... | collective-permute-start | bytes 786440 | tf_op jit(solution)/shard_map/ppermute | solution.py:800
  314.8 23.0 %collective-permute-start.39 = (f32[1,1,576]{2,1,0:T(1,128)S(1)}, f32[1,1,576]{2,1,0:T(1,128)S(1)}, u32[]{:S(2)}, u32[]{:S(2)}) collective-permute-start(f32[1,1,576]{2,1,0:T(1,128)S(1)} %fusion.8), channel_id=1, source_target_pairs={{0,16},{2,18},{4,20},{6,22},{8,24},{10,26},{12,28},{14,30},{16,0},... | collective-permute-start | bytes 6920 | tf_op jit(solution)/shard_map/ppermute | solution.py:800
  320.8 22.6 %collective-permute-start.43 = (f32[1,64,1024]{2,1,0:T(8,128)S(1)}, f32[1,64,1024]{2,1,0:T(8,128)S(1)}, u32[]{:S(2)}, u32[]{:S(2)}) collective-permute-start(f32[1,64,1024]{2,1,0:T(8,128)S(1)} %slice_add_fusion.8), channel_id=1, source_target_pairs={{0,16},{2,18},{4,20},{6,22},{8,24},{10,26},{12,28},{14,30},{16,0},... | collective-permute-start | bytes 786440 | tf_op jit(solution)/shard_map/ppermute | solution.py:800
  (35 other events, 204.6 us)

commit v6 on v5

--- a/solution.py
+++ b/solution.py
@@ -600,10 +600,11 @@
     )(act, w_fc2)
 
 
-def first_norm_back_kernel(place, *refs, parts):
+def first_norm_back_kernel(place, *refs, parts, riders):
     gpart_refs, refs = refs[: parts[0]], refs[parts[0] :]
     grecv_refs, refs = refs[: parts[1]], refs[parts[1] :]
-    x0_ref, dx1_ref, gain_ref, dx0_ref, sums_ref, keep_ref, gone_ref, turned_ref = refs
+    rider_refs, refs = refs[:riders], refs[riders:]
+    x0_ref, dx1_ref, gain_ref, dx0_ref, sums_ref, keep_ref, gone_ref, block_ref, turned_ref = refs
     normed, inverse = norm_parts(x0_ref[...])
     grad = joined(gpart_refs) + joined(grecv_refs)
     dx0_ref[...] = (dx1_ref[...] + norm_back(normed, inverse, grad, gain_ref[...])).astype(BF16)
@@ -611,20 +612,35 @@
     sums_ref[1:2, :] = column_sum(grad)
     sums_ref[2:8, :] = jnp.zeros((6, sums_ref.shape[1]), F32)
     turn(place, dx0_ref, turned_ref, slice(None))
-    spread(turned_ref, keep_ref, gone_ref)
-
-
-def first_norm_back(place, gparts, grecvs, x0, dx1, gain, estimate):
+    middle = turned_ref.shape[0] // 2
+    keep_ref[...] = turned_ref[:middle, :]
+    gone_ref[:middle, :] = turned_ref[middle:, :].astype(F32)
+    for chip in range(8):
+        lanes = pl.ds(pl.multiple_of(place[chip] * LANES, LANES), LANES)
+        for row in range(2):
+            block_ref[chip : chip + 1, row * LANES : (row + 1) * LANES] = sums_ref[row : row + 1, lanes]
+    gone_ref[middle : middle + 8, :] = block_ref[...]
+    first = middle + 8
+    for rider_ref in rider_refs:
+        gone_ref[first : first + rider_ref.shape[0], :] = rider_ref[...]
+        first += rider_ref.shape[0]
+
+
+def first_norm_back(place, gparts, grecvs, x0, dx1, gain, estimate, riders=()):
     rows, width = x0.shape
-    operands = (*gparts, *grecvs, x0, dx1, gain)
+    operands = (*gparts, *grecvs, *riders, x0, dx1, gain)
+    extra = sum(v.shape[0] for v in riders)
     shapes = [
         jax.ShapeDtypeStruct((rows, width), BF16),
         jax.ShapeDtypeStruct((8, width), F32),
         jax.ShapeDtypeStruct((width // 2, rows), BF16),
-        jax.ShapeDtypeStruct((2, PART, rows), F32),
+        jax.ShapeDtypeStruct((width // 2 + 8 + extra, rows), F32),
+        jax.ShapeDtypeStruct((8, 2 * LANES), F32),
     ]
     return pl.pallas_call(
-        functools.partial(first_norm_back_kernel, parts=(len(gparts), len(grecvs))),
+        functools.partial(
+            first_norm_back_kernel, parts=(len(gparts), len(grecvs)), riders=len(riders)
+        ),
         grid_spec=pltpu.PrefetchScalarGridSpec(
             num_scalar_prefetch=1,
             grid=(1,),
@@ -639,10 +655,52 @@
     )(place, *operands)
 
 
-def pixel_grad_kernel(kinds, da_ref, db_ref, wspec_ref, wrgb_ref, pick_ref, out_ref):
-    item = pl.program_id(0)
+def pack_vectors_kernel(place, sa_ref, sb_ref, qa_ref, qb_ref, ba_ref, bb_ref, out_ref, *refs):
+    sums_ref, qv_ref, hidden_ref = refs
+    sums_ref[...] = sa_ref[...] + sb_ref[...]
+    qv_ref[...] = qa_ref[...] + qb_ref[...]
+    hidden_ref[...] = ba_ref[...] + bb_ref[...]
+    out_ref[...] = jnp.zeros_like(out_ref)
+    half = LANES // 2
+    for pos in range(8):
+        chip = place[pos]
+        lanes = pl.ds(pl.multiple_of(chip * LANES, LANES), LANES)
+        for row in range(4):
+            first = row % 2 * LANES
+            spot = 4 * pos + row // 2
+            out_ref[spot : spot + 1, first : first + LANES] = sums_ref[row : row + 1, lanes]
+        both = pl.ds(pl.multiple_of(chip // 2 * LANES, LANES), LANES)
+        spot = 4 * pos + 2
+        for row in range(2):
+            pair = qv_ref[row : row + 1, both]
+            own = jnp.where(chip % 2 == 0, pair[:, :half], pair[:, half:])
+            out_ref[spot : spot + 1, row * half : (row + 1) * half] = own
+        wide = pl.ds(pl.multiple_of(chip * 2 * LANES, 2 * LANES), 2 * LANES)
+        out_ref[spot + 1 : spot + 2, :] = hidden_ref[0:1, wide]
+
+
+def pack_vectors(place, sums, qv, hidden):
+    operands = (*sums, *qv, *hidden)
+    return pl.pallas_call(
+        pack_vectors_kernel,
+        grid_spec=pltpu.PrefetchScalarGridSpec(
+            num_scalar_prefetch=1,
+            grid=(1,),
+            in_specs=[whole(v.shape) for v in operands],
+            out_specs=whole((32, 2 * LANES)),
+            scratch_shapes=[pltpu.VMEM(v[0].shape, F32) for v in (sums, qv, hidden)],
+        ),
+        out_shape=jax.ShapeDtypeStruct((32, 2 * LANES), F32),
+        compiler_params=params(4),
+        cost_estimate=short_cost(),
+        name="pack_vectors",
+    )(place, *operands)
+
+
+def pixel_grad_kernel(kinds, grad_ref, wspec_ref, wrgb_ref, pick_ref, *refs, item):
+    out_ref = refs[-1]
     spectral = kinds[item] == 1
-    grad = jnp.where(item == 0, da_ref[...], db_ref[...])
+    grad = grad_ref[...]
     wide = wspec_ref.shape[0]
     cut = (wide // 2 + LANES - 1) // LANES * LANES
 
@@ -657,28 +715,30 @@
         out_ref[...] = nt(small, pick_ref[...]).astype(BF16)
 
 
-def pixel_grad(kinds, grad_a, grad_b, w_spectral, w_rgb, pick):
-    rows = grad_a.shape[0]
+def pixel_grad(kinds, grad, w_spectral, w_rgb, pick, item, items, filled=None):
+    rows = grad.shape[0]
     wide, width = w_spectral.shape
+    more = [] if filled is None else [filled]
     return pl.pallas_call(
-        pixel_grad_kernel,
+        functools.partial(pixel_grad_kernel, item=item),
         grid_spec=pltpu.PrefetchScalarGridSpec(
             num_scalar_prefetch=1,
-            grid=(2,),
+            grid=(1,),
             in_specs=[
-                whole(grad_a.shape),
-                whole(grad_b.shape),
+                whole(grad.shape),
                 whole(w_spectral.shape),
                 whole(w_rgb.shape),
                 whole(pick.shape),
-            ],
-            out_specs=pl.BlockSpec((rows, wide), lambda i, *_: (i, 0)),
+            ]
+            + [pl.BlockSpec(memory_space=pl.ANY)] * len(more),
+            out_specs=pl.BlockSpec((rows, wide), lambda i, *_: (item, 0)),
         ),
-        out_shape=jax.ShapeDtypeStruct((2 * rows, wide), BF16),
-        compiler_params=params(8),
+        out_shape=jax.ShapeDtypeStruct((items * rows, wide), BF16),
+        input_output_aliases={5: 0} if more else {},
+        compiler_params=params(12),
         cost_estimate=long_cost(),
         name="pixel_grad",
-    )(kinds, grad_a, grad_b, w_spectral, w_rgb, pick)
+    )(kinds, grad, w_spectral, w_rgb, pick, *more)
 
 
 def gather_left(keep_refs, gone_refs, first, left_ref):
@@ -688,6 +748,9 @@
     base = len(keep_refs) * rows
     for pos, gone_ref in enumerate(gone_refs):
         columns = slice(base + pos * rows, base + (pos + 1) * rows)
+        if len(gone_ref.shape) == 2:
+            left_ref[:, columns] = gone_ref[: left_ref.shape[0], :].astype(BF16)
+            continue
         for part in range(2):
             left_ref[part * PART : (part + 1) * PART, columns] = gone_ref[first + part].astype(BF16)
 
@@ -698,13 +761,14 @@
     half = LANES // 2
     for pos, block in enumerate(moves):
         out_ref = send_ref if pos < 4 else keep_ref
-        out_ref[pos % 4, :, columns] = total[block * half : (block + 1) * half]
+        out_ref[pos % 4, :half, columns] = total[block * half : (block + 1) * half]
 
 
 def plain_grad_kernel(
-    ka_ref, kb_ref, la_ref, lb_ref, ra_ref, rb_ref, oa_ref, ob_ref, send_ref, keep_ref, left_ref,
-    *, moves,
+    ka_ref, kb_ref, la_ref, lb_ref, ra_ref, rb_ref, oa_ref, ob_ref, *refs, moves, vectors
 ):
+    send_ref, keep_ref, left_ref = refs[-3:]
+
     @pl.when(pl.program_id(0) == 0)
     def _():
         gather_left((ka_ref, kb_ref), (la_ref, lb_ref), 0, left_ref)
@@ -713,9 +777,21 @@
         columns = slice(part * PART, (part + 1) * PART)
         rights = (ra_ref[:, columns], rb_ref[:, columns], oa_ref[part], ob_ref[part])
         emit(left_ref, rights, send_ref, keep_ref, moves, columns)
-
-
-def plain_grad(keeps, lefts, rights, others, moves, name, skip=0, columns=None, lead=0):
+    if vectors:
+        early_ref, sa_ref, sb_ref = refs[:3]
+        half = LANES // 2
+        middle = left_ref.shape[0]
+        late = sa_ref[...] + sb_ref[...] + (la_ref[middle:, :] + lb_ref[middle:, :])
+        for pos, block in enumerate(moves):
+            out_ref = send_ref if pos < 4 else keep_ref
+            out_ref[pos % 4, half:, :] = early_ref[block]
+
+            @pl.when(pl.program_id(0) == 0)
+            def _(out_ref=out_ref, pos=pos, block=block):
+                out_ref[pos % 4, half + 1 : half + 2, : late.shape[1]] = late[block : block + 1]
+
+
+def plain_grad(keeps, lefts, rights, others, moves, name, skip=0, columns=None, lead=0, vectors=()):
     half_width, rows = keeps[0][0].shape[-2:]
     columns = columns or rights[0].shape[1]
     wide = WIDE
@@ -729,21 +805,33 @@
 
     right = pl.BlockSpec((rows, wide * PART), lambda n: (0, n + base))
     other = pl.BlockSpec((wide, rows, PART), lambda n: (n + base + lead // wide, 0, 0))
-    out = pl.BlockSpec((4, half, wide * PART), lambda n: (0, 0, n))
-    shape = jax.ShapeDtypeStruct((4, half, columns), F32)
+    height = half + 8 if vectors else half
+    out = pl.BlockSpec((4, height, wide * PART), lambda n: (0, 0, n))
+    shape = jax.ShapeDtypeStruct((4, height, columns), F32)
+
+    def left_spec(array, item):
+        if array.ndim == 2:
+            return pl.BlockSpec((half_width + 8, rows), lambda n: (item, 0))
+        return pl.BlockSpec((2, PART, rows), lambda n: (item, 0, 0))
+
+    vector_specs = []
+    if vectors:
+        vector_specs = [pl.BlockSpec((8, 8, wide * PART), lambda n: (0, 0, n))]
+        vector_specs += [whole(v.shape) for v in vectors[1:]]
     return pl.pallas_call(
-        functools.partial(plain_grad_kernel, moves=moves),
+        functools.partial(plain_grad_kernel, moves=moves, vectors=bool(vectors)),
         grid=(columns // (wide * PART),),
         in_specs=[keep_spec(*k) for k in keeps]
-        + [pl.BlockSpec((2, PART, rows), lambda n, q=i: (q, 0, 0)) for _, i in lefts]
-        + [right, right, other, other],
+        + [left_spec(*v) for v in lefts]
+        + [right, right, other, other]
+        + vector_specs,
         out_specs=[out, out],
         scratch_shapes=[pltpu.VMEM((half_width, 4 * rows), BF16)],
         out_shape=[shape, shape],
         compiler_params=params(14),
         cost_estimate=short_cost(),
         name=name,
-    )(*[k for k, _ in keeps], *[v for v, _ in lefts], *rights, *others)
+    )(*[k for k, _ in keeps], *[v for v, _ in lefts], *rights, *others, *vectors)
 
 
 def attn_grad_kernel(
@@ -1012,70 +1100,80 @@
         order.mark(att_h.sent)
         fc1_h.step(order)
     arecv[1] = [send(order.tie(da1[1][0]))]
+    riders = ()
     for i in range(items):
         estimate = long_cost() if i == 0 else short_cost()
-        last[i] = first_norm_back(place, da1[i], arecv[i], x0[i], dx1[i], order.tie(g1), estimate)
+        last[i] = first_norm_back(
+            place, da1[i], arecv[i], x0[i], dx1[i], order.tie(g1), estimate, riders
+        )
         order.mark(last[i][0])
         if custom and i == 0:
             fc2_h.step(order)
+        if custom and i == 0:
+            cube = pack_vectors(order.tie(place), sums2, qvsum, b1sum)
+            order.mark(cube)
+            riders = (last[0][3], cube)
     summed = list(none)
-    gdx0 = [other(order.tie(last[0][3])), other(last[1][3])]
-    dx0, sums1, kdx0, _ = zip(*last)
-    pixels_grad = pixel_grad(order.tie(item_kinds), dx0[0], dx0[1], w_spectral, w_rgb, pick)
+    dx0, sums1, kdx0, gone, blocks = zip(*last)
+    pixels_grad = pixel_grad(order.tie(item_kinds), dx0[0], w_spectral, w_rgb, pick, 0, items)
     order.mark(pixels_grad)
     if custom:
         mid = mixed[0].shape[1] // 2
-        gdx0 = [order.tie(v) for v in gdx0]
-        sides = ([(kdx0[0], 0), (kdx0[1], 0)], [(gdx0[0], 0), (gdx0[1], 0)], mixed, gmix)
+        gdx0 = order.tie(other(gone[1]))
+        sides = ([(kdx0[0], 0), (kdx0[1], 0)], [(gdx0, 1), (gdx0, 0)], mixed, gmix)
         embx_h = Halving(*plain_grad(*sides, move_x, "embed_grad_a", 0, mid), X_FIRST, size)
         order.mark(embx_h.sent)
         sides[3][1] = order.tie(gmix[1])
-        embz_h = Halving(*plain_grad(*sides, move_z, "embed_grad_b", mid, mid), Z_FIRST, size)
+        cube = (cube + order.tie(gdx0)[-cube.shape[0] :]).reshape(8, 1, -1)
+        cube = jnp.pad(cube, ((0, 0), (0, 7), (0, 0)))
+        embz_h = Halving(
+            *plain_grad(*sides, move_z, "embed_grad_b", mid, mid, vectors=(cube, *blocks)),
+            Z_FIRST, size,
+        )
         order.mark(embz_h.sent)
+    pixels_grad = pixel_grad(
+        order.tie(item_kinds), dx0[1], w_spectral, w_rgb, pick, 1, items, pixels_grad
+    )
+    order.mark(pixels_grad)
+    if custom:
         fc1_h.step(order)
-
-    sums2, sums1, qvsum, b1sum = order.tie((sums2, sums1, qvsum, b1sum))
-    vec2 = sums2[0] + sums2[1]
-    vec1 = sums1[0] + sums1[1]
-    qv = qvsum[0] + qvsum[1]
-    b1s = b1sum[0] + b1sum[1]
-    pieces = [vec2[0], vec2[1], vec2[2], vec2[3], vec1[0], vec1[1], qv[0], qv[1], b1s[0]]
-    small = jnp.concatenate([v.reshape(size, -1) for v in pieces], 1)
-    if custom:
-        cube = small.reshape(2, 2, 2, 2, -1)
-        chip, core = lax.axis_index("dp") // 2, lax.axis_index("dp") % 2
-        for axis, bit in ((0, 4), (1, 2), (2, 1)):
-            cube = jnp.where((chip & bit) == 0, jnp.flip(cube, axis), cube)
-        cube = jnp.transpose(cube, (2, 1, 0, 3, 4)).reshape(8, 2, 1, -1)
-        kept = jnp.where(core == 0, cube[:, 0], cube[:, 1])
-        gone = jnp.where(core == 0, cube[:, 1], cube[:, 0])
-        order.mark(gone)
+        att_h.step(order)
         embz_h.step(order)
-        att_h.step(order)
+        embx_h.step(order)
         fc2_g = fc2_h.step(order)
         fc1_g = fc1_h.step(order)
     summed[0] = send(order.tie(ycot[0]))
     if custom:
-        gone = exchange(order.tie(gone), "dp", 1, size)
-        embx_h.step(order)
-        gone = order.tie(gone)
-        small_h = Halving(kept[:4] + gone[:4], kept[4:] + gone[4:], X_FIRST, size)
-        order.mark(small_h.sent)
+        embz_h.step(order)
+        att_h.step(order)
     summed[0] = settle(summed[0])
     summed[1] = send(order.tie(ycot[1]))
     if custom:
-        att_h.step(order)
-        small_h.step(order)
-        embz_h.step(order)
-        small_h.step(order)
         embx_h.step(order)
-        small = small_h.step(order)[0]
-        summed[1] = settle(summed[1])
+        embz_g = embz_h.step(order)
+    summed[1] = settle(summed[1])
+    block_out = jnp.concatenate(
+        [(x1[i] + (ycot[i] + summed[i] + fc2_bias)).astype(BF16) for i in range(items)], 0
+    )
+    order.mark(block_out)
+    if custom:
         att_g = att_h.step(order)
-        embz_g = embz_h.step(order)
         embx_g = embx_h.step(order)
+        shard = width // size
+        core = lax.axis_index("dp") % 2
+        spans = [(shard, row * LANES, LANES) for row in range(4)]
+        spans += [(shard, 4 * LANES + row * LANES // 2, LANES // 2) for row in range(2)]
+        spans += [(shard, 6 * LANES, 2 * LANES)]
+        spans += [(shard + 1, row * LANES, LANES) for row in range(2)]
+        outs = []
+        for row, first, length in spans:
+            low = embz_g[row, first : first + length // 2]
+            high = embz_g[row, first + length // 2 : first + length]
+            outs.append(jnp.where(core == 0, low, high))
+        ln2_g, ln2_b, ob_g, b2_g, q_g, v_g, b1_g, ln1_g, ln1_b = outs
+        embz_g = embz_g[:shard]
         emb_g = jnp.concatenate([embx_g, embz_g], 1)
-        att_g = att_g.reshape(4, width // size, -1)
+        att_g = att_g.reshape(4, shard, -1)
         qkv_grad = jnp.transpose(att_g[:3], (1, 0, 2))
         out_grad = att_g[3].T
     else:
@@ -1092,17 +1190,10 @@
             )
         )
         out_grad = scatter(both(dya, mix)).T
-        small = scatter(small)[0]
-    block_out = jnp.concatenate(
-        [(x1[i] + (ycot[i] + summed[i] + fc2_bias)).astype(BF16) for i in range(items)], 0
-    )
-    outs = []
-    start = 0
-    for v in pieces:
-        length = v.shape[0] // size
-        outs.append(small[start : start + length])
-        start += length
-    ln2_g, ln2_b, ob_g, b2_g, ln1_g, ln1_b, q_g, v_g, b1_g = outs
+        totals = [v[0] + v[1] for v in (sums2, qvsum, b1sum, sums1)]
+        rows_of = [(0, 0), (0, 1), (0, 2), (0, 3), (1, 0), (1, 1), (2, 0), (3, 0), (3, 1)]
+        outs = [scatter(totals[n][row]) for n, row in rows_of]
+        ln2_g, ln2_b, ob_g, b2_g, q_g, v_g, b1_g, ln1_g, ln1_b = outs
     spectral_grad = emb_g[:, :wide].T
     rgb_grad = emb_g[:, wide:].T
     return (

time: 352 us -> 345 us (0.980)
  starting transfers between devices: 43.2 us -> 37.3 us
  local copies, waits for them, and re-layouts: 13 us -> 8.95 us
  Pallas kernels: 95.4 us -> 99.3 us
    ppermute x44 -> x39, starting transfers between devices: 43.2 us -> 37.3 us  [exchange(): return lax.ppermute(values, axis, [(i, i ^ bit) for i in range(size)])]
    ppermute x44 -> x39, waiting for transfers between devices: 168 us -> 166 us  [exchange(): return lax.ppermute(values, axis, [(i, i ^ bit) for i in range(size)])]
    unnamed x110 -> x142, local copies, waits for them, and re-layouts: 8.29 us -> 6.81 us
    pallas_call x5 -> x7, Pallas kernels: 19.5 us -> 20.7 us  [the longest x4 14.9 us: plain_grad(): pl.pallas_call(functools.partial(plain_grad_kernel, moves=moves, vectors=...]
    add x17 -> x14, other arithmetic: 22.5 us -> 22.2 us  [step(): value = value + recv[first:first + count]]
  transfers between devices with their start and end apart: 44 -> 39, of which waited for: 17 -> 19; matrix products, arithmetic and copies ran while one was open for 8% -> 9% of each run, Pallas kernels for 26% -> 28%
where the time goes in v6:
time: 345 us; the launch traced here: 342 us
  waiting for transfers between devices  166 us (48%)
  Pallas kernels  99.3 us (29%)
  starting transfers between devices  37.3 us (11%)
  other arithmetic  28.5 us (8%)
  local copies, waits for them, and re-layouts  8.95 us (3%)
    ppermute x39, waiting for transfers between devices, exchange(): return lax.ppermute(values, axis, [(i, i ^ bit) for i in range(size)])  166 us
    ppermute x39, starting transfers between devices, exchange(): return lax.ppermute(values, axis, [(i, i ^ bit) for i in range(size)])  37.3 us
    add x14, other arithmetic, step(): value = value + recv[first:first + count]  22.2 us
    pallas_call x2, Pallas kernels, attn_backward(): pl.pallas_call(functools.partial(attn_backward_kernel, parts=(len(gparts)...  17.3 us
    pallas_call x2, Pallas kernels, mlp(): pl.pallas_call(mlp_kernel, grid_spec=pltpu.PrefetchScalarGridSpec(num_sca...  16.6 us
    pallas_call x4, Pallas kernels, plain_grad(): pl.pallas_call(functools.partial(plain_grad_kernel, moves=moves, vectors=...  14.9 us
    pallas_call x2, Pallas kernels, embed(): pl.pallas_call(functools.partial(embed_kernel, item=item), grid_spec=pltp...  9.99 us
    pallas_call x2, Pallas kernels, attn_forward(): pl.pallas_call(attn_forward_kernel, grid=(steps,), in_specs=[whole(part.s...  8.69 us
  transfers between devices with their start and end apart: 39, of which 19 were waited for; matrix products, arithmetic and copies ran while one was open for 9% of the time, Pallas kernels for 28%

profile of v6, /device:TPU:0, one launch (start us, length us, event | category | flops | bytes accessed | tf_op | source)
XLA Modules:
  0.0 342.0 jit_solution(9061166100850843477)
XLA Ops:
  0.7 5.1 %embed.2 = (f32[256,1024]{1,0:T(8,128)}, bf16[256,2048]{1,0:T(8,128)(2,1)}) custom-call(s32[2]{0:T(128)} %kinds.4, bf16[512,1664]{1,0:T(8,128)(2,1)} %pix_ref.3, bf16[1664,1024]{1,0:T(8,128)(2,1)} %wspec_ref.7, bf16[384,1024]{1,0:T(8,128)(2,1)} %wrgb_ref.7, bf16[1664,384]{1,0:T(8,128)(2,1)} %constant.50.clone.pick_ref), custom_call_target="tpu_custom_call" | custom-call | flops 1000 | bytes 1000 | tf_op jit(solution)/shard_map/embed/pallas_call | solution.py:242
  5.8 3.0 collective-permute-start
  8.9 4.9 %embed.3 = (f32[256,1024]{1,0:T(8,128)}, bf16[256,2048]{1,0:T(8,128)(2,1)}) custom-call(s32[2]{0:T(128)} %kinds.4, bf16[512,1664]{1,0:T(8,128)(2,1)} %pix_ref.3, bf16[1664,1024]{1,0:T(8,128)(2,1)} %wspec_ref.7, bf16[384,1024]{1,0:T(8,128)(2,1)} %wrgb_ref.7, bf16[1664,384]{1,0:T(8,128)(2,1)} %constant.50.clone.pick_ref), custom_call_target="tpu_custom_call" | custom-call | flops 1000 | bytes 1000 | tf_op jit(solution)/shard_map/embed/pallas_call | solution.py:242
  15.0 3.1 pack_pixels.2
  18.7 3.1 pack_pixels.3
  22.2 10.0 %collective-permute-done.recv_ref = f32[256,1024]{1,0:T(8,128)S(1)} collective-permute-done((f32[256,1024]{1,0:T(8,128)}, f32[256,1024]{1,0:T(8,128)S(1)}, u32[]{:S(2)}, u32[]{:S(2)}) %collective-permute-start) | collective-permute-done | bytes 1048608 | tf_op jit(solution)/shard_map/ppermute | solution.py:888
  32.2 1.7 collective-permute-start.1
  33.9 4.4 %attn_forward.2 = (f32[256,1024]{1,0:T(8,128)S(1)}, bf16[256,1024]{1,0:T(8,128)(2,1)S(1)}, bf16[3,256,512]{2,1,0:T(8,128)(2,1)S(1)}, bf16[256,512]{1,0:T(8,128)(2,1)S(1)}, f32[256,1024]{1,0:T(8,128)S(1)}) custom-call(f32[256,1024]{1,0:T(8,128)S(1)} %copy-done.46, f32[256,1024]{1,0:T(8,128)S(1)} %collective-permute-done.recv_ref, ...), custom_call_target="tpu_custom_call" | custom-call | flops 99999997952 | bytes 1000 | tf_op jit(solution)/shard_map/attn_forward/pallas_call | solution.py:330
  38.3 1.8 pack_attn.2
  40.8 15.7 %collective-permute-done.1.recv_ref = f32[256,1024]{1,0:T(8,128)S(1)} collective-permute-done((f32[256,1024]{1,0:T(8,128)S(1)}, f32[256,1024]{1,0:T(8,128)S(1)}, u32[]{:S(2)}, u32[]{:S(2)}) %collective-permute-start.1) | collective-permute-done | bytes 1048608 | tf_op jit(solution)/shard_map/ppermute | solution.py:888
  56.5 1.4 collective-permute-start.2
  58.0 4.3 %attn_forward.3 = (f32[256,1024]{1,0:T(8,128)S(1)}, bf16[256,1024]{1,0:T(8,128)(2,1)S(1)}, bf16[3,256,512]{2,1,0:T(8,128)(2,1)S(1)}, bf16[256,512]{1,0:T(8,128)(2,1)S(1)}, f32[256,1024]{1,0:T(8,128)S(1)}) custom-call(f32[256,1024]{1,0:T(8,128)S(1)} %copy-done.47, f32[256,1024]{1,0:T(8,128)S(1)} %collective-permute-done.1.recv_ref, ...), custom_call_target="tpu_custom_call" | custom-call | flops 99999997952 | bytes 1000 | tf_op jit(solution)/shard_map/attn_forward/pallas_call | solution.py:330
  64.1 15.8 %collective-permute-done.2.orecv_ref = f32[256,1024]{1,0:T(8,128)S(1)} collective-permute-done((f32[256,1024]{1,0:T(8,128)S(1)}, f32[256,1024]{1,0:T(8,128)S(1)}, u32[]{:S(2)}, u32[]{:S(2)}) %collective-permute-start.2) | collective-permute-done | bytes 1048608 | tf_op jit(solution)/shard_map/ppermute | solution.py:888
  79.9 1.3 collective-permute-start.6
  81.3 7.7 %mlp.2 = (f32[256,1024]{1,0:T(8,128)S(1)}, bf16[256,1024]{1,0:T(8,128)(2,1)}, bf16[256,2048]{1,0:T(8,128)(2,1)S(1)}, bf16[256,2048]{1,0:T(8,128)(2,1)S(1)}, f32[...) custom-call(s32[9]{0:T(128)S(1)} %pad_add_fusion.place, ...), custom_call_target="tpu_custom_call" | custom-call | flops 99999997952 | bytes 1000 | tf_op jit(solution)/shard_map/mlp/pallas_call | solution.py:536
  90.6 12.7 %collective-permute-done.6.orecv_ref = f32[256,1024]{1,0:T(8,128)S(1)} collective-permute-done((f32[256,1024]{1,0:T(8,128)S(1)}, f32[256,1024]{1,0:T(8,128)S(1)}, u32[]{:S(2)}, u32[]{:S(2)}) %collective-permute-start.6) | collective-permute-done | bytes 1048608 | tf_op jit(solution)/shard_map/ppermute | solution.py:888
  103.3 1.3 collective-permute-start.9
  104.6 8.9 %mlp.3 = (f32[256,1024]{1,0:T(8,128)S(1)}, bf16[256,1024]{1,0:T(8,128)(2,1)}, bf16[256,2048]{1,0:T(8,128)(2,1)S(1)}, bf16[256,2048]{1,0:T(8,128)(2,1)S(1)}, f32[...) custom-call(s32[9]{0:T(128)S(1)} %pad_add_fusion.place, ...), custom_call_target="tpu_custom_call" | custom-call | flops 99999997952 | bytes 1000 | tf_op jit(solution)/shard_map/mlp/pallas_call | solution.py:536
  114.7 1.9 mlp_out.2
  117.6 2.4 collective-permute-done.13.ob_ref
  120.0 4.1 %fc2_grad.1 = (f32[4,64,2048]{2,1,0:T(8,128)}, f32[4,64,2048]{2,1,0:T(8,128)S(1)}) custom-call(bf16[2,512,256]{2,1,0:T(8,128)(2,1)S(1)} %get-tuple-element.200.ka_ref.kb_ref, bf16[2,512,256]{2,1,0:T(8,128)(2,1)S(1)} %get-tuple-element.200.ka_ref.kb_ref, f32[4,256,256]{2,1,0:T(8,128)S(1)} %copy-done.9, f32[4,256,256]{2,1,0:T(8,128)S(1)} %copy-done.9, ...), custom_call_target="tpu_custom_call" | custom-call | flops 1000 | bytes 1000 | tf_op jit(solution)/shard_map/fc2_grad/pallas_call | solution.py:821
  125.0 4.4 %fc1_grad.1 = (f32[4,64,2048]{2,1,0:T(8,128)}, f32[4,64,2048]{2,1,0:T(8,128)S(1)}) custom-call(bf16[512,256]{1,0:T(8,128)(2,1)S(1)} %get-tuple-element.194.ka_ref, bf16[512,256]{1,0:T(8,128)(2,1)S(1)} %get-tuple-element.195.kb_ref, f32[10,256,256]{2,1,0:T(8,128)S(1)} %collective-permute-done.12.la_ref.oa_ref, ...), custom_call_target="tpu_custom_call" | custom-call | flops 1000 | bytes 1000 | tf_op jit(solution)/shard_map/fc1_grad/pallas_call | solution.py:821
  129.4 2.6 collective-permute-start.20
  132.5 8.1 %attn_backward.2 = (f32[256,1024]{1,0:T(8,128)S(1)}, bf16[256,1024]{1,0:T(8,128)(2,1)}, bf16[3,256,512]{2,1,0:T(8,128)(2,1)S(1)}, f32[8,1024]{1,0:T(8,128)S(1)},...) custom-call(s32[9]{0:T(128)S(1)} %pad_add_fusion.place, ...), custom_call_target="tpu_custom_call" | custom-call | flops 99999997952 | bytes 1000 | tf_op jit(solution)/shard_map/attn_backward/pallas_call | solution.py:446
  140.6 16.3 %collective-permute-done.15.refs_1_ = f32[256,1024]{1,0:T(8,128)S(1)} collective-permute-done((f32[256,1024]{1,0:T(8,128)}, f32[256,1024]{1,0:T(8,128)S(1)}, u32[]{:S(2)}, u32[]{:S(2)}) %collective-permute-start.15) | collective-permute-done | bytes 1048608 | tf_op jit(solution)/shard_map/ppermute | solution.py:888
  157.3 9.2 %attn_backward.3 = (f32[256,1024]{1,0:T(8,128)S(1)}, bf16[256,1024]{1,0:T(8,128)(2,1)}, bf16[3,256,512]{2,1,0:T(8,128)(2,1)S(1)}, f32[8,1024]{1,0:T(8,128)S(1)},...) custom-call(s32[9]{0:T(128)S(1)} %pad_add_fusion.place, ...), custom_call_target="tpu_custom_call" | custom-call | flops 99999997952 | bytes 1000 | tf_op jit(solution)/shard_map/attn_backward/pallas_call | solution.py:446
  167.0 2.6 mlp_out.3
  169.6 1.5 collective-permute-start.21
  172.1 1.4 slice_add_fusion.2
  173.4 1.8 collective-permute-start.23
  175.2 7.3 %attn_grad.1 = (f32[4,256,512]{2,1,0:T(8,128)}, f32[4,256,512]{2,1,0:T(8,128)S(1)}) custom-call(bf16[512,256]{1,0:T(8,128)(2,1)S(1)} %get-tuple-element.225.aa_ref, bf16[512,256]{1,0:T(8,128)(2,1)S(1)} %get-tuple-element.226.ab_ref, bf16[512,256]{1,0:T(8,128)(2,1)S(1)} %get-tuple-element.227.ya_ref, bf16[512,256]{1,0:T(8,128)(2,1)S(1)} %get-tuple-element.228.yb_ref, ...), custom_call_target="tpu_custom_call" | custom-call | flops 1000 | bytes 1000 | tf_op jit(solution)/shard_map/attn_grad/pallas_call | solution.py:872
  182.6 3.1 slice_add_fusion.1
  185.8 1.7 collective-permute-start.25
  188.3 2.2 first_norm_back.2
  190.5 9.8 %collective-permute-done.23 = f32[2,64,2048]{2,1,0:T(8,128)S(1)} collective-permute-done((f32[2,64,2048]{2,1,0:T(8,128)S(1)}, f32[2,64,2048]{2,1,0:T(8,128)S(1)}, u32[]{:S(2)}, u32[]{:S(2)}) %collective-permute-start.23) | collective-permute-done | bytes 1048608 | tf_op jit(solution)/shard_map/ppermute | solution.py:888
  200.3 2.3 slice_add_fusion.7
  202.6 1.9 collective-permute-start.29
  205.2 6.4 %collective-permute-done.22.refs_1_ = f32[256,1024]{1,0:T(8,128)S(1)} collective-permute-done((f32[256,1024]{1,0:T(8,128)S(1)}, f32[256,1024]{1,0:T(8,128)S(1)}, u32[]{:S(2)}, u32[]{:S(2)}) %collective-permute-start.22) | collective-permute-done | bytes 1048608 | tf_op jit(solution)/shard_map/ppermute | solution.py:888
  211.7 2.2 first_norm_back.3
  214.0 2.6 pixel_grad.2.refs_0_
  216.7 3.1 embed_grad_a.1
  222.8 3.3 embed_grad_b.1
  226.5 1.4 collective-permute-start.28
  227.9 2.5 pixel_grad.3
  230.4 1.4 slice_add_fusion.6
  231.9 2.1 collective-permute-start.30
  234.0 23.1 %collective-permute-done.26 = f32[4,256,512]{2,1,0:T(8,128)} collective-permute-done((f32[4,256,512]{2,1,0:T(8,128)}, f32[4,256,512]{2,1,0:T(8,128)}, u32[]{:S(2)}, u32[]{:S(2)}) %collective-permute-start.26) | collective-permute-done | bytes 2097184 | tf_op jit(solution)/shard_map/ppermute | solution.py:888
  257.1 2.5 slice_add_fusion
  260.0 6.2 %collective-permute-done.27 = f32[4,72,1024]{2,1,0:T(8,128)S(1)} collective-permute-done((f32[4,72,1024]{2,1,0:T(8,128)S(1)}, f32[4,72,1024]{2,1,0:T(8,128)S(1)}, u32[]{:S(2)}, u32[]{:S(2)}) %collective-permute-start.27) | collective-permute-done | bytes 1179680 | tf_op jit(solution)/shard_map/ppermute | solution.py:888
  267.2 1.4 collective-permute-start.31
  268.6 10.9 %collective-permute-done.28 = f32[4,64,1024]{2,1,0:T(8,128)S(1)} collective-permute-done((f32[4,64,1024]{2,1,0:T(8,128)S(1)}, f32[4,64,1024]{2,1,0:T(8,128)S(1)}, u32[]{:S(2)}, u32[]{:S(2)}) %collective-permute-start.28) | collective-permute-done | bytes 1048608 | tf_op jit(solution)/shard_map/ppermute | solution.py:888
  280.5 2.3 add_add_fusion.1
  282.8 2.1 add_add_fusion.2
  285.9 4.6 %collective-permute-done.31 = f32[2,72,1024]{2,1,0:T(8,128)} collective-permute-done((f32[2,72,1024]{2,1,0:T(8,128)}, f32[2,72,1024]{2,1,0:T(8,128)}, u32[]{:S(2)}, u32[]{:S(2)}) %collective-permute-start.31) | collective-permute-done | bytes 589856 | tf_op jit(solution)/shard_map/ppermute | solution.py:888
  290.6 1.1 slice_add_fusion.8
  291.7 2.6 collective-permute-start.35
  294.3 1.3 slice_add_fusion.4
  296.2 12.2 %collective-permute-done.33 = f32[256,1024]{1,0:T(8,128)} collective-permute-done((f32[256,1024]{1,0:T(8,128)}, f32[256,1024]{1,0:T(8,128)}, u32[]{:S(2)}, u32[]{:S(2)}) %collective-permute-start.33) | collective-permute-done | bytes 1048608 | tf_op jit(solution)/shard_map/ppermute | solution.py:888
  309.0 2.9 collective-permute-start.38
  311.9 13.8 %collective-permute-done.35 = f32[1,72,1024]{2,1,0:T(8,128)S(1)} collective-permute-done((f32[1,72,1024]{2,1,0:T(8,128)S(1)}, f32[1,72,1024]{2,1,0:T(8,128)S(1)}, u32[]{:S(2)}, u32[]{:S(2)}) %collective-permute-start.35) | collective-permute-done | bytes 294944 | tf_op jit(solution)/shard_map/ppermute | solution.py:888
  325.8 1.1 add_add_fusion.3
  329.5 2.3 add_convert_fusion.1
  332.9 4.1 %collective-permute-done.37 = f32[1,256,512]{2,1,0:T(8,128)S(1)} collective-permute-done((f32[1,256,512]{2,1,0:T(8,128)S(1)}, f32[1,256,512]{2,1,0:T(8,128)S(1)}, u32[]{:S(2)}, u32[]{:S(2)}) %collective-permute-start.37) | collective-permute-done | bytes 524320 | tf_op jit(solution)/shard_map/ppermute | solution.py:888
  337.0 1.4 add_add_fusion
  (216 shorter events, 28.2 us)
Async XLA Ops:
  5.8 26.4 %collective-permute-start = (f32[256,1024]{1,0:T(8,128)}, f32[256,1024]{1,0:T(8,128)S(1)}, u32[]{:S(2)}, u32[]{:S(2)}) collective-permute-start(f32[256,1024]{1,0:T(8,128)} %get-tuple-element.155.part_ref), channel_id=1, source_target_pairs={{0,1},{1,0},{2,3},{3,2},{4,5},{5,4},{6,7},{7,6},{8,9},{9,8},{10,11... | collective-permute-start | bytes 3145736 | tf_op jit(solution)/shard_map/ppermute | solution.py:888
  14.9 23.4 %collective-permute-start.3 = (f32[4,256,256]{2,1,0:T(8,128)S(1)}, f32[4,256,256]{2,1,0:T(8,128)S(1)}, u32[]{:S(2)}, u32[]{:S(2)}) collective-permute-start(f32[4,256,256]{2,1,0:T(8,128)S(1)} %get-tuple-element.159), channel_id=1, source_target_pairs={{0,2},{2,0},{4,6},{6,4},{8,10},{10,8},{12,14},{14,12},{16,18},{18,... | collective-permute-start | bytes 3145736 | tf_op jit(solution)/shard_map/ppermute | solution.py:888
  18.2 45.1 %collective-permute-start.4 = (f32[8,256,256]{2,1,0:T(8,128)}, f32[8,256,256]{2,1,0:T(8,128)}, u32[]{:S(2)}, u32[]{:S(2)}) collective-permute-start(f32[8,256,256]{2,1,0:T(8,128)} %pack_pixels.2), channel_id=1, source_target_pairs={{0,2},{2,0},{4,6},{6,4},{8,10},{10,8},{12,14},{14,12},{16,18},{18,... | collective-permute-start | bytes 6291464 | tf_op jit(solution)/shard_map/ppermute | solution.py:888
  21.8 41.4 %collective-permute-start.5 = (f32[8,256,256]{2,1,0:T(8,128)}, f32[8,256,256]{2,1,0:T(8,128)}, u32[]{:S(2)}, u32[]{:S(2)}) collective-permute-start(f32[8,256,256]{2,1,0:T(8,128)} %pack_pixels.3), channel_id=1, source_target_pairs={{0,2},{2,0},{4,6},{6,4},{8,10},{10,8},{12,14},{14,12},{16,18},{18,... | collective-permute-start | bytes 6291464 | tf_op jit(solution)/shard_map/ppermute | solution.py:888
  32.2 24.3 %collective-permute-start.1 = (f32[256,1024]{1,0:T(8,128)S(1)}, f32[256,1024]{1,0:T(8,128)S(1)}, u32[]{:S(2)}, u32[]{:S(2)}) collective-permute-start(f32[256,1024]{1,0:T(8,128)S(1)} %copy-done.47), channel_id=1, source_target_pairs={{0,1},{1,0},{2,3},{3,2},{4,5},{5,4},{6,7},{7,6},{8,9},{9,8},{10,11... | collective-permute-start | bytes 3145736 | tf_op jit(solution)/shard_map/ppermute | solution.py:888
  38.3 24.0 %copy-start.8 = (f32[4,256,256]{2,1,0:T(8,128)}, f32[4,256,256]{2,1,0:T(8,128)S(1)}, u32[]{:S(2)}) copy-start(f32[4,256,256]{2,1,0:T(8,128)S(1)} %collective-permute-done.3.la_ref.lb_ref) | copy-start | bytes 3145732
  40.8 49.2 %collective-permute-start.7 = (f32[4,256,256]{2,1,0:T(8,128)}, f32[4,256,256]{2,1,0:T(8,128)}, u32[]{:S(2)}, u32[]{:S(2)}) collective-permute-start(f32[4,256,256]{2,1,0:T(8,128)} %get-tuple-element.173), channel_id=1, source_target_pairs={{0,2},{2,0},{4,6},{6,4},{8,10},{10,8},{12,14},{14,12},{16,18},{18,... | collective-permute-start | bytes 3145736 | tf_op jit(solution)/shard_map/ppermute | solution.py:888
  56.5 23.4 %collective-permute-start.2 = (f32[256,1024]{1,0:T(8,128)S(1)}, f32[256,1024]{1,0:T(8,128)S(1)}, u32[]{:S(2)}, u32[]{:S(2)}) collective-permute-start(f32[256,1024]{1,0:T(8,128)S(1)} %get-tuple-element.168.opart_ref), channel_id=1, source_target_pairs={{0,1},{1,0},{2,3},{3,2},{4,5},{5,4},{6,7},{7,6},{8,9},{9,8},{10,11... | collective-permute-start | bytes 3145736 | tf_op jit(solution)/shard_map/ppermute | solution.py:888
  57.9 23.3 %copy-start.42 = (bf16[1024,2048]{1,0:T(8,128)(2,1)S(1)}, bf16[1024,2048]{1,0:T(8,128)(2,1)}, u32[]{:S(2)}) copy-start(bf16[1024,2048]{1,0:T(8,128)(2,1)} %wfc1_ref.3) | copy-start | bytes 12582916
  57.9 23.3 %copy-start.43 = (bf16[2048,1024]{1,0:T(8,128)(2,1)S(1)}, bf16[2048,1024]{1,0:T(8,128)(2,1)}, u32[]{:S(2)}) copy-start(bf16[2048,1024]{1,0:T(8,128)(2,1)} %wfc2_ref.7) | copy-start | bytes 12582916
  57.9 23.3 %copy-start.52 = (f32[2048]{0:T(1024)S(1)}, f32[2048]{0:T(1024)}, u32[]{:S(2)}) copy-start(f32[2048]{0:T(1024)} %param.36) | copy-start | bytes 24580
  57.9 23.3 %copy-start.54 = (f32[1024]{0:T(1024)S(1)}, f32[1024]{0:T(1024)}, u32[]{:S(2)}) copy-start(f32[1024]{0:T(1024)} %param.32) | copy-start | bytes 12292
  57.9 23.3 %copy-start.55 = (f32[1024]{0:T(1024)S(1)}, f32[1024]{0:T(1024)}, u32[]{:S(2)}) copy-start(f32[1024]{0:T(1024)} %param.34) | copy-start | bytes 12292
  58.0 23.3 %copy-start.56 = (f32[1024]{0:T(1024)S(1)}, f32[1024]{0:T(1024)}, u32[]{:S(2)}) copy-start(f32[1024]{0:T(1024)} %param.33) | copy-start | bytes 12292
  63.2 41.4 %copy-start.37 = (f32[256,1024]{1,0:T(8,128)}, f32[256,1024]{1,0:T(8,128)S(1)}, u32[]{:S(2)}) copy-start(f32[256,1024]{1,0:T(8,128)S(1)} %get-tuple-element.184.x0_ref.refs_4_) | copy-start | bytes 3145732
  64.0 26.0 %collective-permute-start.8 = (f32[4,256,256]{2,1,0:T(8,128)S(1)}, f32[4,256,256]{2,1,0:T(8,128)S(1)}, u32[]{:S(2)}, u32[]{:S(2)}) collective-permute-start(f32[4,256,256]{2,1,0:T(8,128)S(1)} %get-tuple-element.181), channel_id=1, source_target_pairs={{0,2},{2,0},{4,6},{6,4},{8,10},{10,8},{12,14},{14,12},{16,18},{18,... | collective-permute-start | bytes 3145736 | tf_op jit(solution)/shard_map/ppermute | solution.py:888
  79.9 23.3 %collective-permute-start.6 = (f32[256,1024]{1,0:T(8,128)S(1)}, f32[256,1024]{1,0:T(8,128)S(1)}, u32[]{:S(2)}, u32[]{:S(2)}) collective-permute-start(f32[256,1024]{1,0:T(8,128)S(1)} %get-tuple-element.185.opart_ref), channel_id=1, source_target_pairs={{0,1},{1,0},{2,3},{3,2},{4,5},{5,4},{6,7},{7,6},{8,9},{9,8},{10,11... | collective-permute-start | bytes 3145736 | tf_op jit(solution)/shard_map/ppermute | solution.py:888
  90.0 42.5 %copy-start.19 = (f32[256,1024]{1,0:T(8,128)}, f32[256,1024]{1,0:T(8,128)S(1)}, u32[]{:S(2)}) copy-start(f32[256,1024]{1,0:T(8,128)S(1)} %get-tuple-element.183.refs_4_) | copy-start | bytes 3145732
  90.0 23.5 %copy-start.25 = (f32[4,256,256]{2,1,0:T(8,128)}, f32[4,256,256]{2,1,0:T(8,128)S(1)}, u32[]{:S(2)}) copy-start(f32[4,256,256]{2,1,0:T(8,128)S(1)} %collective-permute-done.8.fb_ref) | copy-start | bytes 3145732
  90.0 24.7 %collective-permute-start.12 = (f32[10,256,256]{2,1,0:T(8,128)S(1)}, f32[10,256,256]{2,1,0:T(8,128)S(1)}, u32[]{:S(2)}, u32[]{:S(2)}) collective-permute-start(f32[10,256,256]{2,1,0:T(8,128)S(1)} %get-tuple-element.198), channel_id=1, source_target_pairs={{0,2},{2,0},{4,6},{6,4},{8,10},{10,8},{12,14},{14,12},{16,18},{18,... | collective-permute-start | bytes 7864328 | tf_op jit(solution)/shard_map/ppermute | solution.py:888
  90.1 24.6 %collective-permute-start.11 = (f32[8,256,256]{2,1,0:T(8,128)S(1)}, f32[8,256,256]{2,1,0:T(8,128)S(1)}, u32[]{:S(2)}, u32[]{:S(2)}) collective-permute-start(f32[8,256,256]{2,1,0:T(8,128)S(1)} %get-tuple-element.197), channel_id=1, source_target_pairs={{0,2},{2,0},{4,6},{6,4},{8,10},{10,8},{12,14},{14,12},{16,18},{18,... | collective-permute-start | bytes 6291464 | tf_op jit(solution)/shard_map/ppermute | solution.py:888
  103.3 10.8 %collective-permute-start.9 = (f32[96,1024]{1,0:T(8,128)S(1)}, f32[96,1024]{1,0:T(8,128)S(1)}, u32[]{:S(2)}, u32[]{:S(2)}) collective-permute-start(f32[96,1024]{1,0:T(8,128)S(1)} %get-tuple-element.191.refs_0_), channel_id=1, source_target_pairs={{0,1},{1,0},{2,3},{3,2},{4,5},{5,4},{6,7},{7,6},{8,9},{9,8},{10,11... | collective-permute-start | bytes 1179656 | tf_op jit(solution)/shard_map/ppermute | solution.py:888
  113.5 43.8 %copy-start.21 = (f32[256,1024]{1,0:T(8,128)}, f32[256,1024]{1,0:T(8,128)S(1)}, u32[]{:S(2)}) copy-start(f32[256,1024]{1,0:T(8,128)S(1)} %get-tuple-element.215.refs_2_) | copy-start | bytes 3145732
  113.5 6.4 %collective-permute-start.13 = (f32[8,256,256]{2,1,0:T(8,128)S(1)}, f32[8,256,256]{2,1,0:T(8,128)S(1)}, u32[]{:S(2)}, u32[]{:S(2)}) collective-permute-start(f32[8,256,256]{2,1,0:T(8,128)S(1)} %get-tuple-element.205), channel_id=1, source_target_pairs={{0,2},{2,0},{4,6},{6,4},{8,10},{10,8},{12,14},{14,12},{16,18},{18,... | collective-permute-start | bytes 6291464 | tf_op jit(solution)/shard_map/ppermute | solution.py:888
  113.5 11.5 %collective-permute-start.14 = (f32[10,256,256]{2,1,0:T(8,128)}, f32[10,256,256]{2,1,0:T(8,128)S(1)}, u32[]{:S(2)}, u32[]{:S(2)}) collective-permute-start(f32[10,256,256]{2,1,0:T(8,128)} %get-tuple-element.208), channel_id=1, source_target_pairs={{0,2},{2,0},{4,6},{6,4},{8,10},{10,8},{12,14},{14,12},{16,18},{18,... | collective-permute-start | bytes 7864328 | tf_op jit(solution)/shard_map/ppermute | solution.py:888
  114.0 17.9 %collective-permute-start.10 = (f32[160,1024]{1,0:T(8,128)S(1)}, f32[160,1024]{1,0:T(8,128)S(1)}, u32[]{:S(2)}, u32[]{:S(2)}) collective-permute-start(f32[160,1024]{1,0:T(8,128)S(1)} %get-tuple-element.193.refs_1_), channel_id=1, source_target_pairs={{0,1},{1,0},{2,3},{3,2},{4,5},{5,4},{6,7},{7,6},{8,9},{9,8},{10,11... | collective-permute-start | bytes 1966088 | tf_op jit(solution)/shard_map/ppermute | solution.py:888
  124.1 76.2 %copy-start.12 = (f32[4,64,2048]{2,1,0:T(8,128)}, f32[4,64,2048]{2,1,0:T(8,128)S(1)}, u32[]{:S(2)}) copy-start(f32[4,64,2048]{2,1,0:T(8,128)S(1)} %get-tuple-element.229) | copy-start | bytes 6291460
  124.1 48.0 %collective-permute-start.17 = (f32[4,64,2048]{2,1,0:T(8,128)}, f32[4,64,2048]{2,1,0:T(8,128)}, u32[]{:S(2)}, u32[]{:S(2)}) collective-permute-start(f32[4,64,2048]{2,1,0:T(8,128)} %get-tuple-element.207), channel_id=1, source_target_pairs={{0,4},{2,6},{4,0},{6,2},{8,12},{10,14},{12,8},{14,10},{16,20},{18,... | collective-permute-start | bytes 6291464 | tf_op jit(solution)/shard_map/ppermute | solution.py:888
  129.4 53.2 %copy-start.13 = (f32[4,64,2048]{2,1,0:T(8,128)}, f32[4,64,2048]{2,1,0:T(8,128)S(1)}, u32[]{:S(2)}) copy-start(f32[4,64,2048]{2,1,0:T(8,128)S(1)} %get-tuple-element.239) | copy-start | bytes 6291460
  129.4 53.2 %collective-permute-start.20 = (f32[4,64,2048]{2,1,0:T(8,128)}, f32[4,64,2048]{2,1,0:T(8,128)}, u32[]{:S(2)}, u32[]{:S(2)}) collective-permute-start(f32[4,64,2048]{2,1,0:T(8,128)} %get-tuple-element.212), channel_id=1, source_target_pairs={{0,8},{2,10},{4,12},{6,14},{8,0},{10,2},{12,4},{14,6},{16,24},{18,... | collective-permute-start | bytes 6291464 | tf_op jit(solution)/shard_map/ppermute | solution.py:888
  132.0 24.9 %collective-permute-start.15 = (f32[256,1024]{1,0:T(8,128)}, f32[256,1024]{1,0:T(8,128)S(1)}, u32[]{:S(2)}, u32[]{:S(2)}) collective-permute-start(f32[256,1024]{1,0:T(8,128)} %get-tuple-element.214.refs_0_), channel_id=1, source_target_pairs={{0,1},{1,0},{2,3},{3,2},{4,5},{5,4},{6,7},{7,6},{8,9},{9,8},{10,11... | collective-permute-start | bytes 3145736 | tf_op jit(solution)/shard_map/ppermute | solution.py:888
  132.5 24.9 %copy-start.62 = (bf16[3,256,512]{2,1,0:T(8,128)(2,1)S(1)}, bf16[3,256,512]{2,1,0:T(8,128)(2,1)}, u32[]{:S(2)}) copy-start(bf16[3,256,512]{2,1,0:T(8,128)(2,1)} %copy-done.61) | copy-start | bytes 2359300
  156.8 9.8 %collective-permute-start.16 = (f32[96,1024]{1,0:T(8,128)S(1)}, f32[96,1024]{1,0:T(8,128)S(1)}, u32[]{:S(2)}, u32[]{:S(2)}) collective-permute-start(f32[96,1024]{1,0:T(8,128)S(1)} %get-tuple-element.222.refs_0_), channel_id=1, source_target_pairs={{0,1},{1,0},{2,3},{3,2},{4,5},{5,4},{6,7},{7,6},{8,9},{9,8},{10,11... | collective-permute-start | bytes 1179656 | tf_op jit(solution)/shard_map/ppermute | solution.py:888
  166.5 8.7 %collective-permute-start.19 = (f32[8,256,256]{2,1,0:T(8,128)S(1)}, f32[8,256,256]{2,1,0:T(8,128)S(1)}, u32[]{:S(2)}, u32[]{:S(2)}) collective-permute-start(f32[8,256,256]{2,1,0:T(8,128)S(1)} %get-tuple-element.234), channel_id=1, source_target_pairs={{0,2},{2,0},{4,6},{6,4},{8,10},{10,8},{12,14},{14,12},{16,18},{18,... | collective-permute-start | bytes 6291464 | tf_op jit(solution)/shard_map/ppermute | solution.py:888
  166.6 8.6 %collective-permute-start.18 = (f32[8,256,256]{2,1,0:T(8,128)S(1)}, f32[8,256,256]{2,1,0:T(8,128)S(1)}, u32[]{:S(2)}, u32[]{:S(2)}) collective-permute-start(f32[8,256,256]{2,1,0:T(8,128)S(1)} %get-tuple-element.232), channel_id=1, source_target_pairs={{0,2},{2,0},{4,6},{6,4},{8,10},{10,8},{12,14},{14,12},{16,18},{18,... | collective-permute-start | bytes 6291464 | tf_op jit(solution)/shard_map/ppermute | solution.py:888
  169.6 18.2 %collective-permute-start.21 = (f32[160,1024]{1,0:T(8,128)S(1)}, f32[160,1024]{1,0:T(8,128)S(1)}, u32[]{:S(2)}, u32[]{:S(2)}) collective-permute-start(f32[160,1024]{1,0:T(8,128)S(1)} %get-tuple-element.243.refs_1_), channel_id=1, source_target_pairs={{0,1},{1,0},{2,3},{3,2},{4,5},{5,4},{6,7},{7,6},{8,9},{9,8},{10,11... | collective-permute-start | bytes 1966088 | tf_op jit(solution)/shard_map/ppermute | solution.py:888
  173.4 26.9 %collective-permute-start.23 = (f32[2,64,2048]{2,1,0:T(8,128)S(1)}, f32[2,64,2048]{2,1,0:T(8,128)S(1)}, u32[]{:S(2)}, u32[]{:S(2)}) collective-permute-start(f32[2,64,2048]{2,1,0:T(8,128)S(1)} %slice_add_fusion.2), channel_id=1, source_target_pairs={{0,8},{2,10},{4,12},{6,14},{8,0},{10,2},{12,4},{14,6},{16,24},{18,... | collective-permute-start | bytes 3145736 | tf_op jit(solution)/shard_map/ppermute | solution.py:888
  185.8 44.7 %collective-permute-start.25 = (f32[2,64,2048]{2,1,0:T(8,128)}, f32[2,64,2048]{2,1,0:T(8,128)}, u32[]{:S(2)}, u32[]{:S(2)}) collective-permute-start(f32[2,64,2048]{2,1,0:T(8,128)} %slice_add_fusion.1), channel_id=1, source_target_pairs={{0,4},{2,6},{4,0},{6,2},{8,12},{10,14},{12,8},{14,10},{16,20},{18,... | collective-permute-start | bytes 3145736 | tf_op jit(solution)/shard_map/ppermute | solution.py:888
  187.5 69.6 %collective-permute-start.26 = (f32[4,256,512]{2,1,0:T(8,128)}, f32[4,256,512]{2,1,0:T(8,128)}, u32[]{:S(2)}, u32[]{:S(2)}) collective-permute-start(f32[4,256,512]{2,1,0:T(8,128)} %get-tuple-element.240), channel_id=1, source_target_pairs={{0,4},{2,6},{4,0},{6,2},{8,12},{10,14},{12,8},{14,10},{16,20},{18,... | collective-permute-start | bytes 6291464 | tf_op jit(solution)/shard_map/ppermute | solution.py:888
  187.8 23.9 %collective-permute-start.22 = (f32[256,1024]{1,0:T(8,128)S(1)}, f32[256,1024]{1,0:T(8,128)S(1)}, u32[]{:S(2)}, u32[]{:S(2)}) collective-permute-start(f32[256,1024]{1,0:T(8,128)S(1)} %get-tuple-element.248.refs_0_), channel_id=1, source_target_pairs={{0,1},{1,0},{2,3},{3,2},{4,5},{5,4},{6,7},{7,6},{8,9},{9,8},{10,11... | collective-permute-start | bytes 3145736 | tf_op jit(solution)/shard_map/ppermute | solution.py:888
  188.3 25.6 %copy-start.10 = (bf16[384,1024]{1,0:T(8,128)(2,1)S(1)}, bf16[384,1024]{1,0:T(8,128)(2,1)}, u32[]{:S(2)}) copy-start(bf16[384,1024]{1,0:T(8,128)(2,1)} %wrgb_ref.7) | copy-start | bytes 2359300
  190.5 21.2 %copy-start.38 = (f32[256,1024]{1,0:T(8,128)S(1)}, f32[256,1024]{1,0:T(8,128)}, u32[]{:S(2)}) copy-start(f32[256,1024]{1,0:T(8,128)} %copy-done.37) | copy-start | bytes 3145732
  202.6 77.9 %collective-permute-start.29 = (f32[1,64,2048]{2,1,0:T(8,128)}, f32[1,64,2048]{2,1,0:T(8,128)}, u32[]{:S(2)}, u32[]{:S(2)}) collective-permute-start(f32[1,64,2048]{2,1,0:T(8,128)} %slice_add_fusion.7), channel_id=1, source_target_pairs={{0,16},{2,18},{4,20},{6,22},{8,24},{10,26},{12,28},{14,30},{16,0},... | collective-permute-start | bytes 1572872 | tf_op jit(solution)/shard_map/ppermute | solution.py:888
  213.9 2.8 collective-permute-start.24
  226.1 40.1 %copy-start.17 = (f32[4,72,1024]{2,1,0:T(8,128)}, f32[4,72,1024]{2,1,0:T(8,128)S(1)}, u32[]{:S(2)}) copy-start(f32[4,72,1024]{2,1,0:T(8,128)S(1)} %get-tuple-element.275) | copy-start | bytes 3538948
  226.1 40.1 %collective-permute-start.27 = (f32[4,72,1024]{2,1,0:T(8,128)S(1)}, f32[4,72,1024]{2,1,0:T(8,128)S(1)}, u32[]{:S(2)}, u32[]{:S(2)}) collective-permute-start(f32[4,72,1024]{2,1,0:T(8,128)S(1)} %get-tuple-element.271), channel_id=1, source_target_pairs={{0,8},{2,10},{4,12},{6,14},{8,0},{10,2},{12,4},{14,6},{16,24},{18,... | collective-permute-start | bytes 3538952 | tf_op jit(solution)/shard_map/ppermute | solution.py:888
  226.5 53.0 %collective-permute-start.28 = (f32[4,64,1024]{2,1,0:T(8,128)S(1)}, f32[4,64,1024]{2,1,0:T(8,128)S(1)}, u32[]{:S(2)}, u32[]{:S(2)}) collective-permute-start(f32[4,64,1024]{2,1,0:T(8,128)S(1)} %copy-done.49), channel_id=1, source_target_pairs={{0,4},{2,6},{4,0},{6,2},{8,12},{10,14},{12,8},{14,10},{16,20},{18,... | collective-permute-start | bytes 3145736 | tf_op jit(solution)/shard_map/ppermute | solution.py:888
  230.4 26.7 %copy-start.16 = (f32[4,256,512]{2,1,0:T(8,128)S(1)}, f32[4,256,512]{2,1,0:T(8,128)}, u32[]{:S(2)}) copy-start(f32[4,256,512]{2,1,0:T(8,128)} %copy-done.15) | copy-start | bytes 6291460
  231.9 50.9 %collective-permute-start.30 = (f32[1,64,2048]{2,1,0:T(8,128)S(1)}, f32[1,64,2048]{2,1,0:T(8,128)S(1)}, u32[]{:S(2)}, u32[]{:S(2)}) collective-permute-start(f32[1,64,2048]{2,1,0:T(8,128)S(1)} %slice_add_fusion.6), channel_id=1, source_target_pairs={{0,16},{2,18},{4,20},{6,22},{8,24},{10,26},{12,28},{14,30},{16,0},... | collective-permute-start | bytes 1572872 | tf_op jit(solution)/shard_map/ppermute | solution.py:888
  257.1 22.4 %copy-start.30 = (f32[4,64,1024]{2,1,0:T(8,128)S(1)}, f32[4,64,1024]{2,1,0:T(8,128)}, u32[]{:S(2)}) copy-start(f32[4,64,1024]{2,1,0:T(8,128)} %copy-done.29) | copy-start | bytes 3145732
  259.6 34.6 %collective-permute-start.32 = (f32[2,256,512]{2,1,0:T(8,128)}, f32[2,256,512]{2,1,0:T(8,128)}, u32[]{:S(2)}, u32[]{:S(2)}) collective-permute-start(f32[2,256,512]{2,1,0:T(8,128)} %slice_add_fusion), channel_id=1, source_target_pairs={{0,8},{2,10},{4,12},{6,14},{8,0},{10,2},{12,4},{14,6},{16,24},{18,... | collective-permute-start | bytes 3145736 | tf_op jit(solution)/shard_map/ppermute | solution.py:888
  267.2 23.4 %collective-permute-start.31 = (f32[2,72,1024]{2,1,0:T(8,128)}, f32[2,72,1024]{2,1,0:T(8,128)}, u32[]{:S(2)}, u32[]{:S(2)}) collective-permute-start(f32[2,72,1024]{2,1,0:T(8,128)} %slice_add_fusion.3), channel_id=1, source_target_pairs={{0,4},{2,6},{4,0},{6,2},{8,12},{10,14},{12,8},{14,10},{16,20},{18,... | collective-permute-start | bytes 1769480 | tf_op jit(solution)/shard_map/ppermute | solution.py:888
  284.9 23.5 %collective-permute-start.33 = (f32[256,1024]{1,0:T(8,128)}, f32[256,1024]{1,0:T(8,128)}, u32[]{:S(2)}, u32[]{:S(2)}) collective-permute-start(f32[256,1024]{1,0:T(8,128)} %mlp_out.3), channel_id=1, source_target_pairs={{0,1},{1,0},{2,3},{3,2},{4,5},{5,4},{6,7},{7,6},{8,9},{9,8},{10,11... | collective-permute-start | bytes 3145736 | tf_op jit(solution)/shard_map/ppermute | solution.py:888
  285.4 23.0 %copy-start.24 = (f32[256,1024]{1,0:T(8,128)S(1)}, f32[256,1024]{1,0:T(8,128)}, u32[]{:S(2)}) copy-start(f32[256,1024]{1,0:T(8,128)} %copy-done.23) | copy-start | bytes 3145732
  285.4 23.5 %copy-start.31 = (f32[4,64,1024]{2,1,0:T(8,128)S(1)}, f32[4,64,1024]{2,1,0:T(8,128)}, u32[]{:S(2)}) copy-start(f32[4,64,1024]{2,1,0:T(8,128)} %copy-done.29) | copy-start | bytes 3145732
  285.4 23.5 %copy-start.65 = (f32[4,64,1024]{2,1,0:T(8,128)S(1)}, f32[4,64,1024]{2,1,0:T(8,128)}, u32[]{:S(2)}) copy-start(f32[4,64,1024]{2,1,0:T(8,128)} %copy-done.64) | copy-start | bytes 3145732
  285.4 23.5 %collective-permute-start.34 = (f32[2,64,1024]{2,1,0:T(8,128)}, f32[2,64,1024]{2,1,0:T(8,128)S(1)}, u32[]{:S(2)}, u32[]{:S(2)}) collective-permute-start(f32[2,64,1024]{2,1,0:T(8,128)} %slice_add_fusion.5), channel_id=1, source_target_pairs={{0,8},{2,10},{4,12},{6,14},{8,0},{10,2},{12,4},{14,6},{16,24},{18,... | collective-permute-start | bytes 1572872 | tf_op jit(solution)/shard_map/ppermute | solution.py:888
  291.7 37.9 %copy-start.20 = (f32[256,1024]{1,0:T(8,128)S(1)}, f32[256,1024]{1,0:T(8,128)}, u32[]{:S(2)}) copy-start(f32[256,1024]{1,0:T(8,128)} %copy-done.19) | copy-start | bytes 3145732
  291.7 37.9 %copy-start.22 = (f32[256,1024]{1,0:T(8,128)S(1)}, f32[256,1024]{1,0:T(8,128)}, u32[]{:S(2)}) copy-start(f32[256,1024]{1,0:T(8,128)} %copy-done.21) | copy-start | bytes 3145732
  291.7 37.9 %copy-start.68 = (f32[1024]{0:T(1024)S(1)}, f32[1024]{0:T(1024)}, u32[]{:S(2)}) copy-start(f32[1024]{0:T(1024)} %param.38) | copy-start | bytes 12292
  291.7 34.1 %collective-permute-start.35 = (f32[1,72,1024]{2,1,0:T(8,128)S(1)}, f32[1,72,1024]{2,1,0:T(8,128)S(1)}, u32[]{:S(2)}, u32[]{:S(2)}) collective-permute-start(f32[1,72,1024]{2,1,0:T(8,128)S(1)} %slice_add_fusion.8), channel_id=1, source_target_pairs={{0,16},{2,18},{4,20},{6,22},{8,24},{10,26},{12,28},{14,30},{16,0},... | collective-permute-start | bytes 884744 | tf_op jit(solution)/shard_map/ppermute | solution.py:888
  295.6 41.4 %collective-permute-start.37 = (f32[1,256,512]{2,1,0:T(8,128)S(1)}, f32[1,256,512]{2,1,0:T(8,128)S(1)}, u32[]{:S(2)}, u32[]{:S(2)}) collective-permute-start(f32[1,256,512]{2,1,0:T(8,128)S(1)} %slice_add_fusion.4), channel_id=1, source_target_pairs={{0,16},{2,18},{4,20},{6,22},{8,24},{10,26},{12,28},{14,30},{16,0},... | collective-permute-start | bytes 1572872 | tf_op jit(solution)/shard_map/ppermute | solution.py:888
  308.5 21.1 %collective-permute-start.36 = (f32[256,1024]{1,0:T(8,128)S(1)}, f32[256,1024]{1,0:T(8,128)S(1)}, u32[]{:S(2)}, u32[]{:S(2)}) collective-permute-start(f32[256,1024]{1,0:T(8,128)S(1)} %copy-done.24), channel_id=1, source_target_pairs={{0,1},{1,0},{2,3},{3,2},{4,5},{5,4},{6,7},{7,6},{8,9},{9,8},{10,11... | collective-permute-start | bytes 3145736 | tf_op jit(solution)/shard_map/ppermute | solution.py:888
  309.0 31.0 %collective-permute-start.38 = (f32[1,64,1024]{2,1,0:T(8,128)S(1)}, f32[1,64,1024]{2,1,0:T(8,128)S(1)}, u32[]{:S(2)}, u32[]{:S(2)}) collective-permute-start(f32[1,64,1024]{2,1,0:T(8,128)S(1)} %slice_add_fusion.9), channel_id=1, source_target_pairs={{0,16},{2,18},{4,20},{6,22},{8,24},{10,26},{12,28},{14,30},{16,0},... | collective-permute-start | bytes 786440 | tf_op jit(solution)/shard_map/ppermute | solution.py:888
  (46 other events, 344.4 us)

commit v7 on v6

--- a/solution.py
+++ b/solution.py
@@ -761,7 +761,11 @@
     half = LANES // 2
     for pos, block in enumerate(moves):
         out_ref = send_ref if pos < 4 else keep_ref
-        out_ref[pos % 4, :half, columns] = total[block * half : (block + 1) * half]
+        value = total[block * half : (block + 1) * half]
+        if len(out_ref.shape) == 4:
+            out_ref[pos % 4, 0, :, columns] = value
+        else:
+            out_ref[pos % 4, :half, columns] = value
 
 
 def plain_grad_kernel(
@@ -791,7 +795,7 @@
                 out_ref[pos % 4, half + 1 : half + 2, : late.shape[1]] = late[block : block + 1]
 
 
-def plain_grad(keeps, lefts, rights, others, moves, name, skip=0, columns=None, lead=0, vectors=()):
+def plain_grad(keeps, lefts, rights, others, moves, name, skip=0, columns=None, lead=0, vectors=(), planes=1):
     half_width, rows = keeps[0][0].shape[-2:]
     columns = columns or rights[0].shape[1]
     wide = WIDE
@@ -808,6 +812,10 @@
     height = half + 8 if vectors else half
     out = pl.BlockSpec((4, height, wide * PART), lambda n: (0, 0, n))
     shape = jax.ShapeDtypeStruct((4, height, columns), F32)
+    if planes > 1:
+        per = columns // planes // (wide * PART)
+        out = pl.BlockSpec((4, 1, half, wide * PART), lambda n: (0, n // per, 0, n % per))
+        shape = jax.ShapeDtypeStruct((4, planes, half, columns // planes), F32)
 
     def left_spec(array, item):
         if array.ndim == 2:
@@ -834,54 +842,74 @@
     )(*[k for k, _ in keeps], *[v for v, _ in lefts], *rights, *others, *vectors)
 
 
-def attn_grad_kernel(
-    aa_ref, ab_ref, ya_ref, yb_ref, fa_ref, fb_ref, ba_ref, bb_ref, da_ref, db_ref, ma_ref, mb_ref,
+def query_key_kernel(
+    aa_ref, ab_ref, fa_ref, fb_ref, ba_ref, bb_ref, da_ref, db_ref, send_ref, keep_ref, left_ref,
+    *, moves,
+):
+    plane, step = pl.program_id(0), pl.program_id(1)
+
+    @pl.when((plane == 0) & (step == 0))
+    def _():
+        gather_left((aa_ref, ab_ref), (fa_ref, fb_ref), 0, left_ref)
+
+    spot = 2 + plane * pl.num_programs(1) + step
+    emit(left_ref, (da_ref[...], db_ref[...], ba_ref[spot], bb_ref[spot]), send_ref, keep_ref, moves)
+
+
+def value_out_kernel(
+    aa_ref, ab_ref, fa_ref, fb_ref, ba_ref, bb_ref, da_ref, db_ref, ya_ref, yb_ref, ma_ref, mb_ref,
     send_ref, keep_ref, left_ref, *, moves,
 ):
     plane, step = pl.program_id(0), pl.program_id(1)
-    steps = pl.num_programs(1)
 
     @pl.when((plane == 0) & (step == 0))
     def _():
         gather_left((aa_ref, ab_ref), (fa_ref, fb_ref), 0, left_ref)
 
-    @pl.when((plane == 3) & (step == 0))
+    @pl.when((plane == 1) & (step == 0))
     def _():
         gather_left((ya_ref, yb_ref), (ba_ref, bb_ref), 0, left_ref)
 
-    @pl.when(plane < 3)
-    def _():
-        spot = 2 + plane * steps + step
+    @pl.when(plane == 0)
+    def _():
+        spot = 2 + 2 * pl.num_programs(1) + step
         emit(left_ref, (da_ref[...], db_ref[...], ba_ref[spot], bb_ref[spot]), send_ref, keep_ref, moves)
 
-    @pl.when(plane == 3)
+    @pl.when(plane == 1)
     def _():
         spot = 2 + step
         emit(left_ref, (ma_ref[...], mb_ref[...], fa_ref[spot], fb_ref[spot]), send_ref, keep_ref, moves)
 
 
-def attn_grad(keep_a1, keep_dya, other_f, other_b, dqkv, mix, moves):
+def attn_grad(keep_a1, other_f, other_b, dqkv, moves, out_side=None):
     half_width, rows = keep_a1[0].shape
-    columns = mix[0].shape[1]
+    columns = dqkv[0].shape[2]
+    steps = columns // PART
     half = LANES // 2
     side = whole((half_width, rows))
-    plane = pl.BlockSpec((None, rows, PART), lambda p, n: (jnp.minimum(p, 2), 0, n))
-    mixed = pl.BlockSpec((rows, PART), lambda p, n: (0, n))
-    out = pl.BlockSpec((4, half, PART), lambda p, n: (0, p, n))
-    shape = jax.ShapeDtypeStruct((4, 4 * half, columns), F32)
+    specs = [side, side] + [whole(v.shape) for v in (*other_f, *other_b)]
+    if out_side is None:
+        kernel, name, more = query_key_kernel, "query_key_grad", []
+        plane = pl.BlockSpec((None, rows, PART), lambda p, n: (p, 0, n))
+        specs += [plane, plane]
+    else:
+        kernel, name, more = value_out_kernel, "value_out_grad", [*out_side[0], *out_side[1]]
+        plane = pl.BlockSpec((None, rows, PART), lambda p, n: (2, 0, n))
+        mixed = pl.BlockSpec((rows, PART), lambda p, n: (0, n))
+        specs += [plane, plane, side, side, mixed, mixed]
+    out = pl.BlockSpec((4, half, PART), lambda p, n: (0, 0, p * steps + n))
+    shape = jax.ShapeDtypeStruct((4, half, 2 * columns), F32)
     return pl.pallas_call(
-        functools.partial(attn_grad_kernel, moves=moves),
-        grid=(4, columns // PART),
-        in_specs=[side, side, side, side]
-        + [whole(v.shape) for v in (*other_f, *other_b)]
-        + [plane, plane, mixed, mixed],
+        functools.partial(kernel, moves=moves),
+        grid=(2, steps),
+        in_specs=specs,
         out_specs=[out, out],
         scratch_shapes=[pltpu.VMEM((half_width, 4 * rows), BF16)],
         out_shape=[shape, shape],
-        compiler_params=params(8),
+        compiler_params=params(12),
         cost_estimate=short_cost(),
-        name="attn_grad",
-    )(*keep_a1, *keep_dya, *other_f, *other_b, *dqkv, *mix)
+        name=name,
+    )(*keep_a1, *other_f, *other_b, *dqkv, *more)
 
 
 def exchange(values, axis, bit, size):
@@ -916,26 +944,35 @@
 
 
 class Halving:
-    def __init__(self, send, keep, bits, size):
+    def __init__(self, send, keep, bits, size, first=True):
         self.keep, self.bits, self.size = keep, bits, size
-        self.recvs = [exchange(send, "dp", bits[0], size)]
+        self.unit = keep.shape[0] // 4
+        self.recvs = [exchange(send, "dp", bits[0], size)] if first else []
         self.left = keep.shape[0]
         self.sent = send
 
-    def step(self, order):
-        self.recvs[-1] = order.tie(self.recvs[-1])
+    def value(self, order, tie=True):
+        if tie:
+            self.recvs[-1] = order.tie(self.recvs[-1])
         left = self.left
-        count = max(left // 2, 1)
+        count = max(left // 2, self.unit)
         total = self.keep.shape[0] - left
         value = self.keep[total : total + count]
         for recv in self.recvs:
             first = recv.shape[0] - left
             value = value + recv[first : first + count]
         order.mark(value)
-        if left == 1:
-            return value[0]
-        self.recvs.append(exchange(value, "dp", self.bits[len(self.recvs)], self.size))
-        self.left = left // 2
+        return value
+
+    def came(self, recv):
+        self.recvs.append(recv)
+        self.left = self.left // 2
+
+    def step(self, order):
+        value = self.value(order)
+        if self.left == self.unit:
+            return value[0] if self.unit == 1 else value
+        self.came(exchange(value, "dp", self.bits[len(self.recvs)], self.size))
         return None
 
 
@@ -1069,12 +1106,12 @@
         )
         order.mark(fc2_h.sent)
         gpre[1] = order.tie(gpre[1])
-        fc1_h = Halving(
-            *plain_grad(
-                [(ka2[0], 0), (ka2[1], 0)], [(gpre[0], 0), (gpre[1], 0)], dpre, gpre, move_z, "fc1_grad", lead=2
-            ),
-            Z_FIRST, size,
+        fc1_s = plain_grad(
+            [(ka2[0], 0), (ka2[1], 0)], [(gpre[0], 0), (gpre[1], 0)], dpre, gpre, move_z, "fc1_grad",
+            lead=2, planes=2,
         )
+        fc1_s = [v.reshape(8, *v.shape[2:]) for v in fc1_s]
+        fc1_h = Halving(*fc1_s, Z_FIRST, size)
         order.mark(fc1_h.sent)
     grecv[1] = [send(order.tie(da2[1][0]))]
     for i in range(items):
@@ -1094,11 +1131,17 @@
     if custom:
         fc2_h.step(order)
         gbwd = [order.tie(v) for v in gbwd]
-        att_h = Halving(
-            *attn_grad([v[0] for v in pk], kdya, gfwd, gbwd, dqkv, mix, move_x), X_FIRST, size
+        keep_a1 = [v[0] for v in pk]
+        attx_h = Halving(*attn_grad(keep_a1, gfwd, gbwd, dqkv, move_x), X_FIRST, size, first=False)
+        order.mark(attx_h.sent)
+        both_x = jnp.concatenate([fc1_h.value(order), attx_h.sent], 0)
+        order.mark(both_x)
+        gbwd[1] = order.tie(gbwd[1])
+        both_x = exchange(both_x, "dp", 2, size)
+        attz_h = Halving(
+            *attn_grad(keep_a1, gfwd, gbwd, dqkv, move_z, (kdya, mix)), Z_FIRST, size
         )
-        order.mark(att_h.sent)
-        fc1_h.step(order)
+        order.mark(attz_h.sent)
     arecv[1] = [send(order.tie(da1[1][0]))]
     riders = ()
     for i in range(items):
@@ -1114,6 +1157,7 @@
             order.mark(cube)
             riders = (last[0][3], cube)
     summed = list(none)
+    summed[0] = send(order.tie(ycot[0]))
     dx0, sums1, kdx0, gone, blocks = zip(*last)
     pixels_grad = pixel_grad(order.tie(item_kinds), dx0[0], w_spectral, w_rgb, pick, 0, items)
     order.mark(pixels_grad)
@@ -1136,20 +1180,29 @@
     )
     order.mark(pixels_grad)
     if custom:
-        fc1_h.step(order)
-        att_h.step(order)
+        both_x = order.tie(both_x)
+        fc1_h.came(both_x[:4])
+        attx_h.recvs.append(both_x[4:])
+        fc1_v = fc1_h.value(order, False)
+        attx_v = attx_h.value(order, False)
+    summed[0] = settle(summed[0])
+    if custom:
+        fc1_h.came(exchange(fc1_v, "dp", 8, size))
+        attx_h.came(exchange(attx_v, "dp", 4, size))
+        attz_h.step(order)
+        fc2_g = fc2_h.step(order)
+        attz_h.step(order)
         embz_h.step(order)
-        embx_h.step(order)
-        fc2_g = fc2_h.step(order)
         fc1_g = fc1_h.step(order)
-    summed[0] = send(order.tie(ycot[0]))
-    if custom:
-        embz_h.step(order)
-        att_h.step(order)
-    summed[0] = settle(summed[0])
     summed[1] = send(order.tie(ycot[1]))
     if custom:
         embx_h.step(order)
+        attx_h.step(order)
+        embz_h.step(order)
+        attz_g = attz_h.step(order)
+    if custom:
+        embx_h.step(order)
+        attx_g = attx_h.step(order)
         embz_g = embz_h.step(order)
     summed[1] = settle(summed[1])
     block_out = jnp.concatenate(
@@ -1157,7 +1210,6 @@
     )
     order.mark(block_out)
     if custom:
-        att_g = att_h.step(order)
         embx_g = embx_h.step(order)
         shard = width // size
         core = lax.axis_index("dp") % 2
@@ -1173,9 +1225,11 @@
         ln2_g, ln2_b, ob_g, b2_g, q_g, v_g, b1_g, ln1_g, ln1_b = outs
         embz_g = embz_g[:shard]
         emb_g = jnp.concatenate([embx_g, embz_g], 1)
-        att_g = att_g.reshape(4, shard, -1)
-        qkv_grad = jnp.transpose(att_g[:3], (1, 0, 2))
-        out_grad = att_g[3].T
+        cut = attx_g.shape[1] // 2
+        planes = [attx_g[:, :cut], attx_g[:, cut:], attz_g[:, :cut]]
+        qkv_grad = jnp.transpose(jnp.stack(planes), (1, 0, 2))
+        out_grad = attz_g[:, cut:].T
+        fc1_g = jnp.concatenate([fc1_g[0], fc1_g[1]], 1)
     else:
         cot = [cotangent[i * rows : (i + 1) * rows] for i in range(items)]
         fc2_g = scatter(both(cot, act))

time: 345 us -> 332 us (0.962)
  waiting for transfers between devices: 166 us -> 145 us
  starting transfers between devices: 37.3 us -> 42.4 us
    ppermute x39 -> x41, waiting for transfers between devices: 166 us -> 145 us  [exchange(): return lax.ppermute(values, axis, [(i, i ^ bit) for i in range(size)])]
    ppermute x39 -> x41, starting transfers between devices: 37.3 us -> 42.4 us  [exchange(): return lax.ppermute(values, axis, [(i, i ^ bit) for i in range(size)])]
    unnamed x142 -> x144, local copies, waits for them, and re-layouts: 6.81 us -> 8.68 us
    add x14 -> x16, other arithmetic: 22.2 us -> 20.9 us  [value(): value = value + recv[first:first + count]]
    pallas_call x1 -> x2, Pallas kernels: 7.34 us -> 8.38 us  [attn_grad(): pl.pallas_call(functools.partial(kernel, moves=moves), grid=(2, steps), i...]
  transfers between devices with their start and end apart: 39 -> 41, of which waited for: 19 -> 20; matrix products, arithmetic and copies ran while one was open for 9% -> 10% of each run, Pallas kernels for 28% -> 28%
where the time goes in v7:
time: 332 us; the launch traced here: 329 us
  waiting for transfers between devices  145 us (44%)
  Pallas kernels  98.2 us (30%)
  starting transfers between devices  42.4 us (13%)
  other arithmetic  30.4 us (9%)
  local copies, waits for them, and re-layouts  11.2 us (3%)
    ppermute x41, waiting for transfers between devices, exchange(): return lax.ppermute(values, axis, [(i, i ^ bit) for i in range(size)])  145 us
    ppermute x41, starting transfers between devices, exchange(): return lax.ppermute(values, axis, [(i, i ^ bit) for i in range(size)])  42.4 us
    add x16, other arithmetic, value(): value = value + recv[first:first + count]  20.9 us
    pallas_call x2, Pallas kernels, attn_backward(): pl.pallas_call(functools.partial(attn_backward_kernel, parts=(len(gparts)...  16.2 us
    pallas_call x4, Pallas kernels, plain_grad(): pl.pallas_call(functools.partial(plain_grad_kernel, moves=moves, vectors=...  15.6 us
    pallas_call x2, Pallas kernels, mlp(): pl.pallas_call(mlp_kernel, grid_spec=pltpu.PrefetchScalarGridSpec(num_sca...  15.2 us
    pallas_call x2, Pallas kernels, embed(): pl.pallas_call(functools.partial(embed_kernel, item=item), grid_spec=pltp...  9.92 us
    unnamed x144, local copies, waits for them, and re-layouts  8.68 us
  transfers between devices with their start and end apart: 41, of which 20 were waited for; matrix products, arithmetic and copies ran while one was open for 10% of the time, Pallas kernels for 28%

profile of v7, /device:TPU:0, one launch (start us, length us, event | category | flops | bytes accessed | tf_op | source)
XLA Modules:
  0.0 328.7 jit_solution(5851322656845070143)
XLA Ops:
  0.7 5.0 %embed.2 = (f32[256,1024]{1,0:T(8,128)}, bf16[256,2048]{1,0:T(8,128)(2,1)}) custom-call(s32[2]{0:T(128)} %kinds.4, bf16[512,1664]{1,0:T(8,128)(2,1)} %pix_ref.3, bf16[1664,1024]{1,0:T(8,128)(2,1)} %wspec_ref.7, bf16[384,1024]{1,0:T(8,128)(2,1)} %wrgb_ref.7, bf16[1664,384]{1,0:T(8,128)(2,1)} %constant.50.clone.pick_ref), custom_call_target="tpu_custom_call" | custom-call | flops 1000 | bytes 1000 | tf_op jit(solution)/shard_map/embed/pallas_call | solution.py:242
  5.7 3.0 collective-permute-start
  8.8 4.9 %embed.3 = (f32[256,1024]{1,0:T(8,128)}, bf16[256,2048]{1,0:T(8,128)(2,1)}) custom-call(s32[2]{0:T(128)} %kinds.4, bf16[512,1664]{1,0:T(8,128)(2,1)} %pix_ref.3, bf16[1664,1024]{1,0:T(8,128)(2,1)} %wspec_ref.7, bf16[384,1024]{1,0:T(8,128)(2,1)} %wrgb_ref.7, bf16[1664,384]{1,0:T(8,128)(2,1)} %constant.50.clone.pick_ref), custom_call_target="tpu_custom_call" | custom-call | flops 1000 | bytes 1000 | tf_op jit(solution)/shard_map/embed/pallas_call | solution.py:242
  15.0 3.1 pack_pixels.2
  18.6 3.1 pack_pixels.3
  22.1 9.7 %collective-permute-done.recv_ref = f32[256,1024]{1,0:T(8,128)S(1)} collective-permute-done((f32[256,1024]{1,0:T(8,128)}, f32[256,1024]{1,0:T(8,128)S(1)}, u32[]{:S(2)}, u32[]{:S(2)}) %collective-permute-start) | collective-permute-done | bytes 1048608 | tf_op jit(solution)/shard_map/ppermute | solution.py:916
  31.8 1.7 collective-permute-start.1
  33.6 4.3 %attn_forward.2 = (f32[256,1024]{1,0:T(8,128)S(1)}, bf16[256,1024]{1,0:T(8,128)(2,1)S(1)}, bf16[3,256,512]{2,1,0:T(8,128)(2,1)S(1)}, bf16[256,512]{1,0:T(8,128)(2,1)S(1)}, f32[256,1024]{1,0:T(8,128)S(1)}) custom-call(f32[256,1024]{1,0:T(8,128)S(1)} %copy-done.49, f32[256,1024]{1,0:T(8,128)S(1)} %collective-permute-done.recv_ref, ...), custom_call_target="tpu_custom_call" | custom-call | flops 99999997952 | bytes 1000 | tf_op jit(solution)/shard_map/attn_forward/pallas_call | solution.py:330
  37.9 1.8 pack_attn.2
  40.4 15.4 %collective-permute-done.1.recv_ref = f32[256,1024]{1,0:T(8,128)S(1)} collective-permute-done((f32[256,1024]{1,0:T(8,128)S(1)}, f32[256,1024]{1,0:T(8,128)S(1)}, u32[]{:S(2)}, u32[]{:S(2)}) %collective-permute-start.1) | collective-permute-done | bytes 1048608 | tf_op jit(solution)/shard_map/ppermute | solution.py:916
  55.8 1.4 collective-permute-start.2
  57.3 4.3 %attn_forward.3 = (f32[256,1024]{1,0:T(8,128)S(1)}, bf16[256,1024]{1,0:T(8,128)(2,1)S(1)}, bf16[3,256,512]{2,1,0:T(8,128)(2,1)S(1)}, bf16[256,512]{1,0:T(8,128)(2,1)S(1)}, f32[256,1024]{1,0:T(8,128)S(1)}) custom-call(f32[256,1024]{1,0:T(8,128)S(1)} %copy-done.51, f32[256,1024]{1,0:T(8,128)S(1)} %collective-permute-done.1.recv_ref, ...), custom_call_target="tpu_custom_call" | custom-call | flops 99999997952 | bytes 1000 | tf_op jit(solution)/shard_map/attn_forward/pallas_call | solution.py:330
  62.6 16.6 %collective-permute-done.2.orecv_ref = f32[256,1024]{1,0:T(8,128)S(1)} collective-permute-done((f32[256,1024]{1,0:T(8,128)S(1)}, f32[256,1024]{1,0:T(8,128)S(1)}, u32[]{:S(2)}, u32[]{:S(2)}) %collective-permute-start.2) | collective-permute-done | bytes 1048608 | tf_op jit(solution)/shard_map/ppermute | solution.py:916
  79.1 1.4 collective-permute-start.6
  80.6 7.6 %mlp.2 = (f32[256,1024]{1,0:T(8,128)S(1)}, bf16[256,1024]{1,0:T(8,128)(2,1)}, bf16[256,2048]{1,0:T(8,128)(2,1)S(1)}, bf16[256,2048]{1,0:T(8,128)(2,1)S(1)}, f32[...) custom-call(s32[9]{0:T(128)S(1)} %pad_add_fusion.place, ...), custom_call_target="tpu_custom_call" | custom-call | flops 99999997952 | bytes 1000 | tf_op jit(solution)/shard_map/mlp/pallas_call | solution.py:536
  90.6 11.8 %collective-permute-done.6.orecv_ref = f32[256,1024]{1,0:T(8,128)S(1)} collective-permute-done((f32[256,1024]{1,0:T(8,128)S(1)}, f32[256,1024]{1,0:T(8,128)S(1)}, u32[]{:S(2)}, u32[]{:S(2)}) %collective-permute-start.6) | collective-permute-done | bytes 1048608 | tf_op jit(solution)/shard_map/ppermute | solution.py:916
  102.5 1.4 collective-permute-start.9
  103.9 7.6 %mlp.3 = (f32[256,1024]{1,0:T(8,128)S(1)}, bf16[256,1024]{1,0:T(8,128)(2,1)}, bf16[256,2048]{1,0:T(8,128)(2,1)S(1)}, bf16[256,2048]{1,0:T(8,128)(2,1)S(1)}, f32[...) custom-call(s32[9]{0:T(128)S(1)} %pad_add_fusion.place, ...), custom_call_target="tpu_custom_call" | custom-call | flops 99999997952 | bytes 1000 | tf_op jit(solution)/shard_map/mlp/pallas_call | solution.py:536
  113.5 1.8 mlp_out.2
  116.3 4.0 %fc2_grad.1 = (f32[4,64,2048]{2,1,0:T(8,128)}, f32[4,64,2048]{2,1,0:T(8,128)S(1)}) custom-call(bf16[2,512,256]{2,1,0:T(8,128)(2,1)S(1)} %get-tuple-element.205.ka_ref.kb_ref, bf16[2,512,256]{2,1,0:T(8,128)(2,1)S(1)} %get-tuple-element.205.ka_ref.kb_ref, f32[4,256,256]{2,1,0:T(8,128)S(1)} %copy-done.9, f32[4,256,256]{2,1,0:T(8,128)S(1)} %copy-done.9, ...), custom_call_target="tpu_custom_call" | custom-call | flops 1000 | bytes 1000 | tf_op jit(solution)/shard_map/fc2_grad/pallas_call | solution.py:829
  120.3 2.4 collective-permute-start.17
  122.7 4.5 %fc1_grad.1 = (f32[4,2,64,1024]{3,2,1,0:T(8,128)}, f32[4,2,64,1024]{3,2,1,0:T(8,128)S(1)}) custom-call(bf16[512,256]{1,0:T(8,128)(2,1)S(1)} %get-tuple-element.199.ka_ref, bf16[512,256]{1,0:T(8,128)(2,1)S(1)} %get-tuple-element.200.kb_ref, f32[10,256,256]{2,1,0:T(8,128)S(1)} %collective-permute-done.12.la_ref.oa_ref, ...), custom_call_target="tpu_custom_call" | custom-call | flops 1000 | bytes 1000 | tf_op jit(solution)/shard_map/fc1_grad/pallas_call | solution.py:829
  129.6 8.1 %attn_backward.2 = (f32[256,1024]{1,0:T(8,128)S(1)}, bf16[256,1024]{1,0:T(8,128)(2,1)}, bf16[3,256,512]{2,1,0:T(8,128)(2,1)S(1)}, f32[8,1024]{1,0:T(8,128)S(1)},...) custom-call(s32[9]{0:T(128)S(1)} %pad_add_fusion.place, ...), custom_call_target="tpu_custom_call" | custom-call | flops 99999997952 | bytes 1000 | tf_op jit(solution)/shard_map/attn_backward/pallas_call | solution.py:446
  139.7 13.3 %collective-permute-done.15.refs_1_ = f32[256,1024]{1,0:T(8,128)S(1)} collective-permute-done((f32[256,1024]{1,0:T(8,128)S(1)}, f32[256,1024]{1,0:T(8,128)S(1)}, u32[]{:S(2)}, u32[]{:S(2)}) %collective-permute-start.15) | collective-permute-done | bytes 1048608 | tf_op jit(solution)/shard_map/ppermute | solution.py:916
  153.8 8.1 %attn_backward.3 = (f32[256,1024]{1,0:T(8,128)S(1)}, bf16[256,1024]{1,0:T(8,128)(2,1)}, bf16[3,256,512]{2,1,0:T(8,128)(2,1)S(1)}, f32[8,1024]{1,0:T(8,128)S(1)},...) custom-call(s32[9]{0:T(128)S(1)} %pad_add_fusion.place, ...), custom_call_target="tpu_custom_call" | custom-call | flops 99999997952 | bytes 1000 | tf_op jit(solution)/shard_map/attn_backward/pallas_call | solution.py:446
  162.4 2.5 mlp_out.3
  166.1 2.4 collective-permute-done.17
  168.5 1.4 slice_add_fusion
  170.9 3.6 %query_key_grad.1 = (f32[4,64,1024]{2,1,0:T(8,128)S(1)}, f32[4,64,1024]{2,1,0:T(8,128)S(1)}) custom-call(bf16[512,256]{1,0:T(8,128)(2,1)S(1)} %get-tuple-element.230.aa_ref, bf16[512,256]{1,0:T(8,128)(2,1)S(1)} %get-tuple-element.231.ab_ref, f32[4,256,256]{2,1,0:T(8,128)} %collective-permute-done.7.fa_ref, f32[4,256,256]{2,1,0:T(8,128)S(1)} %copy-done.11, ...), custom_call_target="tpu_custom_call" | custom-call | flops 1000 | bytes 1000 | tf_op jit(solution)/shard_map/query_key_grad/pallas_call | solution.py:902
  174.5 1.6 collective-permute-done.21
  176.1 1.4 bitcast_add_fusion
  177.5 1.6 pad_maximum_fusion
  179.1 4.8 %value_out_grad.1 = (f32[4,64,1024]{2,1,0:T(8,128)}, f32[4,64,1024]{2,1,0:T(8,128)S(1)}) custom-call(bf16[512,256]{1,0:T(8,128)(2,1)S(1)} %get-tuple-element.230.aa_ref, bf16[512,256]{1,0:T(8,128)(2,1)S(1)} %get-tuple-element.231.ab_ref, f32[4,256,256]{2,1,0:T(8,128)} %collective-permute-done.7.fa_ref, f32[4,256,256]{2,1,0:T(8,128)S(1)} %copy-done.11, ...), custom_call_target="tpu_custom_call" | custom-call | flops 1000 | bytes 1000 | tf_op jit(solution)/shard_map/value_out_grad/pallas_call | solution.py:902
  185.6 1.5 collective-permute-start.22
  187.1 2.1 first_norm_back.2
  189.3 9.1 %collective-permute-done.23 = f32[2,64,2048]{2,1,0:T(8,128)S(1)} collective-permute-done((f32[2,64,2048]{2,1,0:T(8,128)S(1)}, f32[2,64,2048]{2,1,0:T(8,128)S(1)}, u32[]{:S(2)}, u32[]{:S(2)}) %collective-permute-start.23) | collective-permute-done | bytes 1048608 | tf_op jit(solution)/shard_map/ppermute | solution.py:916
  198.4 2.3 slice_add_fusion.5
  200.7 1.9 collective-permute-start.28
  203.4 5.3 %collective-permute-done.22.refs_1_ = f32[256,1024]{1,0:T(8,128)S(1)} collective-permute-done((f32[256,1024]{1,0:T(8,128)S(1)}, f32[256,1024]{1,0:T(8,128)S(1)}, u32[]{:S(2)}, u32[]{:S(2)}) %collective-permute-start.22) | collective-permute-done | bytes 1048608 | tf_op jit(solution)/shard_map/ppermute | solution.py:916
  208.7 2.2 first_norm_back.3
  210.9 1.5 collective-permute-start.26
  212.4 2.6 pixel_grad.2.refs_0_
  215.1 3.1 embed_grad_a.1
  221.3 4.0 %embed_grad_b.1 = (f32[4,72,1024]{2,1,0:T(8,128)}, f32[4,72,1024]{2,1,0:T(8,128)S(1)}) custom-call(bf16[512,256]{1,0:T(8,128)(2,1)S(1)} %get-tuple-element.253.ka_ref, bf16[512,256]{1,0:T(8,128)(2,1)S(1)} %copy-done.26, f32[1072,256]{1,0:T(8,128)S(1)} %collective-permute-done.24.la_ref.lb_ref, f32[1072,256]{1,0:T(8,128)S(1)} %collective-permute-done.24.la_ref.lb_ref, ...), custom_call_target="tpu_custom_call" | custom-call | flops 1000 | bytes 1000 | tf_op jit(solution)/shard_map/embed_grad_b/pallas_call | solution.py:829
  226.4 2.5 pixel_grad.3
  229.3 2.6 fusion
  231.9 1.6 collective-permute-done.26
  233.4 1.9 slice_add_fusion.3
  235.6 1.8 collective-permute-start.32
  238.6 2.3 collective-permute-start.31
  240.9 2.4 add_add_fusion
  243.3 7.3 %collective-permute-done.29 = f32[2,64,1024]{2,1,0:T(8,128)} collective-permute-done((f32[2,64,1024]{2,1,0:T(8,128)}, f32[2,64,1024]{2,1,0:T(8,128)}, u32[]{:S(2)}, u32[]{:S(2)}) %collective-permute-start.29) | collective-permute-done | bytes 524320 | tf_op jit(solution)/shard_map/ppermute | solution.py:916
  251.6 2.4 collective-permute-start.35
  254.0 20.4 %collective-permute-done.30 = f32[4,72,1024]{2,1,0:T(8,128)} collective-permute-done((f32[4,72,1024]{2,1,0:T(8,128)}, f32[4,72,1024]{2,1,0:T(8,128)}, u32[]{:S(2)}, u32[]{:S(2)}) %collective-permute-start.30) | collective-permute-done | bytes 1179680 | tf_op jit(solution)/shard_map/ppermute | solution.py:916
  275.7 2.7 collective-permute-done.31
  278.4 1.4 fusion.2
  279.9 3.2 collective-permute-start.36
  283.1 2.4 collective-permute-done.33
  287.7 1.5 collective-permute-start.39
  291.1 1.9 collective-permute-start.38
  294.0 9.5 %collective-permute-done.36 = f32[2,64,1024]{2,1,0:T(8,128)S(1)} collective-permute-done((f32[2,64,1024]{2,1,0:T(8,128)S(1)}, f32[2,64,1024]{2,1,0:T(8,128)S(1)}, u32[]{:S(2)}, u32[]{:S(2)}) %collective-permute-start.36) | collective-permute-done | bytes 524320 | tf_op jit(solution)/shard_map/ppermute | solution.py:916
  303.9 10.4 %collective-permute-done.37 = f32[1,64,1024]{2,1,0:T(8,128)S(1)} collective-permute-done((f32[1,64,1024]{2,1,0:T(8,128)S(1)}, f32[1,64,1024]{2,1,0:T(8,128)S(1)}, u32[]{:S(2)}, u32[]{:S(2)}) %collective-permute-start.37) | collective-permute-done | bytes 262176 | tf_op jit(solution)/shard_map/ppermute | solution.py:916
  316.7 3.8 %collective-permute-done.38 = f32[1,72,1024]{2,1,0:T(8,128)S(1)} collective-permute-done((f32[1,72,1024]{2,1,0:T(8,128)S(1)}, f32[1,72,1024]{2,1,0:T(8,128)S(1)}, u32[]{:S(2)}, u32[]{:S(2)}) %collective-permute-start.38) | collective-permute-done | bytes 294944 | tf_op jit(solution)/shard_map/ppermute | solution.py:916
  323.3 2.3 add_convert_fusion.1
  (230 shorter events, 41.3 us)
Async XLA Ops:
  5.7 26.1 %collective-permute-start = (f32[256,1024]{1,0:T(8,128)}, f32[256,1024]{1,0:T(8,128)S(1)}, u32[]{:S(2)}, u32[]{:S(2)}) collective-permute-start(f32[256,1024]{1,0:T(8,128)} %get-tuple-element.160.part_ref), channel_id=1, source_target_pairs={{0,1},{1,0},{2,3},{3,2},{4,5},{5,4},{6,7},{7,6},{8,9},{9,8},{10,11... | collective-permute-start | bytes 3145736 | tf_op jit(solution)/shard_map/ppermute | solution.py:916
  14.8 23.1 %collective-permute-start.3 = (f32[4,256,256]{2,1,0:T(8,128)S(1)}, f32[4,256,256]{2,1,0:T(8,128)S(1)}, u32[]{:S(2)}, u32[]{:S(2)}) collective-permute-start(f32[4,256,256]{2,1,0:T(8,128)S(1)} %get-tuple-element.164), channel_id=1, source_target_pairs={{0,2},{2,0},{4,6},{6,4},{8,10},{10,8},{12,14},{14,12},{16,18},{18,... | collective-permute-start | bytes 3145736 | tf_op jit(solution)/shard_map/ppermute | solution.py:916
  14.9 16.8 %copy-start.51 = (f32[256,1024]{1,0:T(8,128)S(1)}, f32[256,1024]{1,0:T(8,128)}, u32[]{:S(2)}) copy-start(f32[256,1024]{1,0:T(8,128)} %get-tuple-element.172.part_ref) | copy-start | bytes 3145732
  14.9 18.6 %copy-start.48 = (bf16[512,1024]{1,0:T(8,128)(2,1)S(1)}, bf16[512,1024]{1,0:T(8,128)(2,1)}, u32[]{:S(2)}) copy-start(bf16[512,1024]{1,0:T(8,128)(2,1)} %refs_5_.3) | copy-start | bytes 3145732
  15.0 18.6 %copy-start.49 = (f32[256,1024]{1,0:T(8,128)S(1)}, f32[256,1024]{1,0:T(8,128)}, u32[]{:S(2)}) copy-start(f32[256,1024]{1,0:T(8,128)} %get-tuple-element.160.part_ref) | copy-start | bytes 3145732
  18.1 15.5 %copy-start.61 = (f32[512]{0:T(512)S(1)}, f32[512]{0:T(512)}, u32[]{:S(2)}) copy-start(f32[512]{0:T(512)} %param.29) | copy-start | bytes 6148
  18.1 15.5 %copy-start.62 = (f32[512]{0:T(512)S(1)}, f32[512]{0:T(512)}, u32[]{:S(2)}) copy-start(f32[512]{0:T(512)} %param.30) | copy-start | bytes 6148
  18.1 43.6 %collective-permute-start.4 = (f32[8,256,256]{2,1,0:T(8,128)}, f32[8,256,256]{2,1,0:T(8,128)}, u32[]{:S(2)}, u32[]{:S(2)}) collective-permute-start(f32[8,256,256]{2,1,0:T(8,128)} %pack_pixels.2), channel_id=1, source_target_pairs={{0,2},{2,0},{4,6},{6,4},{8,10},{10,8},{12,14},{14,12},{16,18},{18,... | collective-permute-start | bytes 6291464 | tf_op jit(solution)/shard_map/ppermute | solution.py:916
  21.7 39.9 %collective-permute-start.5 = (f32[8,256,256]{2,1,0:T(8,128)}, f32[8,256,256]{2,1,0:T(8,128)}, u32[]{:S(2)}, u32[]{:S(2)}) collective-permute-start(f32[8,256,256]{2,1,0:T(8,128)} %pack_pixels.3), channel_id=1, source_target_pairs={{0,2},{2,0},{4,6},{6,4},{8,10},{10,8},{12,14},{14,12},{16,18},{18,... | collective-permute-start | bytes 6291464 | tf_op jit(solution)/shard_map/ppermute | solution.py:916
  31.8 24.0 %collective-permute-start.1 = (f32[256,1024]{1,0:T(8,128)S(1)}, f32[256,1024]{1,0:T(8,128)S(1)}, u32[]{:S(2)}, u32[]{:S(2)}) collective-permute-start(f32[256,1024]{1,0:T(8,128)S(1)} %copy-done.51), channel_id=1, source_target_pairs={{0,1},{1,0},{2,3},{3,2},{4,5},{5,4},{6,7},{7,6},{8,9},{9,8},{10,11... | collective-permute-start | bytes 3145736 | tf_op jit(solution)/shard_map/ppermute | solution.py:916
  37.9 23.7 %copy-start.8 = (f32[4,256,256]{2,1,0:T(8,128)}, f32[4,256,256]{2,1,0:T(8,128)S(1)}, u32[]{:S(2)}) copy-start(f32[4,256,256]{2,1,0:T(8,128)S(1)} %collective-permute-done.3.la_ref.lb_ref) | copy-start | bytes 3145732
  40.4 48.8 %collective-permute-start.7 = (f32[4,256,256]{2,1,0:T(8,128)}, f32[4,256,256]{2,1,0:T(8,128)}, u32[]{:S(2)}, u32[]{:S(2)}) collective-permute-start(f32[4,256,256]{2,1,0:T(8,128)} %get-tuple-element.178), channel_id=1, source_target_pairs={{0,2},{2,0},{4,6},{6,4},{8,10},{10,8},{12,14},{14,12},{16,18},{18,... | collective-permute-start | bytes 3145736 | tf_op jit(solution)/shard_map/ppermute | solution.py:916
  55.8 23.3 %collective-permute-start.2 = (f32[256,1024]{1,0:T(8,128)S(1)}, f32[256,1024]{1,0:T(8,128)S(1)}, u32[]{:S(2)}, u32[]{:S(2)}) collective-permute-start(f32[256,1024]{1,0:T(8,128)S(1)} %get-tuple-element.173.opart_ref), channel_id=1, source_target_pairs={{0,1},{1,0},{2,3},{3,2},{4,5},{5,4},{6,7},{7,6},{8,9},{9,8},{10,11... | collective-permute-start | bytes 3145736 | tf_op jit(solution)/shard_map/ppermute | solution.py:916
  57.2 23.3 %copy-start.45 = (bf16[1024,2048]{1,0:T(8,128)(2,1)S(1)}, bf16[1024,2048]{1,0:T(8,128)(2,1)}, u32[]{:S(2)}) copy-start(bf16[1024,2048]{1,0:T(8,128)(2,1)} %wfc1_ref.3) | copy-start | bytes 12582916
  57.2 23.3 %copy-start.46 = (bf16[2048,1024]{1,0:T(8,128)(2,1)S(1)}, bf16[2048,1024]{1,0:T(8,128)(2,1)}, u32[]{:S(2)}) copy-start(bf16[2048,1024]{1,0:T(8,128)(2,1)} %wfc2_ref.7) | copy-start | bytes 12582916
  57.2 23.3 %copy-start.56 = (f32[2048]{0:T(1024)S(1)}, f32[2048]{0:T(1024)}, u32[]{:S(2)}) copy-start(f32[2048]{0:T(1024)} %param.36) | copy-start | bytes 24580
  57.2 23.3 %copy-start.58 = (f32[1024]{0:T(1024)S(1)}, f32[1024]{0:T(1024)}, u32[]{:S(2)}) copy-start(f32[1024]{0:T(1024)} %param.32) | copy-start | bytes 12292
  57.3 23.3 %copy-start.59 = (f32[1024]{0:T(1024)S(1)}, f32[1024]{0:T(1024)}, u32[]{:S(2)}) copy-start(f32[1024]{0:T(1024)} %param.34) | copy-start | bytes 12292
  57.3 23.3 %copy-start.60 = (f32[1024]{0:T(1024)S(1)}, f32[1024]{0:T(1024)}, u32[]{:S(2)}) copy-start(f32[1024]{0:T(1024)} %param.33) | copy-start | bytes 12292
  61.6 18.9 %copy-start.38 = (bf16[256,512]{1,0:T(8,128)(2,1)}, bf16[256,512]{1,0:T(8,128)(2,1)S(1)}, u32[]{:S(2)}) copy-start(bf16[256,512]{1,0:T(8,128)(2,1)S(1)} %get-tuple-element.185.o_ref.mb_ref) | copy-start | bytes 786436
  61.6 26.5 %copy-start.65 = (bf16[3,256,512]{2,1,0:T(8,128)(2,1)}, bf16[3,256,512]{2,1,0:T(8,128)(2,1)S(1)}, u32[]{:S(2)}) copy-start(bf16[3,256,512]{2,1,0:T(8,128)(2,1)S(1)} %get-tuple-element.225.refs_6_) | copy-start | bytes 2359300
  61.6 42.3 %copy-start.40 = (f32[256,1024]{1,0:T(8,128)}, f32[256,1024]{1,0:T(8,128)S(1)}, u32[]{:S(2)}) copy-start(f32[256,1024]{1,0:T(8,128)S(1)} %get-tuple-element.189.x0_ref.refs_4_) | copy-start | bytes 3145732
  62.5 26.7 %collective-permute-start.8 = (f32[4,256,256]{2,1,0:T(8,128)S(1)}, f32[4,256,256]{2,1,0:T(8,128)S(1)}, u32[]{:S(2)}, u32[]{:S(2)}) collective-permute-start(f32[4,256,256]{2,1,0:T(8,128)S(1)} %get-tuple-element.186), channel_id=1, source_target_pairs={{0,2},{2,0},{4,6},{6,4},{8,10},{10,8},{12,14},{14,12},{16,18},{18,... | collective-permute-start | bytes 3145736 | tf_op jit(solution)/shard_map/ppermute | solution.py:916
  79.1 23.3 %collective-permute-start.6 = (f32[256,1024]{1,0:T(8,128)S(1)}, f32[256,1024]{1,0:T(8,128)S(1)}, u32[]{:S(2)}, u32[]{:S(2)}) collective-permute-start(f32[256,1024]{1,0:T(8,128)S(1)} %get-tuple-element.190.opart_ref), channel_id=1, source_target_pairs={{0,1},{1,0},{2,3},{3,2},{4,5},{5,4},{6,7},{7,6},{8,9},{9,8},{10,11... | collective-permute-start | bytes 3145736 | tf_op jit(solution)/shard_map/ppermute | solution.py:916
  90.1 23.3 %collective-permute-start.12 = (f32[10,256,256]{2,1,0:T(8,128)S(1)}, f32[10,256,256]{2,1,0:T(8,128)S(1)}, u32[]{:S(2)}, u32[]{:S(2)}) collective-permute-start(f32[10,256,256]{2,1,0:T(8,128)S(1)} %get-tuple-element.203), channel_id=1, source_target_pairs={{0,2},{2,0},{4,6},{6,4},{8,10},{10,8},{12,14},{14,12},{16,18},{18,... | collective-permute-start | bytes 7864328 | tf_op jit(solution)/shard_map/ppermute | solution.py:916
  90.1 23.3 %collective-permute-start.11 = (f32[8,256,256]{2,1,0:T(8,128)S(1)}, f32[8,256,256]{2,1,0:T(8,128)S(1)}, u32[]{:S(2)}, u32[]{:S(2)}) collective-permute-start(f32[8,256,256]{2,1,0:T(8,128)S(1)} %get-tuple-element.202), channel_id=1, source_target_pairs={{0,2},{2,0},{4,6},{6,4},{8,10},{10,8},{12,14},{14,12},{16,18},{18,... | collective-permute-start | bytes 6291464 | tf_op jit(solution)/shard_map/ppermute | solution.py:916
  102.5 9.6 %collective-permute-start.9 = (f32[96,1024]{1,0:T(8,128)S(1)}, f32[96,1024]{1,0:T(8,128)S(1)}, u32[]{:S(2)}, u32[]{:S(2)}) collective-permute-start(f32[96,1024]{1,0:T(8,128)S(1)} %get-tuple-element.196.refs_0_), channel_id=1, source_target_pairs={{0,1},{1,0},{2,3},{3,2},{4,5},{5,4},{6,7},{7,6},{8,9},{9,8},{10,11... | collective-permute-start | bytes 1179656 | tf_op jit(solution)/shard_map/ppermute | solution.py:916
  111.5 42.3 %copy-start.21 = (f32[256,1024]{1,0:T(8,128)}, f32[256,1024]{1,0:T(8,128)S(1)}, u32[]{:S(2)}) copy-start(f32[256,1024]{1,0:T(8,128)S(1)} %get-tuple-element.220.refs_2_) | copy-start | bytes 3145732
  111.5 4.8 %collective-permute-start.13 = (f32[8,256,256]{2,1,0:T(8,128)S(1)}, f32[8,256,256]{2,1,0:T(8,128)S(1)}, u32[]{:S(2)}, u32[]{:S(2)}) collective-permute-start(f32[8,256,256]{2,1,0:T(8,128)S(1)} %get-tuple-element.210), channel_id=1, source_target_pairs={{0,2},{2,0},{4,6},{6,4},{8,10},{10,8},{12,14},{14,12},{16,18},{18,... | collective-permute-start | bytes 6291464 | tf_op jit(solution)/shard_map/ppermute | solution.py:916
  111.5 11.2 %collective-permute-start.14 = (f32[10,256,256]{2,1,0:T(8,128)S(1)}, f32[10,256,256]{2,1,0:T(8,128)S(1)}, u32[]{:S(2)}, u32[]{:S(2)}) collective-permute-start(f32[10,256,256]{2,1,0:T(8,128)S(1)} %get-tuple-element.213), channel_id=1, source_target_pairs={{0,2},{2,0},{4,6},{6,4},{8,10},{10,8},{12,14},{14,12},{16,18},{18,... | collective-permute-start | bytes 7864328 | tf_op jit(solution)/shard_map/ppermute | solution.py:916
  112.0 16.6 %collective-permute-start.10 = (f32[160,1024]{1,0:T(8,128)S(1)}, f32[160,1024]{1,0:T(8,128)S(1)}, u32[]{:S(2)}, u32[]{:S(2)}) collective-permute-start(f32[160,1024]{1,0:T(8,128)S(1)} %get-tuple-element.198.refs_1_), channel_id=1, source_target_pairs={{0,1},{1,0},{2,3},{3,2},{4,5},{5,4},{6,7},{7,6},{8,9},{9,8},{10,11... | collective-permute-start | bytes 1966088 | tf_op jit(solution)/shard_map/ppermute | solution.py:916
  120.3 78.1 %copy-start.16 = (f32[4,64,2048]{2,1,0:T(8,128)}, f32[4,64,2048]{2,1,0:T(8,128)S(1)}, u32[]{:S(2)}) copy-start(f32[4,64,2048]{2,1,0:T(8,128)S(1)} %get-tuple-element.232) | copy-start | bytes 6291460
  120.3 48.2 %collective-permute-start.17 = (f32[4,64,2048]{2,1,0:T(8,128)}, f32[4,64,2048]{2,1,0:T(8,128)}, u32[]{:S(2)}, u32[]{:S(2)}) collective-permute-start(f32[4,64,2048]{2,1,0:T(8,128)} %get-tuple-element.212), channel_id=1, source_target_pairs={{0,4},{2,6},{4,0},{6,2},{8,12},{10,14},{12,8},{14,10},{16,20},{18,... | collective-permute-start | bytes 6291464 | tf_op jit(solution)/shard_map/ppermute | solution.py:916
  127.2 48.9 %collective-permute-start.21 = (f32[8,64,1024]{2,1,0:T(8,128)}, f32[8,64,1024]{2,1,0:T(8,128)}, u32[]{:S(2)}, u32[]{:S(2)}) collective-permute-start(f32[8,64,1024]{2,1,0:T(8,128)} %bitcast.12), channel_id=1, source_target_pairs={{0,8},{2,10},{4,12},{6,14},{8,0},{10,2},{12,4},{14,6},{16,24},{18,... | collective-permute-start | bytes 6291464 | tf_op jit(solution)/shard_map/ppermute | solution.py:916
  128.7 24.3 %collective-permute-start.15 = (f32[256,1024]{1,0:T(8,128)S(1)}, f32[256,1024]{1,0:T(8,128)S(1)}, u32[]{:S(2)}, u32[]{:S(2)}) collective-permute-start(f32[256,1024]{1,0:T(8,128)S(1)} %get-tuple-element.219.refs_0_), channel_id=1, source_target_pairs={{0,1},{1,0},{2,3},{3,2},{4,5},{5,4},{6,7},{7,6},{8,9},{9,8},{10,11... | collective-permute-start | bytes 3145736 | tf_op jit(solution)/shard_map/ppermute | solution.py:916
  153.0 9.5 %collective-permute-start.16 = (f32[96,1024]{1,0:T(8,128)S(1)}, f32[96,1024]{1,0:T(8,128)S(1)}, u32[]{:S(2)}, u32[]{:S(2)}) collective-permute-start(f32[96,1024]{1,0:T(8,128)S(1)} %get-tuple-element.227.refs_0_), channel_id=1, source_target_pairs={{0,1},{1,0},{2,3},{3,2},{4,5},{5,4},{6,7},{7,6},{8,9},{9,8},{10,11... | collective-permute-start | bytes 1179656 | tf_op jit(solution)/shard_map/ppermute | solution.py:916
  161.9 8.9 %collective-permute-start.19 = (f32[8,256,256]{2,1,0:T(8,128)S(1)}, f32[8,256,256]{2,1,0:T(8,128)S(1)}, u32[]{:S(2)}, u32[]{:S(2)}) collective-permute-start(f32[8,256,256]{2,1,0:T(8,128)S(1)} %get-tuple-element.237), channel_id=1, source_target_pairs={{0,2},{2,0},{4,6},{6,4},{8,10},{10,8},{12,14},{14,12},{16,18},{18,... | collective-permute-start | bytes 6291464 | tf_op jit(solution)/shard_map/ppermute | solution.py:916
  162.4 8.4 %collective-permute-start.18 = (f32[8,256,256]{2,1,0:T(8,128)S(1)}, f32[8,256,256]{2,1,0:T(8,128)S(1)}, u32[]{:S(2)}, u32[]{:S(2)}) collective-permute-start(f32[8,256,256]{2,1,0:T(8,128)S(1)} %get-tuple-element.235), channel_id=1, source_target_pairs={{0,2},{2,0},{4,6},{6,4},{8,10},{10,8},{12,14},{14,12},{16,18},{18,... | collective-permute-start | bytes 6291464 | tf_op jit(solution)/shard_map/ppermute | solution.py:916
  165.0 20.7 %collective-permute-start.20 = (f32[160,1024]{1,0:T(8,128)S(1)}, f32[160,1024]{1,0:T(8,128)S(1)}, u32[]{:S(2)}, u32[]{:S(2)}) collective-permute-start(f32[160,1024]{1,0:T(8,128)S(1)} %get-tuple-element.243.refs_1_), channel_id=1, source_target_pairs={{0,1},{1,0},{2,3},{3,2},{4,5},{5,4},{6,7},{7,6},{8,9},{9,8},{10,11... | collective-permute-start | bytes 1966088 | tf_op jit(solution)/shard_map/ppermute | solution.py:916
  169.9 28.5 %collective-permute-start.23 = (f32[2,64,2048]{2,1,0:T(8,128)S(1)}, f32[2,64,2048]{2,1,0:T(8,128)S(1)}, u32[]{:S(2)}, u32[]{:S(2)}) collective-permute-start(f32[2,64,2048]{2,1,0:T(8,128)S(1)} %slice_add_fusion), channel_id=1, source_target_pairs={{0,8},{2,10},{4,12},{6,14},{8,0},{10,2},{12,4},{14,6},{16,24},{18,... | collective-permute-start | bytes 3145736 | tf_op jit(solution)/shard_map/ppermute | solution.py:916
  184.0 45.3 %collective-permute-start.25 = (f32[8,64,1024]{2,1,0:T(8,128)}, f32[8,64,1024]{2,1,0:T(8,128)}, u32[]{:S(2)}, u32[]{:S(2)}) collective-permute-start(f32[8,64,1024]{2,1,0:T(8,128)} %pad_maximum_fusion), channel_id=1, source_target_pairs={{0,4},{2,6},{4,0},{6,2},{8,12},{10,14},{12,8},{14,10},{16,20},{18,... | collective-permute-start | bytes 6291464 | tf_op jit(solution)/shard_map/ppermute | solution.py:916
  184.5 48.9 %collective-permute-start.27 = (f32[4,64,1024]{2,1,0:T(8,128)}, f32[4,64,1024]{2,1,0:T(8,128)}, u32[]{:S(2)}, u32[]{:S(2)}) collective-permute-start(f32[4,64,1024]{2,1,0:T(8,128)} %get-tuple-element.251), channel_id=1, source_target_pairs={{0,8},{2,10},{4,12},{6,14},{8,0},{10,2},{12,4},{14,6},{16,24},{18,... | collective-permute-start | bytes 3145736 | tf_op jit(solution)/shard_map/ppermute | solution.py:916
  185.6 23.1 %collective-permute-start.22 = (f32[256,1024]{1,0:T(8,128)S(1)}, f32[256,1024]{1,0:T(8,128)S(1)}, u32[]{:S(2)}, u32[]{:S(2)}) collective-permute-start(f32[256,1024]{1,0:T(8,128)S(1)} %get-tuple-element.255.refs_0_), channel_id=1, source_target_pairs={{0,1},{1,0},{2,3},{3,2},{4,5},{5,4},{6,7},{7,6},{8,9},{9,8},{10,11... | collective-permute-start | bytes 3145736 | tf_op jit(solution)/shard_map/ppermute | solution.py:916
  187.1 25.2 %copy-start.12 = (bf16[384,1024]{1,0:T(8,128)(2,1)S(1)}, bf16[384,1024]{1,0:T(8,128)(2,1)}, u32[]{:S(2)}) copy-start(bf16[384,1024]{1,0:T(8,128)(2,1)} %wrgb_ref.7) | copy-start | bytes 2359300
  189.3 19.4 %copy-start.41 = (f32[256,1024]{1,0:T(8,128)S(1)}, f32[256,1024]{1,0:T(8,128)}, u32[]{:S(2)}) copy-start(f32[256,1024]{1,0:T(8,128)} %copy-done.40) | copy-start | bytes 3145732
  200.7 37.8 %collective-permute-start.28 = (f32[1,64,2048]{2,1,0:T(8,128)}, f32[1,64,2048]{2,1,0:T(8,128)}, u32[]{:S(2)}, u32[]{:S(2)}) collective-permute-start(f32[1,64,2048]{2,1,0:T(8,128)} %slice_add_fusion.5), channel_id=1, source_target_pairs={{0,16},{2,18},{4,20},{6,22},{8,24},{10,26},{12,28},{14,30},{16,0},... | collective-permute-start | bytes 1572872 | tf_op jit(solution)/shard_map/ppermute | solution.py:916
  210.9 22.6 %collective-permute-start.26 = (f32[256,1024]{1,0:T(8,128)}, f32[256,1024]{1,0:T(8,128)}, u32[]{:S(2)}, u32[]{:S(2)}) collective-permute-start(f32[256,1024]{1,0:T(8,128)} %mlp_out.3), channel_id=1, source_target_pairs={{0,1},{1,0},{2,3},{3,2},{4,5},{5,4},{6,7},{7,6},{8,9},{9,8},{10,11... | collective-permute-start | bytes 3145736 | tf_op jit(solution)/shard_map/ppermute | solution.py:916
  212.4 2.7 collective-permute-start.24
  225.3 49.1 %collective-permute-start.30 = (f32[4,72,1024]{2,1,0:T(8,128)}, f32[4,72,1024]{2,1,0:T(8,128)}, u32[]{:S(2)}, u32[]{:S(2)}) collective-permute-start(f32[4,72,1024]{2,1,0:T(8,128)} %get-tuple-element.278), channel_id=1, source_target_pairs={{0,8},{2,10},{4,12},{6,14},{8,0},{10,2},{12,4},{14,6},{16,24},{18,... | collective-permute-start | bytes 3538952 | tf_op jit(solution)/shard_map/ppermute | solution.py:916
  235.4 39.0 %copy-start.18 = (f32[4,72,1024]{2,1,0:T(8,128)S(1)}, f32[4,72,1024]{2,1,0:T(8,128)}, u32[]{:S(2)}) copy-start(f32[4,72,1024]{2,1,0:T(8,128)} %copy-done.17) | copy-start | bytes 3538948
  235.4 15.2 %collective-permute-start.29 = (f32[2,64,1024]{2,1,0:T(8,128)}, f32[2,64,1024]{2,1,0:T(8,128)}, u32[]{:S(2)}, u32[]{:S(2)}) collective-permute-start(f32[2,64,1024]{2,1,0:T(8,128)} %slice_add_fusion.3), channel_id=1, source_target_pairs={{0,4},{2,6},{4,0},{6,2},{8,12},{10,14},{12,8},{14,10},{16,20},{18,... | collective-permute-start | bytes 1572872 | tf_op jit(solution)/shard_map/ppermute | solution.py:916
  235.6 44.2 %collective-permute-start.32 = (f32[4,64,1024]{2,1,0:T(8,128)}, f32[4,64,1024]{2,1,0:T(8,128)S(1)}, u32[]{:S(2)}, u32[]{:S(2)}) collective-permute-start(f32[4,64,1024]{2,1,0:T(8,128)} %copy-done.50), channel_id=1, source_target_pairs={{0,4},{2,6},{4,0},{6,2},{8,12},{10,14},{12,8},{14,10},{16,20},{18,... | collective-permute-start | bytes 3145736 | tf_op jit(solution)/shard_map/ppermute | solution.py:916
  237.4 48.1 %collective-permute-start.33 = (f32[2,64,1024]{2,1,0:T(8,128)}, f32[2,64,1024]{2,1,0:T(8,128)S(1)}, u32[]{:S(2)}, u32[]{:S(2)}) collective-permute-start(f32[2,64,1024]{2,1,0:T(8,128)} %get-tuple-element.304), channel_id=1, source_target_pairs={{0,8},{2,10},{4,12},{6,14},{8,0},{10,2},{12,4},{14,6},{16,24},{18,... | collective-permute-start | bytes 1572872 | tf_op jit(solution)/shard_map/ppermute | solution.py:916
  238.6 39.8 %collective-permute-start.31 = (f32[2,64,1024]{2,1,0:T(8,128)}, f32[2,64,1024]{2,1,0:T(8,128)S(1)}, u32[]{:S(2)}, u32[]{:S(2)}) collective-permute-start(f32[2,64,1024]{2,1,0:T(8,128)} %get-tuple-element.303), channel_id=1, source_target_pairs={{0,16},{2,18},{4,20},{6,22},{8,24},{10,26},{12,28},{14,30},{16,0},... | collective-permute-start | bytes 1572872 | tf_op jit(solution)/shard_map/ppermute | solution.py:916
  251.6 41.3 %collective-permute-start.35 = (f32[1,64,1024]{2,1,0:T(8,128)S(1)}, f32[1,64,1024]{2,1,0:T(8,128)S(1)}, u32[]{:S(2)}, u32[]{:S(2)}) collective-permute-start(f32[1,64,1024]{2,1,0:T(8,128)S(1)} %slice_add_fusion.9), channel_id=1, source_target_pairs={{0,16},{2,18},{4,20},{6,22},{8,24},{10,26},{12,28},{14,30},{16,0},... | collective-permute-start | bytes 786440 | tf_op jit(solution)/shard_map/ppermute | solution.py:916
  275.6 14.5 %collective-permute-start.34 = (f32[2,72,1024]{2,1,0:T(8,128)S(1)}, f32[2,72,1024]{2,1,0:T(8,128)S(1)}, u32[]{:S(2)}, u32[]{:S(2)}) collective-permute-start(f32[2,72,1024]{2,1,0:T(8,128)S(1)} %slice_add_fusion.1), channel_id=1, source_target_pairs={{0,4},{2,6},{4,0},{6,2},{8,12},{10,14},{12,8},{14,10},{16,20},{18,... | collective-permute-start | bytes 1769480 | tf_op jit(solution)/shard_map/ppermute | solution.py:916
  279.9 23.6 %collective-permute-start.36 = (f32[2,64,1024]{2,1,0:T(8,128)S(1)}, f32[2,64,1024]{2,1,0:T(8,128)S(1)}, u32[]{:S(2)}, u32[]{:S(2)}) collective-permute-start(f32[2,64,1024]{2,1,0:T(8,128)S(1)} %slice_add_fusion.2), channel_id=1, source_target_pairs={{0,8},{2,10},{4,12},{6,14},{8,0},{10,2},{12,4},{14,6},{16,24},{18,... | collective-permute-start | bytes 1572872 | tf_op jit(solution)/shard_map/ppermute | solution.py:916
  286.5 27.7 %collective-permute-start.37 = (f32[1,64,1024]{2,1,0:T(8,128)S(1)}, f32[1,64,1024]{2,1,0:T(8,128)S(1)}, u32[]{:S(2)}, u32[]{:S(2)}) collective-permute-start(f32[1,64,1024]{2,1,0:T(8,128)S(1)} %slice_add_fusion.8), channel_id=1, source_target_pairs={{0,16},{2,18},{4,20},{6,22},{8,24},{10,26},{12,28},{14,30},{16,0},... | collective-permute-start | bytes 786440 | tf_op jit(solution)/shard_map/ppermute | solution.py:916
  287.7 35.6 %collective-permute-start.39 = (f32[256,1024]{1,0:T(8,128)S(1)}, f32[256,1024]{1,0:T(8,128)S(1)}, u32[]{:S(2)}, u32[]{:S(2)}) collective-permute-start(f32[256,1024]{1,0:T(8,128)S(1)} %copy-done.24), channel_id=1, source_target_pairs={{0,1},{1,0},{2,3},{3,2},{4,5},{5,4},{6,7},{7,6},{8,9},{9,8},{10,11... | collective-permute-start | bytes 3145736 | tf_op jit(solution)/shard_map/ppermute | solution.py:916
  291.1 29.5 %collective-permute-start.38 = (f32[1,72,1024]{2,1,0:T(8,128)S(1)}, f32[1,72,1024]{2,1,0:T(8,128)S(1)}, u32[]{:S(2)}, u32[]{:S(2)}) collective-permute-start(f32[1,72,1024]{2,1,0:T(8,128)S(1)} %slice_add_fusion.6), channel_id=1, source_target_pairs={{0,16},{2,18},{4,20},{6,22},{8,24},{10,26},{12,28},{14,30},{16,0},... | collective-permute-start | bytes 884744 | tf_op jit(solution)/shard_map/ppermute | solution.py:916
  303.5 19.8 %copy-start.20 = (f32[256,1024]{1,0:T(8,128)S(1)}, f32[256,1024]{1,0:T(8,128)}, u32[]{:S(2)}) copy-start(f32[256,1024]{1,0:T(8,128)} %copy-done.19) | copy-start | bytes 3145732
  303.6 19.7 %copy-start.22 = (f32[256,1024]{1,0:T(8,128)S(1)}, f32[256,1024]{1,0:T(8,128)}, u32[]{:S(2)}) copy-start(f32[256,1024]{1,0:T(8,128)} %copy-done.21) | copy-start | bytes 3145732
  303.6 19.7 %copy-start.69 = (f32[1024]{0:T(1024)S(1)}, f32[1024]{0:T(1024)}, u32[]{:S(2)}) copy-start(f32[1024]{0:T(1024)} %param.38) | copy-start | bytes 12292
  303.6 23.1 %collective-permute-start.40 = (f32[1,64,1024]{2,1,0:T(8,128)S(1)}, f32[1,64,1024]{2,1,0:T(8,128)S(1)}, u32[]{:S(2)}, u32[]{:S(2)}) collective-permute-start(f32[1,64,1024]{2,1,0:T(8,128)S(1)} %slice_add_fusion.7), channel_id=1, source_target_pairs={{0,16},{2,18},{4,20},{6,22},{8,24},{10,26},{12,28},{14,30},{16,0},... | collective-permute-start | bytes 786440 | tf_op jit(solution)/shard_map/ppermute | solution.py:916
  (49 other events, 283.1 us)

commit v8 on v7

--- a/solution.py
+++ b/solution.py
@@ -1165,9 +1165,6 @@
         mid = mixed[0].shape[1] // 2
         gdx0 = order.tie(other(gone[1]))
         sides = ([(kdx0[0], 0), (kdx0[1], 0)], [(gdx0, 1), (gdx0, 0)], mixed, gmix)
-        embx_h = Halving(*plain_grad(*sides, move_x, "embed_grad_a", 0, mid), X_FIRST, size)
-        order.mark(embx_h.sent)
-        sides[3][1] = order.tie(gmix[1])
         cube = (cube + order.tie(gdx0)[-cube.shape[0] :]).reshape(8, 1, -1)
         cube = jnp.pad(cube, ((0, 0), (0, 7), (0, 0)))
         embz_h = Halving(
@@ -1175,6 +1172,9 @@
             Z_FIRST, size,
         )
         order.mark(embz_h.sent)
+        sides[3][1] = order.tie(gmix[1])
+        embx_h = Halving(*plain_grad(*sides, move_x, "embed_grad_a", 0, mid), X_FIRST, size)
+        order.mark(embx_h.sent)
     pixels_grad = pixel_grad(
         order.tie(item_kinds), dx0[1], w_spectral, w_rgb, pick, 1, items, pixels_grad
     )
@@ -1203,13 +1203,13 @@
     if custom:
         embx_h.step(order)
         attx_g = attx_h.step(order)
-        embz_g = embz_h.step(order)
     summed[1] = settle(summed[1])
     block_out = jnp.concatenate(
         [(x1[i] + (ycot[i] + summed[i] + fc2_bias)).astype(BF16) for i in range(items)], 0
     )
     order.mark(block_out)
     if custom:
+        embz_g = embz_h.step(order)
         embx_g = embx_h.step(order)
         shard = width // size
         core = lax.axis_index("dp") % 2

time: 332 us -> 329 us (level)
  waiting for transfers between devices: 145 us -> 137 us
    ppermute x41, waiting for transfers between devices: 145 us -> 137 us  [exchange(): return lax.ppermute(values, axis, [(i, i ^ bit) for i in range(size)])]
    unnamed x144 -> x136, local copies, waits for them, and re-layouts: 8.68 us -> 9.61 us
  transfers between devices with their start and end apart: 41 -> 41, of which waited for: 20 -> 21; matrix products, arithmetic and copies ran while one was open for 10% -> 10% of each run, Pallas kernels for 28% -> 29%
where the time goes in v8:
time: 329 us; the launch traced here: 325 us
  waiting for transfers between devices  137 us (42%)
  Pallas kernels  99 us (30%)
  starting transfers between devices  44.7 us (14%)
  other arithmetic  30.3 us (9%)
  local copies, waits for them, and re-layouts  12.1 us (4%)
    ppermute x41, waiting for transfers between devices, exchange(): return lax.ppermute(values, axis, [(i, i ^ bit) for i in range(size)])  137 us
    ppermute x41, starting transfers between devices, exchange(): return lax.ppermute(values, axis, [(i, i ^ bit) for i in range(size)])  44.7 us
    add x16, other arithmetic, value(): value = value + recv[first:first + count]  21.2 us
    pallas_call x2, Pallas kernels, attn_backward(): pl.pallas_call(functools.partial(attn_backward_kernel, parts=(len(gparts)...  16.2 us
    pallas_call x4, Pallas kernels, plain_grad(): pl.pallas_call(functools.partial(plain_grad_kernel, moves=moves, vectors=...  15.6 us
    pallas_call x2, Pallas kernels, mlp(): pl.pallas_call(mlp_kernel, grid_spec=pltpu.PrefetchScalarGridSpec(num_sca...  15.6 us
    pallas_call x2, Pallas kernels, embed(): pl.pallas_call(functools.partial(embed_kernel, item=item), grid_spec=pltp...  9.87 us
    unnamed x136, local copies, waits for them, and re-layouts  9.61 us
  transfers between devices with their start and end apart: 41, of which 21 were waited for; matrix products, arithmetic and copies ran while one was open for 10% of the time, Pallas kernels for 29%

profile of v8, /device:TPU:0, one launch (start us, length us, event | category | flops | bytes accessed | tf_op | source)
XLA Modules:
  0.0 324.5 jit_solution(11380008757410041255)
XLA Ops:
  0.7 5.0 %embed.2 = (f32[256,1024]{1,0:T(8,128)}, bf16[256,2048]{1,0:T(8,128)(2,1)}) custom-call(s32[2]{0:T(128)} %kinds.4, bf16[512,1664]{1,0:T(8,128)(2,1)} %pix_ref.3, bf16[1664,1024]{1,0:T(8,128)(2,1)} %wspec_ref.7, bf16[384,1024]{1,0:T(8,128)(2,1)} %wrgb_ref.7, bf16[1664,384]{1,0:T(8,128)(2,1)} %constant.50.clone.pick_ref), custom_call_target="tpu_custom_call" | custom-call | flops 1000 | bytes 1000 | tf_op jit(solution)/shard_map/embed/pallas_call | solution.py:242
  5.7 3.0 collective-permute-start
  8.8 4.9 %embed.3 = (f32[256,1024]{1,0:T(8,128)}, bf16[256,2048]{1,0:T(8,128)(2,1)}) custom-call(s32[2]{0:T(128)} %kinds.4, bf16[512,1664]{1,0:T(8,128)(2,1)} %pix_ref.3, bf16[1664,1024]{1,0:T(8,128)(2,1)} %wspec_ref.7, bf16[384,1024]{1,0:T(8,128)(2,1)} %wrgb_ref.7, bf16[1664,384]{1,0:T(8,128)(2,1)} %constant.50.clone.pick_ref), custom_call_target="tpu_custom_call" | custom-call | flops 1000 | bytes 1000 | tf_op jit(solution)/shard_map/embed/pallas_call | solution.py:242
  14.9 3.1 pack_pixels.2
  18.6 3.1 pack_pixels.3
  22.1 10.0 %collective-permute-done.recv_ref = f32[256,1024]{1,0:T(8,128)S(1)} collective-permute-done((f32[256,1024]{1,0:T(8,128)}, f32[256,1024]{1,0:T(8,128)S(1)}, u32[]{:S(2)}, u32[]{:S(2)}) %collective-permute-start) | collective-permute-done | bytes 1048608 | tf_op jit(solution)/shard_map/ppermute | solution.py:916
  32.1 1.7 collective-permute-start.1
  33.8 4.4 %attn_forward.2 = (f32[256,1024]{1,0:T(8,128)S(1)}, bf16[256,1024]{1,0:T(8,128)(2,1)S(1)}, bf16[3,256,512]{2,1,0:T(8,128)(2,1)S(1)}, bf16[256,512]{1,0:T(8,128)(2,1)S(1)}, f32[256,1024]{1,0:T(8,128)S(1)}) custom-call(f32[256,1024]{1,0:T(8,128)S(1)} %copy-done.49, f32[256,1024]{1,0:T(8,128)S(1)} %collective-permute-done.recv_ref, ...), custom_call_target="tpu_custom_call" | custom-call | flops 99999997952 | bytes 1000 | tf_op jit(solution)/shard_map/attn_forward/pallas_call | solution.py:330
  38.2 1.8 pack_attn.2
  40.7 15.7 %collective-permute-done.1.recv_ref = f32[256,1024]{1,0:T(8,128)S(1)} collective-permute-done((f32[256,1024]{1,0:T(8,128)S(1)}, f32[256,1024]{1,0:T(8,128)S(1)}, u32[]{:S(2)}, u32[]{:S(2)}) %collective-permute-start.1) | collective-permute-done | bytes 1048608 | tf_op jit(solution)/shard_map/ppermute | solution.py:916
  56.4 1.4 collective-permute-start.2
  57.9 4.4 %attn_forward.3 = (f32[256,1024]{1,0:T(8,128)S(1)}, bf16[256,1024]{1,0:T(8,128)(2,1)S(1)}, bf16[3,256,512]{2,1,0:T(8,128)(2,1)S(1)}, bf16[256,512]{1,0:T(8,128)(2,1)S(1)}, f32[256,1024]{1,0:T(8,128)S(1)}) custom-call(f32[256,1024]{1,0:T(8,128)S(1)} %copy-done.51, f32[256,1024]{1,0:T(8,128)S(1)} %collective-permute-done.1.recv_ref, ...), custom_call_target="tpu_custom_call" | custom-call | flops 99999997952 | bytes 1000 | tf_op jit(solution)/shard_map/attn_forward/pallas_call | solution.py:330
  63.2 16.7 %collective-permute-done.2.orecv_ref = f32[256,1024]{1,0:T(8,128)S(1)} collective-permute-done((f32[256,1024]{1,0:T(8,128)S(1)}, f32[256,1024]{1,0:T(8,128)S(1)}, u32[]{:S(2)}, u32[]{:S(2)}) %collective-permute-start.2) | collective-permute-done | bytes 1048608 | tf_op jit(solution)/shard_map/ppermute | solution.py:916
  79.8 1.3 collective-permute-start.6
  81.2 7.8 %mlp.2 = (f32[256,1024]{1,0:T(8,128)S(1)}, bf16[256,1024]{1,0:T(8,128)(2,1)}, bf16[256,2048]{1,0:T(8,128)(2,1)S(1)}, bf16[256,2048]{1,0:T(8,128)(2,1)S(1)}, f32[...) custom-call(s32[9]{0:T(128)S(1)} %pad_add_fusion.place, ...), custom_call_target="tpu_custom_call" | custom-call | flops 99999997952 | bytes 1000 | tf_op jit(solution)/shard_map/mlp/pallas_call | solution.py:536
  91.5 11.6 %collective-permute-done.6.orecv_ref = f32[256,1024]{1,0:T(8,128)S(1)} collective-permute-done((f32[256,1024]{1,0:T(8,128)S(1)}, f32[256,1024]{1,0:T(8,128)S(1)}, u32[]{:S(2)}, u32[]{:S(2)}) %collective-permute-start.6) | collective-permute-done | bytes 1048608 | tf_op jit(solution)/shard_map/ppermute | solution.py:916
  103.2 1.3 collective-permute-start.9
  104.5 7.8 %mlp.3 = (f32[256,1024]{1,0:T(8,128)S(1)}, bf16[256,1024]{1,0:T(8,128)(2,1)}, bf16[256,2048]{1,0:T(8,128)(2,1)S(1)}, bf16[256,2048]{1,0:T(8,128)(2,1)S(1)}, f32[...) custom-call(s32[9]{0:T(128)S(1)} %pad_add_fusion.place, ...), custom_call_target="tpu_custom_call" | custom-call | flops 99999997952 | bytes 1000 | tf_op jit(solution)/shard_map/mlp/pallas_call | solution.py:536
  113.5 1.8 mlp_out.2
  116.4 4.1 %fc2_grad.1 = (f32[4,64,2048]{2,1,0:T(8,128)}, f32[4,64,2048]{2,1,0:T(8,128)S(1)}) custom-call(bf16[2,512,256]{2,1,0:T(8,128)(2,1)S(1)} %get-tuple-element.205.ka_ref.kb_ref, bf16[2,512,256]{2,1,0:T(8,128)(2,1)S(1)} %get-tuple-element.205.ka_ref.kb_ref, f32[4,256,256]{2,1,0:T(8,128)S(1)} %copy-done.9, f32[4,256,256]{2,1,0:T(8,128)S(1)} %copy-done.9, ...), custom_call_target="tpu_custom_call" | custom-call | flops 1000 | bytes 1000 | tf_op jit(solution)/shard_map/fc2_grad/pallas_call | solution.py:829
  121.4 4.5 %fc1_grad.1 = (f32[4,2,64,1024]{3,2,1,0:T(8,128)}, f32[4,2,64,1024]{3,2,1,0:T(8,128)S(1)}) custom-call(bf16[512,256]{1,0:T(8,128)(2,1)S(1)} %get-tuple-element.199.ka_ref, bf16[512,256]{1,0:T(8,128)(2,1)S(1)} %get-tuple-element.200.kb_ref, f32[10,256,256]{2,1,0:T(8,128)S(1)} %collective-permute-done.12.la_ref.oa_ref, ...), custom_call_target="tpu_custom_call" | custom-call | flops 1000 | bytes 1000 | tf_op jit(solution)/shard_map/fc1_grad/pallas_call | solution.py:829
  125.9 2.1 collective-permute-start.21
  128.1 1.4 collective-permute-done.10.refs_3_
  130.1 8.1 %attn_backward.2 = (f32[256,1024]{1,0:T(8,128)S(1)}, bf16[256,1024]{1,0:T(8,128)(2,1)}, bf16[3,256,512]{2,1,0:T(8,128)(2,1)S(1)}, f32[8,1024]{1,0:T(8,128)S(1)},...) custom-call(s32[9]{0:T(128)S(1)} %pad_add_fusion.place, ...), custom_call_target="tpu_custom_call" | custom-call | flops 99999997952 | bytes 1000 | tf_op jit(solution)/shard_map/attn_backward/pallas_call | solution.py:446
  140.3 13.4 %collective-permute-done.15.refs_1_ = f32[256,1024]{1,0:T(8,128)S(1)} collective-permute-done((f32[256,1024]{1,0:T(8,128)S(1)}, f32[256,1024]{1,0:T(8,128)S(1)}, u32[]{:S(2)}, u32[]{:S(2)}) %collective-permute-start.15) | collective-permute-done | bytes 1048608 | tf_op jit(solution)/shard_map/ppermute | solution.py:916
  154.5 8.1 %attn_backward.3 = (f32[256,1024]{1,0:T(8,128)S(1)}, bf16[256,1024]{1,0:T(8,128)(2,1)}, bf16[3,256,512]{2,1,0:T(8,128)(2,1)S(1)}, f32[8,1024]{1,0:T(8,128)S(1)},...) custom-call(s32[9]{0:T(128)S(1)} %pad_add_fusion.place, ...), custom_call_target="tpu_custom_call" | custom-call | flops 99999997952 | bytes 1000 | tf_op jit(solution)/shard_map/attn_backward/pallas_call | solution.py:446
  163.2 2.6 mlp_out.3
  167.0 1.5 collective-permute-done.17
  168.5 1.4 slice_add_fusion
  169.9 2.0 collective-permute-start.23
  171.9 3.6 %query_key_grad.1 = (f32[4,64,1024]{2,1,0:T(8,128)S(1)}, f32[4,64,1024]{2,1,0:T(8,128)S(1)}) custom-call(bf16[512,256]{1,0:T(8,128)(2,1)S(1)} %get-tuple-element.230.aa_ref, bf16[512,256]{1,0:T(8,128)(2,1)S(1)} %get-tuple-element.231.ab_ref, f32[4,256,256]{2,1,0:T(8,128)} %collective-permute-done.7.fa_ref, f32[4,256,256]{2,1,0:T(8,128)S(1)} %copy-done.11, ...), custom_call_target="tpu_custom_call" | custom-call | flops 1000 | bytes 1000 | tf_op jit(solution)/shard_map/query_key_grad/pallas_call | solution.py:902
  176.6 1.4 bitcast_add_fusion
  178.0 1.5 pad_maximum_fusion
  179.5 4.9 %value_out_grad.1 = (f32[4,64,1024]{2,1,0:T(8,128)}, f32[4,64,1024]{2,1,0:T(8,128)S(1)}) custom-call(bf16[512,256]{1,0:T(8,128)(2,1)S(1)} %get-tuple-element.230.aa_ref, bf16[512,256]{1,0:T(8,128)(2,1)S(1)} %get-tuple-element.231.ab_ref, f32[4,256,256]{2,1,0:T(8,128)} %collective-permute-done.7.fa_ref, f32[4,256,256]{2,1,0:T(8,128)S(1)} %copy-done.11, ...), custom_call_target="tpu_custom_call" | custom-call | flops 1000 | bytes 1000 | tf_op jit(solution)/shard_map/value_out_grad/pallas_call | solution.py:902
  187.9 2.2 first_norm_back.2
  190.1 7.1 %collective-permute-done.23 = f32[2,64,2048]{2,1,0:T(8,128)S(1)} collective-permute-done((f32[2,64,2048]{2,1,0:T(8,128)S(1)}, f32[2,64,2048]{2,1,0:T(8,128)S(1)}, u32[]{:S(2)}, u32[]{:S(2)}) %collective-permute-start.23) | collective-permute-done | bytes 1048608 | tf_op jit(solution)/shard_map/ppermute | solution.py:916
  197.2 2.3 slice_add_fusion.5
  199.5 3.0 collective-permute-start.28
  203.3 7.4 %collective-permute-done.22.refs_1_ = f32[256,1024]{1,0:T(8,128)S(1)} collective-permute-done((f32[256,1024]{1,0:T(8,128)S(1)}, f32[256,1024]{1,0:T(8,128)S(1)}, u32[]{:S(2)}, u32[]{:S(2)}) %collective-permute-start.22) | collective-permute-done | bytes 1048608 | tf_op jit(solution)/shard_map/ppermute | solution.py:916
  210.7 2.2 first_norm_back.3
  213.5 1.5 collective-permute-start.26
  215.1 2.6 pixel_grad.2.refs_0_
  218.8 3.9 %embed_grad_b.1 = (f32[4,72,1024]{2,1,0:T(8,128)}, f32[4,72,1024]{2,1,0:T(8,128)S(1)}) custom-call(bf16[512,256]{1,0:T(8,128)(2,1)S(1)} %get-tuple-element.253.ka_ref, bf16[512,256]{1,0:T(8,128)(2,1)S(1)} %copy-done.26, f32[1072,256]{1,0:T(8,128)S(1)} %collective-permute-done.24.la_ref.lb_ref, f32[1072,256]{1,0:T(8,128)S(1)} %collective-permute-done.24.la_ref.lb_ref, ...), custom_call_target="tpu_custom_call" | custom-call | flops 1000 | bytes 1000 | tf_op jit(solution)/shard_map/embed_grad_b/pallas_call | solution.py:829
  224.1 3.2 embed_grad_a.1
  227.4 2.5 pixel_grad.3
  229.9 2.4 collective-permute-done.25
  232.3 2.7 fusion
  234.9 2.1 collective-permute-done.26
  237.0 1.9 slice_add_fusion.3
  239.7 1.3 collective-permute-start.32
  241.9 3.0 collective-permute-start.31
  244.9 2.4 add_add_fusion
  247.3 6.8 %collective-permute-done.29 = f32[2,64,1024]{2,1,0:T(8,128)} collective-permute-done((f32[2,64,1024]{2,1,0:T(8,128)}, f32[2,64,1024]{2,1,0:T(8,128)}, u32[]{:S(2)}, u32[]{:S(2)}) %collective-permute-start.29) | collective-permute-done | bytes 524320 | tf_op jit(solution)/shard_map/ppermute | solution.py:916
  255.2 3.4 %collective-permute-start.35 = (f32[1,64,1024]{2,1,0:T(8,128)S(1)}, f32[1,64,1024]{2,1,0:T(8,128)S(1)}, u32[]{:S(2)}, u32[]{:S(2)}) collective-permute-start(f32[1,64,1024]{2,1,0:T(8,128)S(1)} %slice_add_fusion.9), channel_id=1, source_target_pairs={{0,16},{2,18},{4,20},{6,22},{8,24},{10,26},{12,28},{14,30},{16,0},... | collective-permute-start | bytes 786440 | tf_op jit(solution)/shard_map/ppermute | solution.py:916
  258.7 14.5 %collective-permute-done.30 = f32[4,72,1024]{2,1,0:T(8,128)} collective-permute-done((f32[4,72,1024]{2,1,0:T(8,128)}, f32[4,72,1024]{2,1,0:T(8,128)}, u32[]{:S(2)}, u32[]{:S(2)}) %collective-permute-start.30) | collective-permute-done | bytes 1179680 | tf_op jit(solution)/shard_map/ppermute | solution.py:916
  273.2 1.3 slice_add_fusion.1
  275.5 2.8 collective-permute-done.31
  278.4 1.4 fusion.2
  279.9 3.4 %collective-permute-start.36 = (f32[2,64,1024]{2,1,0:T(8,128)S(1)}, f32[2,64,1024]{2,1,0:T(8,128)S(1)}, u32[]{:S(2)}, u32[]{:S(2)}) collective-permute-start(f32[2,64,1024]{2,1,0:T(8,128)S(1)} %slice_add_fusion.2), channel_id=1, source_target_pairs={{0,8},{2,10},{4,12},{6,14},{8,0},{10,2},{12,4},{14,6},{16,24},{18,... | collective-permute-start | bytes 1572872 | tf_op jit(solution)/shard_map/ppermute | solution.py:916
  285.3 2.7 collective-permute-start.37
  292.7 11.8 %collective-permute-done.36 = f32[2,64,1024]{2,1,0:T(8,128)S(1)} collective-permute-done((f32[2,64,1024]{2,1,0:T(8,128)S(1)}, f32[2,64,1024]{2,1,0:T(8,128)S(1)}, u32[]{:S(2)}, u32[]{:S(2)}) %collective-permute-start.36) | collective-permute-done | bytes 524320 | tf_op jit(solution)/shard_map/ppermute | solution.py:916
  307.2 3.5 %collective-permute-done.38 = f32[256,1024]{1,0:T(8,128)S(1)} collective-permute-done((f32[256,1024]{1,0:T(8,128)S(1)}, f32[256,1024]{1,0:T(8,128)S(1)}, u32[]{:S(2)}, u32[]{:S(2)}) %collective-permute-start.38) | collective-permute-done | bytes 1048608 | tf_op jit(solution)/shard_map/ppermute | solution.py:916
  310.7 2.1 add_convert_fusion.1
  313.9 5.1 %collective-permute-done.39 = f32[1,72,1024]{2,1,0:T(8,128)S(1)} collective-permute-done((f32[1,72,1024]{2,1,0:T(8,128)S(1)}, f32[1,72,1024]{2,1,0:T(8,128)S(1)}, u32[]{:S(2)}, u32[]{:S(2)}) %collective-permute-start.39) | collective-permute-done | bytes 294944 | tf_op jit(solution)/shard_map/ppermute | solution.py:916
  (222 shorter events, 42.7 us)
Async XLA Ops:
  5.7 26.4 %collective-permute-start = (f32[256,1024]{1,0:T(8,128)}, f32[256,1024]{1,0:T(8,128)S(1)}, u32[]{:S(2)}, u32[]{:S(2)}) collective-permute-start(f32[256,1024]{1,0:T(8,128)} %get-tuple-element.160.part_ref), channel_id=1, source_target_pairs={{0,1},{1,0},{2,3},{3,2},{4,5},{5,4},{6,7},{7,6},{8,9},{9,8},{10,11... | collective-permute-start | bytes 3145736 | tf_op jit(solution)/shard_map/ppermute | solution.py:916
  14.8 23.4 %collective-permute-start.3 = (f32[4,256,256]{2,1,0:T(8,128)S(1)}, f32[4,256,256]{2,1,0:T(8,128)S(1)}, u32[]{:S(2)}, u32[]{:S(2)}) collective-permute-start(f32[4,256,256]{2,1,0:T(8,128)S(1)} %get-tuple-element.164), channel_id=1, source_target_pairs={{0,2},{2,0},{4,6},{6,4},{8,10},{10,8},{12,14},{14,12},{16,18},{18,... | collective-permute-start | bytes 3145736 | tf_op jit(solution)/shard_map/ppermute | solution.py:916
  14.9 17.2 %copy-start.51 = (f32[256,1024]{1,0:T(8,128)S(1)}, f32[256,1024]{1,0:T(8,128)}, u32[]{:S(2)}) copy-start(f32[256,1024]{1,0:T(8,128)} %get-tuple-element.172.part_ref) | copy-start | bytes 3145732
  14.9 18.9 %copy-start.47 = (bf16[512,1024]{1,0:T(8,128)(2,1)S(1)}, bf16[512,1024]{1,0:T(8,128)(2,1)}, u32[]{:S(2)}) copy-start(bf16[512,1024]{1,0:T(8,128)(2,1)} %refs_5_.3) | copy-start | bytes 3145732
  14.9 18.9 %copy-start.49 = (f32[256,1024]{1,0:T(8,128)S(1)}, f32[256,1024]{1,0:T(8,128)}, u32[]{:S(2)}) copy-start(f32[256,1024]{1,0:T(8,128)} %get-tuple-element.160.part_ref) | copy-start | bytes 3145732
  18.0 15.8 %copy-start.41 = (f32[1024]{0:T(1024)S(1)}, f32[1024]{0:T(1024)}, u32[]{:S(2)}) copy-start(f32[1024]{0:T(1024)} %param.26) | copy-start | bytes 12292
  18.0 15.8 %copy-start.46 = (bf16[1024,3,512]{2,0,1:T(8,128)(2,1)S(1)}, bf16[1024,3,512]{2,0,1:T(8,128)(2,1)}, u32[]{:S(2)}) copy-start(bf16[1024,3,512]{2,0,1:T(8,128)(2,1)} %param.28) | copy-start | bytes 9437188
  18.0 15.8 %copy-start.55 = (f32[1024]{0:T(1024)S(1)}, f32[1024]{0:T(1024)}, u32[]{:S(2)}) copy-start(f32[1024]{0:T(1024)} %param.27) | copy-start | bytes 12292
  18.0 15.8 %copy-start.59 = (f32[512]{0:T(512)S(1)}, f32[512]{0:T(512)}, u32[]{:S(2)}) copy-start(f32[512]{0:T(512)} %param.29) | copy-start | bytes 6148
  18.0 15.8 %copy-start.60 = (f32[512]{0:T(512)S(1)}, f32[512]{0:T(512)}, u32[]{:S(2)}) copy-start(f32[512]{0:T(512)} %param.30) | copy-start | bytes 6148
  18.0 44.2 %collective-permute-start.4 = (f32[8,256,256]{2,1,0:T(8,128)}, f32[8,256,256]{2,1,0:T(8,128)}, u32[]{:S(2)}, u32[]{:S(2)}) collective-permute-start(f32[8,256,256]{2,1,0:T(8,128)} %pack_pixels.2), channel_id=1, source_target_pairs={{0,2},{2,0},{4,6},{6,4},{8,10},{10,8},{12,14},{14,12},{16,18},{18,... | collective-permute-start | bytes 6291464 | tf_op jit(solution)/shard_map/ppermute | solution.py:916
  21.7 40.6 %collective-permute-start.5 = (f32[8,256,256]{2,1,0:T(8,128)}, f32[8,256,256]{2,1,0:T(8,128)}, u32[]{:S(2)}, u32[]{:S(2)}) collective-permute-start(f32[8,256,256]{2,1,0:T(8,128)} %pack_pixels.3), channel_id=1, source_target_pairs={{0,2},{2,0},{4,6},{6,4},{8,10},{10,8},{12,14},{14,12},{16,18},{18,... | collective-permute-start | bytes 6291464 | tf_op jit(solution)/shard_map/ppermute | solution.py:916
  32.1 24.3 %collective-permute-start.1 = (f32[256,1024]{1,0:T(8,128)S(1)}, f32[256,1024]{1,0:T(8,128)S(1)}, u32[]{:S(2)}, u32[]{:S(2)}) collective-permute-start(f32[256,1024]{1,0:T(8,128)S(1)} %copy-done.51), channel_id=1, source_target_pairs={{0,1},{1,0},{2,3},{3,2},{4,5},{5,4},{6,7},{7,6},{8,9},{9,8},{10,11... | collective-permute-start | bytes 3145736 | tf_op jit(solution)/shard_map/ppermute | solution.py:916
  38.2 24.0 %copy-start.8 = (f32[4,256,256]{2,1,0:T(8,128)}, f32[4,256,256]{2,1,0:T(8,128)S(1)}, u32[]{:S(2)}) copy-start(f32[4,256,256]{2,1,0:T(8,128)S(1)} %collective-permute-done.3.la_ref.lb_ref) | copy-start | bytes 3145732
  40.7 49.3 %collective-permute-start.7 = (f32[4,256,256]{2,1,0:T(8,128)}, f32[4,256,256]{2,1,0:T(8,128)}, u32[]{:S(2)}, u32[]{:S(2)}) collective-permute-start(f32[4,256,256]{2,1,0:T(8,128)} %get-tuple-element.178), channel_id=1, source_target_pairs={{0,2},{2,0},{4,6},{6,4},{8,10},{10,8},{12,14},{14,12},{16,18},{18,... | collective-permute-start | bytes 3145736 | tf_op jit(solution)/shard_map/ppermute | solution.py:916
  56.4 23.4 %collective-permute-start.2 = (f32[256,1024]{1,0:T(8,128)S(1)}, f32[256,1024]{1,0:T(8,128)S(1)}, u32[]{:S(2)}, u32[]{:S(2)}) collective-permute-start(f32[256,1024]{1,0:T(8,128)S(1)} %get-tuple-element.173.opart_ref), channel_id=1, source_target_pairs={{0,1},{1,0},{2,3},{3,2},{4,5},{5,4},{6,7},{7,6},{8,9},{9,8},{10,11... | collective-permute-start | bytes 3145736 | tf_op jit(solution)/shard_map/ppermute | solution.py:916
  57.8 23.3 %copy-start.44 = (bf16[1024,2048]{1,0:T(8,128)(2,1)S(1)}, bf16[1024,2048]{1,0:T(8,128)(2,1)}, u32[]{:S(2)}) copy-start(bf16[1024,2048]{1,0:T(8,128)(2,1)} %wfc1_ref.3) | copy-start | bytes 12582916
  57.8 23.3 %copy-start.45 = (bf16[2048,1024]{1,0:T(8,128)(2,1)S(1)}, bf16[2048,1024]{1,0:T(8,128)(2,1)}, u32[]{:S(2)}) copy-start(bf16[2048,1024]{1,0:T(8,128)(2,1)} %wfc2_ref.7) | copy-start | bytes 12582916
  57.8 23.3 %copy-start.54 = (f32[2048]{0:T(1024)S(1)}, f32[2048]{0:T(1024)}, u32[]{:S(2)}) copy-start(f32[2048]{0:T(1024)} %param.36) | copy-start | bytes 24580
  57.8 23.3 %copy-start.56 = (f32[1024]{0:T(1024)S(1)}, f32[1024]{0:T(1024)}, u32[]{:S(2)}) copy-start(f32[1024]{0:T(1024)} %param.32) | copy-start | bytes 12292
  57.8 23.3 %copy-start.57 = (f32[1024]{0:T(1024)S(1)}, f32[1024]{0:T(1024)}, u32[]{:S(2)}) copy-start(f32[1024]{0:T(1024)} %param.34) | copy-start | bytes 12292
  57.9 23.3 %copy-start.58 = (f32[1024]{0:T(1024)S(1)}, f32[1024]{0:T(1024)}, u32[]{:S(2)}) copy-start(f32[1024]{0:T(1024)} %param.33) | copy-start | bytes 12292
  62.3 18.9 %copy-start.39 = (bf16[256,512]{1,0:T(8,128)(2,1)}, bf16[256,512]{1,0:T(8,128)(2,1)S(1)}, u32[]{:S(2)}) copy-start(bf16[256,512]{1,0:T(8,128)(2,1)S(1)} %get-tuple-element.185.o_ref.mb_ref) | copy-start | bytes 786436
  63.1 26.9 %collective-permute-start.8 = (f32[4,256,256]{2,1,0:T(8,128)S(1)}, f32[4,256,256]{2,1,0:T(8,128)S(1)}, u32[]{:S(2)}, u32[]{:S(2)}) collective-permute-start(f32[4,256,256]{2,1,0:T(8,128)S(1)} %get-tuple-element.186), channel_id=1, source_target_pairs={{0,2},{2,0},{4,6},{6,4},{8,10},{10,8},{12,14},{14,12},{16,18},{18,... | collective-permute-start | bytes 3145736 | tf_op jit(solution)/shard_map/ppermute | solution.py:916
  79.8 23.3 %collective-permute-start.6 = (f32[256,1024]{1,0:T(8,128)S(1)}, f32[256,1024]{1,0:T(8,128)S(1)}, u32[]{:S(2)}, u32[]{:S(2)}) collective-permute-start(f32[256,1024]{1,0:T(8,128)S(1)} %get-tuple-element.190.opart_ref), channel_id=1, source_target_pairs={{0,1},{1,0},{2,3},{3,2},{4,5},{5,4},{6,7},{7,6},{8,9},{9,8},{10,11... | collective-permute-start | bytes 3145736 | tf_op jit(solution)/shard_map/ppermute | solution.py:916
  91.0 22.5 %collective-permute-start.12 = (f32[10,256,256]{2,1,0:T(8,128)S(1)}, f32[10,256,256]{2,1,0:T(8,128)S(1)}, u32[]{:S(2)}, u32[]{:S(2)}) collective-permute-start(f32[10,256,256]{2,1,0:T(8,128)S(1)} %get-tuple-element.203), channel_id=1, source_target_pairs={{0,2},{2,0},{4,6},{6,4},{8,10},{10,8},{12,14},{14,12},{16,18},{18,... | collective-permute-start | bytes 7864328 | tf_op jit(solution)/shard_map/ppermute | solution.py:916
  91.0 22.5 %collective-permute-start.11 = (f32[8,256,256]{2,1,0:T(8,128)S(1)}, f32[8,256,256]{2,1,0:T(8,128)S(1)}, u32[]{:S(2)}, u32[]{:S(2)}) collective-permute-start(f32[8,256,256]{2,1,0:T(8,128)S(1)} %get-tuple-element.202), channel_id=1, source_target_pairs={{0,2},{2,0},{4,6},{6,4},{8,10},{10,8},{12,14},{14,12},{16,18},{18,... | collective-permute-start | bytes 6291464 | tf_op jit(solution)/shard_map/ppermute | solution.py:916
  103.2 9.6 %collective-permute-start.9 = (f32[96,1024]{1,0:T(8,128)S(1)}, f32[96,1024]{1,0:T(8,128)S(1)}, u32[]{:S(2)}, u32[]{:S(2)}) collective-permute-start(f32[96,1024]{1,0:T(8,128)S(1)} %get-tuple-element.196.refs_0_), channel_id=1, source_target_pairs={{0,1},{1,0},{2,3},{3,2},{4,5},{5,4},{6,7},{7,6},{8,9},{9,8},{10,11... | collective-permute-start | bytes 1179656 | tf_op jit(solution)/shard_map/ppermute | solution.py:916
  112.3 42.2 %copy-start.21 = (f32[256,1024]{1,0:T(8,128)}, f32[256,1024]{1,0:T(8,128)S(1)}, u32[]{:S(2)}) copy-start(f32[256,1024]{1,0:T(8,128)S(1)} %get-tuple-element.220.refs_2_) | copy-start | bytes 3145732
  112.3 4.2 %collective-permute-start.13 = (f32[8,256,256]{2,1,0:T(8,128)S(1)}, f32[8,256,256]{2,1,0:T(8,128)S(1)}, u32[]{:S(2)}, u32[]{:S(2)}) collective-permute-start(f32[8,256,256]{2,1,0:T(8,128)S(1)} %get-tuple-element.210), channel_id=1, source_target_pairs={{0,2},{2,0},{4,6},{6,4},{8,10},{10,8},{12,14},{14,12},{16,18},{18,... | collective-permute-start | bytes 6291464 | tf_op jit(solution)/shard_map/ppermute | solution.py:916
  112.3 9.2 %collective-permute-start.14 = (f32[10,256,256]{2,1,0:T(8,128)S(1)}, f32[10,256,256]{2,1,0:T(8,128)S(1)}, u32[]{:S(2)}, u32[]{:S(2)}) collective-permute-start(f32[10,256,256]{2,1,0:T(8,128)S(1)} %get-tuple-element.213), channel_id=1, source_target_pairs={{0,2},{2,0},{4,6},{6,4},{8,10},{10,8},{12,14},{14,12},{16,18},{18,... | collective-permute-start | bytes 7864328 | tf_op jit(solution)/shard_map/ppermute | solution.py:916
  112.8 16.6 %collective-permute-start.10 = (f32[160,1024]{1,0:T(8,128)S(1)}, f32[160,1024]{1,0:T(8,128)S(1)}, u32[]{:S(2)}, u32[]{:S(2)}) collective-permute-start(f32[160,1024]{1,0:T(8,128)S(1)} %get-tuple-element.198.refs_1_), channel_id=1, source_target_pairs={{0,1},{1,0},{2,3},{3,2},{4,5},{5,4},{6,7},{7,6},{8,9},{9,8},{10,11... | collective-permute-start | bytes 1966088 | tf_op jit(solution)/shard_map/ppermute | solution.py:916
  120.5 76.7 %copy-start.16 = (f32[4,64,2048]{2,1,0:T(8,128)}, f32[4,64,2048]{2,1,0:T(8,128)S(1)}, u32[]{:S(2)}) copy-start(f32[4,64,2048]{2,1,0:T(8,128)S(1)} %get-tuple-element.232) | copy-start | bytes 6291460
  120.5 48.0 %collective-permute-start.17 = (f32[4,64,2048]{2,1,0:T(8,128)}, f32[4,64,2048]{2,1,0:T(8,128)}, u32[]{:S(2)}, u32[]{:S(2)}) collective-permute-start(f32[4,64,2048]{2,1,0:T(8,128)} %get-tuple-element.212), channel_id=1, source_target_pairs={{0,4},{2,6},{4,0},{6,2},{8,12},{10,14},{12,8},{14,10},{16,20},{18,... | collective-permute-start | bytes 6291464 | tf_op jit(solution)/shard_map/ppermute | solution.py:916
  125.9 50.6 %collective-permute-start.21 = (f32[8,64,1024]{2,1,0:T(8,128)}, f32[8,64,1024]{2,1,0:T(8,128)}, u32[]{:S(2)}, u32[]{:S(2)}) collective-permute-start(f32[8,64,1024]{2,1,0:T(8,128)} %bitcast.12), channel_id=1, source_target_pairs={{0,8},{2,10},{4,12},{6,14},{8,0},{10,2},{12,4},{14,6},{16,24},{18,... | collective-permute-start | bytes 6291464 | tf_op jit(solution)/shard_map/ppermute | solution.py:916
  129.4 24.3 %collective-permute-start.15 = (f32[256,1024]{1,0:T(8,128)S(1)}, f32[256,1024]{1,0:T(8,128)S(1)}, u32[]{:S(2)}, u32[]{:S(2)}) collective-permute-start(f32[256,1024]{1,0:T(8,128)S(1)} %get-tuple-element.219.refs_0_), channel_id=1, source_target_pairs={{0,1},{1,0},{2,3},{3,2},{4,5},{5,4},{6,7},{7,6},{8,9},{9,8},{10,11... | collective-permute-start | bytes 3145736 | tf_op jit(solution)/shard_map/ppermute | solution.py:916
  153.8 9.5 %collective-permute-start.16 = (f32[96,1024]{1,0:T(8,128)S(1)}, f32[96,1024]{1,0:T(8,128)S(1)}, u32[]{:S(2)}, u32[]{:S(2)}) collective-permute-start(f32[96,1024]{1,0:T(8,128)S(1)} %get-tuple-element.227.refs_0_), channel_id=1, source_target_pairs={{0,1},{1,0},{2,3},{3,2},{4,5},{5,4},{6,7},{7,6},{8,9},{9,8},{10,11... | collective-permute-start | bytes 1179656 | tf_op jit(solution)/shard_map/ppermute | solution.py:916
  162.5 9.4 %collective-permute-start.19 = (f32[8,256,256]{2,1,0:T(8,128)S(1)}, f32[8,256,256]{2,1,0:T(8,128)S(1)}, u32[]{:S(2)}, u32[]{:S(2)}) collective-permute-start(f32[8,256,256]{2,1,0:T(8,128)S(1)} %get-tuple-element.237), channel_id=1, source_target_pairs={{0,2},{2,0},{4,6},{6,4},{8,10},{10,8},{12,14},{14,12},{16,18},{18,... | collective-permute-start | bytes 6291464 | tf_op jit(solution)/shard_map/ppermute | solution.py:916
  163.2 8.7 %collective-permute-start.18 = (f32[8,256,256]{2,1,0:T(8,128)S(1)}, f32[8,256,256]{2,1,0:T(8,128)S(1)}, u32[]{:S(2)}, u32[]{:S(2)}) collective-permute-start(f32[8,256,256]{2,1,0:T(8,128)S(1)} %get-tuple-element.235), channel_id=1, source_target_pairs={{0,2},{2,0},{4,6},{6,4},{8,10},{10,8},{12,14},{14,12},{16,18},{18,... | collective-permute-start | bytes 6291464 | tf_op jit(solution)/shard_map/ppermute | solution.py:916
  165.9 20.8 %collective-permute-start.20 = (f32[160,1024]{1,0:T(8,128)S(1)}, f32[160,1024]{1,0:T(8,128)S(1)}, u32[]{:S(2)}, u32[]{:S(2)}) collective-permute-start(f32[160,1024]{1,0:T(8,128)S(1)} %get-tuple-element.243.refs_1_), channel_id=1, source_target_pairs={{0,1},{1,0},{2,3},{3,2},{4,5},{5,4},{6,7},{7,6},{8,9},{9,8},{10,11... | collective-permute-start | bytes 1966088 | tf_op jit(solution)/shard_map/ppermute | solution.py:916
  169.9 27.3 %collective-permute-start.23 = (f32[2,64,2048]{2,1,0:T(8,128)S(1)}, f32[2,64,2048]{2,1,0:T(8,128)S(1)}, u32[]{:S(2)}, u32[]{:S(2)}) collective-permute-start(f32[2,64,2048]{2,1,0:T(8,128)S(1)} %slice_add_fusion), channel_id=1, source_target_pairs={{0,8},{2,10},{4,12},{6,14},{8,0},{10,2},{12,4},{14,6},{16,24},{18,... | collective-permute-start | bytes 3145736 | tf_op jit(solution)/shard_map/ppermute | solution.py:916
  185.4 46.9 %collective-permute-start.25 = (f32[8,64,1024]{2,1,0:T(8,128)}, f32[8,64,1024]{2,1,0:T(8,128)}, u32[]{:S(2)}, u32[]{:S(2)}) collective-permute-start(f32[8,64,1024]{2,1,0:T(8,128)} %pad_maximum_fusion), channel_id=1, source_target_pairs={{0,4},{2,6},{4,0},{6,2},{8,12},{10,14},{12,8},{14,10},{16,20},{18,... | collective-permute-start | bytes 6291464 | tf_op jit(solution)/shard_map/ppermute | solution.py:916
  186.5 50.6 %collective-permute-start.27 = (f32[4,64,1024]{2,1,0:T(8,128)}, f32[4,64,1024]{2,1,0:T(8,128)}, u32[]{:S(2)}, u32[]{:S(2)}) collective-permute-start(f32[4,64,1024]{2,1,0:T(8,128)} %get-tuple-element.251), channel_id=1, source_target_pairs={{0,8},{2,10},{4,12},{6,14},{8,0},{10,2},{12,4},{14,6},{16,24},{18,... | collective-permute-start | bytes 3145736 | tf_op jit(solution)/shard_map/ppermute | solution.py:916
  186.7 24.0 %collective-permute-start.22 = (f32[256,1024]{1,0:T(8,128)S(1)}, f32[256,1024]{1,0:T(8,128)S(1)}, u32[]{:S(2)}, u32[]{:S(2)}) collective-permute-start(f32[256,1024]{1,0:T(8,128)S(1)} %get-tuple-element.255.refs_0_), channel_id=1, source_target_pairs={{0,1},{1,0},{2,3},{3,2},{4,5},{5,4},{6,7},{7,6},{8,9},{9,8},{10,11... | collective-permute-start | bytes 3145736 | tf_op jit(solution)/shard_map/ppermute | solution.py:916
  187.9 27.1 %copy-start.12 = (bf16[384,1024]{1,0:T(8,128)(2,1)S(1)}, bf16[384,1024]{1,0:T(8,128)(2,1)}, u32[]{:S(2)}) copy-start(bf16[384,1024]{1,0:T(8,128)(2,1)} %wrgb_ref.7) | copy-start | bytes 2359300
  199.5 42.4 %collective-permute-start.28 = (f32[1,64,2048]{2,1,0:T(8,128)}, f32[1,64,2048]{2,1,0:T(8,128)}, u32[]{:S(2)}, u32[]{:S(2)}) collective-permute-start(f32[1,64,2048]{2,1,0:T(8,128)} %slice_add_fusion.5), channel_id=1, source_target_pairs={{0,16},{2,18},{4,20},{6,22},{8,24},{10,26},{12,28},{14,30},{16,0},... | collective-permute-start | bytes 1572872 | tf_op jit(solution)/shard_map/ppermute | solution.py:916
  213.5 23.5 %collective-permute-start.26 = (f32[256,1024]{1,0:T(8,128)}, f32[256,1024]{1,0:T(8,128)}, u32[]{:S(2)}, u32[]{:S(2)}) collective-permute-start(f32[256,1024]{1,0:T(8,128)} %mlp_out.3), channel_id=1, source_target_pairs={{0,1},{1,0},{2,3},{3,2},{4,5},{5,4},{6,7},{7,6},{8,9},{9,8},{10,11... | collective-permute-start | bytes 3145736 | tf_op jit(solution)/shard_map/ppermute | solution.py:916
  215.0 2.7 collective-permute-start.24
  223.8 49.4 %collective-permute-start.30 = (f32[4,72,1024]{2,1,0:T(8,128)}, f32[4,72,1024]{2,1,0:T(8,128)}, u32[]{:S(2)}, u32[]{:S(2)}) collective-permute-start(f32[4,72,1024]{2,1,0:T(8,128)} %get-tuple-element.276), channel_id=1, source_target_pairs={{0,8},{2,10},{4,12},{6,14},{8,0},{10,2},{12,4},{14,6},{16,24},{18,... | collective-permute-start | bytes 3538952 | tf_op jit(solution)/shard_map/ppermute | solution.py:916
  239.0 34.2 %copy-start.18 = (f32[4,72,1024]{2,1,0:T(8,128)S(1)}, f32[4,72,1024]{2,1,0:T(8,128)}, u32[]{:S(2)}) copy-start(f32[4,72,1024]{2,1,0:T(8,128)} %copy-done.17) | copy-start | bytes 3538948
  239.0 15.2 %collective-permute-start.29 = (f32[2,64,1024]{2,1,0:T(8,128)}, f32[2,64,1024]{2,1,0:T(8,128)}, u32[]{:S(2)}, u32[]{:S(2)}) collective-permute-start(f32[2,64,1024]{2,1,0:T(8,128)} %slice_add_fusion.3), channel_id=1, source_target_pairs={{0,4},{2,6},{4,0},{6,2},{8,12},{10,14},{12,8},{14,10},{16,20},{18,... | collective-permute-start | bytes 1572872 | tf_op jit(solution)/shard_map/ppermute | solution.py:916
  239.7 40.1 %collective-permute-start.32 = (f32[4,64,1024]{2,1,0:T(8,128)}, f32[4,64,1024]{2,1,0:T(8,128)S(1)}, u32[]{:S(2)}, u32[]{:S(2)}) collective-permute-start(f32[4,64,1024]{2,1,0:T(8,128)} %copy-done.50), channel_id=1, source_target_pairs={{0,4},{2,6},{4,0},{6,2},{8,12},{10,14},{12,8},{14,10},{16,20},{18,... | collective-permute-start | bytes 3145736 | tf_op jit(solution)/shard_map/ppermute | solution.py:916
  241.0 43.3 %collective-permute-start.33 = (f32[2,64,1024]{2,1,0:T(8,128)}, f32[2,64,1024]{2,1,0:T(8,128)S(1)}, u32[]{:S(2)}, u32[]{:S(2)}) collective-permute-start(f32[2,64,1024]{2,1,0:T(8,128)} %get-tuple-element.304), channel_id=1, source_target_pairs={{0,8},{2,10},{4,12},{6,14},{8,0},{10,2},{12,4},{14,6},{16,24},{18,... | collective-permute-start | bytes 1572872 | tf_op jit(solution)/shard_map/ppermute | solution.py:916
  241.9 36.4 %collective-permute-start.31 = (f32[2,64,1024]{2,1,0:T(8,128)}, f32[2,64,1024]{2,1,0:T(8,128)S(1)}, u32[]{:S(2)}, u32[]{:S(2)}) collective-permute-start(f32[2,64,1024]{2,1,0:T(8,128)} %get-tuple-element.303), channel_id=1, source_target_pairs={{0,16},{2,18},{4,20},{6,22},{8,24},{10,26},{12,28},{14,30},{16,0},... | collective-permute-start | bytes 1572872 | tf_op jit(solution)/shard_map/ppermute | solution.py:916
  255.2 36.3 %collective-permute-start.35 = (f32[1,64,1024]{2,1,0:T(8,128)S(1)}, f32[1,64,1024]{2,1,0:T(8,128)S(1)}, u32[]{:S(2)}, u32[]{:S(2)}) collective-permute-start(f32[1,64,1024]{2,1,0:T(8,128)S(1)} %slice_add_fusion.9), channel_id=1, source_target_pairs={{0,16},{2,18},{4,20},{6,22},{8,24},{10,26},{12,28},{14,30},{16,0},... | collective-permute-start | bytes 786440 | tf_op jit(solution)/shard_map/ppermute | solution.py:916
  274.4 15.7 %collective-permute-start.34 = (f32[2,72,1024]{2,1,0:T(8,128)S(1)}, f32[2,72,1024]{2,1,0:T(8,128)S(1)}, u32[]{:S(2)}, u32[]{:S(2)}) collective-permute-start(f32[2,72,1024]{2,1,0:T(8,128)S(1)} %slice_add_fusion.1), channel_id=1, source_target_pairs={{0,4},{2,6},{4,0},{6,2},{8,12},{10,14},{12,8},{14,10},{16,20},{18,... | collective-permute-start | bytes 1769480 | tf_op jit(solution)/shard_map/ppermute | solution.py:916
  279.9 24.7 %collective-permute-start.36 = (f32[2,64,1024]{2,1,0:T(8,128)S(1)}, f32[2,64,1024]{2,1,0:T(8,128)S(1)}, u32[]{:S(2)}, u32[]{:S(2)}) collective-permute-start(f32[2,64,1024]{2,1,0:T(8,128)S(1)} %slice_add_fusion.2), channel_id=1, source_target_pairs={{0,8},{2,10},{4,12},{6,14},{8,0},{10,2},{12,4},{14,6},{16,24},{18,... | collective-permute-start | bytes 1572872 | tf_op jit(solution)/shard_map/ppermute | solution.py:916
  285.3 19.4 %collective-permute-start.37 = (f32[1,64,1024]{2,1,0:T(8,128)S(1)}, f32[1,64,1024]{2,1,0:T(8,128)S(1)}, u32[]{:S(2)}, u32[]{:S(2)}) collective-permute-start(f32[1,64,1024]{2,1,0:T(8,128)S(1)} %slice_add_fusion.8), channel_id=1, source_target_pairs={{0,16},{2,18},{4,20},{6,22},{8,24},{10,26},{12,28},{14,30},{16,0},... | collective-permute-start | bytes 786440 | tf_op jit(solution)/shard_map/ppermute | solution.py:916
  288.0 22.7 %collective-permute-start.38 = (f32[256,1024]{1,0:T(8,128)S(1)}, f32[256,1024]{1,0:T(8,128)S(1)}, u32[]{:S(2)}, u32[]{:S(2)}) collective-permute-start(f32[256,1024]{1,0:T(8,128)S(1)} %copy-done.24), channel_id=1, source_target_pairs={{0,1},{1,0},{2,3},{3,2},{4,5},{5,4},{6,7},{7,6},{8,9},{9,8},{10,11... | collective-permute-start | bytes 3145736 | tf_op jit(solution)/shard_map/ppermute | solution.py:916
  291.2 27.8 %collective-permute-start.39 = (f32[1,72,1024]{2,1,0:T(8,128)S(1)}, f32[1,72,1024]{2,1,0:T(8,128)S(1)}, u32[]{:S(2)}, u32[]{:S(2)}) collective-permute-start(f32[1,72,1024]{2,1,0:T(8,128)S(1)} %slice_add_fusion.6), channel_id=1, source_target_pairs={{0,16},{2,18},{4,20},{6,22},{8,24},{10,26},{12,28},{14,30},{16,0},... | collective-permute-start | bytes 884744 | tf_op jit(solution)/shard_map/ppermute | solution.py:916
  292.7 18.0 %copy-start.20 = (f32[256,1024]{1,0:T(8,128)S(1)}, f32[256,1024]{1,0:T(8,128)}, u32[]{:S(2)}) copy-start(f32[256,1024]{1,0:T(8,128)} %copy-done.19) | copy-start | bytes 3145732
  292.7 18.0 %copy-start.22 = (f32[256,1024]{1,0:T(8,128)S(1)}, f32[256,1024]{1,0:T(8,128)}, u32[]{:S(2)}) copy-start(f32[256,1024]{1,0:T(8,128)} %copy-done.21) | copy-start | bytes 3145732
  292.7 18.0 %copy-start.65 = (f32[1024]{0:T(1024)S(1)}, f32[1024]{0:T(1024)}, u32[]{:S(2)}) copy-start(f32[1024]{0:T(1024)} %param.38) | copy-start | bytes 12292
  304.6 18.0 %collective-permute-start.40 = (f32[1,64,1024]{2,1,0:T(8,128)S(1)}, f32[1,64,1024]{2,1,0:T(8,128)S(1)}, u32[]{:S(2)}, u32[]{:S(2)}) collective-permute-start(f32[1,64,1024]{2,1,0:T(8,128)S(1)} %slice_add_fusion.7), channel_id=1, source_target_pairs={{0,16},{2,18},{4,20},{6,22},{8,24},{10,26},{12,28},{14,30},{16,0},... | collective-permute-start | bytes 786440 | tf_op jit(solution)/shard_map/ppermute | solution.py:916
  (45 other events, 220.6 us)

commit v9 on v8

--- a/solution.py
+++ b/solution.py
@@ -513,6 +513,8 @@
         gact_ref[part] = act[:, columns].astype(F32)
         gpre_ref[2 + step * (act.shape[1] // PART) + part] = dpre[:, columns].astype(F32)
     b1sum_ref[...] = column_sum(dpre.astype(F32))
+    if not da2_refs:
+        return
     da2 = nt(dpre, wfc1_ref[...])
 
     @pl.when(step == 0)
@@ -580,11 +582,31 @@
     )(place, x0, opart, orecv, out_bias, gain, bias, w_fc1, fc1_bias, w_fc2, cotangent)
 
 
+def mlp_back_kernel(dpre_ref, wfc1_ref, out_ref):
+    out_ref[...] = nt(dpre_ref[...], wfc1_ref[...])
+
+
+def mlp_back(dpre, w_fc1):
+    rows, hidden = dpre.shape
+    width = w_fc1.shape[0]
+    tile = 512
+    return pl.pallas_call(
+        mlp_back_kernel,
+        grid=(width // tile,),
+        in_specs=[whole(dpre.shape), pl.BlockSpec((tile, hidden), lambda n: (n, 0))],
+        out_specs=pl.BlockSpec((rows, tile), lambda n: (0, n)),
+        out_shape=jax.ShapeDtypeStruct((rows, width), F32),
+        compiler_params=params(6),
+        cost_estimate=long_cost(),
+        name="mlp_back",
+    )(dpre, w_fc1)
+
+
 def mlp_out_kernel(act_ref, wfc2_ref, out_ref):
     out_ref[...] = nn(act_ref[...], wfc2_ref[...])
 
 
-def mlp_out(act, w_fc2):
+def mlp_out(act, w_fc2, estimate):
     rows, hidden = act.shape
     width = w_fc2.shape[1]
     tile = 512
@@ -595,7 +617,7 @@
         out_specs=pl.BlockSpec((rows, tile), lambda n: (0, n)),
         out_shape=jax.ShapeDtypeStruct((rows, width), F32),
         compiler_params=params(6),
-        cost_estimate=long_cost(),
+        cost_estimate=estimate,
         name="mlp_out",
     )(act, w_fc2)
 
@@ -1080,10 +1102,10 @@
     for i in range(items):
         ffn[i] = mlp(
             place, x0[i], fwd[i][4], orecv[i], order.tie(ob), g2, c2, w_fc1, b1, w_fc2, cotangent, i,
-            cuts[i],
+            cuts[i] if i == 0 else (),
         )
         da2[i] = ffn[i][8:]
-        order.mark(da2[i][0])
+        order.mark(da2[i][0] if i == 0 else ffn[i][6])
         if i == 0:
             grecv[i] = [send(v) for v in da2[i]]
         gact[i] = other(ffn[i][6])
@@ -1093,8 +1115,8 @@
         else:
             grecv[0][0] = settle(grecv[0][0])
             gact[0], gpre[0] = settle((gact[0], gpre[0]))
-            ycot[1] = mlp_out(order.tie(ffn[1][2]), w_fc2)
-            order.mark(ycot[1])
+            da2[1] = [mlp_back(order.tie(ffn[1][3]), w_fc1)]
+            order.mark(da2[1][0])
     x1, a2, act, dpre, b1sum, ka2 = list(zip(*[v[:6] for v in ffn]))
     if custom:
         gact[1] = order.tie(gact[1])
@@ -1122,10 +1144,12 @@
         order.mark(da1[i][0])
         if i == 0:
             arecv[i] = [send(v) for v in da1[i]]
+            ycot[1] = mlp_out(order.tie(ffn[1][2]), w_fc2, short_cost())
+            order.mark(ycot[1])
         else:
             arecv[0][0] = settle(arecv[0][0])
             gbwd = [other(order.tie(bwd[0][6])), other(bwd[1][6])]
-            ycot[0] = mlp_out(order.tie(ffn[0][2]), w_fc2)
+            ycot[0] = mlp_out(order.tie(ffn[0][2]), w_fc2, long_cost())
             order.mark(ycot[0])
     dx1, dya, dqkv, sums2, qvsum, kdya = list(zip(*[v[:6] for v in bwd]))
     if custom:

time: 329 us -> 325 us (0.988)
    unnamed x136 -> x142, local copies, waits for them, and re-layouts: 9.61 us -> 8.06 us
where the time goes in v9:
time: 325 us; the launch traced here: 321 us
  waiting for transfers between devices  139 us (43%)
  Pallas kernels  97.5 us (30%)
  starting transfers between devices  42.6 us (13%)
  other arithmetic  30.3 us (9%)
  local copies, waits for them, and re-layouts  10.6 us (3%)
    ppermute x41, waiting for transfers between devices, exchange(): return lax.ppermute(values, axis, [(i, i ^ bit) for i in range(size)])  139 us
    ppermute x41, starting transfers between devices, exchange(): return lax.ppermute(values, axis, [(i, i ^ bit) for i in range(size)])  42.6 us
    add x16, other arithmetic, value(): value = value + recv[first:first + count]  21.2 us
    pallas_call x2, Pallas kernels, attn_backward(): pl.pallas_call(functools.partial(attn_backward_kernel, parts=(len(gparts)...  16.4 us
    pallas_call x4, Pallas kernels, plain_grad(): pl.pallas_call(functools.partial(plain_grad_kernel, moves=moves, vectors=...  15.6 us
    pallas_call x2, Pallas kernels, mlp(): pl.pallas_call(mlp_kernel, grid_spec=pltpu.PrefetchScalarGridSpec(num_sca...  12.7 us
    pallas_call x2, Pallas kernels, embed(): pl.pallas_call(functools.partial(embed_kernel, item=item), grid_spec=pltp...  9.44 us
    pallas_call x2, Pallas kernels, attn_forward(): pl.pallas_call(attn_forward_kernel, grid=(steps,), in_specs=[whole(part.s...  8.75 us
  transfers between devices with their start and end apart: 41, of which 21 were waited for; matrix products, arithmetic and copies ran while one was open for 10% of the time, Pallas kernels for 29%

profile of v9, /device:TPU:0, one launch (start us, length us, event | category | flops | bytes accessed | tf_op | source)
XLA Modules:
  0.0 321.4 jit_solution(13975511475297139276)
XLA Ops:
  0.7 4.7 %embed.2 = (f32[256,1024]{1,0:T(8,128)}, bf16[256,2048]{1,0:T(8,128)(2,1)}) custom-call(s32[2]{0:T(128)} %kinds.4, bf16[512,1664]{1,0:T(8,128)(2,1)} %pix_ref.3, bf16[1664,1024]{1,0:T(8,128)(2,1)} %wspec_ref.7, bf16[384,1024]{1,0:T(8,128)(2,1)} %wrgb_ref.7, bf16[1664,384]{1,0:T(8,128)(2,1)} %constant.50.clone.pick_ref), custom_call_target="tpu_custom_call" | custom-call | flops 1000 | bytes 1000 | tf_op jit(solution)/shard_map/embed/pallas_call | solution.py:242
  5.4 3.0 collective-permute-start
  8.5 4.7 %embed.3 = (f32[256,1024]{1,0:T(8,128)}, bf16[256,2048]{1,0:T(8,128)(2,1)}) custom-call(s32[2]{0:T(128)} %kinds.4, bf16[512,1664]{1,0:T(8,128)(2,1)} %pix_ref.3, bf16[1664,1024]{1,0:T(8,128)(2,1)} %wspec_ref.7, bf16[384,1024]{1,0:T(8,128)(2,1)} %wrgb_ref.7, bf16[1664,384]{1,0:T(8,128)(2,1)} %constant.50.clone.pick_ref), custom_call_target="tpu_custom_call" | custom-call | flops 1000 | bytes 1000 | tf_op jit(solution)/shard_map/embed/pallas_call | solution.py:242
  14.7 3.1 pack_pixels.2
  18.3 3.2 pack_pixels.3
  21.8 10.2 %collective-permute-done.recv_ref = f32[256,1024]{1,0:T(8,128)S(1)} collective-permute-done((f32[256,1024]{1,0:T(8,128)}, f32[256,1024]{1,0:T(8,128)S(1)}, u32[]{:S(2)}, u32[]{:S(2)}) %collective-permute-start) | collective-permute-done | bytes 1048608 | tf_op jit(solution)/shard_map/ppermute | solution.py:938
  32.1 1.7 collective-permute-start.1
  33.8 4.4 %attn_forward.2 = (f32[256,1024]{1,0:T(8,128)S(1)}, bf16[256,1024]{1,0:T(8,128)(2,1)S(1)}, bf16[3,256,512]{2,1,0:T(8,128)(2,1)S(1)}, bf16[256,512]{1,0:T(8,128)(2,1)S(1)}, f32[256,1024]{1,0:T(8,128)S(1)}) custom-call(f32[256,1024]{1,0:T(8,128)S(1)} %copy-done.52, f32[256,1024]{1,0:T(8,128)S(1)} %collective-permute-done.recv_ref, ...), custom_call_target="tpu_custom_call" | custom-call | flops 99999997952 | bytes 1000 | tf_op jit(solution)/shard_map/attn_forward/pallas_call | solution.py:330
  38.3 1.8 pack_attn.2
  40.0 16.7 %collective-permute-done.1.recv_ref = f32[256,1024]{1,0:T(8,128)S(1)} collective-permute-done((f32[256,1024]{1,0:T(8,128)S(1)}, f32[256,1024]{1,0:T(8,128)S(1)}, u32[]{:S(2)}, u32[]{:S(2)}) %collective-permute-start.1) | collective-permute-done | bytes 1048608 | tf_op jit(solution)/shard_map/ppermute | solution.py:938
  56.7 1.4 collective-permute-start.2
  58.2 4.4 %attn_forward.3 = (f32[256,1024]{1,0:T(8,128)S(1)}, bf16[256,1024]{1,0:T(8,128)(2,1)S(1)}, bf16[3,256,512]{2,1,0:T(8,128)(2,1)S(1)}, bf16[256,512]{1,0:T(8,128)(2,1)S(1)}, f32[256,1024]{1,0:T(8,128)S(1)}) custom-call(f32[256,1024]{1,0:T(8,128)S(1)} %copy-done.54, f32[256,1024]{1,0:T(8,128)S(1)} %collective-permute-done.1.recv_ref, ...), custom_call_target="tpu_custom_call" | custom-call | flops 99999997952 | bytes 1000 | tf_op jit(solution)/shard_map/attn_forward/pallas_call | solution.py:330
  63.5 17.0 %collective-permute-done.2.orecv_ref = f32[256,1024]{1,0:T(8,128)S(1)} collective-permute-done((f32[256,1024]{1,0:T(8,128)S(1)}, f32[256,1024]{1,0:T(8,128)S(1)}, u32[]{:S(2)}, u32[]{:S(2)}) %collective-permute-start.2) | collective-permute-done | bytes 1048608 | tf_op jit(solution)/shard_map/ppermute | solution.py:938
  81.6 7.8 %mlp.2 = (f32[256,1024]{1,0:T(8,128)S(1)}, bf16[256,1024]{1,0:T(8,128)(2,1)}, bf16[256,2048]{1,0:T(8,128)(2,1)S(1)}, bf16[256,2048]{1,0:T(8,128)(2,1)S(1)}, f32[...) custom-call(s32[9]{0:T(128)S(1)} %pad_add_fusion.place, ...), custom_call_target="tpu_custom_call" | custom-call | flops 99999997952 | bytes 1000 | tf_op jit(solution)/shard_map/mlp/pallas_call | solution.py:538
  90.9 12.8 %collective-permute-done.6.orecv_ref = f32[256,1024]{1,0:T(8,128)S(1)} collective-permute-done((f32[256,1024]{1,0:T(8,128)S(1)}, f32[256,1024]{1,0:T(8,128)S(1)}, u32[]{:S(2)}, u32[]{:S(2)}) %collective-permute-start.6) | collective-permute-done | bytes 1048608 | tf_op jit(solution)/shard_map/ppermute | solution.py:938
  104.9 4.9 %mlp.3 = (f32[256,1024]{1,0:T(8,128)S(1)}, bf16[256,1024]{1,0:T(8,128)(2,1)}, bf16[256,2048]{1,0:T(8,128)(2,1)S(1)}, bf16[256,2048]{1,0:T(8,128)(2,1)S(1)}, f32[...) custom-call(s32[9]{0:T(128)S(1)} %pad_add_fusion.place, ...), custom_call_target="tpu_custom_call" | custom-call | flops 99999997952 | bytes 1000 | tf_op jit(solution)/shard_map/mlp/pallas_call | solution.py:538
  110.4 1.3 collective-permute-done.9.refs_2_
  112.7 1.6 mlp_back.1.refs_0_
  114.3 4.1 %fc2_grad.1 = (f32[4,64,2048]{2,1,0:T(8,128)}, f32[4,64,2048]{2,1,0:T(8,128)S(1)}) custom-call(bf16[2,512,256]{2,1,0:T(8,128)(2,1)S(1)} %get-tuple-element.208.ka_ref.kb_ref, bf16[2,512,256]{2,1,0:T(8,128)(2,1)S(1)} %get-tuple-element.208.ka_ref.kb_ref, f32[4,256,256]{2,1,0:T(8,128)S(1)} %copy-done.9, f32[4,256,256]{2,1,0:T(8,128)S(1)} %copy-done.9, ...), custom_call_target="tpu_custom_call" | custom-call | flops 1000 | bytes 1000 | tf_op jit(solution)/shard_map/fc2_grad/pallas_call | solution.py:851
  118.9 4.3 %fc1_grad.1 = (f32[4,2,64,1024]{3,2,1,0:T(8,128)}, f32[4,2,64,1024]{3,2,1,0:T(8,128)S(1)}) custom-call(bf16[512,256]{1,0:T(8,128)(2,1)S(1)} %get-tuple-element.205.ka_ref, bf16[512,256]{1,0:T(8,128)(2,1)S(1)} %get-tuple-element.206.kb_ref, f32[10,256,256]{2,1,0:T(8,128)S(1)} %collective-permute-done.11.la_ref.oa_ref, ...), custom_call_target="tpu_custom_call" | custom-call | flops 1000 | bytes 1000 | tf_op jit(solution)/shard_map/fc1_grad/pallas_call | solution.py:851
  123.2 2.2 collective-permute-start.21
  125.4 1.8 collective-permute-done.12.refs_3_
  128.1 8.3 %attn_backward.2 = (f32[256,1024]{1,0:T(8,128)S(1)}, bf16[256,1024]{1,0:T(8,128)(2,1)}, bf16[3,256,512]{2,1,0:T(8,128)(2,1)S(1)}, f32[8,1024]{1,0:T(8,128)S(1)},...) custom-call(s32[9]{0:T(128)S(1)} %pad_add_fusion.place, ...), custom_call_target="tpu_custom_call" | custom-call | flops 99999997952 | bytes 1000 | tf_op jit(solution)/shard_map/attn_backward/pallas_call | solution.py:446
  137.4 1.8 mlp_out.2
  141.3 9.0 %collective-permute-done.15.refs_1_ = f32[256,1024]{1,0:T(8,128)S(1)} collective-permute-done((f32[256,1024]{1,0:T(8,128)S(1)}, f32[256,1024]{1,0:T(8,128)S(1)}, u32[]{:S(2)}, u32[]{:S(2)}) %collective-permute-start.15) | collective-permute-done | bytes 1048608 | tf_op jit(solution)/shard_map/ppermute | solution.py:938
  151.3 8.1 %attn_backward.3 = (f32[256,1024]{1,0:T(8,128)S(1)}, bf16[256,1024]{1,0:T(8,128)(2,1)}, bf16[3,256,512]{2,1,0:T(8,128)(2,1)S(1)}, f32[8,1024]{1,0:T(8,128)S(1)},...) custom-call(s32[9]{0:T(128)S(1)} %pad_add_fusion.place, ...), custom_call_target="tpu_custom_call" | custom-call | flops 99999997952 | bytes 1000 | tf_op jit(solution)/shard_map/attn_backward/pallas_call | solution.py:446
  159.9 2.5 mlp_out.3
  163.5 2.6 collective-permute-done.17
  166.1 1.4 slice_add_fusion
  167.5 1.6 collective-permute-start.23
  169.2 3.6 %query_key_grad.1 = (f32[4,64,1024]{2,1,0:T(8,128)S(1)}, f32[4,64,1024]{2,1,0:T(8,128)S(1)}) custom-call(bf16[512,256]{1,0:T(8,128)(2,1)S(1)} %get-tuple-element.230.aa_ref, bf16[512,256]{1,0:T(8,128)(2,1)S(1)} %get-tuple-element.231.ab_ref, f32[4,256,256]{2,1,0:T(8,128)} %collective-permute-done.7.fa_ref, f32[4,256,256]{2,1,0:T(8,128)S(1)} %copy-done.14, ...), custom_call_target="tpu_custom_call" | custom-call | flops 1000 | bytes 1000 | tf_op jit(solution)/shard_map/query_key_grad/pallas_call | solution.py:924
  173.8 1.4 bitcast_add_fusion
  175.2 1.5 pad_maximum_fusion
  176.7 4.9 %value_out_grad.1 = (f32[4,64,1024]{2,1,0:T(8,128)}, f32[4,64,1024]{2,1,0:T(8,128)S(1)}) custom-call(bf16[512,256]{1,0:T(8,128)(2,1)S(1)} %get-tuple-element.230.aa_ref, bf16[512,256]{1,0:T(8,128)(2,1)S(1)} %get-tuple-element.231.ab_ref, f32[4,256,256]{2,1,0:T(8,128)} %collective-permute-done.7.fa_ref, f32[4,256,256]{2,1,0:T(8,128)S(1)} %copy-done.14, ...), custom_call_target="tpu_custom_call" | custom-call | flops 1000 | bytes 1000 | tf_op jit(solution)/shard_map/value_out_grad/pallas_call | solution.py:924
  184.5 2.2 first_norm_back.2
  186.6 7.9 %collective-permute-done.23 = f32[2,64,2048]{2,1,0:T(8,128)S(1)} collective-permute-done((f32[2,64,2048]{2,1,0:T(8,128)S(1)}, f32[2,64,2048]{2,1,0:T(8,128)S(1)}, u32[]{:S(2)}, u32[]{:S(2)}) %collective-permute-start.23) | collective-permute-done | bytes 1048608 | tf_op jit(solution)/shard_map/ppermute | solution.py:938
  194.6 2.3 slice_add_fusion.5
  196.8 2.8 collective-permute-start.28
  200.3 6.9 %collective-permute-done.22.refs_1_ = f32[256,1024]{1,0:T(8,128)S(1)} collective-permute-done((f32[256,1024]{1,0:T(8,128)S(1)}, f32[256,1024]{1,0:T(8,128)S(1)}, u32[]{:S(2)}, u32[]{:S(2)}) %collective-permute-start.22) | collective-permute-done | bytes 1048608 | tf_op jit(solution)/shard_map/ppermute | solution.py:938
  207.2 2.2 first_norm_back.3
  210.1 1.5 collective-permute-start.26
  211.6 2.5 pixel_grad.2.refs_0_
  215.4 3.8 %embed_grad_b.1 = (f32[4,72,1024]{2,1,0:T(8,128)}, f32[4,72,1024]{2,1,0:T(8,128)S(1)}) custom-call(bf16[512,256]{1,0:T(8,128)(2,1)S(1)} %get-tuple-element.253.ka_ref, bf16[512,256]{1,0:T(8,128)(2,1)S(1)} %copy-done.27, f32[1072,256]{1,0:T(8,128)S(1)} %collective-permute-done.24.la_ref.lb_ref, f32[1072,256]{1,0:T(8,128)S(1)} %collective-permute-done.24.la_ref.lb_ref, ...), custom_call_target="tpu_custom_call" | custom-call | flops 1000 | bytes 1000 | tf_op jit(solution)/shard_map/embed_grad_b/pallas_call | solution.py:851
  221.1 3.4 %embed_grad_a.1 = (f32[4,64,1024]{2,1,0:T(8,128)S(1)}, f32[4,64,1024]{2,1,0:T(8,128)S(1)}) custom-call(bf16[512,256]{1,0:T(8,128)(2,1)S(1)} %get-tuple-element.253.ka_ref, bf16[512,256]{1,0:T(8,128)(2,1)S(1)} %copy-done.28, f32[1072,256]{1,0:T(8,128)S(1)} %collective-permute-done.24.la_ref.lb_ref, f32[1072,256]{1,0:T(8,128)S(1)} %collective-permute-done.24.la_ref.lb_ref, ...), custom_call_target="tpu_custom_call" | custom-call | flops 1000 | bytes 1000 | tf_op jit(solution)/shard_map/embed_grad_a/pallas_call | solution.py:851
  224.6 2.5 pixel_grad.3
  227.1 2.0 collective-permute-done.25
  229.2 2.6 fusion
  231.8 1.8 collective-permute-done.26
  233.6 1.9 slice_add_fusion.3
  235.9 1.6 collective-permute-start.32
  238.6 2.6 collective-permute-start.31
  241.1 2.4 add_add_fusion
  243.5 7.1 %collective-permute-done.29 = f32[2,64,1024]{2,1,0:T(8,128)} collective-permute-done((f32[2,64,1024]{2,1,0:T(8,128)}, f32[2,64,1024]{2,1,0:T(8,128)}, u32[]{:S(2)}, u32[]{:S(2)}) %collective-permute-start.29) | collective-permute-done | bytes 524320 | tf_op jit(solution)/shard_map/ppermute | solution.py:938
  251.8 2.8 collective-permute-start.35
  254.5 16.0 %collective-permute-done.30 = f32[4,72,1024]{2,1,0:T(8,128)} collective-permute-done((f32[4,72,1024]{2,1,0:T(8,128)}, f32[4,72,1024]{2,1,0:T(8,128)}, u32[]{:S(2)}, u32[]{:S(2)}) %collective-permute-start.30) | collective-permute-done | bytes 1179680 | tf_op jit(solution)/shard_map/ppermute | solution.py:938
  271.8 1.5 collective-permute-start.34
  273.3 2.4 collective-permute-done.31
  275.7 1.4 fusion.2
  277.2 3.2 collective-permute-start.36
  282.6 2.3 collective-permute-start.37
  289.3 12.0 %collective-permute-done.36 = f32[2,64,1024]{2,1,0:T(8,128)S(1)} collective-permute-done((f32[2,64,1024]{2,1,0:T(8,128)S(1)}, f32[2,64,1024]{2,1,0:T(8,128)S(1)}, u32[]{:S(2)}, u32[]{:S(2)}) %collective-permute-start.36) | collective-permute-done | bytes 524320 | tf_op jit(solution)/shard_map/ppermute | solution.py:938
  304.0 3.0 collective-permute-done.38
  307.1 2.1 add_convert_fusion.1
  310.2 6.0 %collective-permute-done.39 = f32[1,72,1024]{2,1,0:T(8,128)S(1)} collective-permute-done((f32[1,72,1024]{2,1,0:T(8,128)S(1)}, f32[1,72,1024]{2,1,0:T(8,128)S(1)}, u32[]{:S(2)}, u32[]{:S(2)}) %collective-permute-start.39) | collective-permute-done | bytes 294944 | tf_op jit(solution)/shard_map/ppermute | solution.py:938
  (229 shorter events, 43.1 us)
Async XLA Ops:
  5.4 26.7 %collective-permute-start = (f32[256,1024]{1,0:T(8,128)}, f32[256,1024]{1,0:T(8,128)S(1)}, u32[]{:S(2)}, u32[]{:S(2)}) collective-permute-start(f32[256,1024]{1,0:T(8,128)} %get-tuple-element.160.part_ref), channel_id=1, source_target_pairs={{0,1},{1,0},{2,3},{3,2},{4,5},{5,4},{6,7},{7,6},{8,9},{9,8},{10,11... | collective-permute-start | bytes 3145736 | tf_op jit(solution)/shard_map/ppermute | solution.py:938
  14.5 23.7 %collective-permute-start.3 = (f32[4,256,256]{2,1,0:T(8,128)S(1)}, f32[4,256,256]{2,1,0:T(8,128)S(1)}, u32[]{:S(2)}, u32[]{:S(2)}) collective-permute-start(f32[4,256,256]{2,1,0:T(8,128)S(1)} %get-tuple-element.164), channel_id=1, source_target_pairs={{0,2},{2,0},{4,6},{6,4},{8,10},{10,8},{12,14},{14,12},{16,18},{18,... | collective-permute-start | bytes 3145736 | tf_op jit(solution)/shard_map/ppermute | solution.py:938
  14.6 17.4 %copy-start.54 = (f32[256,1024]{1,0:T(8,128)S(1)}, f32[256,1024]{1,0:T(8,128)}, u32[]{:S(2)}) copy-start(f32[256,1024]{1,0:T(8,128)} %get-tuple-element.172.part_ref) | copy-start | bytes 3145732
  14.6 19.2 %copy-start.50 = (bf16[512,1024]{1,0:T(8,128)(2,1)S(1)}, bf16[512,1024]{1,0:T(8,128)(2,1)}, u32[]{:S(2)}) copy-start(bf16[512,1024]{1,0:T(8,128)(2,1)} %refs_5_.3) | copy-start | bytes 3145732
  14.7 19.2 %copy-start.52 = (f32[256,1024]{1,0:T(8,128)S(1)}, f32[256,1024]{1,0:T(8,128)}, u32[]{:S(2)}) copy-start(f32[256,1024]{1,0:T(8,128)} %get-tuple-element.160.part_ref) | copy-start | bytes 3145732
  17.8 44.8 %collective-permute-start.4 = (f32[8,256,256]{2,1,0:T(8,128)}, f32[8,256,256]{2,1,0:T(8,128)}, u32[]{:S(2)}, u32[]{:S(2)}) collective-permute-start(f32[8,256,256]{2,1,0:T(8,128)} %pack_pixels.2), channel_id=1, source_target_pairs={{0,2},{2,0},{4,6},{6,4},{8,10},{10,8},{12,14},{14,12},{16,18},{18,... | collective-permute-start | bytes 6291464 | tf_op jit(solution)/shard_map/ppermute | solution.py:938
  21.5 41.1 %collective-permute-start.5 = (f32[8,256,256]{2,1,0:T(8,128)}, f32[8,256,256]{2,1,0:T(8,128)}, u32[]{:S(2)}, u32[]{:S(2)}) collective-permute-start(f32[8,256,256]{2,1,0:T(8,128)} %pack_pixels.3), channel_id=1, source_target_pairs={{0,2},{2,0},{4,6},{6,4},{8,10},{10,8},{12,14},{14,12},{16,18},{18,... | collective-permute-start | bytes 6291464 | tf_op jit(solution)/shard_map/ppermute | solution.py:938
  32.1 24.7 %collective-permute-start.1 = (f32[256,1024]{1,0:T(8,128)S(1)}, f32[256,1024]{1,0:T(8,128)S(1)}, u32[]{:S(2)}, u32[]{:S(2)}) collective-permute-start(f32[256,1024]{1,0:T(8,128)S(1)} %copy-done.54), channel_id=1, source_target_pairs={{0,1},{1,0},{2,3},{3,2},{4,5},{5,4},{6,7},{7,6},{8,9},{9,8},{10,11... | collective-permute-start | bytes 3145736 | tf_op jit(solution)/shard_map/ppermute | solution.py:938
  38.2 19.9 %copy-start.38 = (bf16[256,512]{1,0:T(8,128)(2,1)}, bf16[256,512]{1,0:T(8,128)(2,1)S(1)}, u32[]{:S(2)}) copy-start(bf16[256,512]{1,0:T(8,128)(2,1)S(1)} %get-tuple-element.177.o_ref.ma_ref) | copy-start | bytes 786436
  38.2 43.3 %copy-start.64 = (f32[256,1024]{1,0:T(8,128)}, f32[256,1024]{1,0:T(8,128)S(1)}, u32[]{:S(2)}) copy-start(f32[256,1024]{1,0:T(8,128)S(1)} %get-tuple-element.170.x0_ref.refs_4_) | copy-start | bytes 3145732
  38.3 24.3 %copy-start.8 = (f32[4,256,256]{2,1,0:T(8,128)}, f32[4,256,256]{2,1,0:T(8,128)S(1)}, u32[]{:S(2)}) copy-start(f32[4,256,256]{2,1,0:T(8,128)S(1)} %collective-permute-done.3.la_ref.lb_ref) | copy-start | bytes 3145732
  40.0 49.4 %collective-permute-start.7 = (f32[4,256,256]{2,1,0:T(8,128)}, f32[4,256,256]{2,1,0:T(8,128)}, u32[]{:S(2)}, u32[]{:S(2)}) collective-permute-start(f32[4,256,256]{2,1,0:T(8,128)} %get-tuple-element.178), channel_id=1, source_target_pairs={{0,2},{2,0},{4,6},{6,4},{8,10},{10,8},{12,14},{14,12},{16,18},{18,... | collective-permute-start | bytes 3145736 | tf_op jit(solution)/shard_map/ppermute | solution.py:938
  56.7 23.7 %collective-permute-start.2 = (f32[256,1024]{1,0:T(8,128)S(1)}, f32[256,1024]{1,0:T(8,128)S(1)}, u32[]{:S(2)}, u32[]{:S(2)}) collective-permute-start(f32[256,1024]{1,0:T(8,128)S(1)} %get-tuple-element.173.opart_ref), channel_id=1, source_target_pairs={{0,1},{1,0},{2,3},{3,2},{4,5},{5,4},{6,7},{7,6},{8,9},{9,8},{10,11... | collective-permute-start | bytes 3145736 | tf_op jit(solution)/shard_map/ppermute | solution.py:938
  58.1 23.4 %copy-start.10 = (bf16[2048,1024]{1,0:T(8,128)(2,1)S(1)}, bf16[2048,1024]{1,0:T(8,128)(2,1)}, u32[]{:S(2)}) copy-start(bf16[2048,1024]{1,0:T(8,128)(2,1)} %wfc2_ref.7) | copy-start | bytes 12582916
  58.1 23.4 %copy-start.47 = (bf16[1024,2048]{1,0:T(8,128)(2,1)S(1)}, bf16[1024,2048]{1,0:T(8,128)(2,1)}, u32[]{:S(2)}) copy-start(bf16[1024,2048]{1,0:T(8,128)(2,1)} %wfc1_ref.5) | copy-start | bytes 12582916
  58.1 23.4 %copy-start.57 = (f32[2048]{0:T(1024)S(1)}, f32[2048]{0:T(1024)}, u32[]{:S(2)}) copy-start(f32[2048]{0:T(1024)} %param.36) | copy-start | bytes 24580
  58.1 23.4 %copy-start.59 = (f32[1024]{0:T(1024)S(1)}, f32[1024]{0:T(1024)}, u32[]{:S(2)}) copy-start(f32[1024]{0:T(1024)} %param.32) | copy-start | bytes 12292
  58.2 23.4 %copy-start.60 = (f32[1024]{0:T(1024)S(1)}, f32[1024]{0:T(1024)}, u32[]{:S(2)}) copy-start(f32[1024]{0:T(1024)} %param.34) | copy-start | bytes 12292
  58.2 23.4 %copy-start.61 = (f32[1024]{0:T(1024)S(1)}, f32[1024]{0:T(1024)}, u32[]{:S(2)}) copy-start(f32[1024]{0:T(1024)} %param.33) | copy-start | bytes 12292
  62.6 19.0 %copy-start.40 = (bf16[256,512]{1,0:T(8,128)(2,1)}, bf16[256,512]{1,0:T(8,128)(2,1)S(1)}, u32[]{:S(2)}) copy-start(bf16[256,512]{1,0:T(8,128)(2,1)S(1)} %get-tuple-element.185.o_ref.mb_ref) | copy-start | bytes 786436
  62.6 42.3 %copy-start.42 = (f32[256,1024]{1,0:T(8,128)}, f32[256,1024]{1,0:T(8,128)S(1)}, u32[]{:S(2)}) copy-start(f32[256,1024]{1,0:T(8,128)S(1)} %get-tuple-element.189.x0_ref.refs_4_) | copy-start | bytes 3145732
  63.4 26.0 %collective-permute-start.8 = (f32[4,256,256]{2,1,0:T(8,128)S(1)}, f32[4,256,256]{2,1,0:T(8,128)S(1)}, u32[]{:S(2)}, u32[]{:S(2)}) collective-permute-start(f32[4,256,256]{2,1,0:T(8,128)S(1)} %get-tuple-element.186), channel_id=1, source_target_pairs={{0,2},{2,0},{4,6},{6,4},{8,10},{10,8},{12,14},{14,12},{16,18},{18,... | collective-permute-start | bytes 3145736 | tf_op jit(solution)/shard_map/ppermute | solution.py:938
  80.5 23.3 %collective-permute-start.6 = (f32[256,1024]{1,0:T(8,128)S(1)}, f32[256,1024]{1,0:T(8,128)S(1)}, u32[]{:S(2)}, u32[]{:S(2)}) collective-permute-start(f32[256,1024]{1,0:T(8,128)S(1)} %get-tuple-element.190.opart_ref), channel_id=1, source_target_pairs={{0,1},{1,0},{2,3},{3,2},{4,5},{5,4},{6,7},{7,6},{8,9},{9,8},{10,11... | collective-permute-start | bytes 3145736 | tf_op jit(solution)/shard_map/ppermute | solution.py:938
  90.4 22.2 %collective-permute-start.11 = (f32[10,256,256]{2,1,0:T(8,128)S(1)}, f32[10,256,256]{2,1,0:T(8,128)S(1)}, u32[]{:S(2)}, u32[]{:S(2)}) collective-permute-start(f32[10,256,256]{2,1,0:T(8,128)S(1)} %get-tuple-element.199), channel_id=1, source_target_pairs={{0,2},{2,0},{4,6},{6,4},{8,10},{10,8},{12,14},{14,12},{16,18},{18,... | collective-permute-start | bytes 7864328 | tf_op jit(solution)/shard_map/ppermute | solution.py:938
  90.4 22.2 %collective-permute-start.10 = (f32[8,256,256]{2,1,0:T(8,128)S(1)}, f32[8,256,256]{2,1,0:T(8,128)S(1)}, u32[]{:S(2)}, u32[]{:S(2)}) collective-permute-start(f32[8,256,256]{2,1,0:T(8,128)S(1)} %get-tuple-element.198), channel_id=1, source_target_pairs={{0,2},{2,0},{4,6},{6,4},{8,10},{10,8},{12,14},{14,12},{16,18},{18,... | collective-permute-start | bytes 6291464 | tf_op jit(solution)/shard_map/ppermute | solution.py:938
  103.8 7.9 %collective-permute-start.9 = (f32[96,1024]{1,0:T(8,128)S(1)}, f32[96,1024]{1,0:T(8,128)S(1)}, u32[]{:S(2)}, u32[]{:S(2)}) collective-permute-start(f32[96,1024]{1,0:T(8,128)S(1)} %get-tuple-element.196.refs_0_), channel_id=1, source_target_pairs={{0,1},{1,0},{2,3},{3,2},{4,5},{5,4},{6,7},{7,6},{8,9},{9,8},{10,11... | collective-permute-start | bytes 1179656 | tf_op jit(solution)/shard_map/ppermute | solution.py:938
  109.8 41.5 %copy-start.24 = (f32[256,1024]{1,0:T(8,128)}, f32[256,1024]{1,0:T(8,128)S(1)}, u32[]{:S(2)}) copy-start(f32[256,1024]{1,0:T(8,128)S(1)} %get-tuple-element.219.refs_2_) | copy-start | bytes 3145732
  109.8 4.4 %collective-permute-start.13 = (f32[8,256,256]{2,1,0:T(8,128)S(1)}, f32[8,256,256]{2,1,0:T(8,128)S(1)}, u32[]{:S(2)}, u32[]{:S(2)}) collective-permute-start(f32[8,256,256]{2,1,0:T(8,128)S(1)} %get-tuple-element.195), channel_id=1, source_target_pairs={{0,2},{2,0},{4,6},{6,4},{8,10},{10,8},{12,14},{14,12},{16,18},{18,... | collective-permute-start | bytes 6291464 | tf_op jit(solution)/shard_map/ppermute | solution.py:938
  109.9 9.0 %collective-permute-start.14 = (f32[10,256,256]{2,1,0:T(8,128)S(1)}, f32[10,256,256]{2,1,0:T(8,128)S(1)}, u32[]{:S(2)}, u32[]{:S(2)}) collective-permute-start(f32[10,256,256]{2,1,0:T(8,128)S(1)} %get-tuple-element.213), channel_id=1, source_target_pairs={{0,2},{2,0},{4,6},{6,4},{8,10},{10,8},{12,14},{14,12},{16,18},{18,... | collective-permute-start | bytes 7864328 | tf_op jit(solution)/shard_map/ppermute | solution.py:938
  111.7 15.4 %collective-permute-start.12 = (f32[160,1024]{1,0:T(8,128)S(1)}, f32[160,1024]{1,0:T(8,128)S(1)}, u32[]{:S(2)}, u32[]{:S(2)}) collective-permute-start(f32[160,1024]{1,0:T(8,128)S(1)} %get-tuple-element.204.refs_1_), channel_id=1, source_target_pairs={{0,1},{1,0},{2,3},{3,2},{4,5},{5,4},{6,7},{7,6},{8,9},{9,8},{10,11... | collective-permute-start | bytes 1966088 | tf_op jit(solution)/shard_map/ppermute | solution.py:938
  118.4 76.2 %copy-start.19 = (f32[4,64,2048]{2,1,0:T(8,128)}, f32[4,64,2048]{2,1,0:T(8,128)S(1)}, u32[]{:S(2)}) copy-start(f32[4,64,2048]{2,1,0:T(8,128)S(1)} %get-tuple-element.232) | copy-start | bytes 6291460
  118.4 47.7 %collective-permute-start.17 = (f32[4,64,2048]{2,1,0:T(8,128)}, f32[4,64,2048]{2,1,0:T(8,128)}, u32[]{:S(2)}, u32[]{:S(2)}) collective-permute-start(f32[4,64,2048]{2,1,0:T(8,128)} %get-tuple-element.212), channel_id=1, source_target_pairs={{0,4},{2,6},{4,0},{6,2},{8,12},{10,14},{12,8},{14,10},{16,20},{18,... | collective-permute-start | bytes 6291464 | tf_op jit(solution)/shard_map/ppermute | solution.py:938
  123.2 17.1 %copy-start.17 = (f32[4,2,64,1024]{3,2,1,0:T(8,128)}, f32[4,2,64,1024]{3,2,1,0:T(8,128)S(1)}, u32[]{:S(2)}) copy-start(f32[4,2,64,1024]{3,2,1,0:T(8,128)S(1)} %get-tuple-element.245) | copy-start | bytes 6291460
  123.2 50.6 %collective-permute-start.21 = (f32[8,64,1024]{2,1,0:T(8,128)}, f32[8,64,1024]{2,1,0:T(8,128)}, u32[]{:S(2)}, u32[]{:S(2)}) collective-permute-start(f32[8,64,1024]{2,1,0:T(8,128)} %bitcast.12), channel_id=1, source_target_pairs={{0,8},{2,10},{4,12},{6,14},{8,0},{10,2},{12,4},{14,6},{16,24},{18,... | collective-permute-start | bytes 6291464 | tf_op jit(solution)/shard_map/ppermute | solution.py:938
  127.1 23.2 %collective-permute-start.15 = (f32[256,1024]{1,0:T(8,128)S(1)}, f32[256,1024]{1,0:T(8,128)S(1)}, u32[]{:S(2)}, u32[]{:S(2)}) collective-permute-start(f32[256,1024]{1,0:T(8,128)S(1)} %mlp_back.1.refs_0_), channel_id=1, source_target_pairs={{0,1},{1,0},{2,3},{3,2},{4,5},{5,4},{6,7},{7,6},{8,9},{9,8},{10,11... | collective-permute-start | bytes 3145736 | tf_op jit(solution)/shard_map/ppermute | solution.py:938
  150.4 9.0 %collective-permute-start.16 = (f32[96,1024]{1,0:T(8,128)S(1)}, f32[96,1024]{1,0:T(8,128)S(1)}, u32[]{:S(2)}, u32[]{:S(2)}) collective-permute-start(f32[96,1024]{1,0:T(8,128)S(1)} %get-tuple-element.227.refs_0_), channel_id=1, source_target_pairs={{0,1},{1,0},{2,3},{3,2},{4,5},{5,4},{6,7},{7,6},{8,9},{9,8},{10,11... | collective-permute-start | bytes 1179656 | tf_op jit(solution)/shard_map/ppermute | solution.py:938
  159.4 9.8 %collective-permute-start.19 = (f32[8,256,256]{2,1,0:T(8,128)S(1)}, f32[8,256,256]{2,1,0:T(8,128)S(1)}, u32[]{:S(2)}, u32[]{:S(2)}) collective-permute-start(f32[8,256,256]{2,1,0:T(8,128)S(1)} %get-tuple-element.237), channel_id=1, source_target_pairs={{0,2},{2,0},{4,6},{6,4},{8,10},{10,8},{12,14},{14,12},{16,18},{18,... | collective-permute-start | bytes 6291464 | tf_op jit(solution)/shard_map/ppermute | solution.py:938
  159.4 9.8 %collective-permute-start.18 = (f32[8,256,256]{2,1,0:T(8,128)S(1)}, f32[8,256,256]{2,1,0:T(8,128)S(1)}, u32[]{:S(2)}, u32[]{:S(2)}) collective-permute-start(f32[8,256,256]{2,1,0:T(8,128)S(1)} %get-tuple-element.235), channel_id=1, source_target_pairs={{0,2},{2,0},{4,6},{6,4},{8,10},{10,8},{12,14},{14,12},{16,18},{18,... | collective-permute-start | bytes 6291464 | tf_op jit(solution)/shard_map/ppermute | solution.py:938
  162.4 21.5 %collective-permute-start.20 = (f32[160,1024]{1,0:T(8,128)S(1)}, f32[160,1024]{1,0:T(8,128)S(1)}, u32[]{:S(2)}, u32[]{:S(2)}) collective-permute-start(f32[160,1024]{1,0:T(8,128)S(1)} %get-tuple-element.243.refs_1_), channel_id=1, source_target_pairs={{0,1},{1,0},{2,3},{3,2},{4,5},{5,4},{6,7},{7,6},{8,9},{9,8},{10,11... | collective-permute-start | bytes 1966088 | tf_op jit(solution)/shard_map/ppermute | solution.py:938
  167.5 27.0 %collective-permute-start.23 = (f32[2,64,2048]{2,1,0:T(8,128)S(1)}, f32[2,64,2048]{2,1,0:T(8,128)S(1)}, u32[]{:S(2)}, u32[]{:S(2)}) collective-permute-start(f32[2,64,2048]{2,1,0:T(8,128)S(1)} %slice_add_fusion), channel_id=1, source_target_pairs={{0,8},{2,10},{4,12},{6,14},{8,0},{10,2},{12,4},{14,6},{16,24},{18,... | collective-permute-start | bytes 3145736 | tf_op jit(solution)/shard_map/ppermute | solution.py:938
  182.6 46.6 %collective-permute-start.25 = (f32[8,64,1024]{2,1,0:T(8,128)}, f32[8,64,1024]{2,1,0:T(8,128)}, u32[]{:S(2)}, u32[]{:S(2)}) collective-permute-start(f32[8,64,1024]{2,1,0:T(8,128)} %pad_maximum_fusion), channel_id=1, source_target_pairs={{0,4},{2,6},{4,0},{6,2},{8,12},{10,14},{12,8},{14,10},{16,20},{18,... | collective-permute-start | bytes 6291464 | tf_op jit(solution)/shard_map/ppermute | solution.py:938
  183.6 49.9 %collective-permute-start.27 = (f32[4,64,1024]{2,1,0:T(8,128)}, f32[4,64,1024]{2,1,0:T(8,128)}, u32[]{:S(2)}, u32[]{:S(2)}) collective-permute-start(f32[4,64,1024]{2,1,0:T(8,128)} %get-tuple-element.251), channel_id=1, source_target_pairs={{0,8},{2,10},{4,12},{6,14},{8,0},{10,2},{12,4},{14,6},{16,24},{18,... | collective-permute-start | bytes 3145736 | tf_op jit(solution)/shard_map/ppermute | solution.py:938
  183.9 23.3 %collective-permute-start.22 = (f32[256,1024]{1,0:T(8,128)S(1)}, f32[256,1024]{1,0:T(8,128)S(1)}, u32[]{:S(2)}, u32[]{:S(2)}) collective-permute-start(f32[256,1024]{1,0:T(8,128)S(1)} %get-tuple-element.255.refs_0_), channel_id=1, source_target_pairs={{0,1},{1,0},{2,3},{3,2},{4,5},{5,4},{6,7},{7,6},{8,9},{9,8},{10,11... | collective-permute-start | bytes 3145736 | tf_op jit(solution)/shard_map/ppermute | solution.py:938
  184.5 27.1 %copy-start.15 = (bf16[384,1024]{1,0:T(8,128)(2,1)S(1)}, bf16[384,1024]{1,0:T(8,128)(2,1)}, u32[]{:S(2)}) copy-start(bf16[384,1024]{1,0:T(8,128)(2,1)} %wrgb_ref.7) | copy-start | bytes 2359300
  186.6 20.6 %copy-start.43 = (f32[256,1024]{1,0:T(8,128)S(1)}, f32[256,1024]{1,0:T(8,128)}, u32[]{:S(2)}) copy-start(f32[256,1024]{1,0:T(8,128)} %copy-done.42) | copy-start | bytes 3145732
  196.8 41.7 %collective-permute-start.28 = (f32[1,64,2048]{2,1,0:T(8,128)}, f32[1,64,2048]{2,1,0:T(8,128)}, u32[]{:S(2)}, u32[]{:S(2)}) collective-permute-start(f32[1,64,2048]{2,1,0:T(8,128)} %slice_add_fusion.5), channel_id=1, source_target_pairs={{0,16},{2,18},{4,20},{6,22},{8,24},{10,26},{12,28},{14,30},{16,0},... | collective-permute-start | bytes 1572872 | tf_op jit(solution)/shard_map/ppermute | solution.py:938
  210.1 23.4 %collective-permute-start.26 = (f32[256,1024]{1,0:T(8,128)}, f32[256,1024]{1,0:T(8,128)}, u32[]{:S(2)}, u32[]{:S(2)}) collective-permute-start(f32[256,1024]{1,0:T(8,128)} %mlp_out.3), channel_id=1, source_target_pairs={{0,1},{1,0},{2,3},{3,2},{4,5},{5,4},{6,7},{7,6},{8,9},{9,8},{10,11... | collective-permute-start | bytes 3145736 | tf_op jit(solution)/shard_map/ppermute | solution.py:938
  211.6 2.7 collective-permute-start.24
  220.3 50.2 %collective-permute-start.30 = (f32[4,72,1024]{2,1,0:T(8,128)}, f32[4,72,1024]{2,1,0:T(8,128)}, u32[]{:S(2)}, u32[]{:S(2)}) collective-permute-start(f32[4,72,1024]{2,1,0:T(8,128)} %get-tuple-element.276), channel_id=1, source_target_pairs={{0,8},{2,10},{4,12},{6,14},{8,0},{10,2},{12,4},{14,6},{16,24},{18,... | collective-permute-start | bytes 3538952 | tf_op jit(solution)/shard_map/ppermute | solution.py:938
  235.5 35.0 %copy-start.21 = (f32[4,72,1024]{2,1,0:T(8,128)S(1)}, f32[4,72,1024]{2,1,0:T(8,128)}, u32[]{:S(2)}) copy-start(f32[4,72,1024]{2,1,0:T(8,128)} %copy-done.20) | copy-start | bytes 3538948
  235.5 15.2 %collective-permute-start.29 = (f32[2,64,1024]{2,1,0:T(8,128)}, f32[2,64,1024]{2,1,0:T(8,128)}, u32[]{:S(2)}, u32[]{:S(2)}) collective-permute-start(f32[2,64,1024]{2,1,0:T(8,128)} %slice_add_fusion.3), channel_id=1, source_target_pairs={{0,4},{2,6},{4,0},{6,2},{8,12},{10,14},{12,8},{14,10},{16,20},{18,... | collective-permute-start | bytes 1572872 | tf_op jit(solution)/shard_map/ppermute | solution.py:938
  235.9 41.2 %collective-permute-start.32 = (f32[4,64,1024]{2,1,0:T(8,128)}, f32[4,64,1024]{2,1,0:T(8,128)S(1)}, u32[]{:S(2)}, u32[]{:S(2)}) collective-permute-start(f32[4,64,1024]{2,1,0:T(8,128)} %copy-done.53), channel_id=1, source_target_pairs={{0,4},{2,6},{4,0},{6,2},{8,12},{10,14},{12,8},{14,10},{16,20},{18,... | collective-permute-start | bytes 3145736 | tf_op jit(solution)/shard_map/ppermute | solution.py:938
  237.5 44.1 %collective-permute-start.33 = (f32[2,64,1024]{2,1,0:T(8,128)}, f32[2,64,1024]{2,1,0:T(8,128)S(1)}, u32[]{:S(2)}, u32[]{:S(2)}) collective-permute-start(f32[2,64,1024]{2,1,0:T(8,128)} %get-tuple-element.304), channel_id=1, source_target_pairs={{0,8},{2,10},{4,12},{6,14},{8,0},{10,2},{12,4},{14,6},{16,24},{18,... | collective-permute-start | bytes 1572872 | tf_op jit(solution)/shard_map/ppermute | solution.py:938
  238.6 37.1 %collective-permute-start.31 = (f32[2,64,1024]{2,1,0:T(8,128)}, f32[2,64,1024]{2,1,0:T(8,128)S(1)}, u32[]{:S(2)}, u32[]{:S(2)}) collective-permute-start(f32[2,64,1024]{2,1,0:T(8,128)} %get-tuple-element.303), channel_id=1, source_target_pairs={{0,16},{2,18},{4,20},{6,22},{8,24},{10,26},{12,28},{14,30},{16,0},... | collective-permute-start | bytes 1572872 | tf_op jit(solution)/shard_map/ppermute | solution.py:938
  251.8 36.4 %collective-permute-start.35 = (f32[1,64,1024]{2,1,0:T(8,128)S(1)}, f32[1,64,1024]{2,1,0:T(8,128)S(1)}, u32[]{:S(2)}, u32[]{:S(2)}) collective-permute-start(f32[1,64,1024]{2,1,0:T(8,128)S(1)} %slice_add_fusion.9), channel_id=1, source_target_pairs={{0,16},{2,18},{4,20},{6,22},{8,24},{10,26},{12,28},{14,30},{16,0},... | collective-permute-start | bytes 786440 | tf_op jit(solution)/shard_map/ppermute | solution.py:938
  271.8 14.6 %collective-permute-start.34 = (f32[2,72,1024]{2,1,0:T(8,128)S(1)}, f32[2,72,1024]{2,1,0:T(8,128)S(1)}, u32[]{:S(2)}, u32[]{:S(2)}) collective-permute-start(f32[2,72,1024]{2,1,0:T(8,128)S(1)} %slice_add_fusion.1), channel_id=1, source_target_pairs={{0,4},{2,6},{4,0},{6,2},{8,12},{10,14},{12,8},{14,10},{16,20},{18,... | collective-permute-start | bytes 1769480 | tf_op jit(solution)/shard_map/ppermute | solution.py:938
  277.2 24.1 %collective-permute-start.36 = (f32[2,64,1024]{2,1,0:T(8,128)S(1)}, f32[2,64,1024]{2,1,0:T(8,128)S(1)}, u32[]{:S(2)}, u32[]{:S(2)}) collective-permute-start(f32[2,64,1024]{2,1,0:T(8,128)S(1)} %slice_add_fusion.2), channel_id=1, source_target_pairs={{0,8},{2,10},{4,12},{6,14},{8,0},{10,2},{12,4},{14,6},{16,24},{18,... | collective-permute-start | bytes 1572872 | tf_op jit(solution)/shard_map/ppermute | solution.py:938
  282.6 18.9 %collective-permute-start.37 = (f32[1,64,1024]{2,1,0:T(8,128)S(1)}, f32[1,64,1024]{2,1,0:T(8,128)S(1)}, u32[]{:S(2)}, u32[]{:S(2)}) collective-permute-start(f32[1,64,1024]{2,1,0:T(8,128)S(1)} %slice_add_fusion.8), channel_id=1, source_target_pairs={{0,16},{2,18},{4,20},{6,22},{8,24},{10,26},{12,28},{14,30},{16,0},... | collective-permute-start | bytes 786440 | tf_op jit(solution)/shard_map/ppermute | solution.py:938
  285.0 22.1 %collective-permute-start.38 = (f32[256,1024]{1,0:T(8,128)S(1)}, f32[256,1024]{1,0:T(8,128)S(1)}, u32[]{:S(2)}, u32[]{:S(2)}) collective-permute-start(f32[256,1024]{1,0:T(8,128)S(1)} %copy-done.12), channel_id=1, source_target_pairs={{0,1},{1,0},{2,3},{3,2},{4,5},{5,4},{6,7},{7,6},{8,9},{9,8},{10,11... | collective-permute-start | bytes 3145736 | tf_op jit(solution)/shard_map/ppermute | solution.py:938
  287.4 28.8 %collective-permute-start.39 = (f32[1,72,1024]{2,1,0:T(8,128)S(1)}, f32[1,72,1024]{2,1,0:T(8,128)S(1)}, u32[]{:S(2)}, u32[]{:S(2)}) collective-permute-start(f32[1,72,1024]{2,1,0:T(8,128)S(1)} %slice_add_fusion.6), channel_id=1, source_target_pairs={{0,16},{2,18},{4,20},{6,22},{8,24},{10,26},{12,28},{14,30},{16,0},... | collective-permute-start | bytes 884744 | tf_op jit(solution)/shard_map/ppermute | solution.py:938
  289.3 17.8 %copy-start.23 = (f32[256,1024]{1,0:T(8,128)S(1)}, f32[256,1024]{1,0:T(8,128)}, u32[]{:S(2)}) copy-start(f32[256,1024]{1,0:T(8,128)} %copy-done.22) | copy-start | bytes 3145732
  289.3 17.8 %copy-start.25 = (f32[256,1024]{1,0:T(8,128)S(1)}, f32[256,1024]{1,0:T(8,128)}, u32[]{:S(2)}) copy-start(f32[256,1024]{1,0:T(8,128)} %copy-done.24) | copy-start | bytes 3145732
  289.3 17.8 %copy-start.68 = (f32[1024]{0:T(1024)S(1)}, f32[1024]{0:T(1024)}, u32[]{:S(2)}) copy-start(f32[1024]{0:T(1024)} %param.38) | copy-start | bytes 12292
  301.3 18.1 %collective-permute-start.40 = (f32[1,64,1024]{2,1,0:T(8,128)S(1)}, f32[1,64,1024]{2,1,0:T(8,128)S(1)}, u32[]{:S(2)}, u32[]{:S(2)}) collective-permute-start(f32[1,64,1024]{2,1,0:T(8,128)S(1)} %slice_add_fusion.7), channel_id=1, source_target_pairs={{0,16},{2,18},{4,20},{6,22},{8,24},{10,26},{12,28},{14,30},{16,0},... | collective-permute-start | bytes 786440 | tf_op jit(solution)/shard_map/ppermute | solution.py:938
  (48 other events, 294.3 us)

commit v10 on v9

--- a/solution.py
+++ b/solution.py
@@ -1189,15 +1189,18 @@
         mid = mixed[0].shape[1] // 2
         gdx0 = order.tie(other(gone[1]))
         sides = ([(kdx0[0], 0), (kdx0[1], 0)], [(gdx0, 1), (gdx0, 0)], mixed, gmix)
-        cube = (cube + order.tie(gdx0)[-cube.shape[0] :]).reshape(8, 1, -1)
-        cube = jnp.pad(cube, ((0, 0), (0, 7), (0, 0)))
         embz_h = Halving(
-            *plain_grad(*sides, move_z, "embed_grad_b", mid, mid, vectors=(cube, *blocks)),
+            *plain_grad(*sides, move_z, "embed_grad_b", mid, mid),
             Z_FIRST, size,
         )
         order.mark(embz_h.sent)
         sides[3][1] = order.tie(gmix[1])
-        embx_h = Halving(*plain_grad(*sides, move_x, "embed_grad_a", 0, mid), X_FIRST, size)
+        cube = (cube + order.tie(gdx0)[-cube.shape[0] :]).reshape(8, 1, -1)
+        cube = jnp.pad(cube, ((0, 0), (0, 7), (0, 0)))
+        embx_h = Halving(
+            *plain_grad(*sides, move_x, "embed_grad_a", 0, mid, vectors=(cube, *blocks)),
+            X_FIRST, size,
+        )
         order.mark(embx_h.sent)
     pixels_grad = pixel_grad(
         order.tie(item_kinds), dx0[1], w_spectral, w_rgb, pick, 1, items, pixels_grad
@@ -1243,11 +1246,11 @@
         spans += [(shard + 1, row * LANES, LANES) for row in range(2)]
         outs = []
         for row, first, length in spans:
-            low = embz_g[row, first : first + length // 2]
-            high = embz_g[row, first + length // 2 : first + length]
+            low = embx_g[row, first : first + length // 2]
+            high = embx_g[row, first + length // 2 : first + length]
             outs.append(jnp.where(core == 0, low, high))
         ln2_g, ln2_b, ob_g, b2_g, q_g, v_g, b1_g, ln1_g, ln1_b = outs
-        embz_g = embz_g[:shard]
+        embx_g = embx_g[:shard]
         emb_g = jnp.concatenate([embx_g, embz_g], 1)
         cut = attx_g.shape[1] // 2
         planes = [attx_g[:, :cut], attx_g[:, cut:], attz_g[:, :cut]]

time: 325 us -> 324 us (level)
  starting transfers between devices: 42.6 us -> 46.4 us
    ppermute x41, starting transfers between devices: 42.6 us -> 46.4 us  [exchange(): return lax.ppermute(values, axis, [(i, i ^ bit) for i in range(size)])]
    unnamed x142 -> x136, local copies, waits for them, and re-layouts: 8.06 us -> 6.06 us
    add x16 -> x17, other arithmetic: 21.2 us -> 20.8 us  [value(): value = value + recv[first:first + count]]
  transfers between devices with their start and end apart: 41 -> 41, of which waited for: 21 -> 17; matrix products, arithmetic and copies ran while one was open for 10% -> 9% of each run, Pallas kernels for 29% -> 29%
where the time goes in v10:
time: 324 us; the launch traced here: 320 us
  waiting for transfers between devices  136 us (42%)
  Pallas kernels  97.3 us (30%)
  starting transfers between devices  46.4 us (14%)
  other arithmetic  30.2 us (9%)
  local copies, waits for them, and re-layouts  8.59 us (3%)
    ppermute x41, waiting for transfers between devices, exchange(): return lax.ppermute(values, axis, [(i, i ^ bit) for i in range(size)])  136 us
    ppermute x41, starting transfers between devices, exchange(): return lax.ppermute(values, axis, [(i, i ^ bit) for i in range(size)])  46.4 us
    add x17, other arithmetic, value(): value = value + recv[first:first + count]  20.8 us
    pallas_call x2, Pallas kernels, attn_backward(): pl.pallas_call(functools.partial(attn_backward_kernel, parts=(len(gparts)...  16.4 us
    pallas_call x4, Pallas kernels, plain_grad(): pl.pallas_call(functools.partial(plain_grad_kernel, moves=moves, vectors=...  15.4 us
    pallas_call x2, Pallas kernels, mlp(): pl.pallas_call(mlp_kernel, grid_spec=pltpu.PrefetchScalarGridSpec(num_sca...  12.5 us
    pallas_call x2, Pallas kernels, embed(): pl.pallas_call(functools.partial(embed_kernel, item=item), grid_spec=pltp...  9.9 us
    pallas_call x2, Pallas kernels, attn_forward(): pl.pallas_call(attn_forward_kernel, grid=(steps,), in_specs=[whole(part.s...  8.69 us
  transfers between devices with their start and end apart: 41, of which 17 were waited for; matrix products, arithmetic and copies ran while one was open for 9% of the time, Pallas kernels for 29%

profile of v10, /device:TPU:0, one launch (start us, length us, event | category | flops | bytes accessed | tf_op | source)
XLA Modules:
  0.0 320.0 jit_solution(16723131509222720529)
XLA Ops:
  0.7 5.0 %embed.2 = (f32[256,1024]{1,0:T(8,128)}, bf16[256,2048]{1,0:T(8,128)(2,1)}) custom-call(s32[2]{0:T(128)} %kinds.4, bf16[512,1664]{1,0:T(8,128)(2,1)} %pix_ref.3, bf16[1664,1024]{1,0:T(8,128)(2,1)} %wspec_ref.7, bf16[384,1024]{1,0:T(8,128)(2,1)} %wrgb_ref.7, bf16[1664,384]{1,0:T(8,128)(2,1)} %constant.50.clone.pick_ref), custom_call_target="tpu_custom_call" | custom-call | flops 1000 | bytes 1000 | tf_op jit(solution)/shard_map/embed/pallas_call | solution.py:242
  5.7 3.0 collective-permute-start
  8.8 4.9 %embed.3 = (f32[256,1024]{1,0:T(8,128)}, bf16[256,2048]{1,0:T(8,128)(2,1)}) custom-call(s32[2]{0:T(128)} %kinds.4, bf16[512,1664]{1,0:T(8,128)(2,1)} %pix_ref.3, bf16[1664,1024]{1,0:T(8,128)(2,1)} %wspec_ref.7, bf16[384,1024]{1,0:T(8,128)(2,1)} %wrgb_ref.7, bf16[1664,384]{1,0:T(8,128)(2,1)} %constant.50.clone.pick_ref), custom_call_target="tpu_custom_call" | custom-call | flops 1000 | bytes 1000 | tf_op jit(solution)/shard_map/embed/pallas_call | solution.py:242
  14.9 3.1 pack_pixels.2
  18.6 3.1 pack_pixels.3
  22.1 9.7 %collective-permute-done.recv_ref = f32[256,1024]{1,0:T(8,128)S(1)} collective-permute-done((f32[256,1024]{1,0:T(8,128)}, f32[256,1024]{1,0:T(8,128)S(1)}, u32[]{:S(2)}, u32[]{:S(2)}) %collective-permute-start) | collective-permute-done | bytes 1048608 | tf_op jit(solution)/shard_map/ppermute | solution.py:938
  31.8 1.7 collective-permute-start.1
  33.6 4.4 %attn_forward.2 = (f32[256,1024]{1,0:T(8,128)S(1)}, bf16[256,1024]{1,0:T(8,128)(2,1)S(1)}, bf16[3,256,512]{2,1,0:T(8,128)(2,1)S(1)}, bf16[256,512]{1,0:T(8,128)(2,1)S(1)}, f32[256,1024]{1,0:T(8,128)S(1)}) custom-call(f32[256,1024]{1,0:T(8,128)S(1)} %copy-done.50, f32[256,1024]{1,0:T(8,128)S(1)} %collective-permute-done.recv_ref, ...), custom_call_target="tpu_custom_call" | custom-call | flops 99999997952 | bytes 1000 | tf_op jit(solution)/shard_map/attn_forward/pallas_call | solution.py:330
  38.0 1.8 pack_attn.2
  39.8 16.1 %collective-permute-done.1.recv_ref = f32[256,1024]{1,0:T(8,128)S(1)} collective-permute-done((f32[256,1024]{1,0:T(8,128)S(1)}, f32[256,1024]{1,0:T(8,128)S(1)}, u32[]{:S(2)}, u32[]{:S(2)}) %collective-permute-start.1) | collective-permute-done | bytes 1048608 | tf_op jit(solution)/shard_map/ppermute | solution.py:938
  55.9 1.4 collective-permute-start.2
  57.3 4.3 %attn_forward.3 = (f32[256,1024]{1,0:T(8,128)S(1)}, bf16[256,1024]{1,0:T(8,128)(2,1)S(1)}, bf16[3,256,512]{2,1,0:T(8,128)(2,1)S(1)}, bf16[256,512]{1,0:T(8,128)(2,1)S(1)}, f32[256,1024]{1,0:T(8,128)S(1)}) custom-call(f32[256,1024]{1,0:T(8,128)S(1)} %copy-done.51, f32[256,1024]{1,0:T(8,128)S(1)} %collective-permute-done.1.recv_ref, ...), custom_call_target="tpu_custom_call" | custom-call | flops 99999997952 | bytes 1000 | tf_op jit(solution)/shard_map/attn_forward/pallas_call | solution.py:330
  62.6 16.6 %collective-permute-done.2.orecv_ref = f32[256,1024]{1,0:T(8,128)S(1)} collective-permute-done((f32[256,1024]{1,0:T(8,128)S(1)}, f32[256,1024]{1,0:T(8,128)S(1)}, u32[]{:S(2)}, u32[]{:S(2)}) %collective-permute-start.2) | collective-permute-done | bytes 1048608 | tf_op jit(solution)/shard_map/ppermute | solution.py:938
  79.2 1.4 collective-permute-start.6
  80.7 7.6 %mlp.2 = (f32[256,1024]{1,0:T(8,128)S(1)}, bf16[256,1024]{1,0:T(8,128)(2,1)}, bf16[256,2048]{1,0:T(8,128)(2,1)S(1)}, bf16[256,2048]{1,0:T(8,128)(2,1)S(1)}, f32[...) custom-call(s32[9]{0:T(128)S(1)} %pad_add_fusion.place, ...), custom_call_target="tpu_custom_call" | custom-call | flops 99999997952 | bytes 1000 | tf_op jit(solution)/shard_map/mlp/pallas_call | solution.py:538
  89.7 12.8 %collective-permute-done.6.orecv_ref = f32[256,1024]{1,0:T(8,128)S(1)} collective-permute-done((f32[256,1024]{1,0:T(8,128)S(1)}, f32[256,1024]{1,0:T(8,128)S(1)}, u32[]{:S(2)}, u32[]{:S(2)}) %collective-permute-start.6) | collective-permute-done | bytes 1048608 | tf_op jit(solution)/shard_map/ppermute | solution.py:938
  102.5 1.4 collective-permute-start.9
  103.9 4.9 %mlp.3 = (f32[256,1024]{1,0:T(8,128)S(1)}, bf16[256,1024]{1,0:T(8,128)(2,1)}, bf16[256,2048]{1,0:T(8,128)(2,1)S(1)}, bf16[256,2048]{1,0:T(8,128)(2,1)S(1)}, f32[...) custom-call(s32[9]{0:T(128)S(1)} %pad_add_fusion.place, ...), custom_call_target="tpu_custom_call" | custom-call | flops 99999997952 | bytes 1000 | tf_op jit(solution)/shard_map/mlp/pallas_call | solution.py:538
  110.3 1.4 collective-permute-start.12
  111.7 1.6 mlp_back.1.refs_0_
  113.3 4.1 %fc2_grad.1 = (f32[4,64,2048]{2,1,0:T(8,128)}, f32[4,64,2048]{2,1,0:T(8,128)S(1)}) custom-call(bf16[2,512,256]{2,1,0:T(8,128)(2,1)S(1)} %get-tuple-element.208.ka_ref.kb_ref, bf16[2,512,256]{2,1,0:T(8,128)(2,1)S(1)} %get-tuple-element.208.ka_ref.kb_ref, f32[4,256,256]{2,1,0:T(8,128)S(1)} %copy-done.9, f32[4,256,256]{2,1,0:T(8,128)S(1)} %copy-done.9, ...), custom_call_target="tpu_custom_call" | custom-call | flops 1000 | bytes 1000 | tf_op jit(solution)/shard_map/fc2_grad/pallas_call | solution.py:851
  117.4 1.5 collective-permute-start.17
  118.9 4.3 %fc1_grad.1 = (f32[4,2,64,1024]{3,2,1,0:T(8,128)}, f32[4,2,64,1024]{3,2,1,0:T(8,128)S(1)}) custom-call(bf16[512,256]{1,0:T(8,128)(2,1)S(1)} %get-tuple-element.205.ka_ref, bf16[512,256]{1,0:T(8,128)(2,1)S(1)} %get-tuple-element.206.kb_ref, f32[10,256,256]{2,1,0:T(8,128)S(1)} %collective-permute-done.11.la_ref.oa_ref, ...), custom_call_target="tpu_custom_call" | custom-call | flops 1000 | bytes 1000 | tf_op jit(solution)/shard_map/fc1_grad/pallas_call | solution.py:851
  123.2 1.6 collective-permute-start.21
  124.8 1.4 collective-permute-done.12.refs_3_
  126.8 8.3 %attn_backward.2 = (f32[256,1024]{1,0:T(8,128)S(1)}, bf16[256,1024]{1,0:T(8,128)(2,1)}, bf16[3,256,512]{2,1,0:T(8,128)(2,1)S(1)}, f32[8,1024]{1,0:T(8,128)S(1)},...) custom-call(s32[9]{0:T(128)S(1)} %pad_add_fusion.place, ...), custom_call_target="tpu_custom_call" | custom-call | flops 99999997952 | bytes 1000 | tf_op jit(solution)/shard_map/attn_backward/pallas_call | solution.py:446
  136.0 1.8 mlp_out.2
  139.9 9.8 %collective-permute-done.15.refs_1_ = f32[256,1024]{1,0:T(8,128)S(1)} collective-permute-done((f32[256,1024]{1,0:T(8,128)S(1)}, f32[256,1024]{1,0:T(8,128)S(1)}, u32[]{:S(2)}, u32[]{:S(2)}) %collective-permute-start.15) | collective-permute-done | bytes 1048608 | tf_op jit(solution)/shard_map/ppermute | solution.py:938
  149.9 8.1 %attn_backward.3 = (f32[256,1024]{1,0:T(8,128)S(1)}, bf16[256,1024]{1,0:T(8,128)(2,1)}, bf16[3,256,512]{2,1,0:T(8,128)(2,1)S(1)}, f32[8,1024]{1,0:T(8,128)S(1)},...) custom-call(s32[9]{0:T(128)S(1)} %pad_add_fusion.place, ...), custom_call_target="tpu_custom_call" | custom-call | flops 99999997952 | bytes 1000 | tf_op jit(solution)/shard_map/attn_backward/pallas_call | solution.py:446
  158.5 2.5 mlp_out.3
  161.1 1.7 collective-permute-start.20
  162.8 2.3 collective-permute-done.17
  166.5 2.6 collective-permute-start.23
  169.1 3.6 %query_key_grad.1 = (f32[4,64,1024]{2,1,0:T(8,128)S(1)}, f32[4,64,1024]{2,1,0:T(8,128)S(1)}) custom-call(bf16[512,256]{1,0:T(8,128)(2,1)S(1)} %get-tuple-element.230.aa_ref, bf16[512,256]{1,0:T(8,128)(2,1)S(1)} %get-tuple-element.231.ab_ref, f32[4,256,256]{2,1,0:T(8,128)} %collective-permute-done.7.fa_ref, f32[4,256,256]{2,1,0:T(8,128)S(1)} %copy-done.14, ...), custom_call_target="tpu_custom_call" | custom-call | flops 1000 | bytes 1000 | tf_op jit(solution)/shard_map/query_key_grad/pallas_call | solution.py:924
  173.7 1.4 bitcast_add_fusion
  175.1 1.5 pad_maximum_fusion
  176.7 4.8 %value_out_grad.1 = (f32[4,64,1024]{2,1,0:T(8,128)}, f32[4,64,1024]{2,1,0:T(8,128)S(1)}) custom-call(bf16[512,256]{1,0:T(8,128)(2,1)S(1)} %get-tuple-element.230.aa_ref, bf16[512,256]{1,0:T(8,128)(2,1)S(1)} %get-tuple-element.231.ab_ref, f32[4,256,256]{2,1,0:T(8,128)} %collective-permute-done.7.fa_ref, f32[4,256,256]{2,1,0:T(8,128)S(1)} %copy-done.14, ...), custom_call_target="tpu_custom_call" | custom-call | flops 1000 | bytes 1000 | tf_op jit(solution)/shard_map/value_out_grad/pallas_call | solution.py:924
  183.5 2.2 first_norm_back.2
  185.7 8.7 %collective-permute-done.23 = f32[2,64,2048]{2,1,0:T(8,128)S(1)} collective-permute-done((f32[2,64,2048]{2,1,0:T(8,128)S(1)}, f32[2,64,2048]{2,1,0:T(8,128)S(1)}, u32[]{:S(2)}, u32[]{:S(2)}) %collective-permute-start.23) | collective-permute-done | bytes 1048608 | tf_op jit(solution)/shard_map/ppermute | solution.py:938
  194.4 2.3 slice_add_fusion.5
  196.7 3.2 collective-permute-start.28
  200.6 5.1 %collective-permute-done.22.refs_1_ = f32[256,1024]{1,0:T(8,128)S(1)} collective-permute-done((f32[256,1024]{1,0:T(8,128)S(1)}, f32[256,1024]{1,0:T(8,128)S(1)}, u32[]{:S(2)}, u32[]{:S(2)}) %collective-permute-start.22) | collective-permute-done | bytes 1048608 | tf_op jit(solution)/shard_map/ppermute | solution.py:938
  205.8 2.2 first_norm_back.3
  208.0 1.4 collective-permute-start.26
  209.4 2.6 pixel_grad.2.refs_0_
  212.1 3.7 %embed_grad_b.1 = (f32[4,64,1024]{2,1,0:T(8,128)}, f32[4,64,1024]{2,1,0:T(8,128)S(1)}) custom-call(bf16[512,256]{1,0:T(8,128)(2,1)S(1)} %get-tuple-element.253.ka_ref, bf16[512,256]{1,0:T(8,128)(2,1)S(1)} %get-tuple-element.268.kb_ref, f32[1072,256]{1,0:T(8,128)S(1)} %collective-permute-done.24.la_ref.lb_ref, ...), custom_call_target="tpu_custom_call" | custom-call | flops 1000 | bytes 1000 | tf_op jit(solution)/shard_map/embed_grad_b/pallas_call | solution.py:851
  218.6 3.3 %embed_grad_a.1 = (f32[4,72,1024]{2,1,0:T(8,128)S(1)}, f32[4,72,1024]{2,1,0:T(8,128)S(1)}) custom-call(bf16[512,256]{1,0:T(8,128)(2,1)S(1)} %get-tuple-element.253.ka_ref, bf16[512,256]{1,0:T(8,128)(2,1)S(1)} %copy-done.27, f32[1072,256]{1,0:T(8,128)S(1)} %collective-permute-done.24.la_ref.lb_ref, f32[1072,256]{1,0:T(8,128)S(1)} %collective-permute-done.24.la_ref.lb_ref, ...), custom_call_target="tpu_custom_call" | custom-call | flops 1000 | bytes 1000 | tf_op jit(solution)/shard_map/embed_grad_a/pallas_call | solution.py:851
  221.9 2.5 pixel_grad.3
  224.4 3.7 %collective-permute-done.25 = f32[8,64,1024]{2,1,0:T(8,128)} collective-permute-done((f32[8,64,1024]{2,1,0:T(8,128)}, f32[8,64,1024]{2,1,0:T(8,128)}, u32[]{:S(2)}, u32[]{:S(2)}) %collective-permute-start.25) | collective-permute-done | bytes 2097184 | tf_op jit(solution)/shard_map/ppermute | solution.py:938
  228.1 2.5 fusion
  230.7 1.9 slice_add_fusion.3
  232.6 2.4 collective-permute-start.29
  236.2 2.9 collective-permute-start.31
  239.1 2.4 add_add_fusion
  241.5 6.7 %collective-permute-done.29 = f32[2,64,1024]{2,1,0:T(8,128)} collective-permute-done((f32[2,64,1024]{2,1,0:T(8,128)}, f32[2,64,1024]{2,1,0:T(8,128)}, u32[]{:S(2)}, u32[]{:S(2)}) %collective-permute-start.29) | collective-permute-done | bytes 524320 | tf_op jit(solution)/shard_map/ppermute | solution.py:938
  249.3 2.8 collective-permute-start.35
  252.1 15.5 %collective-permute-done.30 = f32[4,64,1024]{2,1,0:T(8,128)} collective-permute-done((f32[4,64,1024]{2,1,0:T(8,128)}, f32[4,64,1024]{2,1,0:T(8,128)}, u32[]{:S(2)}, u32[]{:S(2)}) %collective-permute-start.30) | collective-permute-done | bytes 1048608 | tf_op jit(solution)/shard_map/ppermute | solution.py:938
  269.8 2.4 collective-permute-done.31
  275.1 4.1 %collective-permute-start.36 = (f32[2,72,1024]{2,1,0:T(8,128)S(1)}, f32[2,72,1024]{2,1,0:T(8,128)S(1)}, u32[]{:S(2)}, u32[]{:S(2)}) collective-permute-start(f32[2,72,1024]{2,1,0:T(8,128)S(1)} %slice_add_fusion.1), channel_id=1, source_target_pairs={{0,8},{2,10},{4,12},{6,14},{8,0},{10,2},{12,4},{14,6},{16,24},{18,... | collective-permute-start | bytes 1769480 | tf_op jit(solution)/shard_map/ppermute | solution.py:938
  280.2 1.6 collective-permute-start.37
  282.9 1.4 collective-permute-start.39
  286.1 15.0 %collective-permute-done.36 = f32[2,72,1024]{2,1,0:T(8,128)S(1)} collective-permute-done((f32[2,72,1024]{2,1,0:T(8,128)S(1)}, f32[2,72,1024]{2,1,0:T(8,128)S(1)}, u32[]{:S(2)}, u32[]{:S(2)}) %collective-permute-start.36) | collective-permute-done | bytes 589856 | tf_op jit(solution)/shard_map/ppermute | solution.py:938
  303.1 2.3 add_convert_fusion.1
  307.5 8.9 %collective-permute-done.40 = f32[1,72,1024]{2,1,0:T(8,128)S(1)} collective-permute-done((f32[1,72,1024]{2,1,0:T(8,128)S(1)}, f32[1,72,1024]{2,1,0:T(8,128)S(1)}, u32[]{:S(2)}, u32[]{:S(2)}) %collective-permute-start.40) | collective-permute-done | bytes 294944 | tf_op jit(solution)/shard_map/ppermute | solution.py:938
  (224 shorter events, 36.7 us)
Async XLA Ops:
  5.7 26.1 %collective-permute-start = (f32[256,1024]{1,0:T(8,128)}, f32[256,1024]{1,0:T(8,128)S(1)}, u32[]{:S(2)}, u32[]{:S(2)}) collective-permute-start(f32[256,1024]{1,0:T(8,128)} %get-tuple-element.160.part_ref), channel_id=1, source_target_pairs={{0,1},{1,0},{2,3},{3,2},{4,5},{5,4},{6,7},{7,6},{8,9},{9,8},{10,11... | collective-permute-start | bytes 3145736 | tf_op jit(solution)/shard_map/ppermute | solution.py:938
  14.8 23.2 %collective-permute-start.3 = (f32[4,256,256]{2,1,0:T(8,128)S(1)}, f32[4,256,256]{2,1,0:T(8,128)S(1)}, u32[]{:S(2)}, u32[]{:S(2)}) collective-permute-start(f32[4,256,256]{2,1,0:T(8,128)S(1)} %get-tuple-element.164), channel_id=1, source_target_pairs={{0,2},{2,0},{4,6},{6,4},{8,10},{10,8},{12,14},{14,12},{16,18},{18,... | collective-permute-start | bytes 3145736 | tf_op jit(solution)/shard_map/ppermute | solution.py:938
  14.9 16.9 %copy-start.51 = (f32[256,1024]{1,0:T(8,128)S(1)}, f32[256,1024]{1,0:T(8,128)}, u32[]{:S(2)}) copy-start(f32[256,1024]{1,0:T(8,128)} %get-tuple-element.172.part_ref) | copy-start | bytes 3145732
  14.9 18.6 %copy-start.48 = (bf16[512,1024]{1,0:T(8,128)(2,1)S(1)}, bf16[512,1024]{1,0:T(8,128)(2,1)}, u32[]{:S(2)}) copy-start(bf16[512,1024]{1,0:T(8,128)(2,1)} %refs_5_.3) | copy-start | bytes 3145732
  14.9 18.6 %copy-start.50 = (f32[256,1024]{1,0:T(8,128)S(1)}, f32[256,1024]{1,0:T(8,128)}, u32[]{:S(2)}) copy-start(f32[256,1024]{1,0:T(8,128)} %get-tuple-element.160.part_ref) | copy-start | bytes 3145732
  18.1 43.6 %collective-permute-start.4 = (f32[8,256,256]{2,1,0:T(8,128)}, f32[8,256,256]{2,1,0:T(8,128)}, u32[]{:S(2)}, u32[]{:S(2)}) collective-permute-start(f32[8,256,256]{2,1,0:T(8,128)} %pack_pixels.2), channel_id=1, source_target_pairs={{0,2},{2,0},{4,6},{6,4},{8,10},{10,8},{12,14},{14,12},{16,18},{18,... | collective-permute-start | bytes 6291464 | tf_op jit(solution)/shard_map/ppermute | solution.py:938
  21.7 40.0 %collective-permute-start.5 = (f32[8,256,256]{2,1,0:T(8,128)}, f32[8,256,256]{2,1,0:T(8,128)}, u32[]{:S(2)}, u32[]{:S(2)}) collective-permute-start(f32[8,256,256]{2,1,0:T(8,128)} %pack_pixels.3), channel_id=1, source_target_pairs={{0,2},{2,0},{4,6},{6,4},{8,10},{10,8},{12,14},{14,12},{16,18},{18,... | collective-permute-start | bytes 6291464 | tf_op jit(solution)/shard_map/ppermute | solution.py:938
  31.8 24.0 %collective-permute-start.1 = (f32[256,1024]{1,0:T(8,128)S(1)}, f32[256,1024]{1,0:T(8,128)S(1)}, u32[]{:S(2)}, u32[]{:S(2)}) collective-permute-start(f32[256,1024]{1,0:T(8,128)S(1)} %copy-done.51), channel_id=1, source_target_pairs={{0,1},{1,0},{2,3},{3,2},{4,5},{5,4},{6,7},{7,6},{8,9},{9,8},{10,11... | collective-permute-start | bytes 3145736 | tf_op jit(solution)/shard_map/ppermute | solution.py:938
  38.0 19.3 %copy-start.36 = (bf16[256,512]{1,0:T(8,128)(2,1)}, bf16[256,512]{1,0:T(8,128)(2,1)S(1)}, u32[]{:S(2)}) copy-start(bf16[256,512]{1,0:T(8,128)(2,1)S(1)} %get-tuple-element.177.o_ref.ma_ref) | copy-start | bytes 786436
  38.0 42.6 %copy-start.61 = (f32[256,1024]{1,0:T(8,128)}, f32[256,1024]{1,0:T(8,128)S(1)}, u32[]{:S(2)}) copy-start(f32[256,1024]{1,0:T(8,128)S(1)} %get-tuple-element.170.x0_ref.refs_4_) | copy-start | bytes 3145732
  38.0 23.6 %copy-start.8 = (f32[4,256,256]{2,1,0:T(8,128)}, f32[4,256,256]{2,1,0:T(8,128)S(1)}, u32[]{:S(2)}) copy-start(f32[4,256,256]{2,1,0:T(8,128)S(1)} %collective-permute-done.3.la_ref.lb_ref) | copy-start | bytes 3145732
  39.8 48.5 %collective-permute-start.7 = (f32[4,256,256]{2,1,0:T(8,128)}, f32[4,256,256]{2,1,0:T(8,128)}, u32[]{:S(2)}, u32[]{:S(2)}) collective-permute-start(f32[4,256,256]{2,1,0:T(8,128)} %get-tuple-element.178), channel_id=1, source_target_pairs={{0,2},{2,0},{4,6},{6,4},{8,10},{10,8},{12,14},{14,12},{16,18},{18,... | collective-permute-start | bytes 3145736 | tf_op jit(solution)/shard_map/ppermute | solution.py:938
  55.9 23.3 %collective-permute-start.2 = (f32[256,1024]{1,0:T(8,128)S(1)}, f32[256,1024]{1,0:T(8,128)S(1)}, u32[]{:S(2)}, u32[]{:S(2)}) collective-permute-start(f32[256,1024]{1,0:T(8,128)S(1)} %get-tuple-element.173.opart_ref), channel_id=1, source_target_pairs={{0,1},{1,0},{2,3},{3,2},{4,5},{5,4},{6,7},{7,6},{8,9},{9,8},{10,11... | collective-permute-start | bytes 3145736 | tf_op jit(solution)/shard_map/ppermute | solution.py:938
  57.3 23.3 %copy-start.10 = (bf16[2048,1024]{1,0:T(8,128)(2,1)S(1)}, bf16[2048,1024]{1,0:T(8,128)(2,1)}, u32[]{:S(2)}) copy-start(bf16[2048,1024]{1,0:T(8,128)(2,1)} %wfc2_ref.7) | copy-start | bytes 12582916
  57.3 23.3 %copy-start.45 = (bf16[1024,2048]{1,0:T(8,128)(2,1)S(1)}, bf16[1024,2048]{1,0:T(8,128)(2,1)}, u32[]{:S(2)}) copy-start(bf16[1024,2048]{1,0:T(8,128)(2,1)} %wfc1_ref.5) | copy-start | bytes 12582916
  57.3 23.3 %copy-start.54 = (f32[2048]{0:T(1024)S(1)}, f32[2048]{0:T(1024)}, u32[]{:S(2)}) copy-start(f32[2048]{0:T(1024)} %param.36) | copy-start | bytes 24580
  57.3 23.3 %copy-start.56 = (f32[1024]{0:T(1024)S(1)}, f32[1024]{0:T(1024)}, u32[]{:S(2)}) copy-start(f32[1024]{0:T(1024)} %param.32) | copy-start | bytes 12292
  57.3 23.3 %copy-start.57 = (f32[1024]{0:T(1024)S(1)}, f32[1024]{0:T(1024)}, u32[]{:S(2)}) copy-start(f32[1024]{0:T(1024)} %param.34) | copy-start | bytes 12292
  57.3 23.3 %copy-start.58 = (f32[1024]{0:T(1024)S(1)}, f32[1024]{0:T(1024)}, u32[]{:S(2)}) copy-start(f32[1024]{0:T(1024)} %param.33) | copy-start | bytes 12292
  61.7 18.9 %copy-start.38 = (bf16[256,512]{1,0:T(8,128)(2,1)}, bf16[256,512]{1,0:T(8,128)(2,1)S(1)}, u32[]{:S(2)}) copy-start(bf16[256,512]{1,0:T(8,128)(2,1)S(1)} %get-tuple-element.185.o_ref.mb_ref) | copy-start | bytes 786436
  61.7 42.3 %copy-start.40 = (f32[256,1024]{1,0:T(8,128)}, f32[256,1024]{1,0:T(8,128)S(1)}, u32[]{:S(2)}) copy-start(f32[256,1024]{1,0:T(8,128)S(1)} %get-tuple-element.189.x0_ref.refs_4_) | copy-start | bytes 3145732
  62.5 25.8 %collective-permute-start.8 = (f32[4,256,256]{2,1,0:T(8,128)S(1)}, f32[4,256,256]{2,1,0:T(8,128)S(1)}, u32[]{:S(2)}, u32[]{:S(2)}) collective-permute-start(f32[4,256,256]{2,1,0:T(8,128)S(1)} %get-tuple-element.186), channel_id=1, source_target_pairs={{0,2},{2,0},{4,6},{6,4},{8,10},{10,8},{12,14},{14,12},{16,18},{18,... | collective-permute-start | bytes 3145736 | tf_op jit(solution)/shard_map/ppermute | solution.py:938
  79.2 23.3 %collective-permute-start.6 = (f32[256,1024]{1,0:T(8,128)S(1)}, f32[256,1024]{1,0:T(8,128)S(1)}, u32[]{:S(2)}, u32[]{:S(2)}) collective-permute-start(f32[256,1024]{1,0:T(8,128)S(1)} %get-tuple-element.190.opart_ref), channel_id=1, source_target_pairs={{0,1},{1,0},{2,3},{3,2},{4,5},{5,4},{6,7},{7,6},{8,9},{9,8},{10,11... | collective-permute-start | bytes 3145736 | tf_op jit(solution)/shard_map/ppermute | solution.py:938
  89.2 22.5 %collective-permute-start.11 = (f32[10,256,256]{2,1,0:T(8,128)S(1)}, f32[10,256,256]{2,1,0:T(8,128)S(1)}, u32[]{:S(2)}, u32[]{:S(2)}) collective-permute-start(f32[10,256,256]{2,1,0:T(8,128)S(1)} %get-tuple-element.199), channel_id=1, source_target_pairs={{0,2},{2,0},{4,6},{6,4},{8,10},{10,8},{12,14},{14,12},{16,18},{18,... | collective-permute-start | bytes 7864328 | tf_op jit(solution)/shard_map/ppermute | solution.py:938
  89.2 22.5 %collective-permute-start.10 = (f32[8,256,256]{2,1,0:T(8,128)S(1)}, f32[8,256,256]{2,1,0:T(8,128)S(1)}, u32[]{:S(2)}, u32[]{:S(2)}) collective-permute-start(f32[8,256,256]{2,1,0:T(8,128)S(1)} %get-tuple-element.198), channel_id=1, source_target_pairs={{0,2},{2,0},{4,6},{6,4},{8,10},{10,8},{12,14},{14,12},{16,18},{18,... | collective-permute-start | bytes 6291464 | tf_op jit(solution)/shard_map/ppermute | solution.py:938
  102.5 7.8 %collective-permute-start.9 = (f32[96,1024]{1,0:T(8,128)S(1)}, f32[96,1024]{1,0:T(8,128)S(1)}, u32[]{:S(2)}, u32[]{:S(2)}) collective-permute-start(f32[96,1024]{1,0:T(8,128)S(1)} %get-tuple-element.196.refs_0_), channel_id=1, source_target_pairs={{0,1},{1,0},{2,3},{3,2},{4,5},{5,4},{6,7},{7,6},{8,9},{9,8},{10,11... | collective-permute-start | bytes 1179656 | tf_op jit(solution)/shard_map/ppermute | solution.py:938
  108.8 41.1 %copy-start.24 = (f32[256,1024]{1,0:T(8,128)}, f32[256,1024]{1,0:T(8,128)S(1)}, u32[]{:S(2)}) copy-start(f32[256,1024]{1,0:T(8,128)S(1)} %get-tuple-element.219.refs_2_) | copy-start | bytes 3145732
  108.9 4.5 %collective-permute-start.13 = (f32[8,256,256]{2,1,0:T(8,128)S(1)}, f32[8,256,256]{2,1,0:T(8,128)S(1)}, u32[]{:S(2)}, u32[]{:S(2)}) collective-permute-start(f32[8,256,256]{2,1,0:T(8,128)S(1)} %get-tuple-element.195), channel_id=1, source_target_pairs={{0,2},{2,0},{4,6},{6,4},{8,10},{10,8},{12,14},{14,12},{16,18},{18,... | collective-permute-start | bytes 6291464 | tf_op jit(solution)/shard_map/ppermute | solution.py:938
  108.9 10.0 %collective-permute-start.14 = (f32[10,256,256]{2,1,0:T(8,128)S(1)}, f32[10,256,256]{2,1,0:T(8,128)S(1)}, u32[]{:S(2)}, u32[]{:S(2)}) collective-permute-start(f32[10,256,256]{2,1,0:T(8,128)S(1)} %get-tuple-element.213), channel_id=1, source_target_pairs={{0,2},{2,0},{4,6},{6,4},{8,10},{10,8},{12,14},{14,12},{16,18},{18,... | collective-permute-start | bytes 7864328 | tf_op jit(solution)/shard_map/ppermute | solution.py:938
  110.3 15.9 %collective-permute-start.12 = (f32[160,1024]{1,0:T(8,128)S(1)}, f32[160,1024]{1,0:T(8,128)S(1)}, u32[]{:S(2)}, u32[]{:S(2)}) collective-permute-start(f32[160,1024]{1,0:T(8,128)S(1)} %get-tuple-element.204.refs_1_), channel_id=1, source_target_pairs={{0,1},{1,0},{2,3},{3,2},{4,5},{5,4},{6,7},{7,6},{8,9},{9,8},{10,11... | collective-permute-start | bytes 1966088 | tf_op jit(solution)/shard_map/ppermute | solution.py:938
  117.4 77.0 %copy-start.19 = (f32[4,64,2048]{2,1,0:T(8,128)}, f32[4,64,2048]{2,1,0:T(8,128)S(1)}, u32[]{:S(2)}) copy-start(f32[4,64,2048]{2,1,0:T(8,128)S(1)} %get-tuple-element.232) | copy-start | bytes 6291460
  117.4 47.7 %collective-permute-start.17 = (f32[4,64,2048]{2,1,0:T(8,128)}, f32[4,64,2048]{2,1,0:T(8,128)}, u32[]{:S(2)}, u32[]{:S(2)}) collective-permute-start(f32[4,64,2048]{2,1,0:T(8,128)} %get-tuple-element.212), channel_id=1, source_target_pairs={{0,4},{2,6},{4,0},{6,2},{8,12},{10,14},{12,8},{14,10},{16,20},{18,... | collective-permute-start | bytes 6291464 | tf_op jit(solution)/shard_map/ppermute | solution.py:938
  123.2 50.5 %collective-permute-start.21 = (f32[8,64,1024]{2,1,0:T(8,128)}, f32[8,64,1024]{2,1,0:T(8,128)}, u32[]{:S(2)}, u32[]{:S(2)}) collective-permute-start(f32[8,64,1024]{2,1,0:T(8,128)} %bitcast.12), channel_id=1, source_target_pairs={{0,8},{2,10},{4,12},{6,14},{8,0},{10,2},{12,4},{14,6},{16,24},{18,... | collective-permute-start | bytes 6291464 | tf_op jit(solution)/shard_map/ppermute | solution.py:938
  126.2 23.5 %collective-permute-start.15 = (f32[256,1024]{1,0:T(8,128)S(1)}, f32[256,1024]{1,0:T(8,128)S(1)}, u32[]{:S(2)}, u32[]{:S(2)}) collective-permute-start(f32[256,1024]{1,0:T(8,128)S(1)} %mlp_back.1.refs_0_), channel_id=1, source_target_pairs={{0,1},{1,0},{2,3},{3,2},{4,5},{5,4},{6,7},{7,6},{8,9},{9,8},{10,11... | collective-permute-start | bytes 3145736 | tf_op jit(solution)/shard_map/ppermute | solution.py:938
  149.6 8.6 %collective-permute-start.16 = (f32[96,1024]{1,0:T(8,128)S(1)}, f32[96,1024]{1,0:T(8,128)S(1)}, u32[]{:S(2)}, u32[]{:S(2)}) collective-permute-start(f32[96,1024]{1,0:T(8,128)S(1)} %get-tuple-element.227.refs_0_), channel_id=1, source_target_pairs={{0,1},{1,0},{2,3},{3,2},{4,5},{5,4},{6,7},{7,6},{8,9},{9,8},{10,11... | collective-permute-start | bytes 1179656 | tf_op jit(solution)/shard_map/ppermute | solution.py:938
  158.0 11.1 %collective-permute-start.19 = (f32[8,256,256]{2,1,0:T(8,128)S(1)}, f32[8,256,256]{2,1,0:T(8,128)S(1)}, u32[]{:S(2)}, u32[]{:S(2)}) collective-permute-start(f32[8,256,256]{2,1,0:T(8,128)S(1)} %get-tuple-element.237), channel_id=1, source_target_pairs={{0,2},{2,0},{4,6},{6,4},{8,10},{10,8},{12,14},{14,12},{16,18},{18,... | collective-permute-start | bytes 6291464 | tf_op jit(solution)/shard_map/ppermute | solution.py:938
  158.3 10.9 %collective-permute-start.18 = (f32[8,256,256]{2,1,0:T(8,128)S(1)}, f32[8,256,256]{2,1,0:T(8,128)S(1)}, u32[]{:S(2)}, u32[]{:S(2)}) collective-permute-start(f32[8,256,256]{2,1,0:T(8,128)S(1)} %get-tuple-element.235), channel_id=1, source_target_pairs={{0,2},{2,0},{4,6},{6,4},{8,10},{10,8},{12,14},{14,12},{16,18},{18,... | collective-permute-start | bytes 6291464 | tf_op jit(solution)/shard_map/ppermute | solution.py:938
  161.1 22.0 %collective-permute-start.20 = (f32[160,1024]{1,0:T(8,128)S(1)}, f32[160,1024]{1,0:T(8,128)S(1)}, u32[]{:S(2)}, u32[]{:S(2)}) collective-permute-start(f32[160,1024]{1,0:T(8,128)S(1)} %get-tuple-element.243.refs_1_), channel_id=1, source_target_pairs={{0,1},{1,0},{2,3},{3,2},{4,5},{5,4},{6,7},{7,6},{8,9},{9,8},{10,11... | collective-permute-start | bytes 1966088 | tf_op jit(solution)/shard_map/ppermute | solution.py:938
  166.5 27.9 %collective-permute-start.23 = (f32[2,64,2048]{2,1,0:T(8,128)S(1)}, f32[2,64,2048]{2,1,0:T(8,128)S(1)}, u32[]{:S(2)}, u32[]{:S(2)}) collective-permute-start(f32[2,64,2048]{2,1,0:T(8,128)S(1)} %slice_add_fusion), channel_id=1, source_target_pairs={{0,8},{2,10},{4,12},{6,14},{8,0},{10,2},{12,4},{14,6},{16,24},{18,... | collective-permute-start | bytes 3145736 | tf_op jit(solution)/shard_map/ppermute | solution.py:938
  181.5 46.6 %collective-permute-start.25 = (f32[8,64,1024]{2,1,0:T(8,128)}, f32[8,64,1024]{2,1,0:T(8,128)}, u32[]{:S(2)}, u32[]{:S(2)}) collective-permute-start(f32[8,64,1024]{2,1,0:T(8,128)} %pad_maximum_fusion), channel_id=1, source_target_pairs={{0,4},{2,6},{4,0},{6,2},{8,12},{10,14},{12,8},{14,10},{16,20},{18,... | collective-permute-start | bytes 6291464 | tf_op jit(solution)/shard_map/ppermute | solution.py:938
  182.1 48.6 %collective-permute-start.27 = (f32[4,64,1024]{2,1,0:T(8,128)}, f32[4,64,1024]{2,1,0:T(8,128)}, u32[]{:S(2)}, u32[]{:S(2)}) collective-permute-start(f32[4,64,1024]{2,1,0:T(8,128)} %get-tuple-element.251), channel_id=1, source_target_pairs={{0,8},{2,10},{4,12},{6,14},{8,0},{10,2},{12,4},{14,6},{16,24},{18,... | collective-permute-start | bytes 3145736 | tf_op jit(solution)/shard_map/ppermute | solution.py:938
  183.0 22.7 %collective-permute-start.22 = (f32[256,1024]{1,0:T(8,128)S(1)}, f32[256,1024]{1,0:T(8,128)S(1)}, u32[]{:S(2)}, u32[]{:S(2)}) collective-permute-start(f32[256,1024]{1,0:T(8,128)S(1)} %get-tuple-element.255.refs_0_), channel_id=1, source_target_pairs={{0,1},{1,0},{2,3},{3,2},{4,5},{5,4},{6,7},{7,6},{8,9},{9,8},{10,11... | collective-permute-start | bytes 3145736 | tf_op jit(solution)/shard_map/ppermute | solution.py:938
  183.5 25.8 %copy-start.15 = (bf16[384,1024]{1,0:T(8,128)(2,1)S(1)}, bf16[384,1024]{1,0:T(8,128)(2,1)}, u32[]{:S(2)}) copy-start(bf16[384,1024]{1,0:T(8,128)(2,1)} %wrgb_ref.7) | copy-start | bytes 2359300
  185.7 20.0 %copy-start.41 = (f32[256,1024]{1,0:T(8,128)S(1)}, f32[256,1024]{1,0:T(8,128)}, u32[]{:S(2)}) copy-start(f32[256,1024]{1,0:T(8,128)} %copy-done.40) | copy-start | bytes 3145732
  194.4 17.6 %copy-start.64 = (f32[2,64,2048]{2,1,0:T(8,128)}, f32[2,64,2048]{2,1,0:T(8,128)S(1)}, u32[]{:S(2)}) copy-start(f32[2,64,2048]{2,1,0:T(8,128)S(1)} %collective-permute-done.23) | copy-start | bytes 3145732
  196.7 39.5 %collective-permute-start.28 = (f32[1,64,2048]{2,1,0:T(8,128)}, f32[1,64,2048]{2,1,0:T(8,128)}, u32[]{:S(2)}, u32[]{:S(2)}) collective-permute-start(f32[1,64,2048]{2,1,0:T(8,128)} %slice_add_fusion.5), channel_id=1, source_target_pairs={{0,16},{2,18},{4,20},{6,22},{8,24},{10,26},{12,28},{14,30},{16,0},... | collective-permute-start | bytes 1572872 | tf_op jit(solution)/shard_map/ppermute | solution.py:938
  208.0 22.7 %collective-permute-start.26 = (f32[256,1024]{1,0:T(8,128)}, f32[256,1024]{1,0:T(8,128)}, u32[]{:S(2)}, u32[]{:S(2)}) collective-permute-start(f32[256,1024]{1,0:T(8,128)} %mlp_out.3), channel_id=1, source_target_pairs={{0,1},{1,0},{2,3},{3,2},{4,5},{5,4},{6,7},{7,6},{8,9},{9,8},{10,11... | collective-permute-start | bytes 3145736 | tf_op jit(solution)/shard_map/ppermute | solution.py:938
  209.3 2.7 collective-permute-start.24
  216.8 50.8 %collective-permute-start.30 = (f32[4,64,1024]{2,1,0:T(8,128)}, f32[4,64,1024]{2,1,0:T(8,128)}, u32[]{:S(2)}, u32[]{:S(2)}) collective-permute-start(f32[4,64,1024]{2,1,0:T(8,128)} %get-tuple-element.273), channel_id=1, source_target_pairs={{0,8},{2,10},{4,12},{6,14},{8,0},{10,2},{12,4},{14,6},{16,24},{18,... | collective-permute-start | bytes 3145736 | tf_op jit(solution)/shard_map/ppermute | solution.py:938
  232.6 15.6 %collective-permute-start.29 = (f32[2,64,1024]{2,1,0:T(8,128)}, f32[2,64,1024]{2,1,0:T(8,128)}, u32[]{:S(2)}, u32[]{:S(2)}) collective-permute-start(f32[2,64,1024]{2,1,0:T(8,128)} %slice_add_fusion.3), channel_id=1, source_target_pairs={{0,4},{2,6},{4,0},{6,2},{8,12},{10,14},{12,8},{14,10},{16,20},{18,... | collective-permute-start | bytes 1572872 | tf_op jit(solution)/shard_map/ppermute | solution.py:938
  235.0 32.5 %copy-start.34 = (f32[4,64,1024]{2,1,0:T(8,128)S(1)}, f32[4,64,1024]{2,1,0:T(8,128)}, u32[]{:S(2)}) copy-start(f32[4,64,1024]{2,1,0:T(8,128)} %copy-done.33) | copy-start | bytes 3145732
  235.0 39.9 %collective-permute-start.32 = (f32[4,72,1024]{2,1,0:T(8,128)}, f32[4,72,1024]{2,1,0:T(8,128)S(1)}, u32[]{:S(2)}, u32[]{:S(2)}) collective-permute-start(f32[4,72,1024]{2,1,0:T(8,128)} %copy-done.47), channel_id=1, source_target_pairs={{0,4},{2,6},{4,0},{6,2},{8,12},{10,14},{12,8},{14,10},{16,20},{18,... | collective-permute-start | bytes 3538952 | tf_op jit(solution)/shard_map/ppermute | solution.py:938
  235.1 44.1 %collective-permute-start.33 = (f32[2,64,1024]{2,1,0:T(8,128)}, f32[2,64,1024]{2,1,0:T(8,128)S(1)}, u32[]{:S(2)}, u32[]{:S(2)}) collective-permute-start(f32[2,64,1024]{2,1,0:T(8,128)} %get-tuple-element.304), channel_id=1, source_target_pairs={{0,8},{2,10},{4,12},{6,14},{8,0},{10,2},{12,4},{14,6},{16,24},{18,... | collective-permute-start | bytes 1572872 | tf_op jit(solution)/shard_map/ppermute | solution.py:938
  236.2 35.9 %collective-permute-start.31 = (f32[2,64,1024]{2,1,0:T(8,128)}, f32[2,64,1024]{2,1,0:T(8,128)S(1)}, u32[]{:S(2)}, u32[]{:S(2)}) collective-permute-start(f32[2,64,1024]{2,1,0:T(8,128)} %get-tuple-element.303), channel_id=1, source_target_pairs={{0,16},{2,18},{4,20},{6,22},{8,24},{10,26},{12,28},{14,30},{16,0},... | collective-permute-start | bytes 1572872 | tf_op jit(solution)/shard_map/ppermute | solution.py:938
  249.3 35.0 %collective-permute-start.35 = (f32[1,64,1024]{2,1,0:T(8,128)S(1)}, f32[1,64,1024]{2,1,0:T(8,128)S(1)}, u32[]{:S(2)}, u32[]{:S(2)}) collective-permute-start(f32[1,64,1024]{2,1,0:T(8,128)S(1)} %slice_add_fusion.9), channel_id=1, source_target_pairs={{0,16},{2,18},{4,20},{6,22},{8,24},{10,26},{12,28},{14,30},{16,0},... | collective-permute-start | bytes 786440 | tf_op jit(solution)/shard_map/ppermute | solution.py:938
  268.7 13.2 %collective-permute-start.34 = (f32[2,64,1024]{2,1,0:T(8,128)S(1)}, f32[2,64,1024]{2,1,0:T(8,128)S(1)}, u32[]{:S(2)}, u32[]{:S(2)}) collective-permute-start(f32[2,64,1024]{2,1,0:T(8,128)S(1)} %slice_add_fusion.2), channel_id=1, source_target_pairs={{0,4},{2,6},{4,0},{6,2},{8,12},{10,14},{12,8},{14,10},{16,20},{18,... | collective-permute-start | bytes 1572872 | tf_op jit(solution)/shard_map/ppermute | solution.py:938
  273.6 29.5 %collective-permute-start.38 = (f32[256,1024]{1,0:T(8,128)S(1)}, f32[256,1024]{1,0:T(8,128)S(1)}, u32[]{:S(2)}, u32[]{:S(2)}) collective-permute-start(f32[256,1024]{1,0:T(8,128)S(1)} %copy-done.12), channel_id=1, source_target_pairs={{0,1},{1,0},{2,3},{3,2},{4,5},{5,4},{6,7},{7,6},{8,9},{9,8},{10,11... | collective-permute-start | bytes 3145736 | tf_op jit(solution)/shard_map/ppermute | solution.py:938
  275.1 26.1 %collective-permute-start.36 = (f32[2,72,1024]{2,1,0:T(8,128)S(1)}, f32[2,72,1024]{2,1,0:T(8,128)S(1)}, u32[]{:S(2)}, u32[]{:S(2)}) collective-permute-start(f32[2,72,1024]{2,1,0:T(8,128)S(1)} %slice_add_fusion.1), channel_id=1, source_target_pairs={{0,8},{2,10},{4,12},{6,14},{8,0},{10,2},{12,4},{14,6},{16,24},{18,... | collective-permute-start | bytes 1769480 | tf_op jit(solution)/shard_map/ppermute | solution.py:938
  280.2 21.0 %collective-permute-start.37 = (f32[1,64,1024]{2,1,0:T(8,128)S(1)}, f32[1,64,1024]{2,1,0:T(8,128)S(1)}, u32[]{:S(2)}, u32[]{:S(2)}) collective-permute-start(f32[1,64,1024]{2,1,0:T(8,128)S(1)} %slice_add_fusion.8), channel_id=1, source_target_pairs={{0,16},{2,18},{4,20},{6,22},{8,24},{10,26},{12,28},{14,30},{16,0},... | collective-permute-start | bytes 786440 | tf_op jit(solution)/shard_map/ppermute | solution.py:938
  282.9 23.6 %collective-permute-start.39 = (f32[1,64,1024]{2,1,0:T(8,128)S(1)}, f32[1,64,1024]{2,1,0:T(8,128)S(1)}, u32[]{:S(2)}, u32[]{:S(2)}) collective-permute-start(f32[1,64,1024]{2,1,0:T(8,128)S(1)} %slice_add_fusion.7), channel_id=1, source_target_pairs={{0,16},{2,18},{4,20},{6,22},{8,24},{10,26},{12,28},{14,30},{16,0},... | collective-permute-start | bytes 786440 | tf_op jit(solution)/shard_map/ppermute | solution.py:938
  285.4 17.7 %copy-start.23 = (f32[256,1024]{1,0:T(8,128)S(1)}, f32[256,1024]{1,0:T(8,128)}, u32[]{:S(2)}) copy-start(f32[256,1024]{1,0:T(8,128)} %copy-done.22) | copy-start | bytes 3145732
  285.4 17.7 %copy-start.25 = (f32[256,1024]{1,0:T(8,128)S(1)}, f32[256,1024]{1,0:T(8,128)}, u32[]{:S(2)}) copy-start(f32[256,1024]{1,0:T(8,128)} %copy-done.24) | copy-start | bytes 3145732
  285.4 17.7 %copy-start.65 = (f32[1024]{0:T(1024)S(1)}, f32[1024]{0:T(1024)}, u32[]{:S(2)}) copy-start(f32[1024]{0:T(1024)} %param.38) | copy-start | bytes 12292
  301.2 15.2 %collective-permute-start.40 = (f32[1,72,1024]{2,1,0:T(8,128)S(1)}, f32[1,72,1024]{2,1,0:T(8,128)S(1)}, u32[]{:S(2)}, u32[]{:S(2)}) collective-permute-start(f32[1,72,1024]{2,1,0:T(8,128)S(1)} %slice_add_fusion.6), channel_id=1, source_target_pairs={{0,16},{2,18},{4,20},{6,22},{8,24},{10,26},{12,28},{14,30},{16,0},... | collective-permute-start | bytes 884744 | tf_op jit(solution)/shard_map/ppermute | solution.py:938
  (45 other events, 261.9 us)

commit v11 on v10

--- a/solution.py
+++ b/solution.py
@@ -421,22 +421,23 @@
         dqkv_ref[0, :, span] = (totals[0] * scale).astype(BF16)
         dqkv_ref[1, :, span] = (totals[1] * scale).astype(BF16)
         dqkv_ref[2, :, span] = totals[2].astype(BF16)
-    da1 = nt(dqkv_ref[0], wqkv_ref[0]) + nt(dqkv_ref[1], wqkv_ref[1]) + nt(dqkv_ref[2], wqkv_ref[2])
-
-    @pl.when(quad == 0)
-    def _():
-        put_rows(da1_refs, da1, False)
-
-    @pl.when(quad != 0)
-    def _():
-        put_rows(da1_refs, da1, True)
-
     steps = pl.num_programs(0)
     for plane in range(3):
         gone_ref[2 + plane * steps + quad] = dqkv_ref[plane].astype(F32)
     qvsum_ref[0:1, :] = column_sum(dqkv_ref[0].astype(F32))
     qvsum_ref[1:2, :] = column_sum(dqkv_ref[2].astype(F32))
     qvsum_ref[2:8, :] = jnp.zeros((6, qvsum_ref.shape[1]), F32)
+    if not da1_refs:
+        return
+    da1 = nt(dqkv_ref[0], wqkv_ref[0]) + nt(dqkv_ref[1], wqkv_ref[1]) + nt(dqkv_ref[2], wqkv_ref[2])
+
+    @pl.when(quad == 0)
+    def _():
+        put_rows(da1_refs, da1, False)
+
+    @pl.when(quad != 0)
+    def _():
+        put_rows(da1_refs, da1, True)
 
 
 def attn_backward(place, gparts, grecvs, x1, cotangent, gain, w_out, qkv, w_qkv, item, cuts):
@@ -483,6 +484,28 @@
         cost_estimate=long_cost(),
         name="attn_backward",
     )(place, *gparts, *grecvs, x1, cotangent, gain, w_out, qkv, w_qkv)
+
+
+def attn_in_back_kernel(dqkv_ref, wqkv_ref, out_ref):
+    out_ref[...] = (
+        nt(dqkv_ref[0], wqkv_ref[0]) + nt(dqkv_ref[1], wqkv_ref[1]) + nt(dqkv_ref[2], wqkv_ref[2])
+    )
+
+
+def attn_in_back(dqkv, w_qkv):
+    rows, columns = dqkv.shape[1:]
+    width = w_qkv.shape[1]
+    tile = 512
+    return pl.pallas_call(
+        attn_in_back_kernel,
+        grid=(width // tile,),
+        in_specs=[whole(dqkv.shape), pl.BlockSpec((3, tile, columns), lambda n: (0, n, 0))],
+        out_specs=pl.BlockSpec((rows, tile), lambda n: (0, n)),
+        out_shape=jax.ShapeDtypeStruct((rows, width), F32),
+        compiler_params=params(8),
+        cost_estimate=long_cost(),
+        name="attn_in_back",
+    )(dqkv, w_qkv)
 
 
 def mlp_kernel(
@@ -1138,19 +1161,21 @@
     grecv[1] = [send(order.tie(da2[1][0]))]
     for i in range(items):
         bwd[i] = attn_backward(
-            place, da2[i], grecv[i], x1[i], cotangent, order.tie(g2), w_out, qkv[i], wqkv, i, cuts[i]
+            place, da2[i], grecv[i], x1[i], cotangent, order.tie(g2), w_out, qkv[i], wqkv, i,
+            cuts[i] if i == 0 else (),
         )
         da1[i] = bwd[i][7:]
-        order.mark(da1[i][0])
+        order.mark(da1[i][0] if i == 0 else bwd[i][6])
         if i == 0:
             arecv[i] = [send(v) for v in da1[i]]
-            ycot[1] = mlp_out(order.tie(ffn[1][2]), w_fc2, short_cost())
-            order.mark(ycot[1])
+            for n in range(items):
+                ycot[n] = mlp_out(order.tie(ffn[n][2]), w_fc2, short_cost())
+                order.mark(ycot[n])
         else:
             arecv[0][0] = settle(arecv[0][0])
             gbwd = [other(order.tie(bwd[0][6])), other(bwd[1][6])]
-            ycot[0] = mlp_out(order.tie(ffn[0][2]), w_fc2, long_cost())
-            order.mark(ycot[0])
+            da1[1] = [attn_in_back(order.tie(bwd[1][2]), wqkv)]
+            order.mark(da1[1][0])
     dx1, dya, dqkv, sums2, qvsum, kdya = list(zip(*[v[:6] for v in bwd]))
     if custom:
         fc2_h.step(order)

time: 324 us -> 324 us (level)
  waiting for transfers between devices: 136 us -> 141 us
  starting transfers between devices: 46.4 us -> 42.3 us
    ppermute x41, waiting for transfers between devices: 136 us -> 141 us  [exchange(): return lax.ppermute(values, axis, [(i, i ^ bit) for i in range(size)])]
    ppermute x41, starting transfers between devices: 46.4 us -> 42.3 us  [exchange(): return lax.ppermute(values, axis, [(i, i ^ bit) for i in range(size)])]
  transfers between devices with their start and end apart: 41 -> 41, of which waited for: 17 -> 22; matrix products, arithmetic and copies ran while one was open for 9% -> 9% of each run, Pallas kernels for 29% -> 29%
where the time goes in v11:
time: 324 us; the launch traced here: 321 us
  waiting for transfers between devices  141 us (44%)
  Pallas kernels  96.5 us (30%)
  starting transfers between devices  42.3 us (13%)
  other arithmetic  30.3 us (9%)
  local copies, waits for them, and re-layouts  8.57 us (3%)
    ppermute x41, waiting for transfers between devices, exchange(): return lax.ppermute(values, axis, [(i, i ^ bit) for i in range(size)])  141 us
    ppermute x41, starting transfers between devices, exchange(): return lax.ppermute(values, axis, [(i, i ^ bit) for i in range(size)])  42.3 us
    add x17, other arithmetic, value(): value = value + recv[first:first + count]  20.9 us
    pallas_call x4, Pallas kernels, plain_grad(): pl.pallas_call(functools.partial(plain_grad_kernel, moves=moves, vectors=...  15.4 us
    pallas_call x2, Pallas kernels, attn_backward(): pl.pallas_call(functools.partial(attn_backward_kernel, parts=(len(gparts)...  14.5 us
    pallas_call x2, Pallas kernels, mlp(): pl.pallas_call(mlp_kernel, grid_spec=pltpu.PrefetchScalarGridSpec(num_sca...  12.5 us
    pallas_call x2, Pallas kernels, embed(): pl.pallas_call(functools.partial(embed_kernel, item=item), grid_spec=pltp...  9.42 us
    pallas_call x2, Pallas kernels, attn_forward(): pl.pallas_call(attn_forward_kernel, grid=(steps,), in_specs=[whole(part.s...  8.72 us
  transfers between devices with their start and end apart: 41, of which 22 were waited for; matrix products, arithmetic and copies ran while one was open for 9% of the time, Pallas kernels for 29%

profile of v11, /device:TPU:0, one launch (start us, length us, event | category | flops | bytes accessed | tf_op | source)
XLA Modules:
  0.0 320.6 jit_solution(8639362008721810998)
XLA Ops:
  0.7 4.7 %embed.2 = (f32[256,1024]{1,0:T(8,128)}, bf16[256,2048]{1,0:T(8,128)(2,1)}) custom-call(s32[2]{0:T(128)} %kinds.4, bf16[512,1664]{1,0:T(8,128)(2,1)} %pix_ref.3, bf16[1664,1024]{1,0:T(8,128)(2,1)} %wspec_ref.7, bf16[384,1024]{1,0:T(8,128)(2,1)} %wrgb_ref.7, bf16[1664,384]{1,0:T(8,128)(2,1)} %constant.50.clone.pick_ref), custom_call_target="tpu_custom_call" | custom-call | flops 1000 | bytes 1000 | tf_op jit(solution)/shard_map/embed/pallas_call | solution.py:242
  5.4 3.0 collective-permute-start
  8.5 4.7 %embed.3 = (f32[256,1024]{1,0:T(8,128)}, bf16[256,2048]{1,0:T(8,128)(2,1)}) custom-call(s32[2]{0:T(128)} %kinds.4, bf16[512,1664]{1,0:T(8,128)(2,1)} %pix_ref.3, bf16[1664,1024]{1,0:T(8,128)(2,1)} %wspec_ref.7, bf16[384,1024]{1,0:T(8,128)(2,1)} %wrgb_ref.7, bf16[1664,384]{1,0:T(8,128)(2,1)} %constant.50.clone.pick_ref), custom_call_target="tpu_custom_call" | custom-call | flops 1000 | bytes 1000 | tf_op jit(solution)/shard_map/embed/pallas_call | solution.py:242
  14.7 3.1 pack_pixels.2
  18.3 3.2 pack_pixels.3
  21.9 10.2 %collective-permute-done.recv_ref = f32[256,1024]{1,0:T(8,128)S(1)} collective-permute-done((f32[256,1024]{1,0:T(8,128)}, f32[256,1024]{1,0:T(8,128)S(1)}, u32[]{:S(2)}, u32[]{:S(2)}) %collective-permute-start) | collective-permute-done | bytes 1048608 | tf_op jit(solution)/shard_map/ppermute | solution.py:961
  32.0 1.7 collective-permute-start.1
  33.8 4.4 %attn_forward.2 = (f32[256,1024]{1,0:T(8,128)S(1)}, bf16[256,1024]{1,0:T(8,128)(2,1)S(1)}, bf16[3,256,512]{2,1,0:T(8,128)(2,1)S(1)}, bf16[256,512]{1,0:T(8,128)(2,1)S(1)}, f32[256,1024]{1,0:T(8,128)S(1)}) custom-call(f32[256,1024]{1,0:T(8,128)S(1)} %copy-done.50, f32[256,1024]{1,0:T(8,128)S(1)} %collective-permute-done.recv_ref, ...), custom_call_target="tpu_custom_call" | custom-call | flops 99999997952 | bytes 1000 | tf_op jit(solution)/shard_map/attn_forward/pallas_call | solution.py:330
  38.2 1.8 pack_attn.2
  40.0 16.7 %collective-permute-done.1.recv_ref = f32[256,1024]{1,0:T(8,128)S(1)} collective-permute-done((f32[256,1024]{1,0:T(8,128)S(1)}, f32[256,1024]{1,0:T(8,128)S(1)}, u32[]{:S(2)}, u32[]{:S(2)}) %collective-permute-start.1) | collective-permute-done | bytes 1048608 | tf_op jit(solution)/shard_map/ppermute | solution.py:961
  56.7 1.4 collective-permute-start.2
  58.2 4.4 %attn_forward.3 = (f32[256,1024]{1,0:T(8,128)S(1)}, bf16[256,1024]{1,0:T(8,128)(2,1)S(1)}, bf16[3,256,512]{2,1,0:T(8,128)(2,1)S(1)}, bf16[256,512]{1,0:T(8,128)(2,1)S(1)}, f32[256,1024]{1,0:T(8,128)S(1)}) custom-call(f32[256,1024]{1,0:T(8,128)S(1)} %copy-done.51, f32[256,1024]{1,0:T(8,128)S(1)} %collective-permute-done.1.recv_ref, ...), custom_call_target="tpu_custom_call" | custom-call | flops 99999997952 | bytes 1000 | tf_op jit(solution)/shard_map/attn_forward/pallas_call | solution.py:330
  64.3 16.1 %collective-permute-done.2.orecv_ref = f32[256,1024]{1,0:T(8,128)S(1)} collective-permute-done((f32[256,1024]{1,0:T(8,128)S(1)}, f32[256,1024]{1,0:T(8,128)S(1)}, u32[]{:S(2)}, u32[]{:S(2)}) %collective-permute-start.2) | collective-permute-done | bytes 1048608 | tf_op jit(solution)/shard_map/ppermute | solution.py:961
  81.6 7.6 %mlp.2 = (f32[256,1024]{1,0:T(8,128)S(1)}, bf16[256,1024]{1,0:T(8,128)(2,1)}, bf16[256,2048]{1,0:T(8,128)(2,1)S(1)}, bf16[256,2048]{1,0:T(8,128)(2,1)S(1)}, f32[...) custom-call(s32[9]{0:T(128)S(1)} %pad_add_fusion.place, ...), custom_call_target="tpu_custom_call" | custom-call | flops 99999997952 | bytes 1000 | tf_op jit(solution)/shard_map/mlp/pallas_call | solution.py:561
  89.8 14.0 %collective-permute-done.6.orecv_ref = f32[256,1024]{1,0:T(8,128)S(1)} collective-permute-done((f32[256,1024]{1,0:T(8,128)S(1)}, f32[256,1024]{1,0:T(8,128)S(1)}, u32[]{:S(2)}, u32[]{:S(2)}) %collective-permute-start.6) | collective-permute-done | bytes 1048608 | tf_op jit(solution)/shard_map/ppermute | solution.py:961
  104.9 4.9 %mlp.3 = (f32[256,1024]{1,0:T(8,128)S(1)}, bf16[256,1024]{1,0:T(8,128)(2,1)}, bf16[256,2048]{1,0:T(8,128)(2,1)S(1)}, bf16[256,2048]{1,0:T(8,128)(2,1)S(1)}, f32[...) custom-call(s32[9]{0:T(128)S(1)} %pad_add_fusion.place, ...), custom_call_target="tpu_custom_call" | custom-call | flops 99999997952 | bytes 1000 | tf_op jit(solution)/shard_map/mlp/pallas_call | solution.py:561
  112.6 1.6 mlp_back.1.refs_0_
  114.3 4.1 %fc2_grad.1 = (f32[4,64,2048]{2,1,0:T(8,128)}, f32[4,64,2048]{2,1,0:T(8,128)S(1)}) custom-call(bf16[2,512,256]{2,1,0:T(8,128)(2,1)S(1)} %get-tuple-element.205.ka_ref.kb_ref, bf16[2,512,256]{2,1,0:T(8,128)(2,1)S(1)} %get-tuple-element.205.ka_ref.kb_ref, f32[4,256,256]{2,1,0:T(8,128)S(1)} %copy-done.10, f32[4,256,256]{2,1,0:T(8,128)S(1)} %copy-done.10, ...), custom_call_target="tpu_custom_call" | custom-call | flops 1000 | bytes 1000 | tf_op jit(solution)/shard_map/fc2_grad/pallas_call | solution.py:874
  118.9 4.3 %fc1_grad.1 = (f32[4,2,64,1024]{3,2,1,0:T(8,128)}, f32[4,2,64,1024]{3,2,1,0:T(8,128)S(1)}) custom-call(bf16[512,256]{1,0:T(8,128)(2,1)S(1)} %get-tuple-element.200.ka_ref, bf16[512,256]{1,0:T(8,128)(2,1)S(1)} %get-tuple-element.201.kb_ref, f32[10,256,256]{2,1,0:T(8,128)S(1)} %collective-permute-done.12.la_ref.oa_ref, ...), custom_call_target="tpu_custom_call" | custom-call | flops 1000 | bytes 1000 | tf_op jit(solution)/shard_map/fc1_grad/pallas_call | solution.py:874
  123.2 2.6 collective-permute-start.21
  125.7 1.4 collective-permute-done.10.refs_3_
  128.0 8.3 %attn_backward.2 = (f32[256,1024]{1,0:T(8,128)S(1)}, bf16[256,1024]{1,0:T(8,128)(2,1)}, bf16[3,256,512]{2,1,0:T(8,128)(2,1)S(1)}, f32[8,1024]{1,0:T(8,128)S(1)},...) custom-call(s32[9]{0:T(128)S(1)} %pad_add_fusion.place, ...), custom_call_target="tpu_custom_call" | custom-call | flops 99999997952 | bytes 1000 | tf_op jit(solution)/shard_map/attn_backward/pallas_call | solution.py:447
  136.3 2.5 mlp_out.2
  138.8 1.8 mlp_out.3
  142.7 7.6 %collective-permute-done.15.refs_1_ = f32[256,1024]{1,0:T(8,128)S(1)} collective-permute-done((f32[256,1024]{1,0:T(8,128)S(1)}, f32[256,1024]{1,0:T(8,128)S(1)}, u32[]{:S(2)}, u32[]{:S(2)}) %collective-permute-start.15) | collective-permute-done | bytes 1048608 | tf_op jit(solution)/shard_map/ppermute | solution.py:961
  151.2 6.2 %attn_backward.3 = (f32[256,1024]{1,0:T(8,128)S(1)}, bf16[256,1024]{1,0:T(8,128)(2,1)}, bf16[3,256,512]{2,1,0:T(8,128)(2,1)S(1)}, f32[8,1024]{1,0:T(8,128)S(1)},...) custom-call(s32[9]{0:T(128)S(1)} %pad_add_fusion.place, ...), custom_call_target="tpu_custom_call" | custom-call | flops 99999997952 | bytes 1000 | tf_op jit(solution)/shard_map/attn_backward/pallas_call | solution.py:447
  158.5 1.5 attn_in_back.1.refs_0_
  161.1 5.0 %collective-permute-done.17 = f32[4,64,2048]{2,1,0:T(8,128)} collective-permute-done((f32[4,64,2048]{2,1,0:T(8,128)}, f32[4,64,2048]{2,1,0:T(8,128)}, u32[]{:S(2)}, u32[]{:S(2)}) %collective-permute-start.17) | collective-permute-done | bytes 2097184 | tf_op jit(solution)/shard_map/ppermute | solution.py:961
  167.5 1.4 collective-permute-start.23
  168.9 3.6 %query_key_grad.1 = (f32[4,64,1024]{2,1,0:T(8,128)S(1)}, f32[4,64,1024]{2,1,0:T(8,128)S(1)}) custom-call(bf16[512,256]{1,0:T(8,128)(2,1)S(1)} %get-tuple-element.221.aa_ref, bf16[512,256]{1,0:T(8,128)(2,1)S(1)} %get-tuple-element.222.ab_ref, f32[4,256,256]{2,1,0:T(8,128)} %collective-permute-done.7.fa_ref, f32[4,256,256]{2,1,0:T(8,128)S(1)} %copy-done.14, ...), custom_call_target="tpu_custom_call" | custom-call | flops 1000 | bytes 1000 | tf_op jit(solution)/shard_map/query_key_grad/pallas_call | solution.py:947
  173.4 1.4 bitcast_add_fusion
  174.9 1.6 pad_maximum_fusion
  176.5 4.8 %value_out_grad.1 = (f32[4,64,1024]{2,1,0:T(8,128)}, f32[4,64,1024]{2,1,0:T(8,128)S(1)}) custom-call(bf16[512,256]{1,0:T(8,128)(2,1)S(1)} %get-tuple-element.221.aa_ref, bf16[512,256]{1,0:T(8,128)(2,1)S(1)} %get-tuple-element.222.ab_ref, f32[4,256,256]{2,1,0:T(8,128)} %collective-permute-done.7.fa_ref, f32[4,256,256]{2,1,0:T(8,128)S(1)} %copy-done.14, ...), custom_call_target="tpu_custom_call" | custom-call | flops 1000 | bytes 1000 | tf_op jit(solution)/shard_map/value_out_grad/pallas_call | solution.py:947
  182.3 1.7 collective-permute-start.25
  184.6 2.1 first_norm_back.2
  186.7 8.1 %collective-permute-done.23 = f32[2,64,2048]{2,1,0:T(8,128)S(1)} collective-permute-done((f32[2,64,2048]{2,1,0:T(8,128)S(1)}, f32[2,64,2048]{2,1,0:T(8,128)S(1)}, u32[]{:S(2)}, u32[]{:S(2)}) %collective-permute-start.23) | collective-permute-done | bytes 1048608 | tf_op jit(solution)/shard_map/ppermute | solution.py:961
  194.9 2.3 slice_add_fusion.5
  197.2 2.4 collective-permute-start.28
  200.3 7.3 %collective-permute-done.22.refs_1_ = f32[256,1024]{1,0:T(8,128)S(1)} collective-permute-done((f32[256,1024]{1,0:T(8,128)S(1)}, f32[256,1024]{1,0:T(8,128)S(1)}, u32[]{:S(2)}, u32[]{:S(2)}) %collective-permute-start.22) | collective-permute-done | bytes 1048608 | tf_op jit(solution)/shard_map/ppermute | solution.py:961
  207.6 2.2 first_norm_back.3
  210.3 2.5 pixel_grad.2.refs_0_
  213.0 3.8 %embed_grad_b.1 = (f32[4,64,1024]{2,1,0:T(8,128)}, f32[4,64,1024]{2,1,0:T(8,128)S(1)}) custom-call(bf16[512,256]{1,0:T(8,128)(2,1)S(1)} %get-tuple-element.253.ka_ref, bf16[512,256]{1,0:T(8,128)(2,1)S(1)} %get-tuple-element.268.kb_ref, f32[1072,256]{1,0:T(8,128)S(1)} %collective-permute-done.24.la_ref.lb_ref, ...), custom_call_target="tpu_custom_call" | custom-call | flops 1000 | bytes 1000 | tf_op jit(solution)/shard_map/embed_grad_b/pallas_call | solution.py:874
  217.7 1.7 collective-permute-start.30
  220.5 3.3 %embed_grad_a.1 = (f32[4,72,1024]{2,1,0:T(8,128)S(1)}, f32[4,72,1024]{2,1,0:T(8,128)S(1)}) custom-call(bf16[512,256]{1,0:T(8,128)(2,1)S(1)} %get-tuple-element.253.ka_ref, bf16[512,256]{1,0:T(8,128)(2,1)S(1)} %copy-done.27, f32[1072,256]{1,0:T(8,128)S(1)} %collective-permute-done.24.la_ref.lb_ref, f32[1072,256]{1,0:T(8,128)S(1)} %collective-permute-done.24.la_ref.lb_ref, ...), custom_call_target="tpu_custom_call" | custom-call | flops 1000 | bytes 1000 | tf_op jit(solution)/shard_map/embed_grad_a/pallas_call | solution.py:874
  223.9 2.5 pixel_grad.3
  226.4 2.8 collective-permute-done.25
  229.2 2.5 fusion
  232.8 1.9 slice_add_fusion.3
  235.1 1.6 collective-permute-start.32
  236.7 1.4 collective-permute-start.33
  238.2 2.2 collective-permute-start.31
  240.4 2.4 add_add_fusion
  242.8 7.1 %collective-permute-done.29 = f32[2,64,1024]{2,1,0:T(8,128)} collective-permute-done((f32[2,64,1024]{2,1,0:T(8,128)}, f32[2,64,1024]{2,1,0:T(8,128)}, u32[]{:S(2)}, u32[]{:S(2)}) %collective-permute-start.29) | collective-permute-done | bytes 524320 | tf_op jit(solution)/shard_map/ppermute | solution.py:961
  250.9 1.9 collective-permute-start.35
  252.9 15.2 %collective-permute-done.30 = f32[4,64,1024]{2,1,0:T(8,128)} collective-permute-done((f32[4,64,1024]{2,1,0:T(8,128)}, f32[4,64,1024]{2,1,0:T(8,128)}, u32[]{:S(2)}, u32[]{:S(2)}) %collective-permute-start.30) | collective-permute-done | bytes 1048608 | tf_op jit(solution)/shard_map/ppermute | solution.py:961
  270.3 3.0 collective-permute-done.31
  273.2 1.4 fusion.2
  276.1 2.8 collective-permute-start.36
  280.1 2.0 collective-permute-start.37
  283.3 2.2 collective-permute-start.39
  287.4 14.0 %collective-permute-done.36 = f32[2,72,1024]{2,1,0:T(8,128)S(1)} collective-permute-done((f32[2,72,1024]{2,1,0:T(8,128)S(1)}, f32[2,72,1024]{2,1,0:T(8,128)S(1)}, u32[]{:S(2)}, u32[]{:S(2)}) %collective-permute-start.36) | collective-permute-done | bytes 589856 | tf_op jit(solution)/shard_map/ppermute | solution.py:961
  303.7 2.3 add_convert_fusion.1
  307.1 4.0 %collective-permute-done.39 = f32[1,64,1024]{2,1,0:T(8,128)S(1)} collective-permute-done((f32[1,64,1024]{2,1,0:T(8,128)S(1)}, f32[1,64,1024]{2,1,0:T(8,128)S(1)}, u32[]{:S(2)}, u32[]{:S(2)}) %collective-permute-start.39) | collective-permute-done | bytes 262176 | tf_op jit(solution)/shard_map/ppermute | solution.py:961
  312.1 4.8 %collective-permute-done.40 = f32[1,72,1024]{2,1,0:T(8,128)S(1)} collective-permute-done((f32[1,72,1024]{2,1,0:T(8,128)S(1)}, f32[1,72,1024]{2,1,0:T(8,128)S(1)}, u32[]{:S(2)}, u32[]{:S(2)}) %collective-permute-start.40) | collective-permute-done | bytes 294944 | tf_op jit(solution)/shard_map/ppermute | solution.py:961
  (229 shorter events, 41.8 us)
Async XLA Ops:
  5.4 26.7 %collective-permute-start = (f32[256,1024]{1,0:T(8,128)}, f32[256,1024]{1,0:T(8,128)S(1)}, u32[]{:S(2)}, u32[]{:S(2)}) collective-permute-start(f32[256,1024]{1,0:T(8,128)} %get-tuple-element.160.part_ref), channel_id=1, source_target_pairs={{0,1},{1,0},{2,3},{3,2},{4,5},{5,4},{6,7},{7,6},{8,9},{9,8},{10,11... | collective-permute-start | bytes 3145736 | tf_op jit(solution)/shard_map/ppermute | solution.py:961
  14.5 23.7 %collective-permute-start.3 = (f32[4,256,256]{2,1,0:T(8,128)S(1)}, f32[4,256,256]{2,1,0:T(8,128)S(1)}, u32[]{:S(2)}, u32[]{:S(2)}) collective-permute-start(f32[4,256,256]{2,1,0:T(8,128)S(1)} %get-tuple-element.164), channel_id=1, source_target_pairs={{0,2},{2,0},{4,6},{6,4},{8,10},{10,8},{12,14},{14,12},{16,18},{18,... | collective-permute-start | bytes 3145736 | tf_op jit(solution)/shard_map/ppermute | solution.py:961
  14.7 17.4 %copy-start.51 = (f32[256,1024]{1,0:T(8,128)S(1)}, f32[256,1024]{1,0:T(8,128)}, u32[]{:S(2)}) copy-start(f32[256,1024]{1,0:T(8,128)} %get-tuple-element.172.part_ref) | copy-start | bytes 3145732
  14.7 19.1 %copy-start.48 = (bf16[512,1024]{1,0:T(8,128)(2,1)S(1)}, bf16[512,1024]{1,0:T(8,128)(2,1)}, u32[]{:S(2)}) copy-start(bf16[512,1024]{1,0:T(8,128)(2,1)} %refs_5_.3) | copy-start | bytes 3145732
  14.7 19.1 %copy-start.50 = (f32[256,1024]{1,0:T(8,128)S(1)}, f32[256,1024]{1,0:T(8,128)}, u32[]{:S(2)}) copy-start(f32[256,1024]{1,0:T(8,128)} %get-tuple-element.160.part_ref) | copy-start | bytes 3145732
  17.8 45.7 %collective-permute-start.4 = (f32[8,256,256]{2,1,0:T(8,128)}, f32[8,256,256]{2,1,0:T(8,128)}, u32[]{:S(2)}, u32[]{:S(2)}) collective-permute-start(f32[8,256,256]{2,1,0:T(8,128)} %pack_pixels.2), channel_id=1, source_target_pairs={{0,2},{2,0},{4,6},{6,4},{8,10},{10,8},{12,14},{14,12},{16,18},{18,... | collective-permute-start | bytes 6291464 | tf_op jit(solution)/shard_map/ppermute | solution.py:961
  21.5 42.0 %collective-permute-start.5 = (f32[8,256,256]{2,1,0:T(8,128)}, f32[8,256,256]{2,1,0:T(8,128)}, u32[]{:S(2)}, u32[]{:S(2)}) collective-permute-start(f32[8,256,256]{2,1,0:T(8,128)} %pack_pixels.3), channel_id=1, source_target_pairs={{0,2},{2,0},{4,6},{6,4},{8,10},{10,8},{12,14},{14,12},{16,18},{18,... | collective-permute-start | bytes 6291464 | tf_op jit(solution)/shard_map/ppermute | solution.py:961
  32.0 24.7 %collective-permute-start.1 = (f32[256,1024]{1,0:T(8,128)S(1)}, f32[256,1024]{1,0:T(8,128)S(1)}, u32[]{:S(2)}, u32[]{:S(2)}) collective-permute-start(f32[256,1024]{1,0:T(8,128)S(1)} %copy-done.51), channel_id=1, source_target_pairs={{0,1},{1,0},{2,3},{3,2},{4,5},{5,4},{6,7},{7,6},{8,9},{9,8},{10,11... | collective-permute-start | bytes 3145736 | tf_op jit(solution)/shard_map/ppermute | solution.py:961
  38.2 19.9 %copy-start.36 = (bf16[256,512]{1,0:T(8,128)(2,1)}, bf16[256,512]{1,0:T(8,128)(2,1)S(1)}, u32[]{:S(2)}) copy-start(bf16[256,512]{1,0:T(8,128)(2,1)S(1)} %get-tuple-element.177.o_ref.ma_ref) | copy-start | bytes 786436
  38.2 43.3 %copy-start.61 = (f32[256,1024]{1,0:T(8,128)}, f32[256,1024]{1,0:T(8,128)S(1)}, u32[]{:S(2)}) copy-start(f32[256,1024]{1,0:T(8,128)S(1)} %get-tuple-element.170.x0_ref.refs_4_) | copy-start | bytes 3145732
  38.2 24.3 %copy-start.9 = (f32[4,256,256]{2,1,0:T(8,128)}, f32[4,256,256]{2,1,0:T(8,128)S(1)}, u32[]{:S(2)}) copy-start(f32[4,256,256]{2,1,0:T(8,128)S(1)} %collective-permute-done.3.la_ref.lb_ref) | copy-start | bytes 3145732
  40.0 49.2 %collective-permute-start.7 = (f32[4,256,256]{2,1,0:T(8,128)}, f32[4,256,256]{2,1,0:T(8,128)}, u32[]{:S(2)}, u32[]{:S(2)}) collective-permute-start(f32[4,256,256]{2,1,0:T(8,128)} %get-tuple-element.178), channel_id=1, source_target_pairs={{0,2},{2,0},{4,6},{6,4},{8,10},{10,8},{12,14},{14,12},{16,18},{18,... | collective-permute-start | bytes 3145736 | tf_op jit(solution)/shard_map/ppermute | solution.py:961
  56.7 23.7 %collective-permute-start.2 = (f32[256,1024]{1,0:T(8,128)S(1)}, f32[256,1024]{1,0:T(8,128)S(1)}, u32[]{:S(2)}, u32[]{:S(2)}) collective-permute-start(f32[256,1024]{1,0:T(8,128)S(1)} %get-tuple-element.173.opart_ref), channel_id=1, source_target_pairs={{0,1},{1,0},{2,3},{3,2},{4,5},{5,4},{6,7},{7,6},{8,9},{9,8},{10,11... | collective-permute-start | bytes 3145736 | tf_op jit(solution)/shard_map/ppermute | solution.py:961
  58.1 23.4 %copy-start = (bf16[2048,1024]{1,0:T(8,128)(2,1)S(1)}, bf16[2048,1024]{1,0:T(8,128)(2,1)}, u32[]{:S(2)}) copy-start(bf16[2048,1024]{1,0:T(8,128)(2,1)} %wfc2_ref.7) | copy-start | bytes 12582916
  58.1 23.4 %copy-start.45 = (bf16[1024,2048]{1,0:T(8,128)(2,1)S(1)}, bf16[1024,2048]{1,0:T(8,128)(2,1)}, u32[]{:S(2)}) copy-start(bf16[1024,2048]{1,0:T(8,128)(2,1)} %wfc1_ref.5) | copy-start | bytes 12582916
  58.1 23.4 %copy-start.54 = (f32[2048]{0:T(1024)S(1)}, f32[2048]{0:T(1024)}, u32[]{:S(2)}) copy-start(f32[2048]{0:T(1024)} %param.36) | copy-start | bytes 24580
  58.1 23.4 %copy-start.56 = (f32[1024]{0:T(1024)S(1)}, f32[1024]{0:T(1024)}, u32[]{:S(2)}) copy-start(f32[1024]{0:T(1024)} %param.32) | copy-start | bytes 12292
  58.1 23.4 %copy-start.57 = (f32[1024]{0:T(1024)S(1)}, f32[1024]{0:T(1024)}, u32[]{:S(2)}) copy-start(f32[1024]{0:T(1024)} %param.34) | copy-start | bytes 12292
  58.2 23.4 %copy-start.58 = (f32[1024]{0:T(1024)S(1)}, f32[1024]{0:T(1024)}, u32[]{:S(2)}) copy-start(f32[1024]{0:T(1024)} %param.33) | copy-start | bytes 12292
  63.4 18.1 %copy-start.38 = (bf16[256,512]{1,0:T(8,128)(2,1)}, bf16[256,512]{1,0:T(8,128)(2,1)S(1)}, u32[]{:S(2)}) copy-start(bf16[256,512]{1,0:T(8,128)(2,1)S(1)} %get-tuple-element.185.o_ref.mb_ref) | copy-start | bytes 786436
  63.4 41.4 %copy-start.40 = (f32[256,1024]{1,0:T(8,128)}, f32[256,1024]{1,0:T(8,128)S(1)}, u32[]{:S(2)}) copy-start(f32[256,1024]{1,0:T(8,128)S(1)} %get-tuple-element.191.x0_ref.refs_4_) | copy-start | bytes 3145732
  64.3 24.9 %collective-permute-start.8 = (f32[4,256,256]{2,1,0:T(8,128)S(1)}, f32[4,256,256]{2,1,0:T(8,128)S(1)}, u32[]{:S(2)}, u32[]{:S(2)}) collective-permute-start(f32[4,256,256]{2,1,0:T(8,128)S(1)} %get-tuple-element.186), channel_id=1, source_target_pairs={{0,2},{2,0},{4,6},{6,4},{8,10},{10,8},{12,14},{14,12},{16,18},{18,... | collective-permute-start | bytes 3145736 | tf_op jit(solution)/shard_map/ppermute | solution.py:961
  80.4 23.3 %collective-permute-start.6 = (f32[256,1024]{1,0:T(8,128)S(1)}, f32[256,1024]{1,0:T(8,128)S(1)}, u32[]{:S(2)}, u32[]{:S(2)}) collective-permute-start(f32[256,1024]{1,0:T(8,128)S(1)} %get-tuple-element.192.opart_ref), channel_id=1, source_target_pairs={{0,1},{1,0},{2,3},{3,2},{4,5},{5,4},{6,7},{7,6},{8,9},{9,8},{10,11... | collective-permute-start | bytes 3145736 | tf_op jit(solution)/shard_map/ppermute | solution.py:961
  89.2 38.8 %copy-start.22 = (f32[256,1024]{1,0:T(8,128)}, f32[256,1024]{1,0:T(8,128)S(1)}, u32[]{:S(2)}) copy-start(f32[256,1024]{1,0:T(8,128)S(1)} %get-tuple-element.188.refs_4_) | copy-start | bytes 3145732
  89.2 20.6 %copy-start.13 = (f32[4,256,256]{2,1,0:T(8,128)}, f32[4,256,256]{2,1,0:T(8,128)S(1)}, u32[]{:S(2)}) copy-start(f32[4,256,256]{2,1,0:T(8,128)S(1)} %collective-permute-done.8.fb_ref) | copy-start | bytes 3145732
  89.2 23.4 %collective-permute-start.12 = (f32[10,256,256]{2,1,0:T(8,128)S(1)}, f32[10,256,256]{2,1,0:T(8,128)S(1)}, u32[]{:S(2)}, u32[]{:S(2)}) collective-permute-start(f32[10,256,256]{2,1,0:T(8,128)S(1)} %get-tuple-element.203), channel_id=1, source_target_pairs={{0,2},{2,0},{4,6},{6,4},{8,10},{10,8},{12,14},{14,12},{16,18},{18,... | collective-permute-start | bytes 7864328 | tf_op jit(solution)/shard_map/ppermute | solution.py:961
  89.3 23.4 %collective-permute-start.11 = (f32[8,256,256]{2,1,0:T(8,128)S(1)}, f32[8,256,256]{2,1,0:T(8,128)S(1)}, u32[]{:S(2)}, u32[]{:S(2)}) collective-permute-start(f32[8,256,256]{2,1,0:T(8,128)S(1)} %get-tuple-element.202), channel_id=1, source_target_pairs={{0,2},{2,0},{4,6},{6,4},{8,10},{10,8},{12,14},{14,12},{16,18},{18,... | collective-permute-start | bytes 6291464 | tf_op jit(solution)/shard_map/ppermute | solution.py:961
  103.8 7.9 %collective-permute-start.9 = (f32[96,1024]{1,0:T(8,128)S(1)}, f32[96,1024]{1,0:T(8,128)S(1)}, u32[]{:S(2)}, u32[]{:S(2)}) collective-permute-start(f32[96,1024]{1,0:T(8,128)S(1)} %get-tuple-element.197.refs_0_), channel_id=1, source_target_pairs={{0,1},{1,0},{2,3},{3,2},{4,5},{5,4},{6,7},{7,6},{8,9},{9,8},{10,11... | collective-permute-start | bytes 1179656 | tf_op jit(solution)/shard_map/ppermute | solution.py:961
  109.8 41.5 %copy-start.24 = (f32[256,1024]{1,0:T(8,128)}, f32[256,1024]{1,0:T(8,128)S(1)}, u32[]{:S(2)}) copy-start(f32[256,1024]{1,0:T(8,128)S(1)} %get-tuple-element.226.refs_2_) | copy-start | bytes 3145732
  109.8 4.5 %collective-permute-start.13 = (f32[8,256,256]{2,1,0:T(8,128)S(1)}, f32[8,256,256]{2,1,0:T(8,128)S(1)}, u32[]{:S(2)}, u32[]{:S(2)}) collective-permute-start(f32[8,256,256]{2,1,0:T(8,128)S(1)} %get-tuple-element.196), channel_id=1, source_target_pairs={{0,2},{2,0},{4,6},{6,4},{8,10},{10,8},{12,14},{14,12},{16,18},{18,... | collective-permute-start | bytes 6291464 | tf_op jit(solution)/shard_map/ppermute | solution.py:961
  109.9 9.0 %collective-permute-start.14 = (f32[10,256,256]{2,1,0:T(8,128)S(1)}, f32[10,256,256]{2,1,0:T(8,128)S(1)}, u32[]{:S(2)}, u32[]{:S(2)}) collective-permute-start(f32[10,256,256]{2,1,0:T(8,128)S(1)} %get-tuple-element.213), channel_id=1, source_target_pairs={{0,2},{2,0},{4,6},{6,4},{8,10},{10,8},{12,14},{14,12},{16,18},{18,... | collective-permute-start | bytes 7864328 | tf_op jit(solution)/shard_map/ppermute | solution.py:961
  111.7 15.4 %collective-permute-start.10 = (f32[160,1024]{1,0:T(8,128)S(1)}, f32[160,1024]{1,0:T(8,128)S(1)}, u32[]{:S(2)}, u32[]{:S(2)}) collective-permute-start(f32[160,1024]{1,0:T(8,128)S(1)} %get-tuple-element.199.refs_1_), channel_id=1, source_target_pairs={{0,1},{1,0},{2,3},{3,2},{4,5},{5,4},{6,7},{7,6},{8,9},{9,8},{10,11... | collective-permute-start | bytes 1966088 | tf_op jit(solution)/shard_map/ppermute | solution.py:961
  118.4 76.5 %copy-start.19 = (f32[4,64,2048]{2,1,0:T(8,128)}, f32[4,64,2048]{2,1,0:T(8,128)S(1)}, u32[]{:S(2)}) copy-start(f32[4,64,2048]{2,1,0:T(8,128)S(1)} %get-tuple-element.223) | copy-start | bytes 6291460
  118.4 47.7 %collective-permute-start.17 = (f32[4,64,2048]{2,1,0:T(8,128)}, f32[4,64,2048]{2,1,0:T(8,128)}, u32[]{:S(2)}, u32[]{:S(2)}) collective-permute-start(f32[4,64,2048]{2,1,0:T(8,128)} %get-tuple-element.212), channel_id=1, source_target_pairs={{0,4},{2,6},{4,0},{6,2},{8,12},{10,14},{12,8},{14,10},{16,20},{18,... | collective-permute-start | bytes 6291464 | tf_op jit(solution)/shard_map/ppermute | solution.py:961
  123.2 18.5 %copy-start.17 = (f32[4,2,64,1024]{3,2,1,0:T(8,128)}, f32[4,2,64,1024]{3,2,1,0:T(8,128)S(1)}, u32[]{:S(2)}) copy-start(f32[4,2,64,1024]{3,2,1,0:T(8,128)S(1)} %get-tuple-element.245) | copy-start | bytes 6291460
  123.2 50.3 %collective-permute-start.21 = (f32[8,64,1024]{2,1,0:T(8,128)}, f32[8,64,1024]{2,1,0:T(8,128)}, u32[]{:S(2)}, u32[]{:S(2)}) collective-permute-start(f32[8,64,1024]{2,1,0:T(8,128)} %bitcast.12), channel_id=1, source_target_pairs={{0,8},{2,10},{4,12},{6,14},{8,0},{10,2},{12,4},{14,6},{16,24},{18,... | collective-permute-start | bytes 6291464 | tf_op jit(solution)/shard_map/ppermute | solution.py:961
  127.1 23.2 %collective-permute-start.15 = (f32[256,1024]{1,0:T(8,128)S(1)}, f32[256,1024]{1,0:T(8,128)S(1)}, u32[]{:S(2)}, u32[]{:S(2)}) collective-permute-start(f32[256,1024]{1,0:T(8,128)S(1)} %mlp_back.1.refs_0_), channel_id=1, source_target_pairs={{0,1},{1,0},{2,3},{3,2},{4,5},{5,4},{6,7},{7,6},{8,9},{9,8},{10,11... | collective-permute-start | bytes 3145736 | tf_op jit(solution)/shard_map/ppermute | solution.py:961
  150.3 8.2 %collective-permute-start.16 = (f32[96,1024]{1,0:T(8,128)S(1)}, f32[96,1024]{1,0:T(8,128)S(1)}, u32[]{:S(2)}, u32[]{:S(2)}) collective-permute-start(f32[96,1024]{1,0:T(8,128)S(1)} %get-tuple-element.231.refs_0_), channel_id=1, source_target_pairs={{0,1},{1,0},{2,3},{3,2},{4,5},{5,4},{6,7},{7,6},{8,9},{9,8},{10,11... | collective-permute-start | bytes 1179656 | tf_op jit(solution)/shard_map/ppermute | solution.py:961
  157.5 11.4 %collective-permute-start.19 = (f32[8,256,256]{2,1,0:T(8,128)S(1)}, f32[8,256,256]{2,1,0:T(8,128)S(1)}, u32[]{:S(2)}, u32[]{:S(2)}) collective-permute-start(f32[8,256,256]{2,1,0:T(8,128)S(1)} %get-tuple-element.230), channel_id=1, source_target_pairs={{0,2},{2,0},{4,6},{6,4},{8,10},{10,8},{12,14},{14,12},{16,18},{18,... | collective-permute-start | bytes 6291464 | tf_op jit(solution)/shard_map/ppermute | solution.py:961
  158.5 10.3 %collective-permute-start.18 = (f32[8,256,256]{2,1,0:T(8,128)S(1)}, f32[8,256,256]{2,1,0:T(8,128)S(1)}, u32[]{:S(2)}, u32[]{:S(2)}) collective-permute-start(f32[8,256,256]{2,1,0:T(8,128)S(1)} %get-tuple-element.237), channel_id=1, source_target_pairs={{0,2},{2,0},{4,6},{6,4},{8,10},{10,8},{12,14},{14,12},{16,18},{18,... | collective-permute-start | bytes 6291464 | tf_op jit(solution)/shard_map/ppermute | solution.py:961
  160.1 24.0 %collective-permute-start.20 = (f32[160,1024]{1,0:T(8,128)S(1)}, f32[160,1024]{1,0:T(8,128)S(1)}, u32[]{:S(2)}, u32[]{:S(2)}) collective-permute-start(f32[160,1024]{1,0:T(8,128)S(1)} %get-tuple-element.243.refs_1_), channel_id=1, source_target_pairs={{0,1},{1,0},{2,3},{3,2},{4,5},{5,4},{6,7},{7,6},{8,9},{9,8},{10,11... | collective-permute-start | bytes 1966088 | tf_op jit(solution)/shard_map/ppermute | solution.py:961
  167.5 27.4 %collective-permute-start.23 = (f32[2,64,2048]{2,1,0:T(8,128)S(1)}, f32[2,64,2048]{2,1,0:T(8,128)S(1)}, u32[]{:S(2)}, u32[]{:S(2)}) collective-permute-start(f32[2,64,2048]{2,1,0:T(8,128)S(1)} %slice_add_fusion), channel_id=1, source_target_pairs={{0,8},{2,10},{4,12},{6,14},{8,0},{10,2},{12,4},{14,6},{16,24},{18,... | collective-permute-start | bytes 3145736 | tf_op jit(solution)/shard_map/ppermute | solution.py:961
  182.3 46.9 %collective-permute-start.25 = (f32[8,64,1024]{2,1,0:T(8,128)}, f32[8,64,1024]{2,1,0:T(8,128)}, u32[]{:S(2)}, u32[]{:S(2)}) collective-permute-start(f32[8,64,1024]{2,1,0:T(8,128)} %pad_maximum_fusion), channel_id=1, source_target_pairs={{0,4},{2,6},{4,0},{6,2},{8,12},{10,14},{12,8},{14,10},{16,20},{18,... | collective-permute-start | bytes 6291464 | tf_op jit(solution)/shard_map/ppermute | solution.py:961
  184.1 48.7 %collective-permute-start.27 = (f32[4,64,1024]{2,1,0:T(8,128)}, f32[4,64,1024]{2,1,0:T(8,128)}, u32[]{:S(2)}, u32[]{:S(2)}) collective-permute-start(f32[4,64,1024]{2,1,0:T(8,128)} %get-tuple-element.251), channel_id=1, source_target_pairs={{0,8},{2,10},{4,12},{6,14},{8,0},{10,2},{12,4},{14,6},{16,24},{18,... | collective-permute-start | bytes 3145736 | tf_op jit(solution)/shard_map/ppermute | solution.py:961
  184.1 23.5 %collective-permute-start.22 = (f32[256,1024]{1,0:T(8,128)S(1)}, f32[256,1024]{1,0:T(8,128)S(1)}, u32[]{:S(2)}, u32[]{:S(2)}) collective-permute-start(f32[256,1024]{1,0:T(8,128)S(1)} %attn_in_back.1.refs_0_), channel_id=1, source_target_pairs={{0,1},{1,0},{2,3},{3,2},{4,5},{5,4},{6,7},{7,6},{8,9},{9,8},{10,11... | collective-permute-start | bytes 3145736 | tf_op jit(solution)/shard_map/ppermute | solution.py:961
  184.6 25.7 %copy-start.15 = (bf16[384,1024]{1,0:T(8,128)(2,1)S(1)}, bf16[384,1024]{1,0:T(8,128)(2,1)}, u32[]{:S(2)}) copy-start(bf16[384,1024]{1,0:T(8,128)(2,1)} %wrgb_ref.7) | copy-start | bytes 2359300
  186.7 20.9 %copy-start.41 = (f32[256,1024]{1,0:T(8,128)S(1)}, f32[256,1024]{1,0:T(8,128)}, u32[]{:S(2)}) copy-start(f32[256,1024]{1,0:T(8,128)} %copy-done.40) | copy-start | bytes 3145732
  194.9 17.9 %copy-start.66 = (f32[2,64,2048]{2,1,0:T(8,128)}, f32[2,64,2048]{2,1,0:T(8,128)S(1)}, u32[]{:S(2)}) copy-start(f32[2,64,2048]{2,1,0:T(8,128)S(1)} %collective-permute-done.23) | copy-start | bytes 3145732
  197.2 41.0 %collective-permute-start.28 = (f32[1,64,2048]{2,1,0:T(8,128)}, f32[1,64,2048]{2,1,0:T(8,128)}, u32[]{:S(2)}, u32[]{:S(2)}) collective-permute-start(f32[1,64,2048]{2,1,0:T(8,128)} %slice_add_fusion.5), channel_id=1, source_target_pairs={{0,16},{2,18},{4,20},{6,22},{8,24},{10,26},{12,28},{14,30},{16,0},... | collective-permute-start | bytes 1572872 | tf_op jit(solution)/shard_map/ppermute | solution.py:961
  209.8 23.0 %collective-permute-start.26 = (f32[256,1024]{1,0:T(8,128)}, f32[256,1024]{1,0:T(8,128)}, u32[]{:S(2)}, u32[]{:S(2)}) collective-permute-start(f32[256,1024]{1,0:T(8,128)} %mlp_out.2), channel_id=1, source_target_pairs={{0,1},{1,0},{2,3},{3,2},{4,5},{5,4},{6,7},{7,6},{8,9},{9,8},{10,11... | collective-permute-start | bytes 3145736 | tf_op jit(solution)/shard_map/ppermute | solution.py:961
  210.3 2.7 collective-permute-start.24
  217.7 50.3 %collective-permute-start.30 = (f32[4,64,1024]{2,1,0:T(8,128)}, f32[4,64,1024]{2,1,0:T(8,128)}, u32[]{:S(2)}, u32[]{:S(2)}) collective-permute-start(f32[4,64,1024]{2,1,0:T(8,128)} %get-tuple-element.273), channel_id=1, source_target_pairs={{0,8},{2,10},{4,12},{6,14},{8,0},{10,2},{12,4},{14,6},{16,24},{18,... | collective-permute-start | bytes 3145736 | tf_op jit(solution)/shard_map/ppermute | solution.py:961
  234.7 15.2 %collective-permute-start.29 = (f32[2,64,1024]{2,1,0:T(8,128)}, f32[2,64,1024]{2,1,0:T(8,128)}, u32[]{:S(2)}, u32[]{:S(2)}) collective-permute-start(f32[2,64,1024]{2,1,0:T(8,128)} %slice_add_fusion.3), channel_id=1, source_target_pairs={{0,4},{2,6},{4,0},{6,2},{8,12},{10,14},{12,8},{14,10},{16,20},{18,... | collective-permute-start | bytes 1572872 | tf_op jit(solution)/shard_map/ppermute | solution.py:961
  235.1 32.9 %copy-start.34 = (f32[4,64,1024]{2,1,0:T(8,128)S(1)}, f32[4,64,1024]{2,1,0:T(8,128)}, u32[]{:S(2)}) copy-start(f32[4,64,1024]{2,1,0:T(8,128)} %copy-done.33) | copy-start | bytes 3145732
  235.1 41.0 %collective-permute-start.32 = (f32[4,72,1024]{2,1,0:T(8,128)}, f32[4,72,1024]{2,1,0:T(8,128)S(1)}, u32[]{:S(2)}, u32[]{:S(2)}) collective-permute-start(f32[4,72,1024]{2,1,0:T(8,128)} %copy-done.47), channel_id=1, source_target_pairs={{0,4},{2,6},{4,0},{6,2},{8,12},{10,14},{12,8},{14,10},{16,20},{18,... | collective-permute-start | bytes 3538952 | tf_op jit(solution)/shard_map/ppermute | solution.py:961
  236.7 42.3 %collective-permute-start.33 = (f32[2,64,1024]{2,1,0:T(8,128)}, f32[2,64,1024]{2,1,0:T(8,128)S(1)}, u32[]{:S(2)}, u32[]{:S(2)}) collective-permute-start(f32[2,64,1024]{2,1,0:T(8,128)} %get-tuple-element.304), channel_id=1, source_target_pairs={{0,8},{2,10},{4,12},{6,14},{8,0},{10,2},{12,4},{14,6},{16,24},{18,... | collective-permute-start | bytes 1572872 | tf_op jit(solution)/shard_map/ppermute | solution.py:961
  238.2 35.1 %collective-permute-start.31 = (f32[2,64,1024]{2,1,0:T(8,128)}, f32[2,64,1024]{2,1,0:T(8,128)S(1)}, u32[]{:S(2)}, u32[]{:S(2)}) collective-permute-start(f32[2,64,1024]{2,1,0:T(8,128)} %get-tuple-element.303), channel_id=1, source_target_pairs={{0,16},{2,18},{4,20},{6,22},{8,24},{10,26},{12,28},{14,30},{16,0},... | collective-permute-start | bytes 1572872 | tf_op jit(solution)/shard_map/ppermute | solution.py:961
  250.9 34.6 %collective-permute-start.35 = (f32[1,64,1024]{2,1,0:T(8,128)S(1)}, f32[1,64,1024]{2,1,0:T(8,128)S(1)}, u32[]{:S(2)}, u32[]{:S(2)}) collective-permute-start(f32[1,64,1024]{2,1,0:T(8,128)S(1)} %slice_add_fusion.9), channel_id=1, source_target_pairs={{0,16},{2,18},{4,20},{6,22},{8,24},{10,26},{12,28},{14,30},{16,0},... | collective-permute-start | bytes 786440 | tf_op jit(solution)/shard_map/ppermute | solution.py:961
  269.2 13.2 %collective-permute-start.34 = (f32[2,64,1024]{2,1,0:T(8,128)S(1)}, f32[2,64,1024]{2,1,0:T(8,128)S(1)}, u32[]{:S(2)}, u32[]{:S(2)}) collective-permute-start(f32[2,64,1024]{2,1,0:T(8,128)S(1)} %slice_add_fusion.2), channel_id=1, source_target_pairs={{0,4},{2,6},{4,0},{6,2},{8,12},{10,14},{12,8},{14,10},{16,20},{18,... | collective-permute-start | bytes 1572872 | tf_op jit(solution)/shard_map/ppermute | solution.py:961
  274.7 29.1 %collective-permute-start.38 = (f32[256,1024]{1,0:T(8,128)S(1)}, f32[256,1024]{1,0:T(8,128)S(1)}, u32[]{:S(2)}, u32[]{:S(2)}) collective-permute-start(f32[256,1024]{1,0:T(8,128)S(1)} %copy-done.12), channel_id=1, source_target_pairs={{0,1},{1,0},{2,3},{3,2},{4,5},{5,4},{6,7},{7,6},{8,9},{9,8},{10,11... | collective-permute-start | bytes 3145736 | tf_op jit(solution)/shard_map/ppermute | solution.py:961
  276.1 25.2 %collective-permute-start.36 = (f32[2,72,1024]{2,1,0:T(8,128)S(1)}, f32[2,72,1024]{2,1,0:T(8,128)S(1)}, u32[]{:S(2)}, u32[]{:S(2)}) collective-permute-start(f32[2,72,1024]{2,1,0:T(8,128)S(1)} %slice_add_fusion.1), channel_id=1, source_target_pairs={{0,8},{2,10},{4,12},{6,14},{8,0},{10,2},{12,4},{14,6},{16,24},{18,... | collective-permute-start | bytes 1769480 | tf_op jit(solution)/shard_map/ppermute | solution.py:961
  280.1 21.8 %collective-permute-start.37 = (f32[1,64,1024]{2,1,0:T(8,128)S(1)}, f32[1,64,1024]{2,1,0:T(8,128)S(1)}, u32[]{:S(2)}, u32[]{:S(2)}) collective-permute-start(f32[1,64,1024]{2,1,0:T(8,128)S(1)} %slice_add_fusion.8), channel_id=1, source_target_pairs={{0,16},{2,18},{4,20},{6,22},{8,24},{10,26},{12,28},{14,30},{16,0},... | collective-permute-start | bytes 786440 | tf_op jit(solution)/shard_map/ppermute | solution.py:961
  283.3 27.8 %collective-permute-start.39 = (f32[1,64,1024]{2,1,0:T(8,128)S(1)}, f32[1,64,1024]{2,1,0:T(8,128)S(1)}, u32[]{:S(2)}, u32[]{:S(2)}) collective-permute-start(f32[1,64,1024]{2,1,0:T(8,128)S(1)} %slice_add_fusion.7), channel_id=1, source_target_pairs={{0,16},{2,18},{4,20},{6,22},{8,24},{10,26},{12,28},{14,30},{16,0},... | collective-permute-start | bytes 786440 | tf_op jit(solution)/shard_map/ppermute | solution.py:961
  301.4 15.5 %collective-permute-start.40 = (f32[1,72,1024]{2,1,0:T(8,128)S(1)}, f32[1,72,1024]{2,1,0:T(8,128)S(1)}, u32[]{:S(2)}, u32[]{:S(2)}) collective-permute-start(f32[1,72,1024]{2,1,0:T(8,128)S(1)} %slice_add_fusion.6), channel_id=1, source_target_pairs={{0,16},{2,18},{4,20},{6,22},{8,24},{10,26},{12,28},{14,30},{16,0},... | collective-permute-start | bytes 884744 | tf_op jit(solution)/shard_map/ppermute | solution.py:961
  (47 other events, 307.2 us)
